TPU v7x, 128 devices: a whole 4x4x4 slice. The times are simulated.
128 devices in a mesh: loop: 16 (over y_lo, z, core), red: 8 (over y_hi, x).
Axes of the slice: x: 4, y: 4 (y_hi: 2, y_lo: 2; y = y_hi * 2 + y_lo), z: 4, core: 2. Of those that a mesh axis runs over, the one named last changes fastest.
Arguments:
- query_ids: int32 [512], replicated, may hold values from 0 to 8191
- layer_index: int32 [1], replicated, may hold values from 0 to 3
- gradient: bfloat16 [8192, 28672], P('loop', 'red'), may hold values from -6 to 6
- out_basis: bfloat16 [8192, 8192], P('loop'), may hold values from -0.0625 to 0.0625
- in_basis: bfloat16 [28672, 28672], P('red', 'loop'), may hold values from -0.03125 to 0.03125
- out_eigen: float32 [4, 8192], replicated, may hold values from 0.2 to 2
- in_eigen: float32 [4, 28672], P(None, 'loop'), may hold values from 0.2 to 2
Outputs:
- preconditioned: bfloat16 [512, 28672], P('loop', 'red')
All inputs are finite; a program needn't handle non-finite values.
Results may differ from a plain program's by a relative error of at most 0.0055.
Values may be sent and summed in bfloat16 or wider, within the bound.
No kernel may reach another device: no remote copies, remote signals or barrier semaphores. Data moves between devices by JAX's collectives and lax.ppermute only.
A program may use at most 128 MiB of HBM per device.

v0:
```python
import jax
import jax.numpy as jnp
from jax import lax
from jax.sharding import PartitionSpec as P

damping = 0.05


def per_device(query_ids, layer_index, gradient, out_basis, in_basis, out_eigen, in_eigen):
    selected = jnp.take(out_basis, query_ids, axis=1)
    local_rows = lax.dot_general(
        selected, gradient, (((0,), (0,)), ((), ())), preferred_element_type=jnp.float32
    )
    rows_w = lax.psum(local_rows, "loop").astype(jnp.bfloat16)
    eigen_rows = jnp.take(jnp.take(out_eigen, layer_index, axis=0)[0], query_ids)
    eigen_cols = jnp.take(in_eigen, layer_index, axis=0)[0]
    local_rot = jnp.dot(rows_w, in_basis, preferred_element_type=jnp.float32)
    rotated = lax.psum(local_rot, "red")
    scaled = (rotated / (eigen_rows[:, None] * eigen_cols[None, :] + damping)).astype(jnp.bfloat16)
    result = lax.psum_scatter(
        lax.dot_general(
            scaled, in_basis, (((1,), (1,)), ((), ())), preferred_element_type=jnp.float32
        ),
        "loop",
        scatter_dimension=0,
        tiled=True,
    )
    return result.astype(jnp.bfloat16)


def solution(mesh):
    return jax.shard_map(
        per_device,
        mesh=mesh,
        in_specs=(
            P(),
            P(),
            P("loop", "red"),
            P("loop", None),
            P("red", "loop"),
            P(),
            P(None, "loop"),
        ),
        out_specs=P("loop", "red"),
        check_vma=False,
    )
```

profile of v0, /device:TPU:1, one launch (start us, length us, event | category | flops | bytes accessed | tf_op | source)
XLA Modules:
  0.0 338.2 jit_solution(16668026155570244711)
XLA Ops:
  6.5 0.0 all-reduce.3.cloned.1.call-start
  7.2 0.7 compare_select_fusion
  7.9 0.9 broadcast_select_fusion
  8.8 3.1 gather_fusion.1
  12.0 0.7 broadcast_select_fusion.2
  12.7 11.9 %copy.9 = bf16[512,8192]{0,1:T(8,128)(2,1)} copy(bf16[512,8192]{1,0:T(8,128)(2,1)} %param.10) | data formatting | bytes 16777216 | tf_op args[3]
  24.6 6.4 %gather_fusion = bf16[512,512]{1,0:T(8,128)(2,1)S(1)} fusion(bf16[512,8192]{0,1:T(8,128)(2,1)} %copy.9, s32[1024]{0:T(1024)S(1)} %pad_clamp_fusion), kind=kCustom, calls=%fused_computation | custom fusion | bytes 1050624 | tf_op jit(solution)/shard_map/jit(_take)/gather | solution.py:10
  31.1 7.1 %fusion.6 = f32[512,3584]{1,0:T(8,128)} fusion(bf16[512,3584]{1,0:T(8,128)(2,1)} %param.9, bf16[512,512]{1,0:T(8,128)(2,1)S(1)} %gather_fusion, pred[512]{0:T(512)(128)(4,1)S(1)} %get-tuple-element.28), kind=kOutput, calls=%fused_computation.9 | convolution fusion | flops 1879310336 | bytes 11534848 | tf_op jit(solution)/shard_map/dot_general | solution.py:11
  38.2 91.5 %all-reduce.4 = bf16[512,3584]{1,0:T(8,128)(2,1)} all-reduce(f32[512,3584]{1,0:T(8,128)} %fusion.6), channel_id=1, replica_groups=mesh['loop'=16,'red'=8] {'loop'}, use_global_device_ids=true, to_apply=%region_0.1 | all-reduce | flops 1835008 | bytes 11010048 | tf_op jit(solution)/shard_map/psum | solution.py:14
  129.7 13.4 %fusion.13 = f32[512,1792]{1,0:T(8,128)} fusion(bf16[512,3584]{1,0:T(8,128)(2,1)} %all-reduce.4, bf16[3584,1792]{1,0:T(8,128)(2,1)} %param.11), kind=kOutput, calls=%fused_computation.22 | convolution fusion | flops 6576668672 | bytes 20185088 | tf_op jit(solution)/shard_map/dot_general | solution.py:17
  143.1 0.0 all-reduce.3.cloned.1.call-update
  143.1 0.0 reduce-scatter.2.cloned.1.call-start
  143.2 0.8 fusion.10
  144.0 101.8 %all-reduce.3.cloned.1.call-done = f32[512,1792]{1,0:T(8,128)} async-done(((f32[512,1792]{1,0:T(8,128)}), f32[512,1792]{1,0:T(8,128)}) %all-reduce.3.cloned.1.call-update) | async-done | bytes 3670032 | tf_op jit(solution)/shard_map/psum | solution.py:18
  245.8 12.9 %fusion.2 = f32[512,3584]{1,0:T(8,128)} fusion(bf16[3584,1792]{1,0:T(8,128)(2,1)} %param.11, f32[512,1792]{1,0:T(8,128)} %all-reduce.3.cloned.1.call-done, f32[1792]{0:T(1024)S(1)} %fusion.10, f32[512]{0:T(512)S(1)} %get-tuple-element.27), kind=kOutput, calls=%fused_computation.5 | convolution fusion | flops 6580338688 | bytes 23864320 | tf_op jit(solution)/shard_map/dot_general | solution.py:21
  258.7 0.0 reduce-scatter.2.cloned.1.call-update
  258.8 70.9 %reduce-scatter.2.cloned.1.call-done = f32[32,3584]{1,0:T(8,128)} async-done(((f32[512,3584]{1,0:T(8,128)}), f32[32,3584]{1,0:T(8,128)}) %reduce-scatter.2.cloned.1.call-update) | async-done | bytes 458768 | tf_op jit(solution)/shard_map/reduce_scatter | solution.py:20
  329.7 1.7 convert_element_type.11
  (1 shorter events, 0.0 us)
Async XLA Ops:
  6.5 239.3 %all-reduce.3.cloned.1.call-start = ((), (), s32[]{:S(2)}) async-start(), calls=%async_computation.1 | async-start | bytes 7340032 | tf_op jit(solution)/shard_map/psum | solution.py:18
  143.1 186.5 %reduce-scatter.2.cloned.1.call-start = ((), (), s32[]{:S(2)}) async-start(), calls=%async_computation.2 | async-start | bytes 7798784 | tf_op jit(solution)/shard_map/reduce_scatter | solution.py:20
Sparse Core Ops, SparseCore 0:
  143.3 102.4 all-reduce.2
  258.9 70.7 reduce-scatter.1
where the time goes:
time: 342 us; the launch traced here: 338 us
  waiting for transfers between devices  173 us (51%)
  blocking collectives  91.5 us (27%)
  matrix products  33.5 us (10%)
  local copies, waits for them, and re-layouts  21.5 us (6%)
  between operations  14.1 us (4%)
  other arithmetic  4.84 us (1%)
    psum x1, waiting for transfers between devices, per_device(): rotated = lax.psum(local_rot, 'red')  102 us
    psum x1, blocking collectives, per_device(): rows_w = lax.psum(local_rows, 'loop').astype(jnp.bfloat16)  91.5 us
    reduce_scatter x1, waiting for transfers between devices, per_device(): lax.psum_scatter(lax.dot_general(scaled, in_basis, (((1,), (1,)), ((), ()...  70.9 us
    dot_general x1, matrix products, per_device(): local_rot = jnp.dot(rows_w, in_basis, preferred_element_type=jnp.float32)  13.4 us
    dot_general x1, matrix products, per_device(): lax.dot_general(scaled, in_basis, (((1,), (1,)), ((), ())), preferred_ele...  12.9 us
    unnamed x1, local copies, waits for them, and re-layouts  11.9 us
    dot_general x1, matrix products, per_device(): lax.dot_general(selected, gradient, (((0,), (0,)), ((), ())), preferred_e...  7.14 us
  transfers between devices with their start and end apart: 2, of which 2 were waited for; matrix products, arithmetic and copies ran while one was open for 0% of the time, Pallas kernels for 0%

commit v1 on v0

v1 whole, which is shorter than its diff:
```python
import functools

import jax
import jax.numpy as jnp
from jax import lax
from jax.experimental import pallas as pl
from jax.experimental.pallas import tpu as pltpu
from jax.sharding import PartitionSpec as P

damping = 0.05
CHUNKS = 2
F32, BF16 = jnp.float32, jnp.bfloat16
VMEM = pl.BlockSpec(memory_space=pltpu.VMEM)
SMEM = pl.BlockSpec(memory_space=pltpu.SMEM)
NN = (((1,), (0,)), ((), ()))
NT = (((1,), (1,)), ((), ()))


def cost(flops, nbytes):
    return pl.CostEstimate(flops=flops, bytes_accessed=nbytes, transcendentals=0)


def dot(a, b, dims=NN):
    return lax.dot_general(a, b, dims, preferred_element_type=F32)


def select_kernel(ids_ref, basis_ref, out_ref, acc_ref):
    step = pl.program_id(0)
    width = basis_ref.shape[1]
    lanes = lax.broadcasted_iota(jnp.int32, (ids_ref.shape[0], width), 1)
    hot = jnp.where(lanes + step * width == ids_ref[...], 1.0, 0.0).astype(BF16)
    part = dot(hot, basis_ref[...], NT)

    @pl.when(step == 0)
    def _():
        acc_ref[...] = part

    @pl.when(step > 0)
    def _():
        acc_ref[...] += part

    @pl.when(step == pl.num_programs(0) - 1)
    def _():
        out_ref[...] = acc_ref[...].astype(BF16)


def select(ids, basis):
    rows, width = basis.shape
    queries, block = ids.shape[0], 1024
    return pl.pallas_call(
        select_kernel,
        grid=(width // block,),
        in_specs=[
            pl.BlockSpec((queries, 1), lambda i: (0, 0)),
            pl.BlockSpec((rows, block), lambda i: (0, i)),
        ],
        out_specs=pl.BlockSpec((queries, rows), lambda i: (0, 0)),
        out_shape=jax.ShapeDtypeStruct((queries, rows), BF16),
        scratch_shapes=[pltpu.VMEM((queries, rows), F32)],
        cost_estimate=cost(2 * queries * rows * width, rows * width * 2),
        compiler_params=pltpu.CompilerParams(vmem_limit_bytes=16 << 20),
    )(ids[:, None], basis)


def pair_kernel(a1, b1, a2, b2, out, *, tile):
    for j in range(out.shape[1] // tile):
        at = pl.ds(j * tile, tile)
        out[:, at] = (dot(a1[...], b1[:, at]) + dot(a2[...], b2[:, at])).astype(out.dtype)


def pair_matmul(a1, b1, a2, b2):
    m, k = a1.shape
    n = b1.shape[1]
    return pl.pallas_call(
        functools.partial(pair_kernel, tile=256),
        in_specs=[VMEM] * 4,
        out_specs=VMEM,
        out_shape=jax.ShapeDtypeStruct((m, n), BF16),
        cost_estimate=cost(4 * m * k * n, 2 * (2 * m * k + 2 * k * n + m * n)),
        compiler_params=pltpu.CompilerParams(vmem_limit_bytes=16 << 20),
    )(a1, b1, a2, b2)


def rotate_kernel(core, own, other, basis, out, *, tile):
    half = own.shape[1]
    mine = pl.multiple_of(core[0] * half, half)
    theirs = pl.multiple_of((1 - core[0]) * half, half)
    for j in range(out.shape[1] // tile):
        at = pl.ds(j * tile, tile)
        total = dot(own[...], basis[pl.ds(mine, half), at])
        total += dot(other[...], basis[pl.ds(theirs, half), at])
        out[:, at] = total.astype(out.dtype)


def rotate(core, own, other, basis):
    m, half = own.shape
    n = basis.shape[1]
    return pl.pallas_call(
        functools.partial(rotate_kernel, tile=256),
        in_specs=[SMEM, VMEM, VMEM, VMEM],
        out_specs=VMEM,
        out_shape=jax.ShapeDtypeStruct((m, n), BF16),
        cost_estimate=cost(4 * m * half * n, 2 * (2 * m * half + 2 * half * n + m * n)),
        compiler_params=pltpu.CompilerParams(vmem_limit_bytes=32 << 20),
    )(core, own, other, basis)


def back_kernel(core, scaled, basis, other, own, *, tile):
    half = scaled.shape[0] // 2
    mine = pl.multiple_of(core[0] * half, half)
    theirs = pl.multiple_of((1 - core[0]) * half, half)
    for j in range(basis.shape[0] // tile):
        at = pl.ds(j * tile, tile)
        block = basis[at, :]
        other[:, at] = dot(scaled[pl.ds(theirs, half), :], block, NT).astype(BF16)
        own[:, at] = dot(scaled[pl.ds(mine, half), :], block, NT)


def back(core, scaled, basis):
    m, k = scaled.shape
    n = basis.shape[0]
    return pl.pallas_call(
        functools.partial(back_kernel, tile=256),
        in_specs=[SMEM, VMEM, VMEM],
        out_specs=[VMEM, VMEM],
        out_shape=[
            jax.ShapeDtypeStruct((m // 2, n), BF16),
            jax.ShapeDtypeStruct((m // 2, n), F32),
        ],
        cost_estimate=cost(2 * m * k * n, 2 * (m * k + k * n + m * n)),
        compiler_params=pltpu.CompilerParams(vmem_limit_bytes=32 << 20),
    )(core, scaled, basis)


def per_device(query_ids, layer_index, gradient, out_basis, in_basis, out_eigen, in_eigen):
    loops, reds = lax.axis_size("loop"), lax.axis_size("red")
    chips = loops // 2
    queries = query_ids.shape[0]
    chunk = queries // CHUNKS
    core = lax.axis_index("loop") % 2
    core1 = core[None].astype(jnp.int32)
    high = lax.axis_index("red") // 4
    swap = [(i, i ^ 1) for i in range(loops)]
    same_core = [[2 * i + c for i in range(chips)] for c in range(2)]
    rings = [[4 * h + x for x in range(4)] for h in range(2)]
    flip = [(i, (i + 4) % reds) for i in range(reds)]

    ids = query_ids.reshape(chips, 2, CHUNKS, -1).transpose(2, 1, 0, 3).reshape(queries)
    half = gradient.shape[1] // 2
    theirs = lax.dynamic_slice_in_dim(gradient, (1 - core) * half, half, 1)
    mine = lax.dynamic_slice_in_dim(gradient, core * half, half, 1)
    got = lax.ppermute(theirs, "loop", swap)
    sel = select(ids, out_basis)
    sel_got = lax.ppermute(sel, "loop", swap)

    eigen_rows = jnp.take(jnp.take(out_eigen, layer_index, axis=0)[0], ids)
    eigen_cols = jnp.take(in_eigen, layer_index, axis=0)[0]

    outs = []
    for n in range(CHUNKS):
        rows = slice(n * chunk, (n + 1) * chunk)
        part = pair_matmul(sel[rows], mine, sel_got[rows], got)
        part = lax.all_to_all(part.reshape(chips, -1, half), "loop", 0, 0, axis_index_groups=same_core)
        own = part.astype(F32).sum(0).astype(BF16)
        own = jnp.broadcast_to(own[None], (chips,) + own.shape)
        own = lax.all_to_all(own, "loop", 0, 0, axis_index_groups=same_core).reshape(chunk, half)
        other = lax.ppermute(own, "loop", swap)
        rot = rotate(core1, own, other, in_basis)
        rot = lax.all_to_all(rot.reshape(4, -1, rot.shape[1]), "red", 0, 0, axis_index_groups=rings)
        rot = rot.astype(F32).sum(0)
        piece = rot.shape[0] // 2
        send = lax.dynamic_slice_in_dim(rot, (1 - high) * piece, piece, 0).astype(BF16)
        keep = lax.dynamic_slice_in_dim(rot, high * piece, piece, 0)
        rot = keep + lax.ppermute(send, "red", flip).astype(F32)
        first = n * chunk + (lax.axis_index("red") % 4) * 2 * piece + high * piece
        er = lax.dynamic_slice_in_dim(eigen_rows, first, piece, 0)
        scaled = (rot / (er[:, None] * eigen_cols[None, :] + damping)).astype(BF16)
        far = lax.ppermute(scaled, "red", flip)
        scaled = jnp.where(high == 0, jnp.stack([scaled, far]), jnp.stack([far, scaled]))
        scaled = scaled.reshape(1, 2 * piece, -1)
        scaled = jnp.broadcast_to(scaled, (4,) + scaled.shape[1:])
        scaled = lax.all_to_all(scaled, "red", 0, 0, axis_index_groups=rings).reshape(chunk, -1)
        send, keep = back(core1, scaled, in_basis)
        total = (keep + lax.ppermute(send, "loop", swap).astype(F32)).astype(BF16)
        total = lax.all_to_all(total.reshape(chips, -1, total.shape[1]), "loop", 0, 0, axis_index_groups=same_core)
        outs.append(total.astype(F32).sum(0).astype(BF16))
    return jnp.concatenate(outs, 0)


def solution(mesh):
    return jax.shard_map(
        per_device,
        mesh=mesh,
        in_specs=(
            P(),
            P(),
            P("loop", "red"),
            P("loop", None),
            P("red", "loop"),
            P(),
            P(None, "loop"),
        ),
        out_specs=P("loop", "red"),
        check_vma=False,
    )
```

time: 342 us -> 242 us (0.71)
  waiting for transfers between devices: 173 us -> 75.5 us
  blocking collectives: 91.5 us -> 31.3 us
  starting transfers between devices: 0.04 us -> 49.4 us
  Pallas kernels: 0 us -> 41.8 us
  matrix products: 33.5 us -> 0 us
  between operations: 14.1 us -> 0.92 us
  local copies, waits for them, and re-layouts: 21.5 us -> 33.6 us
    psum x1 -> x0, waiting for transfers between devices: 102 us -> none  [per_device(): rotated = lax.psum(local_rot, 'red')]
    psum x1 -> x0, blocking collectives: 91.5 us -> none  [per_device(): rows_w = lax.psum(local_rows, 'loop').astype(jnp.bfloat16)]
    reduce_scatter x1 -> x0, waiting for transfers between devices: 70.9 us -> none  [per_device(): lax.psum_scatter(lax.dot_general(scaled, in_basis, (((1,), (1,)), ((), ()...]
    all_to_all x0 -> x8, waiting for transfers between devices: none -> 66.7 us  [the longest x2 24.4 us: per_device(): lax.all_to_all(total.reshape(chips, -1, total.shape[1]), 'loop', 0, 0, ax...]
    pallas_call x0 -> x7, Pallas kernels: none -> 41.8 us  [the longest x2 18.1 us: back(): pl.pallas_call(functools.partial(back_kernel, tile=256), in_specs=[SMEM,...]
    dot_general x3 -> x0, matrix products: 33.5 us -> none  [the longest x1 13.4 us: per_device(): local_rot = jnp.dot(rows_w, in_basis, preferred_element_type=jnp.float32)]
    all_to_all x0 -> x8, starting transfers between devices: none -> 32.1 us  [the longest x2 7.52 us: per_device(): lax.all_to_all(rot.reshape(4, -1, rot.shape[1]), 'red', 0, 0, axis_index_...]
    all_to_all x0 -> x2, blocking collectives: none -> 31.3 us  [the longest x1 19.5 us: per_device(): lax.all_to_all(part.reshape(chips, -1, half), 'loop', 0, 0, axis_index_gr...]
  transfers between devices with their start and end apart: 2 -> 18, of which waited for: 2 -> 11; matrix products, arithmetic and copies ran while one was open for 0% -> 5% of each run, Pallas kernels for 0% -> 16%
where the time goes in v1:
time: 242 us; the launch traced here: 241 us
  waiting for transfers between devices  75.5 us (31%)
  starting transfers between devices  49.4 us (20%)
  Pallas kernels  41.8 us (17%)
  local copies, waits for them, and re-layouts  33.6 us (14%)
  blocking collectives  31.3 us (13%)
  other arithmetic  8.01 us (3%)
    all_to_all x2, waiting for transfers between devices, per_device(): lax.all_to_all(total.reshape(chips, -1, total.shape[1]), 'loop', 0, 0, ax...  24.4 us
    unnamed x16, local copies, waits for them, and re-layouts  23.2 us
    all_to_all x2, waiting for transfers between devices, per_device(): lax.all_to_all(own, 'loop', 0, 0, axis_index_groups=same_core)  19.7 us
    all_to_all x1, blocking collectives, per_device(): lax.all_to_all(part.reshape(chips, -1, half), 'loop', 0, 0, axis_index_gr...  19.5 us
    pallas_call x2, Pallas kernels, back(): pl.pallas_call(functools.partial(back_kernel, tile=256), in_specs=[SMEM,...  18.1 us
    all_to_all x1, waiting for transfers between devices, per_device(): lax.all_to_all(part.reshape(chips, -1, half), 'loop', 0, 0, axis_index_gr...  12.6 us
    all_to_all x1, blocking collectives, per_device(): lax.all_to_all(scaled, 'red', 0, 0, axis_index_groups=rings)  11.8 us
    pallas_call x2, Pallas kernels, rotate(): pl.pallas_call(functools.partial(rotate_kernel, tile=256), in_specs=[SMEM...  10.1 us
  transfers between devices with their start and end apart: 18, of which 11 were waited for; matrix products, arithmetic and copies ran while one was open for 5% of the time, Pallas kernels for 16%

profile of v1, /device:TPU:1, one launch (start us, length us, event | category | flops | bytes accessed | tf_op | source)
XLA Modules:
  0.0 240.6 jit_solution(4871053409846091245)
XLA Ops:
  8.7 7.5 %shard_map.73 = bf16[512,512]{1,0:T(8,128)(2,1)S(1)} custom-call(s32[512,1]{1,0:T(8,128)S(1)} %copy.11.ids_ref, bf16[512,8192]{1,0:T(8,128)(2,1)S(1)} %copy-done.6), custom_call_target="tpu_custom_call" | custom-call | flops 4294967296 | bytes 8388608 | tf_op jit(solution)/shard_map/pallas_call | solution.py:50
  20.8 19.5 %all_to_all.50 = bf16[8,32,1792]{2,1,0:T(8,128)(2,1)S(1)} all-to-all(bf16[8,32,1792]{2,1,0:T(8,128)(2,1)S(1)} %bitcast.26), channel_id=1, replica_groups={{0,16,32,48,64,80,96,112},{8,24,40,56,72,88,104,120},{1,17,33,49,65,81,..., dimensions={0} | all-to-all | bytes 1835008 | tf_op jit(solution)/shard_map/all_to_all | solution.py:163
  41.5 3.6 %all-to-all-start.6 = ((bf16[8,32,1792]{2,1,0:T(8,128)(2,1)}), bf16[8,32,1792]{2,1,0:T(8,128)(2,1)S(1)}, u32[]{:S(2)}, u32[]{:S(2)}) async-start(bf16[8,32,1792]{2,1,0:T(8,128)(2,1)} %broadcast_in_dim.64), calls=%async_computation.6 | async-start | bytes 1835008 | tf_op jit(solution)/shard_map/all_to_all | solution.py:166
  45.0 3.6 %shard_map.74 = bf16[256,1792]{1,0:T(8,128)(2,1)} custom-call(bf16[256,512]{1,0:T(8,128)(2,1)S(1)} %get-tuple-element.39.a1, bf16[512,1792]{1,0:T(8,128)(2,1)S(1)} %get-tuple-element.36.b1, bf16[256,512]{1,0:T(8,128)(2,1)S(1)} %get-tuple-element.37.a2, bf16[512,1792]{1,0:T(8,128)(2,1)} %collective-permute-done.1.b2), custom_call_target="tpu_custom_call" | custom-call | flops 939524096 | bytes 5111808 | tf_op jit(solution)/shard_map/pallas_call | solution.py:74
  48.6 7.0 %all-to-all-done.6 = bf16[8,32,1792]{2,1,0:T(8,128)(2,1)S(1)} async-done(((bf16[8,32,1792]{2,1,0:T(8,128)(2,1)}), bf16[8,32,1792]{2,1,0:T(8,128)(2,1)S(1)}, u32[]{:S(2)}, u32[]{:S(2)}) %all-to-all-start.6) | async-done | bytes 917536 | tf_op jit(solution)/shard_map/all_to_all | solution.py:166
  55.6 6.5 %all-to-all-start = ((bf16[8,32,1792]{2,1,0:T(8,128)(2,1)}), bf16[8,32,1792]{2,1,0:T(8,128)(2,1)S(1)}, u32[]{:S(2)}, u32[]{:S(2)}) async-start(bf16[8,32,1792]{2,1,0:T(8,128)(2,1)} %bitcast.2), calls=%async_computation | async-start | bytes 1835008 | tf_op jit(solution)/shard_map/all_to_all | solution.py:163
  63.0 12.6 %all-to-all-done = bf16[8,32,1792]{2,1,0:T(8,128)(2,1)S(1)} async-done(((bf16[8,32,1792]{2,1,0:T(8,128)(2,1)}), bf16[8,32,1792]{2,1,0:T(8,128)(2,1)S(1)}, u32[]{:S(2)}, u32[]{:S(2)}) %all-to-all-start) | async-done | bytes 917536 | tf_op jit(solution)/shard_map/all_to_all | solution.py:163
  76.7 3.8 %all-to-all-start.1 = ((bf16[8,32,1792]{2,1,0:T(8,128)(2,1)}), bf16[8,32,1792]{2,1,0:T(8,128)(2,1)S(1)}, u32[]{:S(2)}, u32[]{:S(2)}) async-start(bf16[8,32,1792]{2,1,0:T(8,128)(2,1)} %broadcast_in_dim.56), calls=%async_computation.1 | async-start | bytes 1835008 | tf_op jit(solution)/shard_map/all_to_all | solution.py:166
  81.2 12.7 %all-to-all-done.1 = bf16[8,32,1792]{2,1,0:T(8,128)(2,1)S(1)} async-done(((bf16[8,32,1792]{2,1,0:T(8,128)(2,1)}), bf16[8,32,1792]{2,1,0:T(8,128)(2,1)S(1)}, u32[]{:S(2)}, u32[]{:S(2)}) %all-to-all-start.1) | async-done | bytes 917536 | tf_op jit(solution)/shard_map/all_to_all | solution.py:166
  94.9 4.6 %copy-done = bf16[3584,1792]{1,0:T(8,128)(2,1)S(1)} copy-done((bf16[3584,1792]{1,0:T(8,128)(2,1)S(1)}, bf16[3584,1792]{1,0:T(8,128)(2,1)}, u32[]{:S(2)}) %copy-start) | copy-done | bytes 12845080
  99.5 5.6 %shard_map.78 = bf16[256,1792]{1,0:T(8,128)(2,1)} custom-call(s32[1]{0:T(128)} %bitcast.core, bf16[256,1792]{1,0:T(8,128)(2,1)S(1)} %bitcast.30, bf16[256,1792]{1,0:T(8,128)(2,1)} %collective-permute-done.6.other, bf16[3584,1792]{1,0:T(8,128)(2,1)S(1)} %copy-done), custom_call_target="tpu_custom_call" | custom-call | flops 3288334336 | bytes 15597568 | tf_op jit(solution)/shard_map/pallas_call | solution.py:98
  105.2 4.0 %all-to-all-start.7 = ((bf16[4,64,1792]{2,1,0:T(8,128)(2,1)}), bf16[4,64,1792]{2,1,0:T(8,128)(2,1)S(1)}, u32[]{:S(2)}, u32[]{:S(2)}) async-start(bf16[4,64,1792]{2,1,0:T(8,128)(2,1)} %bitcast.16), calls=%async_computation.7 | async-start | bytes 1835008 | tf_op jit(solution)/shard_map/all_to_all | solution.py:169
  110.2 4.6 %copy-done.1 = bf16[3584,1792]{1,0:T(8,128)(2,1)S(1)} copy-done((bf16[3584,1792]{1,0:T(8,128)(2,1)S(1)}, bf16[3584,1792]{1,0:T(8,128)(2,1)}, u32[]{:S(2)}) %copy-start.1) | copy-done | bytes 12845080
  114.9 4.4 %shard_map.75 = bf16[256,1792]{1,0:T(8,128)(2,1)} custom-call(s32[1]{0:T(128)} %bitcast.core, bf16[256,1792]{1,0:T(8,128)(2,1)S(1)} %bitcast.28, bf16[256,1792]{1,0:T(8,128)(2,1)S(1)} %collective-permute-done.2.other, bf16[3584,1792]{1,0:T(8,128)(2,1)S(1)} %copy-done.1), custom_call_target="tpu_custom_call" | custom-call | flops 3288334336 | bytes 15597568 | tf_op jit(solution)/shard_map/pallas_call | solution.py:98
  132.3 6.5 %all-to-all-done.2 = bf16[4,64,1792]{2,1,0:T(8,128)(2,1)S(1)} async-done(((bf16[4,64,1792]{2,1,0:T(8,128)(2,1)}), bf16[4,64,1792]{2,1,0:T(8,128)(2,1)S(1)}, u32[]{:S(2)}, u32[]{:S(2)}) %all-to-all-start.2) | async-done | bytes 917536 | tf_op jit(solution)/shard_map/all_to_all | solution.py:169
  153.0 11.8 %all_to_all.51 = bf16[4,64,1792]{2,1,0:T(8,128)(2,1)S(1)} all-to-all(bf16[4,64,1792]{2,1,0:T(8,128)(2,1)S(1)} %broadcast_in_dim.63), channel_id=1, replica_groups={{0,1,2,3},{4,5,6,7},{8,9,10,11},{12,13,14,15},{16,17,18,19},{20,21,22,2..., dimensions={0} | all-to-all | bytes 1835008 | tf_op jit(solution)/shard_map/all_to_all | solution.py:182
  169.3 4.6 %copy-done.2 = bf16[3584,1792]{1,0:T(8,128)(2,1)S(1)} copy-done((bf16[3584,1792]{1,0:T(8,128)(2,1)S(1)}, bf16[3584,1792]{1,0:T(8,128)(2,1)}, u32[]{:S(2)}) %copy-start.2) | copy-done | bytes 12845080
  174.0 9.1 %shard_map.76 = (bf16[128,3584]{1,0:T(8,128)(2,1)}, f32[128,3584]{1,0:T(8,128)S(1)}) custom-call(s32[1]{0:T(128)} %bitcast.core, bf16[256,1792]{1,0:T(8,128)(2,1)S(1)} %bitcast.32, bf16[3584,1792]{1,0:T(8,128)(2,1)S(1)} %copy-done.2), custom_call_target="tpu_custom_call" | custom-call | flops 3288334336 | bytes 15597568 | tf_op jit(solution)/shard_map/pallas_call | solution.py:122
  184.3 5.3 %collective-permute-start.5 = (bf16[128,3584]{1,0:T(8,128)(2,1)}, bf16[128,3584]{1,0:T(8,128)(2,1)}, u32[]{:S(2)}, u32[]{:S(2)}) collective-permute-start(bf16[128,3584]{1,0:T(8,128)(2,1)} %get-tuple-element.10), channel_id=1, source_target_pairs={{0,8},{8,0},{16,24},{24,16},{32,40},{40,32},{48,56},{56,48},{64,72... | collective-permute-start | bytes 2752520 | tf_op jit(solution)/shard_map/ppermute | solution.py:184
  189.6 4.6 %copy-done.3 = bf16[3584,1792]{1,0:T(8,128)(2,1)S(1)} copy-done((bf16[3584,1792]{1,0:T(8,128)(2,1)S(1)}, bf16[3584,1792]{1,0:T(8,128)(2,1)}, u32[]{:S(2)}) %copy-start.3) | copy-done | bytes 12845080
  194.3 9.1 %shard_map.79 = (bf16[128,3584]{1,0:T(8,128)(2,1)}, f32[128,3584]{1,0:T(8,128)S(1)}) custom-call(s32[1]{0:T(128)} %bitcast.core, bf16[256,1792]{1,0:T(8,128)(2,1)S(1)} %bitcast.31, bf16[3584,1792]{1,0:T(8,128)(2,1)S(1)} %copy-done.3), custom_call_target="tpu_custom_call" | custom-call | flops 3288334336 | bytes 15597568 | tf_op jit(solution)/shard_map/pallas_call | solution.py:122
  211.5 11.2 %all-to-all-done.4 = bf16[8,16,3584]{2,1,0:T(8,128)(2,1)S(1)} async-done(((bf16[8,16,3584]{2,1,0:T(8,128)(2,1)}), bf16[8,16,3584]{2,1,0:T(8,128)(2,1)S(1)}, u32[]{:S(2)}, u32[]{:S(2)}) %all-to-all-start.4) | async-done | bytes 917536 | tf_op jit(solution)/shard_map/all_to_all | solution.py:185
  222.7 3.6 %all-to-all-start.9 = ((bf16[8,16,3584]{2,1,0:T(8,128)(2,1)}), bf16[8,16,3584]{2,1,0:T(8,128)(2,1)S(1)}, u32[]{:S(2)}, u32[]{:S(2)}) async-start(bf16[8,16,3584]{2,1,0:T(8,128)(2,1)} %bitcast.21), calls=%async_computation.9 | async-start | bytes 1835008 | tf_op jit(solution)/shard_map/all_to_all | solution.py:185
  226.5 13.3 %all-to-all-done.9 = bf16[8,16,3584]{2,1,0:T(8,128)(2,1)S(1)} async-done(((bf16[8,16,3584]{2,1,0:T(8,128)(2,1)}), bf16[8,16,3584]{2,1,0:T(8,128)(2,1)S(1)}, u32[]{:S(2)}, u32[]{:S(2)}) %all-to-all-start.9) | async-done | bytes 917536 | tf_op jit(solution)/shard_map/all_to_all | solution.py:185
  (69 shorter events, 60.4 us)
Async XLA Ops:
  0.0 4.9 %copy-start.7 = (s32[512]{0:T(512)S(1)}, s32[512]{0:T(512)}, u32[]{:S(2)}) copy-start(s32[512]{0:T(512)} %param.7) | copy-start | bytes 6148
  3.5 14.7 %collective-permute-start.1 = (bf16[512,1792]{1,0:T(8,128)(2,1)}, bf16[512,1792]{1,0:T(8,128)(2,1)}, u32[]{:S(2)}, u32[]{:S(2)}) collective-permute-start(bf16[512,1792]{1,0:T(8,128)(2,1)} %get-tuple-element.35), channel_id=1, source_target_pairs={{0,8},{8,0},{16,24},{24,16},{32,40},{40,32},{48,56},{56,48},{64,72... | collective-permute-start | bytes 5505032 | tf_op jit(solution)/shard_map/ppermute | solution.py:152
  16.1 2.0 collective-permute-start
  41.5 14.1 %all-to-all-start.6 = ((bf16[8,32,1792]{2,1,0:T(8,128)(2,1)}), bf16[8,32,1792]{2,1,0:T(8,128)(2,1)S(1)}, u32[]{:S(2)}, u32[]{:S(2)}) async-start(bf16[8,32,1792]{2,1,0:T(8,128)(2,1)} %broadcast_in_dim.64), calls=%async_computation.6 | async-start | bytes 1835008 | tf_op jit(solution)/shard_map/all_to_all | solution.py:166
  55.6 19.9 %all-to-all-start = ((bf16[8,32,1792]{2,1,0:T(8,128)(2,1)}), bf16[8,32,1792]{2,1,0:T(8,128)(2,1)S(1)}, u32[]{:S(2)}, u32[]{:S(2)}) async-start(bf16[8,32,1792]{2,1,0:T(8,128)(2,1)} %bitcast.2), calls=%async_computation | async-start | bytes 1835008 | tf_op jit(solution)/shard_map/all_to_all | solution.py:163
  62.1 32.7 %collective-permute-start.6 = (bf16[256,1792]{1,0:T(8,128)(2,1)S(1)}, bf16[256,1792]{1,0:T(8,128)(2,1)}, u32[]{:S(2)}, u32[]{:S(2)}) collective-permute-start(bf16[256,1792]{1,0:T(8,128)(2,1)S(1)} %bitcast.29), channel_id=1, source_target_pairs={{0,8},{8,0},{16,24},{24,16},{32,40},{40,32},{48,56},{56,48},{64,72... | collective-permute-start | bytes 2752520 | tf_op jit(solution)/shard_map/ppermute | solution.py:167
  76.7 17.2 %all-to-all-start.1 = ((bf16[8,32,1792]{2,1,0:T(8,128)(2,1)}), bf16[8,32,1792]{2,1,0:T(8,128)(2,1)S(1)}, u32[]{:S(2)}, u32[]{:S(2)}) async-start(bf16[8,32,1792]{2,1,0:T(8,128)(2,1)} %broadcast_in_dim.56), calls=%async_computation.1 | async-start | bytes 1835008 | tf_op jit(solution)/shard_map/all_to_all | solution.py:166
  93.9 16.3 %collective-permute-start.2 = (bf16[256,1792]{1,0:T(8,128)(2,1)S(1)}, bf16[256,1792]{1,0:T(8,128)(2,1)S(1)}, u32[]{:S(2)}, u32[]{:S(2)}) collective-permute-start(bf16[256,1792]{1,0:T(8,128)(2,1)S(1)} %bitcast.27), channel_id=1, source_target_pairs={{0,8},{8,0},{16,24},{24,16},{32,40},{40,32},{48,56},{56,48},{64,72... | collective-permute-start | bytes 2752520 | tf_op jit(solution)/shard_map/ppermute | solution.py:167
  94.9 4.7 %copy-start = (bf16[3584,1792]{1,0:T(8,128)(2,1)S(1)}, bf16[3584,1792]{1,0:T(8,128)(2,1)}, u32[]{:S(2)}) copy-start(bf16[3584,1792]{1,0:T(8,128)(2,1)} %basis.7) | copy-start | bytes 38535172
  105.2 17.6 %all-to-all-start.7 = ((bf16[4,64,1792]{2,1,0:T(8,128)(2,1)}), bf16[4,64,1792]{2,1,0:T(8,128)(2,1)S(1)}, u32[]{:S(2)}, u32[]{:S(2)}) async-start(bf16[4,64,1792]{2,1,0:T(8,128)(2,1)} %bitcast.16), calls=%async_computation.7 | async-start | bytes 1835008 | tf_op jit(solution)/shard_map/all_to_all | solution.py:169
  110.2 4.7 %copy-start.1 = (bf16[3584,1792]{1,0:T(8,128)(2,1)S(1)}, bf16[3584,1792]{1,0:T(8,128)(2,1)}, u32[]{:S(2)}) copy-start(bf16[3584,1792]{1,0:T(8,128)(2,1)} %basis.7) | copy-start | bytes 38535172
  122.7 16.1 %all-to-all-start.2 = ((bf16[4,64,1792]{2,1,0:T(8,128)(2,1)}), bf16[4,64,1792]{2,1,0:T(8,128)(2,1)S(1)}, u32[]{:S(2)}, u32[]{:S(2)}) async-start(bf16[4,64,1792]{2,1,0:T(8,128)(2,1)} %bitcast.4), calls=%async_computation.2 | async-start | bytes 1835008 | tf_op jit(solution)/shard_map/all_to_all | solution.py:169
  129.6 13.0 %collective-permute-start.7 = (bf16[32,1792]{1,0:T(8,128)(2,1)S(1)}, bf16[32,1792]{1,0:T(8,128)(2,1)S(1)}, u32[]{:S(2)}, u32[]{:S(2)}) collective-permute-start(bf16[32,1792]{1,0:T(8,128)(2,1)S(1)} %dynamic-slice_convert_fusion), channel_id=1, source_target_pairs={{0,4},{1,5},{2,6},{3,7},{4,0},{5,1},{6,2},{7,3},{8,12},{9,13},{10,... | collective-permute-start | bytes 344072 | tf_op jit(solution)/shard_map/ppermute | solution.py:174
  139.0 5.2 %collective-permute-start.3 = (bf16[32,1792]{1,0:T(8,128)(2,1)S(1)}, bf16[32,1792]{1,0:T(8,128)(2,1)S(1)}, u32[]{:S(2)}, u32[]{:S(2)}) collective-permute-start(bf16[32,1792]{1,0:T(8,128)(2,1)S(1)} %dynamic-slice_convert_fusion.1), channel_id=1, source_target_pairs={{0,4},{1,5},{2,6},{3,7},{4,0},{5,1},{6,2},{7,3},{8,12},{9,13},{10,... | collective-permute-start | bytes 344072 | tf_op jit(solution)/shard_map/ppermute | solution.py:174
  144.4 5.4 %collective-permute-start.4 = (bf16[32,1792]{1,0:T(8,128)(2,1)S(1)}, bf16[32,1792]{1,0:T(8,128)(2,1)S(1)}, u32[]{:S(2)}, u32[]{:S(2)}) collective-permute-start(bf16[32,1792]{1,0:T(8,128)(2,1)S(1)} %get-tuple-element.41), channel_id=1, source_target_pairs={{0,4},{1,5},{2,6},{3,7},{4,0},{5,1},{6,2},{7,3},{8,12},{9,13},{10,... | collective-permute-start | bytes 344072 | tf_op jit(solution)/shard_map/ppermute | solution.py:178
  147.3 5.7 %collective-permute-start.8 = (bf16[32,1792]{1,0:T(8,128)(2,1)S(1)}, bf16[32,1792]{1,0:T(8,128)(2,1)S(1)}, u32[]{:S(2)}, u32[]{:S(2)}) collective-permute-start(bf16[32,1792]{1,0:T(8,128)(2,1)S(1)} %get-tuple-element.42), channel_id=1, source_target_pairs={{0,4},{1,5},{2,6},{3,7},{4,0},{5,1},{6,2},{7,3},{8,12},{9,13},{10,... | collective-permute-start | bytes 344072 | tf_op jit(solution)/shard_map/ppermute | solution.py:178
  165.8 23.8 %all-to-all-start.8 = ((bf16[4,64,1792]{2,1,0:T(8,128)(2,1)}), bf16[4,64,1792]{2,1,0:T(8,128)(2,1)S(1)}, u32[]{:S(2)}, u32[]{:S(2)}) async-start(bf16[4,64,1792]{2,1,0:T(8,128)(2,1)} %broadcast_in_dim.65), calls=%async_computation.8 | async-start | bytes 1835008 | tf_op jit(solution)/shard_map/all_to_all | solution.py:182
  169.3 4.7 %copy-start.2 = (bf16[3584,1792]{1,0:T(8,128)(2,1)S(1)}, bf16[3584,1792]{1,0:T(8,128)(2,1)}, u32[]{:S(2)}) copy-start(bf16[3584,1792]{1,0:T(8,128)(2,1)} %basis.7) | copy-start | bytes 38535172
  184.3 19.0 %collective-permute-start.5 = (bf16[128,3584]{1,0:T(8,128)(2,1)}, bf16[128,3584]{1,0:T(8,128)(2,1)}, u32[]{:S(2)}, u32[]{:S(2)}) collective-permute-start(bf16[128,3584]{1,0:T(8,128)(2,1)} %get-tuple-element.10), channel_id=1, source_target_pairs={{0,8},{8,0},{16,24},{24,16},{32,40},{40,32},{48,56},{56,48},{64,72... | collective-permute-start | bytes 2752520 | tf_op jit(solution)/shard_map/ppermute | solution.py:184
  189.6 4.7 %copy-start.3 = (bf16[3584,1792]{1,0:T(8,128)(2,1)S(1)}, bf16[3584,1792]{1,0:T(8,128)(2,1)}, u32[]{:S(2)}) copy-start(bf16[3584,1792]{1,0:T(8,128)(2,1)} %basis.7) | copy-start | bytes 38535172
  194.3 9.1 %copy-start.5 = (f32[128,3584]{1,0:T(8,128)S(1)}, f32[128,3584]{1,0:T(8,128)}, u32[]{:S(2)}) copy-start(f32[128,3584]{1,0:T(8,128)} %copy-done.4) | copy-start | bytes 5505028
  203.3 5.9 %collective-permute-start.9 = (bf16[128,3584]{1,0:T(8,128)(2,1)}, bf16[128,3584]{1,0:T(8,128)(2,1)}, u32[]{:S(2)}, u32[]{:S(2)}) collective-permute-start(bf16[128,3584]{1,0:T(8,128)(2,1)} %get-tuple-element.12), channel_id=1, source_target_pairs={{0,8},{8,0},{16,24},{24,16},{32,40},{40,32},{48,56},{56,48},{64,72... | collective-permute-start | bytes 2752520 | tf_op jit(solution)/shard_map/ppermute | solution.py:184
  205.7 17.0 %all-to-all-start.4 = ((bf16[8,16,3584]{2,1,0:T(8,128)(2,1)}), bf16[8,16,3584]{2,1,0:T(8,128)(2,1)S(1)}, u32[]{:S(2)}, u32[]{:S(2)}) async-start(bf16[8,16,3584]{2,1,0:T(8,128)(2,1)} %bitcast.13), calls=%async_computation.4 | async-start | bytes 1835008 | tf_op jit(solution)/shard_map/all_to_all | solution.py:185
  222.7 17.0 %all-to-all-start.9 = ((bf16[8,16,3584]{2,1,0:T(8,128)(2,1)}), bf16[8,16,3584]{2,1,0:T(8,128)(2,1)S(1)}, u32[]{:S(2)}, u32[]{:S(2)}) async-start(bf16[8,16,3584]{2,1,0:T(8,128)(2,1)} %bitcast.21), calls=%async_computation.9 | async-start | bytes 1835008 | tf_op jit(solution)/shard_map/all_to_all | solution.py:185
  (2 other events, 4.7 us)

commit v2 on v0

v2 whole, which is shorter than its diff:
```python
import jax
import jax.numpy as jnp
from jax import lax
from jax.experimental import pallas as pl
from jax.experimental.pallas import tpu as pltpu
from jax.sharding import PartitionSpec as P

damping = 0.05
CHUNKS = 2
RING = 4
F32, BF16 = jnp.float32, jnp.bfloat16
NN = (((1,), (0,)), ((), ()))
NT = (((1,), (1,)), ((), ()))


def cost(flops, nbytes):
    return pl.CostEstimate(flops=flops, bytes_accessed=nbytes, transcendentals=0)


def dot(a, b, dims=NN):
    return lax.dot_general(a, b, dims, preferred_element_type=F32)


def params(mib):
    return pltpu.CompilerParams(vmem_limit_bytes=mib << 20)


def fixed(shape, at=(0, 0)):
    return pl.BlockSpec(shape, lambda *_: at)


def select_kernel(ids, basis, out, acc):
    step = pl.program_id(0)
    width = basis.shape[1]
    lanes = lax.broadcasted_iota(jnp.int32, (ids.shape[0], width), 1)
    hot = jnp.where(lanes == ids[...] - step * width, 1.0, 0.0).astype(BF16)
    part = dot(hot, basis[...], NT)

    @pl.when(step == 0)
    def _():
        acc[...] = part

    @pl.when(step > 0)
    def _():
        acc[...] += part

    @pl.when(step == pl.num_programs(0) - 1)
    def _():
        out[...] = acc[...].astype(BF16)


def select(ids, basis, block=1024):
    rows, width = basis.shape
    queries = ids.shape[0]
    return pl.pallas_call(
        select_kernel,
        grid=(width // block,),
        in_specs=[fixed((queries, 1)), pl.BlockSpec((rows, block), lambda i: (0, i))],
        out_specs=fixed((queries, rows)),
        out_shape=jax.ShapeDtypeStruct((queries, rows), BF16),
        scratch_shapes=[pltpu.VMEM((queries, rows), F32)],
        cost_estimate=cost(2 * queries * rows * width, rows * width * 2),
        compiler_params=params(56),
    )(ids[:, None], basis)


def rows_kernel(place, sel, grad, sel2, grad2, out):
    out[...] = (dot(sel[...], grad[...]) + dot(sel2[...], grad2[...])).astype(BF16)


def partial_rows(place, sel, grad, sel2, grad2, block=256):
    queries, units = sel.shape
    half = grad2.shape[1]
    steps = half // block
    return pl.pallas_call(
        rows_kernel,
        grid_spec=pltpu.PrefetchScalarGridSpec(
            num_scalar_prefetch=1,
            grid=(steps,),
            in_specs=[
                fixed((queries, units)),
                pl.BlockSpec((units, block), lambda i, place: (0, place[0] * steps + i)),
                fixed((queries, units)),
                pl.BlockSpec((units, block), lambda i, place: (0, i)),
            ],
            out_specs=pl.BlockSpec((queries, block), lambda i, place: (0, i)),
        ),
        out_shape=jax.ShapeDtypeStruct((queries, half), BF16),
        cost_estimate=cost(4 * queries * units * half, 6 * queries * half),
        compiler_params=params(32),
    )(place, sel, grad, sel2, grad2)


def rotate_kernel(place, own, other, basis, *refs):
    outs, lhs = refs[:RING], refs[RING]
    core, x = place[0], place[1]
    piece, half = outs[0].shape[0], own.shape[1]

    @pl.when(pl.program_id(0) == 0)
    def _():
        for d in range(RING):
            rows = pl.ds(pl.multiple_of(lax.rem(x + d, RING) * piece, piece), piece)
            to = pl.ds(d * piece, piece)
            lhs[core, to, :] = own[rows, :]
            lhs[1 - core, to, :] = other[rows, :]

    total = dot(lhs[0], basis[:half, :]) + dot(lhs[1], basis[half:, :])
    for d in range(RING):
        outs[d][...] = total[d * piece : (d + 1) * piece].astype(outs[d].dtype)


def rotate(place, own, other, basis, chunk_index, block=256):
    m, half = other.shape
    k, n = basis.shape
    piece = m // RING
    return pl.pallas_call(
        rotate_kernel,
        grid_spec=pltpu.PrefetchScalarGridSpec(
            num_scalar_prefetch=1,
            grid=(n // block,),
            in_specs=[
                fixed((m, half), (chunk_index, 0)),
                fixed((m, half)),
                pl.BlockSpec((k, block), lambda i, place: (0, i)),
            ],
            out_specs=[pl.BlockSpec((piece, block), lambda i, place: (0, i))] * RING,
            scratch_shapes=[pltpu.VMEM((2, m, half), BF16)],
        ),
        out_shape=[
            jax.ShapeDtypeStruct((piece, n), F32 if d == 0 else BF16) for d in range(RING)
        ],
        cost_estimate=cost(2 * m * k * n, 2 * (m * k + k * n + m * n)),
        compiler_params=params(50),
    )(place, own, other, basis)


def back_kernel(place, *refs):
    pieces, basis, other, own, lhs = refs[:RING], *refs[RING:]
    core, x = place[0], place[1]
    piece = pieces[0].shape[0]

    @pl.when(pl.program_id(0) == 0)
    def _():
        for d in range(RING):
            block = lax.rem(x + RING - d + 2 * (1 - core), RING)
            lhs[pl.ds(pl.multiple_of(block * piece, piece), piece), :] = pieces[d][...]

    total = dot(lhs[...], basis[...], NT)
    other[...] = total[: 2 * piece].astype(BF16)
    own[...] = total[2 * piece :]


def back(place, pieces, basis, block=512):
    piece, k = pieces[0].shape
    n = basis.shape[0]
    m = RING * piece
    return pl.pallas_call(
        back_kernel,
        grid_spec=pltpu.PrefetchScalarGridSpec(
            num_scalar_prefetch=1,
            grid=(n // block,),
            in_specs=[fixed((piece, k))] * RING
            + [pl.BlockSpec((block, k), lambda i, place: (i, 0))],
            out_specs=[pl.BlockSpec((m // 2, block), lambda i, place: (0, i))] * 2,
            scratch_shapes=[pltpu.VMEM((m, k), BF16)],
        ),
        out_shape=[
            jax.ShapeDtypeStruct((m // 2, n), BF16),
            jax.ShapeDtypeStruct((m // 2, n), F32),
        ],
        cost_estimate=cost(2 * m * k * n, 2 * (m * k + k * n + m * n)),
        compiler_params=params(50),
    )(place, *pieces, basis)


def ring_kernel(own, a, b, c, total, rounded):
    value = own[...] + a[...].astype(F32) + b[...].astype(F32) + c[...].astype(F32)
    total[...] = value
    rounded[...] = value.astype(BF16)


def ring_sum(parts):
    shape = parts[0].shape
    return pl.pallas_call(
        ring_kernel,
        in_specs=[pl.BlockSpec(memory_space=pltpu.VMEM)] * RING,
        out_specs=[pl.BlockSpec(memory_space=pltpu.VMEM)] * 2,
        out_shape=[jax.ShapeDtypeStruct(shape, F32), jax.ShapeDtypeStruct(shape, BF16)],
        cost_estimate=cost(3 * shape[0] * shape[1], 16 * shape[0] * shape[1]),
        compiler_params=params(8),
    )(*parts)


def scale_kernel(total, far, rows, cols, out):
    value = total[...] + far[...].astype(F32)
    out[...] = (value / (rows[...] * cols[...] + damping)).astype(BF16)


def scale(total, far, rows, cols):
    return pl.pallas_call(
        scale_kernel,
        in_specs=[pl.BlockSpec(memory_space=pltpu.VMEM)] * 4,
        out_specs=pl.BlockSpec(memory_space=pltpu.VMEM),
        out_shape=jax.ShapeDtypeStruct(total.shape, BF16),
        cost_estimate=cost(8 * total.size, 8 * total.size),
        compiler_params=params(8),
    )(total, far, rows, cols)


def add_up(parts):
    total = parts[0].astype(F32)
    for i in range(1, parts.shape[0]):
        total += parts[i].astype(F32)
    return total


def per_device(query_ids, layer_index, gradient, out_basis, in_basis, out_eigen, in_eigen):
    loops, reds = lax.axis_size("loop"), lax.axis_size("red")
    chips = loops // 2
    queries = query_ids.shape[0]
    chunk = queries // CHUNKS
    piece = chunk // RING
    core = lax.axis_index("loop") % 2
    x = lax.axis_index("red") % RING
    place = jnp.stack([core, x]).astype(jnp.int32)
    swap = [(i, i ^ 1) for i in range(loops)]
    flip = [(i, (i + RING) % reds) for i in range(reds)]
    shift = [[(i, i - i % RING + (i + d) % RING) for i in range(reds)] for d in range(RING)]
    same_core = [[2 * i + c for i in range(chips)] for c in range(2)]

    ids = query_ids.reshape(chips, 2, CHUNKS, -1).transpose(2, 1, 0, 3).reshape(queries)
    half = gradient.shape[1] // 2
    theirs = lax.dynamic_slice_in_dim(gradient, (1 - core) * half, half, 1)
    got = lax.ppermute(theirs, "loop", swap)
    sel = select(ids, out_basis)
    sel_got = lax.ppermute(sel, "loop", swap)
    part = partial_rows(place, sel, gradient, sel_got, got)
    part = lax.all_to_all(part.reshape(chips, -1, half), "loop", 0, 0, axis_index_groups=same_core)
    own = add_up(part).astype(BF16)
    own = jnp.broadcast_to(own[None], (chips,) + own.shape)
    own = lax.all_to_all(own, "loop", 0, 0, axis_index_groups=same_core).reshape(queries, half)

    eigen_rows = jnp.take(jnp.take(out_eigen, layer_index, axis=0)[0], ids)
    eigen_cols = jnp.take(in_eigen, layer_index, axis=0)[0]

    outs = []
    for n in range(CHUNKS):
        other = lax.ppermute(own[n * chunk : (n + 1) * chunk], "loop", swap)
        rot = rotate(place, own, other, in_basis, n)
        parts = [rot[0]] + [lax.ppermute(rot[d], "red", shift[d]) for d in range(1, RING)]
        total, rounded = ring_sum(parts)
        far = lax.ppermute(rounded, "red", flip)
        er = lax.dynamic_slice_in_dim(eigen_rows, n * chunk + x * piece, piece, 0)
        scaled = scale(total, far, er[:, None], eigen_cols[None, :])
        pieces = [scaled] + [lax.ppermute(scaled, "red", shift[d]) for d in range(1, RING)]
        send, keep = back(place, pieces, in_basis)
        total = (keep + lax.ppermute(send, "loop", swap).astype(F32)).astype(BF16)
        total = total.reshape(chips, -1, total.shape[1])
        total = lax.all_to_all(total, "loop", 0, 0, axis_index_groups=same_core)
        outs.append(add_up(total).astype(BF16))
    return jnp.concatenate(outs, 0)


def solution(mesh):
    return jax.shard_map(
        per_device,
        mesh=mesh,
        in_specs=(
            P(),
            P(),
            P("loop", "red"),
            P("loop", None),
            P("red", "loop"),
            P(),
            P(None, "loop"),
        ),
        out_specs=P("loop", "red"),
        check_vma=False,
    )
```

time: 342 us -> 227 us (0.66)
  waiting for transfers between devices: 173 us -> 54.6 us
  Pallas kernels: 0 us -> 55.8 us
  starting transfers between devices: 0.04 us -> 36.5 us
  blocking collectives: 91.5 us -> 55.6 us
  matrix products: 33.5 us -> 0 us
  between operations: 14.1 us -> 0.82 us
  local copies, waits for them, and re-layouts: 21.5 us -> 13.5 us
  other arithmetic: 4.84 us -> 8.89 us
    psum x1 -> x0, waiting for transfers between devices: 102 us -> none  [per_device(): rotated = lax.psum(local_rot, 'red')]
    psum x1 -> x0, blocking collectives: 91.5 us -> none  [per_device(): rows_w = lax.psum(local_rows, 'loop').astype(jnp.bfloat16)]
    reduce_scatter x1 -> x0, waiting for transfers between devices: 70.9 us -> none  [per_device(): lax.psum_scatter(lax.dot_general(scaled, in_basis, (((1,), (1,)), ((), ()...]
    pallas_call x0 -> x10, Pallas kernels: none -> 55.8 us  [the longest x2 19.7 us: back(): pl.pallas_call(back_kernel, grid_spec=pltpu.PrefetchScalarGridSpec(num_sc...]
    all_to_all x0 -> x2, blocking collectives: none -> 55.6 us  [the longest x1 28.7 us: per_device(): lax.all_to_all(part.reshape(chips, -1, half), 'loop', 0, 0, axis_index_gr...]
    dot_general x3 -> x0, matrix products: 33.5 us -> none  [the longest x1 13.4 us: per_device(): local_rot = jnp.dot(rows_w, in_basis, preferred_element_type=jnp.float32)]
    ppermute x0 -> x20, waiting for transfers between devices: none -> 31.3 us  [the longest x6 12.6 us: per_device(): lax.ppermute(scaled, 'red', shift[d])]
    ppermute x0 -> x20, starting transfers between devices: none -> 28.6 us  [the longest x6 9.35 us: per_device(): lax.ppermute(rot[d], 'red', shift[d])]
  transfers between devices with their start and end apart: 2 -> 22, of which waited for: 2 -> 11; matrix products, arithmetic and copies ran while one was open for 0% -> 5% of each run, Pallas kernels for 0% -> 23%
where the time goes in v2:
time: 227 us; the launch traced here: 226 us
  Pallas kernels  55.8 us (25%)
  blocking collectives  55.6 us (24%)
  waiting for transfers between devices  54.6 us (24%)
  starting transfers between devices  36.5 us (16%)
  local copies, waits for them, and re-layouts  13.5 us (6%)
  other arithmetic  8.89 us (4%)
    all_to_all x1, blocking collectives, per_device(): lax.all_to_all(part.reshape(chips, -1, half), 'loop', 0, 0, axis_index_gr...  28.7 us
    all_to_all x1, blocking collectives, per_device(): lax.all_to_all(own, 'loop', 0, 0, axis_index_groups=same_core)  26.8 us
    all_to_all x2, waiting for transfers between devices, per_device(): total = lax.all_to_all(total, 'loop', 0, 0, axis_index_groups=same_core)  23.2 us
    pallas_call x2, Pallas kernels, back(): pl.pallas_call(back_kernel, grid_spec=pltpu.PrefetchScalarGridSpec(num_sc...  19.7 us
    pallas_call x2, Pallas kernels, rotate(): pl.pallas_call(rotate_kernel, grid_spec=pltpu.PrefetchScalarGridSpec(num_...  19.5 us
    ppermute x6, waiting for transfers between devices, per_device(): lax.ppermute(scaled, 'red', shift[d])  12.6 us
    pallas_call x1, Pallas kernels, select(): pl.pallas_call(select_kernel, grid=(width // block,), in_specs=[fixed((qu...  10.3 us
    ppermute x2, waiting for transfers between devices, per_device(): far = lax.ppermute(rounded, 'red', flip)  10.1 us
  transfers between devices with their start and end apart: 22, of which 11 were waited for; matrix products, arithmetic and copies ran while one was open for 5% of the time, Pallas kernels for 23%

profile of v2, /device:TPU:1, one launch (start us, length us, event | category | flops | bytes accessed | tf_op | source)
XLA Modules:
  0.0 225.7 jit_solution(15062850071451958770)
XLA Ops:
  0.0 2.9 %constant_dynamic-slice_fusion = bf16[512,1792]{1,0:T(8,128)(2,1)} fusion(bf16[512,3584]{1,0:T(8,128)(2,1)} %grad.1, s32[]{:T(128)S(6)} %select_n.63), kind=kLoop, calls=%fused_computation.16 | loop fusion | bytes 3670020 | tf_op jit(solution)/shard_map/dynamic_slice | solution.py:233
  5.4 10.3 %shard_map.73.sel = bf16[512,512]{1,0:T(8,128)(2,1)} custom-call(s32[512,1]{1,0:T(8,128)} %copy.15.ids, bf16[512,8192]{1,0:T(8,128)(2,1)} %basis.3), custom_call_target="tpu_custom_call" | custom-call | flops 4294967296 | bytes 8388608 | tf_op jit(solution)/shard_map/pallas_call | solution.py:55
  20.8 4.1 %shard_map.74 = bf16[512,1792]{1,0:T(8,128)(2,1)S(1)} custom-call(s32[2]{0:T(128)S(1)} %pad_add_fusion.place, bf16[512,512]{1,0:T(8,128)(2,1)S(1)} %copy-done.3, bf16[512,3584]{1,0:T(8,128)(2,1)S(1)} %copy-done, bf16[512,512]{1,0:T(8,128)(2,1)S(1)} %collective-permute-done.sel2, bf16[512,1792]{1,0:T(8,128)(2,1)S(1)} %collective-permute-done.1.grad2), custom_call_target="tpu_custom_call" | custom-call | flops 1879048192 | bytes 5505024 | tf_op jit(solution)/shard_map/pallas_call | solution.py:75
  24.9 28.7 %all_to_all.20 = bf16[8,64,1792]{2,1,0:T(8,128)(2,1)S(1)} all-to-all(bf16[8,64,1792]{2,1,0:T(8,128)(2,1)S(1)} %bitcast.29), channel_id=1, replica_groups={{0,16,32,48,64,80,96,112},{8,24,40,56,72,88,104,120},{1,17,33,49,65,81,..., dimensions={0} | all-to-all | bytes 3670016 | tf_op jit(solution)/shard_map/all_to_all | solution.py:238
  54.0 26.8 %all_to_all.21 = bf16[8,64,1792]{2,1,0:T(8,128)(2,1)S(1)} all-to-all(bf16[8,64,1792]{2,1,0:T(8,128)(2,1)S(1)} %broadcast_in_dim.43), channel_id=1, replica_groups={{0,16,32,48,64,80,96,112},{8,24,40,56,72,88,104,120},{1,17,33,49,65,81,..., dimensions={0} | all-to-all | bytes 3670016 | tf_op jit(solution)/shard_map/all_to_all | solution.py:241
  86.4 10.1 %shard_map.75 = (f32[64,1792]{1,0:T(8,128)S(1)}, bf16[64,1792]{1,0:T(8,128)(2,1)}, bf16[64,1792]{1,0:T(8,128)(2,1)}, bf16[64,1792]{1,0:T(8,128)(2,1)}) custom-call(s32[2]{0:T(128)S(1)} %pad_add_fusion.place, bf16[512,1792]{1,0:T(8,128)(2,1)S(1)} %bitcast.27, bf16[256,1792]{1,0:T(8,128)(2,1)S(1)} %collective-permute-done.2.other, bf16[3584,1792]{1,0:T(8,128)(2,1)} %refs_4_.3), custom_call_target="tpu_custom_call" | custom-call | flops 3288334336 | bytes 15597568 | tf_op jit(solution)/shard_map/pallas_call | solution.py:116
  97.8 2.5 %collective-permute-start.4 = (bf16[64,1792]{1,0:T(8,128)(2,1)}, bf16[64,1792]{1,0:T(8,128)(2,1)}, u32[]{:S(2)}, u32[]{:S(2)}) collective-permute-start(bf16[64,1792]{1,0:T(8,128)(2,1)} %get-tuple-element.23), channel_id=1, source_target_pairs={{0,2},{1,3},{2,0},{3,1},{4,6},{5,7},{6,4},{7,5},{8,10},{9,11},{10,... | collective-permute-start | bytes 688136 | tf_op jit(solution)/shard_map/ppermute | solution.py:250
  101.4 3.1 %gather_fusion = f32[512]{0:T(512)S(1)} fusion(f32[8192]{0:T(1024)S(1)} %bitcast.30, s32[1024]{0:T(1024)S(1)} %pad_clamp_fusion), kind=kCustom, calls=%fused_computation | custom fusion | bytes 6144 | tf_op jit(solution)/shard_map/jit(_take)/gather | solution.py:243
  104.8 6.0 %collective-permute-done.4.b = bf16[64,1792]{1,0:T(8,128)(2,1)} collective-permute-done((bf16[64,1792]{1,0:T(8,128)(2,1)}, bf16[64,1792]{1,0:T(8,128)(2,1)}, u32[]{:S(2)}, u32[]{:S(2)}) %collective-permute-start.4) | collective-permute-done | bytes 229408 | tf_op jit(solution)/shard_map/ppermute | solution.py:250
  113.4 2.6 %collective-permute-start.6 = (bf16[64,1792]{1,0:T(8,128)(2,1)}, bf16[64,1792]{1,0:T(8,128)(2,1)S(1)}, u32[]{:S(2)}, u32[]{:S(2)}) collective-permute-start(bf16[64,1792]{1,0:T(8,128)(2,1)} %get-tuple-element.26), channel_id=1, source_target_pairs={{0,4},{1,5},{2,6},{3,7},{4,0},{5,1},{6,2},{7,3},{8,12},{9,13},{10,... | collective-permute-start | bytes 688136 | tf_op jit(solution)/shard_map/ppermute | solution.py:252
  117.0 4.1 %collective-permute-done.6.far = bf16[64,1792]{1,0:T(8,128)(2,1)S(1)} collective-permute-done((bf16[64,1792]{1,0:T(8,128)(2,1)}, bf16[64,1792]{1,0:T(8,128)(2,1)S(1)}, u32[]{:S(2)}, u32[]{:S(2)}) %collective-permute-start.6) | collective-permute-done | bytes 229408 | tf_op jit(solution)/shard_map/ppermute | solution.py:252
  122.2 3.5 %collective-permute-start.9 = (bf16[64,1792]{1,0:T(8,128)(2,1)S(1)}, bf16[64,1792]{1,0:T(8,128)(2,1)S(1)}, u32[]{:S(2)}, u32[]{:S(2)}) collective-permute-start(bf16[64,1792]{1,0:T(8,128)(2,1)S(1)} %shard_map.77.refs_0_), channel_id=1, source_target_pairs={{0,3},{1,0},{2,1},{3,2},{4,7},{5,4},{6,5},{7,6},{8,11},{9,8},{10,9... | collective-permute-start | bytes 688136 | tf_op jit(solution)/shard_map/ppermute | solution.py:255
  126.4 9.4 %shard_map.79 = (f32[64,1792]{1,0:T(8,128)S(1)}, bf16[64,1792]{1,0:T(8,128)(2,1)S(1)}, bf16[64,1792]{1,0:T(8,128)(2,1)S(1)}, bf16[64,1792]{1,0:T(8,128)(2,1)S(1)}) custom-call(s32[2]{0:T(128)S(1)} %pad_add_fusion.place, bf16[512,1792]{1,0:T(8,128)(2,1)S(1)} %bitcast.28, bf16[256,1792]{1,0:T(8,128)(2,1)S(1)} %collective-permute-done.11.other, ...), custom_call_target="tpu_custom_call" | custom-call | flops 3288334336 | bytes 15597568 | tf_op jit(solution)/shard_map/pallas_call | solution.py:116
  140.4 10.1 %shard_map.78 = (bf16[128,3584]{1,0:T(8,128)(2,1)}, f32[128,3584]{1,0:T(8,128)S(1)}) custom-call(s32[2]{0:T(128)S(1)} %pad_add_fusion.place, bf16[64,1792]{1,0:T(8,128)(2,1)S(1)} %shard_map.77.refs_0_, bf16[64,1792]{1,0:T(8,128)(2,1)S(1)} %collective-permute-done.7.refs_1_, bf16[64,1792]{1,0:T(8,128)(2,1)S(1)} %collective-permute-done.8.refs_2_, ...), custom_call_target="tpu_custom_call" | custom-call | flops 3288334336 | bytes 15597568 | tf_op jit(solution)/shard_map/pallas_call | solution.py:157
  150.5 2.7 %collective-permute-start.10 = (bf16[128,3584]{1,0:T(8,128)(2,1)}, bf16[128,3584]{1,0:T(8,128)(2,1)}, u32[]{:S(2)}, u32[]{:S(2)}) collective-permute-start(bf16[128,3584]{1,0:T(8,128)(2,1)} %get-tuple-element.28), channel_id=1, source_target_pairs={{0,8},{8,0},{16,24},{24,16},{32,40},{40,32},{48,56},{56,48},{64,72... | collective-permute-start | bytes 2752520 | tf_op jit(solution)/shard_map/ppermute | solution.py:257
  153.4 2.7 %collective-permute-start.15 = (bf16[64,1792]{1,0:T(8,128)(2,1)S(1)}, bf16[64,1792]{1,0:T(8,128)(2,1)S(1)}, u32[]{:S(2)}, u32[]{:S(2)}) collective-permute-start(bf16[64,1792]{1,0:T(8,128)(2,1)S(1)} %get-tuple-element.34), channel_id=1, source_target_pairs={{0,4},{1,5},{2,6},{3,7},{4,0},{5,1},{6,2},{7,3},{8,12},{9,13},{10,... | collective-permute-start | bytes 688136 | tf_op jit(solution)/shard_map/ppermute | solution.py:252
  156.2 6.0 %collective-permute-done.15.far = bf16[64,1792]{1,0:T(8,128)(2,1)S(1)} collective-permute-done((bf16[64,1792]{1,0:T(8,128)(2,1)S(1)}, bf16[64,1792]{1,0:T(8,128)(2,1)S(1)}, u32[]{:S(2)}, u32[]{:S(2)}) %collective-permute-start.15) | collective-permute-done | bytes 229408 | tf_op jit(solution)/shard_map/ppermute | solution.py:252
  164.8 3.9 %collective-permute-done.18.refs_3_ = bf16[64,1792]{1,0:T(8,128)(2,1)S(1)} collective-permute-done((bf16[64,1792]{1,0:T(8,128)(2,1)S(1)}, bf16[64,1792]{1,0:T(8,128)(2,1)S(1)}, u32[]{:S(2)}, u32[]{:S(2)}) %collective-permute-start.18) | collective-permute-done | bytes 229408 | tf_op jit(solution)/shard_map/ppermute | solution.py:255
  171.1 6.4 %collective-permute-done.16.refs_1_ = bf16[64,1792]{1,0:T(8,128)(2,1)S(1)} collective-permute-done((bf16[64,1792]{1,0:T(8,128)(2,1)S(1)}, bf16[64,1792]{1,0:T(8,128)(2,1)S(1)}, u32[]{:S(2)}, u32[]{:S(2)}) %collective-permute-start.16) | collective-permute-done | bytes 229408 | tf_op jit(solution)/shard_map/ppermute | solution.py:255
  177.4 9.5 %shard_map.82 = (bf16[128,3584]{1,0:T(8,128)(2,1)S(1)}, f32[128,3584]{1,0:T(8,128)S(1)}) custom-call(s32[2]{0:T(128)S(1)} %pad_add_fusion.place, bf16[64,1792]{1,0:T(8,128)(2,1)S(1)} %shard_map.81.refs_0_, bf16[64,1792]{1,0:T(8,128)(2,1)S(1)} %collective-permute-done.16.refs_1_, bf16[64,1792]{1,0:T(8,128)(2,1)S(1)} %collective-permute-done.17.refs_2_, ...), custom_call_target="tpu_custom_call" | custom-call | flops 3288334336 | bytes 15597568 | tf_op jit(solution)/shard_map/pallas_call | solution.py:157
  189.9 4.3 %all-to-all-start.2 = ((bf16[8,16,3584]{2,1,0:T(8,128)(2,1)}), bf16[8,16,3584]{2,1,0:T(8,128)(2,1)}, u32[]{:S(2)}, u32[]{:S(2)}) async-start(bf16[8,16,3584]{2,1,0:T(8,128)(2,1)} %bitcast.31), calls=%async_computation.2 | async-start | bytes 1835008 | tf_op jit(solution)/shard_map/all_to_all | solution.py:259
  196.6 11.2 %all-to-all-done.2 = bf16[8,16,3584]{2,1,0:T(8,128)(2,1)} async-done(((bf16[8,16,3584]{2,1,0:T(8,128)(2,1)}), bf16[8,16,3584]{2,1,0:T(8,128)(2,1)}, u32[]{:S(2)}, u32[]{:S(2)}) %all-to-all-start.2) | async-done | bytes 917536 | tf_op jit(solution)/shard_map/all_to_all | solution.py:259
  207.8 3.6 %all-to-all-start.3 = ((bf16[8,16,3584]{2,1,0:T(8,128)(2,1)}), bf16[8,16,3584]{2,1,0:T(8,128)(2,1)S(1)}, u32[]{:S(2)}, u32[]{:S(2)}) async-start(bf16[8,16,3584]{2,1,0:T(8,128)(2,1)} %bitcast.16), calls=%async_computation.3 | async-start | bytes 1835008 | tf_op jit(solution)/shard_map/all_to_all | solution.py:259
  212.8 12.0 %all-to-all-done.3 = bf16[8,16,3584]{2,1,0:T(8,128)(2,1)S(1)} async-done(((bf16[8,16,3584]{2,1,0:T(8,128)(2,1)}), bf16[8,16,3584]{2,1,0:T(8,128)(2,1)S(1)}, u32[]{:S(2)}, u32[]{:S(2)}) %all-to-all-start.3) | async-done | bytes 917536 | tf_op jit(solution)/shard_map/all_to_all | solution.py:259
  (70 shorter events, 38.1 us)
Async XLA Ops:
  0.0 4.3 %copy-start.6 = (s32[512]{0:T(512)S(1)}, s32[512]{0:T(512)}, u32[]{:S(2)}) copy-start(s32[512]{0:T(512)} %param.7) | copy-start | bytes 6148
  2.9 14.9 %collective-permute-start.1 = (bf16[512,1792]{1,0:T(8,128)(2,1)}, bf16[512,1792]{1,0:T(8,128)(2,1)S(1)}, u32[]{:S(2)}, u32[]{:S(2)}) collective-permute-start(bf16[512,1792]{1,0:T(8,128)(2,1)} %constant_dynamic-slice_fusion), channel_id=1, source_target_pairs={{0,8},{8,0},{16,24},{24,16},{32,40},{40,32},{48,56},{56,48},{64,72... | collective-permute-start | bytes 5505032 | tf_op jit(solution)/shard_map/ppermute | solution.py:234
  15.6 2.1 collective-permute-start
  81.9 4.5 %collective-permute-start.2 = (bf16[256,1792]{1,0:T(8,128)(2,1)S(1)}, bf16[256,1792]{1,0:T(8,128)(2,1)S(1)}, u32[]{:S(2)}, u32[]{:S(2)}) collective-permute-start(bf16[256,1792]{1,0:T(8,128)(2,1)S(1)} %bitcast.32), channel_id=1, source_target_pairs={{0,8},{8,0},{16,24},{24,16},{32,40},{40,32},{48,56},{56,48},{64,72... | collective-permute-start | bytes 2752520 | tf_op jit(solution)/shard_map/ppermute | solution.py:248
  85.9 40.5 %collective-permute-start.11 = (bf16[256,1792]{1,0:T(8,128)(2,1)}, bf16[256,1792]{1,0:T(8,128)(2,1)S(1)}, u32[]{:S(2)}, u32[]{:S(2)}) collective-permute-start(bf16[256,1792]{1,0:T(8,128)(2,1)} %bitcast.14), channel_id=1, source_target_pairs={{0,8},{8,0},{16,24},{24,16},{32,40},{40,32},{48,56},{56,48},{64,72... | collective-permute-start | bytes 2752520 | tf_op jit(solution)/shard_map/ppermute | solution.py:248
  96.5 8.2 %collective-permute-start.3 = (bf16[64,1792]{1,0:T(8,128)(2,1)}, bf16[64,1792]{1,0:T(8,128)(2,1)S(1)}, u32[]{:S(2)}, u32[]{:S(2)}) collective-permute-start(bf16[64,1792]{1,0:T(8,128)(2,1)} %get-tuple-element.22), channel_id=1, source_target_pairs={{0,1},{1,2},{2,3},{3,0},{4,5},{5,6},{6,7},{7,4},{8,9},{9,10},{10,1... | collective-permute-start | bytes 688136 | tf_op jit(solution)/shard_map/ppermute | solution.py:250
  97.8 13.0 %collective-permute-start.4 = (bf16[64,1792]{1,0:T(8,128)(2,1)}, bf16[64,1792]{1,0:T(8,128)(2,1)}, u32[]{:S(2)}, u32[]{:S(2)}) collective-permute-start(bf16[64,1792]{1,0:T(8,128)(2,1)} %get-tuple-element.23), channel_id=1, source_target_pairs={{0,2},{1,3},{2,0},{3,1},{4,6},{5,7},{6,4},{7,5},{8,10},{9,11},{10,... | collective-permute-start | bytes 688136 | tf_op jit(solution)/shard_map/ppermute | solution.py:250
  100.2 10.6 %collective-permute-start.5 = (bf16[64,1792]{1,0:T(8,128)(2,1)}, bf16[64,1792]{1,0:T(8,128)(2,1)}, u32[]{:S(2)}, u32[]{:S(2)}) collective-permute-start(bf16[64,1792]{1,0:T(8,128)(2,1)} %get-tuple-element.24), channel_id=1, source_target_pairs={{0,3},{1,0},{2,1},{3,2},{4,7},{5,4},{6,5},{7,6},{8,11},{9,8},{10,9... | collective-permute-start | bytes 688136 | tf_op jit(solution)/shard_map/ppermute | solution.py:250
  113.4 7.6 %collective-permute-start.6 = (bf16[64,1792]{1,0:T(8,128)(2,1)}, bf16[64,1792]{1,0:T(8,128)(2,1)S(1)}, u32[]{:S(2)}, u32[]{:S(2)}) collective-permute-start(bf16[64,1792]{1,0:T(8,128)(2,1)} %get-tuple-element.26), channel_id=1, source_target_pairs={{0,4},{1,5},{2,6},{3,7},{4,0},{5,1},{6,2},{7,3},{8,12},{9,13},{10,... | collective-permute-start | bytes 688136 | tf_op jit(solution)/shard_map/ppermute | solution.py:252
  122.2 16.9 %collective-permute-start.9 = (bf16[64,1792]{1,0:T(8,128)(2,1)S(1)}, bf16[64,1792]{1,0:T(8,128)(2,1)S(1)}, u32[]{:S(2)}, u32[]{:S(2)}) collective-permute-start(bf16[64,1792]{1,0:T(8,128)(2,1)S(1)} %shard_map.77.refs_0_), channel_id=1, source_target_pairs={{0,3},{1,0},{2,1},{3,2},{4,7},{5,4},{6,5},{7,6},{8,11},{9,8},{10,9... | collective-permute-start | bytes 688136 | tf_op jit(solution)/shard_map/ppermute | solution.py:255
  125.8 14.6 %collective-permute-start.8 = (bf16[64,1792]{1,0:T(8,128)(2,1)S(1)}, bf16[64,1792]{1,0:T(8,128)(2,1)S(1)}, u32[]{:S(2)}, u32[]{:S(2)}) collective-permute-start(bf16[64,1792]{1,0:T(8,128)(2,1)S(1)} %shard_map.77.refs_0_), channel_id=1, source_target_pairs={{0,2},{1,3},{2,0},{3,1},{4,6},{5,7},{6,4},{7,5},{8,10},{9,11},{10,... | collective-permute-start | bytes 688136 | tf_op jit(solution)/shard_map/ppermute | solution.py:255
  125.8 14.6 %collective-permute-start.7 = (bf16[64,1792]{1,0:T(8,128)(2,1)S(1)}, bf16[64,1792]{1,0:T(8,128)(2,1)S(1)}, u32[]{:S(2)}, u32[]{:S(2)}) collective-permute-start(bf16[64,1792]{1,0:T(8,128)(2,1)S(1)} %shard_map.77.refs_0_), channel_id=1, source_target_pairs={{0,1},{1,2},{2,3},{3,0},{4,5},{5,6},{6,7},{7,4},{8,9},{9,10},{10,1... | collective-permute-start | bytes 688136 | tf_op jit(solution)/shard_map/ppermute | solution.py:255
  135.9 17.4 %collective-permute-start.12 = (bf16[64,1792]{1,0:T(8,128)(2,1)S(1)}, bf16[64,1792]{1,0:T(8,128)(2,1)S(1)}, u32[]{:S(2)}, u32[]{:S(2)}) collective-permute-start(bf16[64,1792]{1,0:T(8,128)(2,1)S(1)} %get-tuple-element.30), channel_id=1, source_target_pairs={{0,1},{1,2},{2,3},{3,0},{4,5},{5,6},{6,7},{7,4},{8,9},{9,10},{10,1... | collective-permute-start | bytes 688136 | tf_op jit(solution)/shard_map/ppermute | solution.py:250
  137.9 15.4 %collective-permute-start.13 = (bf16[64,1792]{1,0:T(8,128)(2,1)S(1)}, bf16[64,1792]{1,0:T(8,128)(2,1)S(1)}, u32[]{:S(2)}, u32[]{:S(2)}) collective-permute-start(bf16[64,1792]{1,0:T(8,128)(2,1)S(1)} %get-tuple-element.31), channel_id=1, source_target_pairs={{0,2},{1,3},{2,0},{3,1},{4,6},{5,7},{6,4},{7,5},{8,10},{9,11},{10,... | collective-permute-start | bytes 688136 | tf_op jit(solution)/shard_map/ppermute | solution.py:250
  139.1 14.2 %collective-permute-start.14 = (bf16[64,1792]{1,0:T(8,128)(2,1)S(1)}, bf16[64,1792]{1,0:T(8,128)(2,1)S(1)}, u32[]{:S(2)}, u32[]{:S(2)}) collective-permute-start(bf16[64,1792]{1,0:T(8,128)(2,1)S(1)} %get-tuple-element.32), channel_id=1, source_target_pairs={{0,3},{1,0},{2,1},{3,2},{4,7},{5,4},{6,5},{7,6},{8,11},{9,8},{10,9... | collective-permute-start | bytes 688136 | tf_op jit(solution)/shard_map/ppermute | solution.py:250
  150.5 37.0 %collective-permute-start.10 = (bf16[128,3584]{1,0:T(8,128)(2,1)}, bf16[128,3584]{1,0:T(8,128)(2,1)}, u32[]{:S(2)}, u32[]{:S(2)}) collective-permute-start(bf16[128,3584]{1,0:T(8,128)(2,1)} %get-tuple-element.28), channel_id=1, source_target_pairs={{0,8},{8,0},{16,24},{24,16},{32,40},{40,32},{48,56},{56,48},{64,72... | collective-permute-start | bytes 2752520 | tf_op jit(solution)/shard_map/ppermute | solution.py:257
  153.4 8.8 %collective-permute-start.15 = (bf16[64,1792]{1,0:T(8,128)(2,1)S(1)}, bf16[64,1792]{1,0:T(8,128)(2,1)S(1)}, u32[]{:S(2)}, u32[]{:S(2)}) collective-permute-start(bf16[64,1792]{1,0:T(8,128)(2,1)S(1)} %get-tuple-element.34), channel_id=1, source_target_pairs={{0,4},{1,5},{2,6},{3,7},{4,0},{5,1},{6,2},{7,3},{8,12},{9,13},{10,... | collective-permute-start | bytes 688136 | tf_op jit(solution)/shard_map/ppermute | solution.py:252
  162.4 6.4 %collective-permute-start.18 = (bf16[64,1792]{1,0:T(8,128)(2,1)S(1)}, bf16[64,1792]{1,0:T(8,128)(2,1)S(1)}, u32[]{:S(2)}, u32[]{:S(2)}) collective-permute-start(bf16[64,1792]{1,0:T(8,128)(2,1)S(1)} %shard_map.81.refs_0_), channel_id=1, source_target_pairs={{0,3},{1,0},{2,1},{3,2},{4,7},{5,4},{6,5},{7,6},{8,11},{9,8},{10,9... | collective-permute-start | bytes 688136 | tf_op jit(solution)/shard_map/ppermute | solution.py:255
  163.5 7.6 %collective-permute-start.17 = (bf16[64,1792]{1,0:T(8,128)(2,1)S(1)}, bf16[64,1792]{1,0:T(8,128)(2,1)S(1)}, u32[]{:S(2)}, u32[]{:S(2)}) collective-permute-start(bf16[64,1792]{1,0:T(8,128)(2,1)S(1)} %shard_map.81.refs_0_), channel_id=1, source_target_pairs={{0,2},{1,3},{2,0},{3,1},{4,6},{5,7},{6,4},{7,5},{8,10},{9,11},{10,... | collective-permute-start | bytes 688136 | tf_op jit(solution)/shard_map/ppermute | solution.py:255
  164.8 12.6 %collective-permute-start.16 = (bf16[64,1792]{1,0:T(8,128)(2,1)S(1)}, bf16[64,1792]{1,0:T(8,128)(2,1)S(1)}, u32[]{:S(2)}, u32[]{:S(2)}) collective-permute-start(bf16[64,1792]{1,0:T(8,128)(2,1)S(1)} %shard_map.81.refs_0_), channel_id=1, source_target_pairs={{0,1},{1,2},{2,3},{3,0},{4,5},{5,6},{6,7},{7,4},{8,9},{9,10},{10,1... | collective-permute-start | bytes 688136 | tf_op jit(solution)/shard_map/ppermute | solution.py:255
  187.0 7.3 %collective-permute-start.19 = (bf16[128,3584]{1,0:T(8,128)(2,1)S(1)}, bf16[128,3584]{1,0:T(8,128)(2,1)}, u32[]{:S(2)}, u32[]{:S(2)}) collective-permute-start(bf16[128,3584]{1,0:T(8,128)(2,1)S(1)} %get-tuple-element.36), channel_id=1, source_target_pairs={{0,8},{8,0},{16,24},{24,16},{32,40},{40,32},{48,56},{56,48},{64,72... | collective-permute-start | bytes 2752520 | tf_op jit(solution)/shard_map/ppermute | solution.py:257
  189.9 4.4 %copy-start.2 = (f32[128,3584]{1,0:T(8,128)S(1)}, f32[128,3584]{1,0:T(8,128)}, u32[]{:S(2)}) copy-start(f32[128,3584]{1,0:T(8,128)} %copy-done.1) | copy-start | bytes 5505028
  189.9 17.9 %all-to-all-start.2 = ((bf16[8,16,3584]{2,1,0:T(8,128)(2,1)}), bf16[8,16,3584]{2,1,0:T(8,128)(2,1)}, u32[]{:S(2)}, u32[]{:S(2)}) async-start(bf16[8,16,3584]{2,1,0:T(8,128)(2,1)} %bitcast.31), calls=%async_computation.2 | async-start | bytes 1835008 | tf_op jit(solution)/shard_map/all_to_all | solution.py:259
  207.8 17.0 %all-to-all-start.3 = ((bf16[8,16,3584]{2,1,0:T(8,128)(2,1)}), bf16[8,16,3584]{2,1,0:T(8,128)(2,1)S(1)}, u32[]{:S(2)}, u32[]{:S(2)}) async-start(bf16[8,16,3584]{2,1,0:T(8,128)(2,1)} %bitcast.16), calls=%async_computation.3 | async-start | bytes 1835008 | tf_op jit(solution)/shard_map/all_to_all | solution.py:259
  (5 other events, 7.8 us)

commit v3 on v2

v3 whole, which is shorter than its diff:
```python
import functools

import jax
import jax.numpy as jnp
from jax import lax
from jax.experimental import pallas as pl
from jax.experimental.pallas import tpu as pltpu
from jax.sharding import PartitionSpec as P

damping = 0.05
CHUNKS = 2
RING = 4
F32, BF16 = jnp.float32, jnp.bfloat16
VMEM = pl.BlockSpec(memory_space=pltpu.VMEM)
ANY = pl.BlockSpec(memory_space=pl.ANY)
SMEM = pl.BlockSpec(memory_space=pltpu.SMEM)
NN = (((1,), (0,)), ((), ()))
NT = (((1,), (1,)), ((), ()))


def cost(flops, nbytes):
    return pl.CostEstimate(flops=flops // 1000, bytes_accessed=nbytes // 1000, transcendentals=0)


def dot(a, b, dims=NN):
    return lax.dot_general(a, b, dims, preferred_element_type=F32)


def params(mib):
    return pltpu.CompilerParams(vmem_limit_bytes=mib << 20)


def fixed(shape, at=(0, 0)):
    return pl.BlockSpec(shape, lambda *_: at)


def select_kernel(ids, basis, out, acc, *, chips):
    step = pl.program_id(0)
    width, queries = basis.shape[1], ids.shape[1]
    want = (ids[...] - step * width).astype(jnp.int16)
    lanes = lax.broadcasted_iota(jnp.int16, (width, queries), 0)
    hot = jnp.where(lanes == want, jnp.ones((), BF16), jnp.zeros((), BF16))
    part = dot(basis[...], hot)

    @pl.when(step == 0)
    def _():
        acc[...] = part

    @pl.when(step > 0)
    def _():
        acc[...] += part

    @pl.when(step == pl.num_programs(0) - 1)
    def _():
        rows = acc[...].T.astype(BF16)
        share = queries // chips // CHUNKS
        run = share // 2
        for chip in range(chips):
            for core in range(2):
                for n in range(CHUNKS):
                    at = (core * chips + chip) * run
                    to = at // share * (share * CHUNKS) + n * share + at % share
                    at = ((chip * 2 + core) * CHUNKS + n) * run
                    out[to : to + run, :] = rows[at : at + run, :]


def select(ids, basis, chips, block=2048):
    rows, width = basis.shape
    queries = ids.shape[0]
    return pl.pallas_call(
        functools.partial(select_kernel, chips=chips),
        grid=(width // block,),
        in_specs=[fixed((1, queries)), pl.BlockSpec((rows, block), lambda i: (0, i))],
        out_specs=fixed((queries, rows)),
        out_shape=jax.ShapeDtypeStruct((queries, rows), BF16),
        scratch_shapes=[pltpu.VMEM((rows, queries), F32)],
        cost_estimate=cost(2 * queries * rows * width, rows * width * 2),
        compiler_params=params(56),
    )(ids[None, :], basis)


def rows_kernel(place, sel, sel2, grad, grad2, out, buf, buf2, sems):
    steps = sems.shape[1]
    half = out.shape[1]
    block = half // steps
    copies = []
    for i in range(steps):
        at = pl.ds(pl.multiple_of(place[0] * half + i * block, block), block)
        to = pl.ds(i * block, block)
        copies.append(
            [
                pltpu.make_async_copy(grad.at[:, at], buf.at[:, to], sems.at[0, i]),
                pltpu.make_async_copy(grad2.at[:, at], buf2.at[:, to], sems.at[1, i]),
            ]
        )
    for first, second in copies:
        first.start()
        second.start()
    for i in range(steps):
        to = pl.ds(i * block, block)
        copies[i][0].wait()
        copies[i][1].wait()
        total = dot(sel[...], buf[:, to]) + dot(sel2[...], buf2[:, to])
        out[:, to] = total.astype(BF16)


def partial_rows(place, sel, sel2, grad, grad2, steps=2):
    queries, units = sel.shape
    half = grad.shape[1] // 2
    return pl.pallas_call(
        rows_kernel,
        in_specs=[SMEM, VMEM, VMEM, ANY, ANY],
        out_specs=VMEM,
        out_shape=jax.ShapeDtypeStruct((queries, half), BF16),
        scratch_shapes=[
            pltpu.VMEM((units, half), BF16),
            pltpu.VMEM((units, half), BF16),
            pltpu.SemaphoreType.DMA((2, steps)),
        ],
        cost_estimate=cost(4 * queries * units * half, 6 * queries * half),
        compiler_params=params(56),
    )(place, sel, sel2, grad, grad2)


def fetch(basis, buf, sems, cuts):
    copies = []
    for i, (start, size) in enumerate(cuts):
        at = pl.ds(start, size)
        copies.append(pltpu.make_async_copy(basis.at[at, :], buf.at[at, :], sems.at[i]))
    for copy in copies:
        copy.start()
    return copies


def rotate_kernel(place, own, other, basis, *refs, cuts):
    outs, (lhs, buf, acc, sems) = refs[:RING], refs[RING:]
    copies = fetch(basis, buf, sems, cuts)
    core, x = place[0], place[1]
    piece, half = outs[0].shape[0], own.shape[1]
    for d in range(RING):
        rows = pl.ds(pl.multiple_of(lax.rem(x + d, RING) * piece, piece), piece)
        to = pl.ds(d * piece, piece)
        lhs[core, to, :] = own[rows, :]
        lhs[1 - core, to, :] = other[rows, :]
    for i, (start, size) in enumerate(cuts):
        copies[i].wait()
        part = lhs[start // half, :, start % half : start % half + size]
        value = dot(part, buf[start : start + size, :])
        if i > 0:
            value += acc[...]
        if i < len(cuts) - 1:
            acc[...] = value
        else:
            for d in range(RING):
                outs[d][...] = value[d * piece : (d + 1) * piece].astype(outs[d].dtype)


def rotate(place, own, other, basis):
    m, half = other.shape
    k, n = basis.shape
    piece = m // RING
    block = half // 7
    cuts = [(h * half + at * block, size * block) for h in range(2) for at, size in ((0, 3), (3, 2), (5, 2))]
    return pl.pallas_call(
        functools.partial(rotate_kernel, cuts=cuts),
        in_specs=[SMEM, VMEM, VMEM, ANY],
        out_specs=[VMEM] * RING,
        out_shape=[
            jax.ShapeDtypeStruct((piece, n), F32 if d == 0 else BF16) for d in range(RING)
        ],
        scratch_shapes=[
            pltpu.VMEM((2, m, half), BF16),
            pltpu.VMEM((k, n), BF16),
            pltpu.VMEM((m, n), F32),
            pltpu.SemaphoreType.DMA((len(cuts),)),
        ],
        cost_estimate=cost(2 * m * k * n, 2 * k * n),
        compiler_params=params(50),
    )(place, own, other, basis)


def back_kernel(place, *refs, cuts):
    pieces, (basis, other, own, lhs, rhs, buf, sems) = refs[:RING], refs[RING:]
    copies = fetch(basis, buf, sems, cuts)
    core, x = place[0], place[1]
    piece = pieces[0].shape[0]
    for d in range(RING):
        to = lax.rem(x + RING - d + 2 * (1 - core), RING)
        lhs[pl.ds(pl.multiple_of(to * piece, piece), piece), :] = pieces[d][...]
    rhs[...] = lhs[...].T
    for i, (start, size) in enumerate(cuts):
        copies[i].wait()
        total = dot(buf[start : start + size, :], rhs[...]).T
        other[:, start : start + size] = total[: 2 * piece].astype(BF16)
        own[:, start : start + size] = total[2 * piece :]


def back(place, pieces, basis):
    piece, k = pieces[0].shape
    n = basis.shape[0]
    m = RING * piece
    cuts = [(i * n // 7, n // 7) for i in range(7)]
    return pl.pallas_call(
        functools.partial(back_kernel, cuts=cuts),
        in_specs=[SMEM] + [VMEM] * RING + [ANY],
        out_specs=[VMEM] * 2,
        out_shape=[
            jax.ShapeDtypeStruct((m // 2, n), BF16),
            jax.ShapeDtypeStruct((m // 2, n), F32),
        ],
        scratch_shapes=[
            pltpu.VMEM((m, k), BF16),
            pltpu.VMEM((k, m), BF16),
            pltpu.VMEM((n, k), BF16),
            pltpu.SemaphoreType.DMA((len(cuts),)),
        ],
        cost_estimate=cost(2 * m * k * n, 2 * k * n),
        compiler_params=params(50),
    )(place, *pieces, basis)


def ring_kernel(own, a, b, c, total, rounded):
    value = own[...] + a[...].astype(F32) + b[...].astype(F32) + c[...].astype(F32)
    total[...] = value
    rounded[...] = value.astype(BF16)


def ring_sum(parts):
    shape = parts[0].shape
    return pl.pallas_call(
        ring_kernel,
        in_specs=[VMEM] * RING,
        out_specs=[VMEM] * 2,
        out_shape=[jax.ShapeDtypeStruct(shape, F32), jax.ShapeDtypeStruct(shape, BF16)],
        cost_estimate=cost(3 * shape[0] * shape[1], 16 * shape[0] * shape[1]),
        compiler_params=params(8),
    )(*parts)


def scale_kernel(total, far, rows, cols, out):
    value = total[...] + far[...].astype(F32)
    out[...] = (value / (rows[...] * cols[...] + damping)).astype(BF16)


def scale(total, far, rows, cols):
    return pl.pallas_call(
        scale_kernel,
        in_specs=[VMEM] * 4,
        out_specs=VMEM,
        out_shape=jax.ShapeDtypeStruct(total.shape, BF16),
        cost_estimate=cost(8 * total.size, 8 * total.size),
        compiler_params=params(8),
    )(total, far, rows, cols)


def add_up(parts):
    total = parts[0].astype(F32)
    for i in range(1, parts.shape[0]):
        total += parts[i].astype(F32)
    return total


def tie(*values):
    return lax.optimization_barrier(values)


def per_device(query_ids, layer_index, gradient, out_basis, in_basis, out_eigen, in_eigen):
    loops, reds = lax.axis_size("loop"), lax.axis_size("red")
    chips = loops // 2
    queries = query_ids.shape[0]
    chunk = queries // CHUNKS
    piece = chunk // RING
    core = lax.axis_index("loop") % 2
    x = lax.axis_index("red") % RING
    place = jnp.stack([core, x]).astype(jnp.int32)
    swap = [(i, i ^ 1) for i in range(loops)]
    flip = [(i, (i + RING) % reds) for i in range(reds)]
    shift = [[(i, i - i % RING + (i + d) % RING) for i in range(reds)] for d in range(RING)]
    same_core = [[2 * i + c for i in range(chips)] for c in range(2)]

    def exchange(value):
        value = value.reshape(chips, -1, value.shape[1])
        return lax.all_to_all(value, "loop", 0, 0, axis_index_groups=same_core)

    got = lax.ppermute(gradient, "loop", swap)
    sel = select(query_ids, out_basis, chips)
    sel_got = lax.ppermute(sel, "loop", swap)
    part = partial_rows(place, sel, sel_got, gradient, got)
    part = exchange(part)
    eigen_rows = jnp.take(jnp.take(out_eigen, layer_index, axis=0)[0], query_ids)
    eigen_rows = eigen_rows.reshape(chips, 2, CHUNKS, -1).transpose(2, 1, 0, 3).reshape(CHUNKS, chunk)
    eigen_cols = jnp.take(in_eigen, layer_index, axis=0)
    factors = [
        lax.dynamic_slice_in_dim(eigen_rows[n], x * piece, piece, 0)[:, None] for n in range(CHUNKS)
    ]
    rows_w, *factors = tie(add_up(part).astype(BF16), *factors)
    share = rows_w.shape[0] // CHUNKS

    def gather(rows):
        rows = jnp.broadcast_to(rows[None], (chips,) + rows.shape).reshape(chunk, -1)
        return exchange(rows).reshape(chunk, -1)

    def ring(parts):
        return [parts[0]] + [lax.ppermute(parts[d], "red", shift[d]) for d in range(1, RING)]

    def swapped(value):
        return lax.ppermute(value, "loop", swap)

    own_a = gather(rows_w[:share])
    rows_b, own_a = tie(rows_w[share:], own_a)
    own_b = gather(rows_b)
    rot_a = rotate(place, own_a, swapped(own_a), in_basis)
    ring_a = ring(rot_a)
    own_b, *ring_a = tie(own_b, *ring_a)
    other_b = swapped(own_b)
    total_a, rounded_a = ring_sum(ring_a)
    other_b, total_a = tie(other_b, total_a)
    rot_b = rotate(place, own_b, other_b, in_basis)
    scaled_a = scale(total_a, lax.ppermute(rounded_a, "red", flip), factors[0], eigen_cols)
    ring_b = ring(rot_b)
    pieces_a = ring([scaled_a] * RING)
    total_b, rounded_b = ring_sum(ring_b)
    pieces_a[0], total_b = tie(pieces_a[0], total_b)
    send_a, keep_a = back(place, pieces_a, in_basis)
    scaled_b = scale(total_b, lax.ppermute(rounded_b, "red", flip), factors[1], eigen_cols)
    pieces_b = ring([scaled_b] * RING)
    part_a = (keep_a + swapped(send_a).astype(F32)).astype(BF16)
    pieces_b[0], part_a = tie(pieces_b[0], part_a)
    part_a = exchange(part_a)
    part_a, *pieces_b = tie(part_a, *pieces_b)
    send_b, keep_b = back(place, pieces_b, in_basis)
    part_b = exchange((keep_b + swapped(send_b).astype(F32)).astype(BF16))
    return jnp.concatenate([add_up(part_a).astype(BF16), add_up(part_b).astype(BF16)], 0)


def solution(mesh):
    return jax.shard_map(
        per_device,
        mesh=mesh,
        in_specs=(
            P(),
            P(),
            P("loop", "red"),
            P("loop", None),
            P("red", "loop"),
            P(),
            P(None, "loop"),
        ),
        out_specs=P("loop", "red"),
        check_vma=False,
    )
```

time: 227 us -> 207 us (0.912)
  blocking collectives: 55.6 us -> 16.7 us
  waiting for transfers between devices: 54.6 us -> 76 us
  starting transfers between devices: 36.5 us -> 49.6 us
  local copies, waits for them, and re-layouts: 13.5 us -> 5.58 us
  Pallas kernels: 55.8 us -> 50.6 us
    all_to_all x2 -> x1, blocking collectives: 55.6 us -> 16.7 us  [exchange(): return lax.all_to_all(value, 'loop', 0, 0, axis_index_groups=same_core)]
    ppermute x19, waiting for transfers between devices: 29.3 us -> 41.6 us  [the longest x12 32.7 us: ring(): lax.ppermute(parts[d], 'red', shift[d])]
    all_to_all x2 -> x4, starting transfers between devices: 7.98 us -> 19.3 us  [exchange(): return lax.all_to_all(value, 'loop', 0, 0, axis_index_groups=same_core)]
    all_to_all x2 -> x4, waiting for transfers between devices: 23.2 us -> 32.8 us  [exchange(): return lax.all_to_all(value, 'loop', 0, 0, axis_index_groups=same_core)]
    pallas_call x10, Pallas kernels: 55.8 us -> 50.6 us  [the longest x2 21.1 us: back(): pl.pallas_call(functools.partial(back_kernel, cuts=cuts), in_specs=[SMEM]...]
    unnamed x14 -> x6, local copies, waits for them, and re-layouts: 4.89 us -> 0.8 us
    dynamic_slice x1 -> x0, local copies, waits for them, and re-layouts: 2.87 us -> none  [per_device(): theirs = lax.dynamic_slice_in_dim(gradient, (1 - core) * half, half, 1)]
    convert_element_type x4 -> x5, other arithmetic: 6.15 us -> 3.83 us  [the longest x1 2.26 us: per_device(): part_a = (keep_a + swapped(send_a).astype(F32)).astype(BF16)]
  transfers between devices with their start and end apart: 22 -> 24, of which waited for: 11 -> 15; matrix products, arithmetic and copies ran while one was open for 5% -> 3% of each run, Pallas kernels for 23% -> 11%
where the time goes in v3:
time: 207 us; the launch traced here: 206 us
  waiting for transfers between devices  76 us (37%)
  Pallas kernels  50.6 us (24%)
  starting transfers between devices  49.6 us (24%)
  blocking collectives  16.7 us (8%)
  other arithmetic  6.81 us (3%)
  local copies, waits for them, and re-layouts  5.58 us (3%)
    all_to_all x4, waiting for transfers between devices, exchange(): return lax.all_to_all(value, 'loop', 0, 0, axis_index_groups=same_core)  32.8 us
    ppermute x12, waiting for transfers between devices, ring(): lax.ppermute(parts[d], 'red', shift[d])  32.7 us
    pallas_call x2, Pallas kernels, back(): pl.pallas_call(functools.partial(back_kernel, cuts=cuts), in_specs=[SMEM]...  21.1 us
    all_to_all x4, starting transfers between devices, exchange(): return lax.all_to_all(value, 'loop', 0, 0, axis_index_groups=same_core)  19.3 us
    ppermute x12, starting transfers between devices, ring(): lax.ppermute(parts[d], 'red', shift[d])  17.6 us
    all_to_all x1, blocking collectives, exchange(): return lax.all_to_all(value, 'loop', 0, 0, axis_index_groups=same_core)  16.7 us
    pallas_call x2, Pallas kernels, rotate(): pl.pallas_call(functools.partial(rotate_kernel, cuts=cuts), in_specs=[SME...  14.3 us
    pallas_call x1, Pallas kernels, select(): pl.pallas_call(functools.partial(select_kernel, chips=chips), grid=(width...  8.3 us
  transfers between devices with their start and end apart: 24, of which 15 were waited for; matrix products, arithmetic and copies ran while one was open for 3% of the time, Pallas kernels for 11%

profile of v3, /device:TPU:1, one launch (start us, length us, event | category | flops | bytes accessed | tf_op | source)
XLA Modules:
  0.0 206.2 jit_solution(16445147546034282300)
XLA Ops:
  1.4 8.3 %shard_map.73.sel = bf16[512,512]{1,0:T(8,128)(2,1)} custom-call(s32[1,512]{1,0:T(1,128)} %bitcast.33, bf16[512,8192]{1,0:T(8,128)(2,1)} %basis.3), custom_call_target="tpu_custom_call" | custom-call | flops 4294967 | bytes 8388 | tf_op jit(solution)/shard_map/pallas_call | solution.py:70
  12.6 6.5 %shard_map.74 = bf16[512,1792]{1,0:T(8,128)(2,1)} custom-call(s32[2]{0:T(128)} %pad_add_fusion.place, bf16[512,512]{1,0:T(8,128)(2,1)} %shard_map.73.sel, bf16[512,512]{1,0:T(8,128)(2,1)} %copy-done.1, bf16[512,3584]{1,0:T(8,128)(2,1)} %grad.1, bf16[512,3584]{1,0:T(8,128)(2,1)} %collective-permute-done.1.grad2), custom_call_target="tpu_custom_call" | custom-call | flops 1879048 | bytes 5505 | tf_op jit(solution)/shard_map/pallas_call | solution.py:110
  19.1 6.1 %all-to-all-start = ((bf16[8,64,1792]{2,1,0:T(8,128)(2,1)}), bf16[8,64,1792]{2,1,0:T(8,128)(2,1)S(1)}, u32[]{:S(2)}, u32[]{:S(2)}) async-start(bf16[8,64,1792]{2,1,0:T(8,128)(2,1)} %bitcast.31), calls=%async_computation | async-start | bytes 3670016 | tf_op jit(solution)/shard_map/all_to_all | solution.py:283
  26.9 3.1 %gather_fusion = f32[512]{0:T(512)S(1)} fusion(f32[8192]{0:T(1024)S(1)} %bitcast.30, s32[1024]{0:T(1024)S(1)} %pad_clamp_fusion), kind=kCustom, calls=%fused_computation | custom fusion | bytes 6144 | tf_op jit(solution)/shard_map/jit(_take)/gather | solution.py:290
  30.5 18.2 %all-to-all-done = bf16[8,64,1792]{2,1,0:T(8,128)(2,1)S(1)} async-done(((bf16[8,64,1792]{2,1,0:T(8,128)(2,1)}), bf16[8,64,1792]{2,1,0:T(8,128)(2,1)S(1)}, u32[]{:S(2)}, u32[]{:S(2)}) %all-to-all-start) | async-done | bytes 1835040 | tf_op jit(solution)/shard_map/all_to_all | solution.py:283
  49.0 16.7 %all_to_all.25 = bf16[8,32,1792]{2,1,0:T(8,128)(2,1)S(1)} all-to-all(bf16[8,32,1792]{2,1,0:T(8,128)(2,1)S(1)} %broadcast_in_dim.59), channel_id=1, replica_groups={{0,16,32,48,64,80,96,112},{8,24,40,56,72,88,104,120},{1,17,33,49,65,81,..., dimensions={0} | all-to-all | bytes 1835008 | tf_op jit(solution)/shard_map/all_to_all | solution.py:283
  68.8 3.6 %all-to-all-start.2 = ((bf16[8,32,1792]{2,1,0:T(8,128)(2,1)}), bf16[8,32,1792]{2,1,0:T(8,128)(2,1)S(1)}, u32[]{:S(2)}, u32[]{:S(2)}) async-start(bf16[8,32,1792]{2,1,0:T(8,128)(2,1)} %broadcast_in_dim.60), calls=%async_computation.2 | async-start | bytes 1835008 | tf_op jit(solution)/shard_map/all_to_all | solution.py:283
  72.4 7.5 %shard_map.75 = (f32[64,1792]{1,0:T(8,128)S(1)}, bf16[64,1792]{1,0:T(8,128)(2,1)}, bf16[64,1792]{1,0:T(8,128)(2,1)}, bf16[64,1792]{1,0:T(8,128)(2,1)S(1)}) custom-call(s32[2]{0:T(128)S(1)} %copy-done, bf16[256,1792]{1,0:T(8,128)(2,1)S(1)} %bitcast.29, bf16[256,1792]{1,0:T(8,128)(2,1)S(1)} %collective-permute-done.2.other, bf16[3584,1792]{1,0:T(8,128)(2,1)} %refs_4_.3), custom_call_target="tpu_custom_call" | custom-call | flops 3288334 | bytes 12845 | tf_op jit(solution)/shard_map/pallas_call | solution.py:164
  88.6 5.9 %collective-permute-done.4.b = bf16[64,1792]{1,0:T(8,128)(2,1)S(1)} collective-permute-done((bf16[64,1792]{1,0:T(8,128)(2,1)}, bf16[64,1792]{1,0:T(8,128)(2,1)S(1)}, u32[]{:S(2)}, u32[]{:S(2)}) %collective-permute-start.4) | collective-permute-done | bytes 229408 | tf_op jit(solution)/shard_map/ppermute | solution.py:304
  95.4 2.9 %collective-permute-start.7 = (bf16[64,1792]{1,0:T(8,128)(2,1)S(1)}, bf16[64,1792]{1,0:T(8,128)(2,1)S(1)}, u32[]{:S(2)}, u32[]{:S(2)}) collective-permute-start(bf16[64,1792]{1,0:T(8,128)(2,1)S(1)} %get-tuple-element.56), channel_id=1, source_target_pairs={{0,4},{1,5},{2,6},{3,7},{4,0},{5,1},{6,2},{7,3},{8,12},{9,13},{10,... | collective-permute-start | bytes 688136 | tf_op jit(solution)/shard_map/ppermute | solution.py:319
  98.3 6.8 %shard_map.78 = (f32[64,1792]{1,0:T(8,128)S(1)}, bf16[64,1792]{1,0:T(8,128)(2,1)S(1)}, bf16[64,1792]{1,0:T(8,128)(2,1)S(1)}, bf16[64,1792]{1,0:T(8,128)(2,1)S(1)}) custom-call(s32[2]{0:T(128)S(1)} %copy-done, bf16[256,1792]{1,0:T(8,128)(2,1)S(1)} %bitcast.27, bf16[256,1792]{1,0:T(8,128)(2,1)S(1)} %collective-permute-done.6.other, bf16[3584,1792]{1,0:T(8,128)(2,1)} %refs_4_.3), custom_call_target="tpu_custom_call" | custom-call | flops 3288334 | bytes 12845 | tf_op jit(solution)/shard_map/pallas_call | solution.py:164
  112.1 3.3 %collective-permute-start.14 = (bf16[64,1792]{1,0:T(8,128)(2,1)S(1)}, bf16[64,1792]{1,0:T(8,128)(2,1)S(1)}, u32[]{:S(2)}, u32[]{:S(2)}) collective-permute-start(bf16[64,1792]{1,0:T(8,128)(2,1)S(1)} %shard_map.77.refs_0_), channel_id=1, source_target_pairs={{0,3},{1,0},{2,1},{3,2},{4,7},{5,4},{6,5},{7,6},{8,11},{9,8},{10,9... | collective-permute-start | bytes 688136 | tf_op jit(solution)/shard_map/ppermute | solution.py:304
  116.5 3.4 %collective-permute-done.9.b = bf16[64,1792]{1,0:T(8,128)(2,1)S(1)} collective-permute-done((bf16[64,1792]{1,0:T(8,128)(2,1)S(1)}, bf16[64,1792]{1,0:T(8,128)(2,1)S(1)}, u32[]{:S(2)}, u32[]{:S(2)}) %collective-permute-start.9) | collective-permute-done | bytes 229408 | tf_op jit(solution)/shard_map/ppermute | solution.py:304
  120.0 6.3 %collective-permute-done.12.refs_1_ = bf16[64,1792]{1,0:T(8,128)(2,1)S(1)} collective-permute-done((bf16[64,1792]{1,0:T(8,128)(2,1)S(1)}, bf16[64,1792]{1,0:T(8,128)(2,1)S(1)}, u32[]{:S(2)}, u32[]{:S(2)}) %collective-permute-start.12) | collective-permute-done | bytes 229408 | tf_op jit(solution)/shard_map/ppermute | solution.py:304
  126.3 3.4 %collective-permute-done.13.refs_2_ = bf16[64,1792]{1,0:T(8,128)(2,1)S(1)} collective-permute-done((bf16[64,1792]{1,0:T(8,128)(2,1)S(1)}, bf16[64,1792]{1,0:T(8,128)(2,1)S(1)}, u32[]{:S(2)}, u32[]{:S(2)}) %collective-permute-start.13) | collective-permute-done | bytes 229408 | tf_op jit(solution)/shard_map/ppermute | solution.py:304
  129.8 11.0 %shard_map.81 = (bf16[128,3584]{1,0:T(8,128)(2,1)}, f32[128,3584]{1,0:T(8,128)S(1)}) custom-call(s32[2]{0:T(128)S(1)} %copy-done, bf16[64,1792]{1,0:T(8,128)(2,1)S(1)} %shard_map.77.refs_0_, bf16[64,1792]{1,0:T(8,128)(2,1)S(1)} %collective-permute-done.12.refs_1_, bf16[64,1792]{1,0:T(8,128)(2,1)S(1)} %collective-permute-done.13.refs_2_, ...), custom_call_target="tpu_custom_call" | custom-call | flops 3288334 | bytes 12845 | tf_op jit(solution)/shard_map/pallas_call | solution.py:203
  144.8 6.8 %collective-permute-done.11.far = bf16[64,1792]{1,0:T(8,128)(2,1)S(1)} collective-permute-done((bf16[64,1792]{1,0:T(8,128)(2,1)S(1)}, bf16[64,1792]{1,0:T(8,128)(2,1)S(1)}, u32[]{:S(2)}, u32[]{:S(2)}) %collective-permute-start.11) | collective-permute-done | bytes 229408 | tf_op jit(solution)/shard_map/ppermute | solution.py:325
  154.1 4.5 %all-to-all-start.3 = ((bf16[8,16,3584]{2,1,0:T(8,128)(2,1)}), bf16[8,16,3584]{2,1,0:T(8,128)(2,1)S(1)}, u32[]{:S(2)}, u32[]{:S(2)}) async-start(bf16[8,16,3584]{2,1,0:T(8,128)(2,1)} %bitcast.13), calls=%async_computation.3 | async-start | bytes 1835008 | tf_op jit(solution)/shard_map/all_to_all | solution.py:283
  158.5 3.3 %collective-permute-start.17 = (bf16[64,1792]{1,0:T(8,128)(2,1)S(1)}, bf16[64,1792]{1,0:T(8,128)(2,1)S(1)}, u32[]{:S(2)}, u32[]{:S(2)}) collective-permute-start(bf16[64,1792]{1,0:T(8,128)(2,1)S(1)} %shard_map.80.refs_0_), channel_id=1, source_target_pairs={{0,2},{1,3},{2,0},{3,1},{4,6},{5,7},{6,4},{7,5},{8,10},{9,11},{10,... | collective-permute-start | bytes 688136 | tf_op jit(solution)/shard_map/ppermute | solution.py:304
  161.8 3.9 %collective-permute-done.16.refs_1_ = bf16[64,1792]{1,0:T(8,128)(2,1)S(1)} collective-permute-done((bf16[64,1792]{1,0:T(8,128)(2,1)S(1)}, bf16[64,1792]{1,0:T(8,128)(2,1)S(1)}, u32[]{:S(2)}, u32[]{:S(2)}) %collective-permute-start.16) | collective-permute-done | bytes 229408 | tf_op jit(solution)/shard_map/ppermute | solution.py:304
  165.7 5.5 %collective-permute-done.17.refs_2_ = bf16[64,1792]{1,0:T(8,128)(2,1)S(1)} collective-permute-done((bf16[64,1792]{1,0:T(8,128)(2,1)S(1)}, bf16[64,1792]{1,0:T(8,128)(2,1)S(1)}, u32[]{:S(2)}, u32[]{:S(2)}) %collective-permute-start.17) | collective-permute-done | bytes 229408 | tf_op jit(solution)/shard_map/ppermute | solution.py:304
  171.8 10.1 %shard_map.82 = (bf16[128,3584]{1,0:T(8,128)(2,1)S(1)}, f32[128,3584]{1,0:T(8,128)S(1)}) custom-call(s32[2]{0:T(128)S(1)} %copy-done, bf16[64,1792]{1,0:T(8,128)(2,1)S(1)} %shard_map.80.refs_0_, bf16[64,1792]{1,0:T(8,128)(2,1)S(1)} %collective-permute-done.16.refs_1_, bf16[64,1792]{1,0:T(8,128)(2,1)S(1)} %collective-permute-done.17.refs_2_, ...), custom_call_target="tpu_custom_call" | custom-call | flops 3288334 | bytes 12845 | tf_op jit(solution)/shard_map/pallas_call | solution.py:203
  186.7 5.1 %all-to-all-start.4 = ((bf16[8,16,3584]{2,1,0:T(8,128)(2,1)}), bf16[8,16,3584]{2,1,0:T(8,128)(2,1)S(1)}, u32[]{:S(2)}, u32[]{:S(2)}) async-start(bf16[8,16,3584]{2,1,0:T(8,128)(2,1)} %bitcast.15), calls=%async_computation.4 | async-start | bytes 1835008 | tf_op jit(solution)/shard_map/all_to_all | solution.py:283
  192.0 13.4 %all-to-all-done.4 = bf16[8,16,3584]{2,1,0:T(8,128)(2,1)S(1)} async-done(((bf16[8,16,3584]{2,1,0:T(8,128)(2,1)}), bf16[8,16,3584]{2,1,0:T(8,128)(2,1)S(1)}, u32[]{:S(2)}, u32[]{:S(2)}) %all-to-all-start.4) | async-done | bytes 917536 | tf_op jit(solution)/shard_map/all_to_all | solution.py:283
  (66 shorter events, 39.6 us)
Async XLA Ops:
  0.0 11.8 %collective-permute-start.1 = (bf16[512,3584]{1,0:T(8,128)(2,1)}, bf16[512,3584]{1,0:T(8,128)(2,1)}, u32[]{:S(2)}, u32[]{:S(2)}) collective-permute-start(bf16[512,3584]{1,0:T(8,128)(2,1)} %grad.1), channel_id=1, source_target_pairs={{0,8},{8,0},{16,24},{24,16},{32,40},{40,32},{48,56},{56,48},{64,72... | collective-permute-start | bytes 11010056 | tf_op jit(solution)/shard_map/ppermute | solution.py:285
  9.7 2.1 %collective-permute-start = (bf16[512,512]{1,0:T(8,128)(2,1)}, bf16[512,512]{1,0:T(8,128)(2,1)S(1)}, u32[]{:S(2)}, u32[]{:S(2)}) collective-permute-start(bf16[512,512]{1,0:T(8,128)(2,1)} %shard_map.73.sel), channel_id=1, source_target_pairs={{0,8},{8,0},{16,24},{24,16},{32,40},{40,32},{48,56},{56,48},{64,72... | collective-permute-start | bytes 1572872 | tf_op jit(solution)/shard_map/ppermute | solution.py:287
  19.1 29.6 %all-to-all-start = ((bf16[8,64,1792]{2,1,0:T(8,128)(2,1)}), bf16[8,64,1792]{2,1,0:T(8,128)(2,1)S(1)}, u32[]{:S(2)}, u32[]{:S(2)}) async-start(bf16[8,64,1792]{2,1,0:T(8,128)(2,1)} %bitcast.31), calls=%async_computation | async-start | bytes 3670016 | tf_op jit(solution)/shard_map/all_to_all | solution.py:283
  65.8 6.6 %collective-permute-start.2 = (bf16[256,1792]{1,0:T(8,128)(2,1)S(1)}, bf16[256,1792]{1,0:T(8,128)(2,1)S(1)}, u32[]{:S(2)}, u32[]{:S(2)}) collective-permute-start(bf16[256,1792]{1,0:T(8,128)(2,1)S(1)} %bitcast.28), channel_id=1, source_target_pairs={{0,8},{8,0},{16,24},{24,16},{32,40},{40,32},{48,56},{56,48},{64,72... | collective-permute-start | bytes 2752520 | tf_op jit(solution)/shard_map/ppermute | solution.py:307
  68.8 17.1 %all-to-all-start.2 = ((bf16[8,32,1792]{2,1,0:T(8,128)(2,1)}), bf16[8,32,1792]{2,1,0:T(8,128)(2,1)S(1)}, u32[]{:S(2)}, u32[]{:S(2)}) async-start(bf16[8,32,1792]{2,1,0:T(8,128)(2,1)} %broadcast_in_dim.60), calls=%async_computation.2 | async-start | bytes 1835008 | tf_op jit(solution)/shard_map/all_to_all | solution.py:283
  79.9 8.7 %collective-permute-start.3 = (bf16[64,1792]{1,0:T(8,128)(2,1)}, bf16[64,1792]{1,0:T(8,128)(2,1)S(1)}, u32[]{:S(2)}, u32[]{:S(2)}) collective-permute-start(bf16[64,1792]{1,0:T(8,128)(2,1)} %get-tuple-element.46), channel_id=1, source_target_pairs={{0,1},{1,2},{2,3},{3,0},{4,5},{5,6},{6,7},{7,4},{8,9},{9,10},{10,1... | collective-permute-start | bytes 688136 | tf_op jit(solution)/shard_map/ppermute | solution.py:304
  81.1 13.3 %collective-permute-start.4 = (bf16[64,1792]{1,0:T(8,128)(2,1)}, bf16[64,1792]{1,0:T(8,128)(2,1)S(1)}, u32[]{:S(2)}, u32[]{:S(2)}) collective-permute-start(bf16[64,1792]{1,0:T(8,128)(2,1)} %get-tuple-element.47), channel_id=1, source_target_pairs={{0,2},{1,3},{2,0},{3,1},{4,6},{5,7},{6,4},{7,5},{8,10},{9,11},{10,... | collective-permute-start | bytes 688136 | tf_op jit(solution)/shard_map/ppermute | solution.py:304
  83.6 10.9 %collective-permute-start.5 = (bf16[64,1792]{1,0:T(8,128)(2,1)S(1)}, bf16[64,1792]{1,0:T(8,128)(2,1)S(1)}, u32[]{:S(2)}, u32[]{:S(2)}) collective-permute-start(bf16[64,1792]{1,0:T(8,128)(2,1)S(1)} %get-tuple-element.48), channel_id=1, source_target_pairs={{0,3},{1,0},{2,1},{3,2},{4,7},{5,4},{6,5},{7,6},{8,11},{9,8},{10,9... | collective-permute-start | bytes 688136 | tf_op jit(solution)/shard_map/ppermute | solution.py:304
  94.5 3.8 %collective-permute-start.6 = (bf16[256,1792]{1,0:T(8,128)(2,1)S(1)}, bf16[256,1792]{1,0:T(8,128)(2,1)S(1)}, u32[]{:S(2)}, u32[]{:S(2)}) collective-permute-start(bf16[256,1792]{1,0:T(8,128)(2,1)S(1)} %bitcast.26), channel_id=1, source_target_pairs={{0,8},{8,0},{16,24},{24,16},{32,40},{40,32},{48,56},{56,48},{64,72... | collective-permute-start | bytes 2752520 | tf_op jit(solution)/shard_map/ppermute | solution.py:307
  95.4 14.5 %collective-permute-start.7 = (bf16[64,1792]{1,0:T(8,128)(2,1)S(1)}, bf16[64,1792]{1,0:T(8,128)(2,1)S(1)}, u32[]{:S(2)}, u32[]{:S(2)}) collective-permute-start(bf16[64,1792]{1,0:T(8,128)(2,1)S(1)} %get-tuple-element.56), channel_id=1, source_target_pairs={{0,4},{1,5},{2,6},{3,7},{4,0},{5,1},{6,2},{7,3},{8,12},{9,13},{10,... | collective-permute-start | bytes 688136 | tf_op jit(solution)/shard_map/ppermute | solution.py:319
  105.0 7.1 %collective-permute-start.10 = (bf16[64,1792]{1,0:T(8,128)(2,1)S(1)}, bf16[64,1792]{1,0:T(8,128)(2,1)S(1)}, u32[]{:S(2)}, u32[]{:S(2)}) collective-permute-start(bf16[64,1792]{1,0:T(8,128)(2,1)S(1)} %get-tuple-element.62), channel_id=1, source_target_pairs={{0,3},{1,0},{2,1},{3,2},{4,7},{5,4},{6,5},{7,6},{8,11},{9,8},{10,9... | collective-permute-start | bytes 688136 | tf_op jit(solution)/shard_map/ppermute | solution.py:304
  107.9 8.7 %collective-permute-start.8 = (bf16[64,1792]{1,0:T(8,128)(2,1)S(1)}, bf16[64,1792]{1,0:T(8,128)(2,1)S(1)}, u32[]{:S(2)}, u32[]{:S(2)}) collective-permute-start(bf16[64,1792]{1,0:T(8,128)(2,1)S(1)} %get-tuple-element.60), channel_id=1, source_target_pairs={{0,1},{1,2},{2,3},{3,0},{4,5},{5,6},{6,7},{7,4},{8,9},{9,10},{10,1... | collective-permute-start | bytes 688136 | tf_op jit(solution)/shard_map/ppermute | solution.py:304
  107.9 11.9 %collective-permute-start.9 = (bf16[64,1792]{1,0:T(8,128)(2,1)S(1)}, bf16[64,1792]{1,0:T(8,128)(2,1)S(1)}, u32[]{:S(2)}, u32[]{:S(2)}) collective-permute-start(bf16[64,1792]{1,0:T(8,128)(2,1)S(1)} %get-tuple-element.61), channel_id=1, source_target_pairs={{0,2},{1,3},{2,0},{3,1},{4,6},{5,7},{6,4},{7,5},{8,10},{9,11},{10,... | collective-permute-start | bytes 688136 | tf_op jit(solution)/shard_map/ppermute | solution.py:304
  110.0 16.3 %collective-permute-start.12 = (bf16[64,1792]{1,0:T(8,128)(2,1)S(1)}, bf16[64,1792]{1,0:T(8,128)(2,1)S(1)}, u32[]{:S(2)}, u32[]{:S(2)}) collective-permute-start(bf16[64,1792]{1,0:T(8,128)(2,1)S(1)} %shard_map.77.refs_0_), channel_id=1, source_target_pairs={{0,1},{1,2},{2,3},{3,0},{4,5},{5,6},{6,7},{7,4},{8,9},{9,10},{10,1... | collective-permute-start | bytes 688136 | tf_op jit(solution)/shard_map/ppermute | solution.py:304
  111.5 18.3 %collective-permute-start.13 = (bf16[64,1792]{1,0:T(8,128)(2,1)S(1)}, bf16[64,1792]{1,0:T(8,128)(2,1)S(1)}, u32[]{:S(2)}, u32[]{:S(2)}) collective-permute-start(bf16[64,1792]{1,0:T(8,128)(2,1)S(1)} %shard_map.77.refs_0_), channel_id=1, source_target_pairs={{0,2},{1,3},{2,0},{3,1},{4,6},{5,7},{6,4},{7,5},{8,10},{9,11},{10,... | collective-permute-start | bytes 688136 | tf_op jit(solution)/shard_map/ppermute | solution.py:304
  112.1 17.6 %collective-permute-start.14 = (bf16[64,1792]{1,0:T(8,128)(2,1)S(1)}, bf16[64,1792]{1,0:T(8,128)(2,1)S(1)}, u32[]{:S(2)}, u32[]{:S(2)}) collective-permute-start(bf16[64,1792]{1,0:T(8,128)(2,1)S(1)} %shard_map.77.refs_0_), channel_id=1, source_target_pairs={{0,3},{1,0},{2,1},{3,2},{4,7},{5,4},{6,5},{7,6},{8,11},{9,8},{10,9... | collective-permute-start | bytes 688136 | tf_op jit(solution)/shard_map/ppermute | solution.py:304
  140.8 11.0 %collective-permute-start.15 = (bf16[128,3584]{1,0:T(8,128)(2,1)}, bf16[128,3584]{1,0:T(8,128)(2,1)}, u32[]{:S(2)}, u32[]{:S(2)}) collective-permute-start(bf16[128,3584]{1,0:T(8,128)(2,1)} %get-tuple-element.69), channel_id=1, source_target_pairs={{0,8},{8,0},{16,24},{24,16},{32,40},{40,32},{48,56},{56,48},{64,72... | collective-permute-start | bytes 2752520 | tf_op jit(solution)/shard_map/ppermute | solution.py:307
  143.0 8.7 %collective-permute-start.11 = (bf16[64,1792]{1,0:T(8,128)(2,1)S(1)}, bf16[64,1792]{1,0:T(8,128)(2,1)S(1)}, u32[]{:S(2)}, u32[]{:S(2)}) collective-permute-start(bf16[64,1792]{1,0:T(8,128)(2,1)S(1)} %get-tuple-element.65), channel_id=1, source_target_pairs={{0,4},{1,5},{2,6},{3,7},{4,0},{5,1},{6,2},{7,3},{8,12},{9,13},{10,... | collective-permute-start | bytes 688136 | tf_op jit(solution)/shard_map/ppermute | solution.py:325
  154.1 17.7 %all-to-all-start.3 = ((bf16[8,16,3584]{2,1,0:T(8,128)(2,1)}), bf16[8,16,3584]{2,1,0:T(8,128)(2,1)S(1)}, u32[]{:S(2)}, u32[]{:S(2)}) async-start(bf16[8,16,3584]{2,1,0:T(8,128)(2,1)} %bitcast.13), calls=%async_computation.3 | async-start | bytes 1835008 | tf_op jit(solution)/shard_map/all_to_all | solution.py:283
  158.5 7.2 %collective-permute-start.16 = (bf16[64,1792]{1,0:T(8,128)(2,1)S(1)}, bf16[64,1792]{1,0:T(8,128)(2,1)S(1)}, u32[]{:S(2)}, u32[]{:S(2)}) collective-permute-start(bf16[64,1792]{1,0:T(8,128)(2,1)S(1)} %shard_map.80.refs_0_), channel_id=1, source_target_pairs={{0,1},{1,2},{2,3},{3,0},{4,5},{5,6},{6,7},{7,4},{8,9},{9,10},{10,1... | collective-permute-start | bytes 688136 | tf_op jit(solution)/shard_map/ppermute | solution.py:304
  158.5 12.7 %collective-permute-start.17 = (bf16[64,1792]{1,0:T(8,128)(2,1)S(1)}, bf16[64,1792]{1,0:T(8,128)(2,1)S(1)}, u32[]{:S(2)}, u32[]{:S(2)}) collective-permute-start(bf16[64,1792]{1,0:T(8,128)(2,1)S(1)} %shard_map.80.refs_0_), channel_id=1, source_target_pairs={{0,2},{1,3},{2,0},{3,1},{4,6},{5,7},{6,4},{7,5},{8,10},{9,11},{10,... | collective-permute-start | bytes 688136 | tf_op jit(solution)/shard_map/ppermute | solution.py:304
  161.8 9.9 %collective-permute-start.18 = (bf16[64,1792]{1,0:T(8,128)(2,1)S(1)}, bf16[64,1792]{1,0:T(8,128)(2,1)S(1)}, u32[]{:S(2)}, u32[]{:S(2)}) collective-permute-start(bf16[64,1792]{1,0:T(8,128)(2,1)S(1)} %shard_map.80.refs_0_), channel_id=1, source_target_pairs={{0,3},{1,0},{2,1},{3,2},{4,7},{5,4},{6,5},{7,6},{8,11},{9,8},{10,9... | collective-permute-start | bytes 688136 | tf_op jit(solution)/shard_map/ppermute | solution.py:304
  181.9 3.7 %collective-permute-start.19 = (bf16[128,3584]{1,0:T(8,128)(2,1)S(1)}, bf16[128,3584]{1,0:T(8,128)(2,1)S(1)}, u32[]{:S(2)}, u32[]{:S(2)}) collective-permute-start(bf16[128,3584]{1,0:T(8,128)(2,1)S(1)} %get-tuple-element.78), channel_id=1, source_target_pairs={{0,8},{8,0},{16,24},{24,16},{32,40},{40,32},{48,56},{56,48},{64,72... | collective-permute-start | bytes 2752520 | tf_op jit(solution)/shard_map/ppermute | solution.py:307
  186.7 18.7 %all-to-all-start.4 = ((bf16[8,16,3584]{2,1,0:T(8,128)(2,1)}), bf16[8,16,3584]{2,1,0:T(8,128)(2,1)S(1)}, u32[]{:S(2)}, u32[]{:S(2)}) async-start(bf16[8,16,3584]{2,1,0:T(8,128)(2,1)} %bitcast.15), calls=%async_computation.4 | async-start | bytes 1835008 | tf_op jit(solution)/shard_map/all_to_all | solution.py:283
  (3 other events, 13.5 us)

commit v4 on v3

v4 whole, which is shorter than its diff:
```python
import functools

import jax
import jax.numpy as jnp
from jax import lax
from jax.experimental import pallas as pl
from jax.experimental.pallas import tpu as pltpu
from jax.sharding import PartitionSpec as P

damping = 0.05
CHUNKS = 1
RING = 4
F32, BF16 = jnp.float32, jnp.bfloat16
VMEM = pl.BlockSpec(memory_space=pltpu.VMEM)
ANY = pl.BlockSpec(memory_space=pl.ANY)
SMEM = pl.BlockSpec(memory_space=pltpu.SMEM)
NN = (((1,), (0,)), ((), ()))
NT = (((1,), (1,)), ((), ()))


def cost(flops, nbytes):
    return pl.CostEstimate(flops=flops // 1000, bytes_accessed=nbytes // 1000, transcendentals=0)


def dot(a, b, dims=NN):
    return lax.dot_general(a, b, dims, preferred_element_type=F32)


def params(mib):
    return pltpu.CompilerParams(vmem_limit_bytes=mib << 20)


def fixed(shape, at=(0, 0)):
    return pl.BlockSpec(shape, lambda *_: at)


def select_kernel(ids, basis, out, acc, *, chips):
    step = pl.program_id(0)
    width, queries = basis.shape[1], ids.shape[1]
    want = (ids[...] - step * width).astype(jnp.int16)
    lanes = lax.broadcasted_iota(jnp.int16, (width, queries), 0)
    hot = jnp.where(lanes == want, jnp.ones((), BF16), jnp.zeros((), BF16))
    part = dot(basis[...], hot)

    @pl.when(step == 0)
    def _():
        acc[...] = part

    @pl.when(step > 0)
    def _():
        acc[...] += part

    @pl.when(step == pl.num_programs(0) - 1)
    def _():
        rows = acc[...].T.astype(BF16)
        share = queries // chips // CHUNKS
        run = share // 2
        for chip in range(chips):
            for core in range(2):
                for n in range(CHUNKS):
                    at = (core * chips + chip) * run
                    to = at // share * (share * CHUNKS) + n * share + at % share
                    at = ((chip * 2 + core) * CHUNKS + n) * run
                    out[to : to + run, :] = rows[at : at + run, :]


def select(ids, basis, chips, block=2048):
    rows, width = basis.shape
    queries = ids.shape[0]
    return pl.pallas_call(
        functools.partial(select_kernel, chips=chips),
        grid=(width // block,),
        in_specs=[fixed((1, queries)), pl.BlockSpec((rows, block), lambda i: (0, i))],
        out_specs=fixed((queries, rows)),
        out_shape=jax.ShapeDtypeStruct((queries, rows), BF16),
        scratch_shapes=[pltpu.VMEM((rows, queries), F32)],
        cost_estimate=cost(2 * queries * rows * width, rows * width * 2),
        compiler_params=params(56),
    )(ids[None, :], basis)


def fetch(source, buf, sems, cuts):
    copies = []
    for i, (at, to) in enumerate(cuts):
        copies.append(pltpu.make_async_copy(source.at[at], buf.at[to], sems.at[i]))
    for copy in copies:
        copy.start()
    return copies


def rows_kernel(place, sel, grad, *refs):
    before, (out, buf, sems) = refs[:-3], refs[-3:]
    half = out.shape[1]
    block = half // sems.shape[0]
    cuts = []
    for i in range(sems.shape[0]):
        at = pl.ds(pl.multiple_of(place[0] * half + i * block, block), block)
        cuts.append(((slice(None), at), (slice(None), pl.ds(i * block, block))))
    copies = fetch(grad, buf, sems, cuts)
    for i in range(sems.shape[0]):
        to = pl.ds(i * block, block)
        copies[i].wait()
        total = dot(sel[...], buf[:, to])
        for ref in before:
            total += ref[:, to]
        out[:, to] = total.astype(out.dtype)


def partial_rows(place, sel, grad, *before, steps=2):
    queries, units = sel.shape
    half = grad.shape[1] // 2
    return pl.pallas_call(
        rows_kernel,
        in_specs=[SMEM, VMEM, ANY] + [VMEM] * len(before),
        out_specs=VMEM,
        out_shape=jax.ShapeDtypeStruct((queries, half), BF16 if before else F32),
        scratch_shapes=[pltpu.VMEM((units, half), BF16), pltpu.SemaphoreType.DMA((steps,))],
        cost_estimate=cost(2 * queries * units * half, 6 * queries * half),
        compiler_params=params(56),
    )(place, sel, grad, *before)


def rotate_own_kernel(place, own, basis, acc, lhs, buf, sems):
    core, x = place[0], place[1]
    half, steps = own.shape[1], sems.shape[0]
    block = basis.shape[1] // steps
    at = pl.ds(pl.multiple_of(core * half, half), half)
    blocks = [pl.ds(i * block, block) for i in range(steps)]
    copies = fetch(basis, buf, sems, [((at, to), (slice(None), to)) for to in blocks])
    piece = own.shape[0] // RING
    for d in range(RING):
        rows = pl.ds(pl.multiple_of(lax.rem(x + d, RING) * piece, piece), piece)
        lhs[d * piece : (d + 1) * piece, :] = own[rows, :]
    for i in range(steps):
        copies[i].wait()
        acc[:, blocks[i]] = dot(lhs[...], buf[:, blocks[i]])


def rotate_other_kernel(place, other, basis, acc, *refs):
    outs, (lhs, buf, sems) = refs[:RING], refs[RING:]
    core, x = place[0], place[1]
    half, steps = other.shape[1], sems.shape[0]
    block = basis.shape[1] // steps
    at = pl.ds(pl.multiple_of((1 - core) * half, half), half)
    blocks = [pl.ds(i * block, block) for i in range(steps)]
    copies = fetch(basis, buf, sems, [((at, to), (slice(None), to)) for to in blocks])
    piece = other.shape[0] // RING
    for d in range(RING):
        rows = pl.ds(pl.multiple_of(lax.rem(x + d, RING) * piece, piece), piece)
        lhs[d * piece : (d + 1) * piece, :] = other[rows, :]
    for i in range(steps):
        copies[i].wait()
        total = dot(lhs[...], buf[:, blocks[i]]) + acc[:, blocks[i]]
        for d in range(RING):
            outs[d][:, blocks[i]] = total[d * piece : (d + 1) * piece].astype(outs[d].dtype)


def rotate(place, rows, basis, acc=None, steps=2):
    m, half = rows.shape
    n = basis.shape[1]
    scratch = [
        pltpu.VMEM((m, half), BF16),
        pltpu.VMEM((half, n), BF16),
        pltpu.SemaphoreType.DMA((steps,)),
    ]
    if acc is None:
        return pl.pallas_call(
            rotate_own_kernel,
            in_specs=[SMEM, VMEM, ANY],
            out_specs=VMEM,
            out_shape=jax.ShapeDtypeStruct((m, n), F32),
            scratch_shapes=scratch,
            cost_estimate=cost(2 * m * half * n, 2 * half * n),
            compiler_params=params(52),
        )(place, rows, basis)
    return pl.pallas_call(
        rotate_other_kernel,
        in_specs=[SMEM, VMEM, ANY, VMEM],
        out_specs=[VMEM] * RING,
        out_shape=[
            jax.ShapeDtypeStruct((m // RING, n), F32 if d == 0 else BF16) for d in range(RING)
        ],
        scratch_shapes=scratch,
        cost_estimate=cost(2 * m * half * n, 2 * half * n),
        compiler_params=params(52),
    )(place, rows, basis, acc)


def back_kernel(place, *refs):
    pieces, (basis, other, own, lhs, rhs, buf, sems) = refs[:RING], refs[RING:]
    block = basis.shape[0] // sems.shape[0]
    blocks = [pl.ds(i * block, block) for i in range(sems.shape[0])]
    copies = fetch(basis, buf, sems, [((at,), (at,)) for at in blocks])
    core, x = place[0], place[1]
    piece = pieces[0].shape[0]
    for d in range(RING):
        to = lax.rem(x + RING - d + 2 * (1 - core), RING)
        lhs[pl.ds(pl.multiple_of(to * piece, piece), piece), :] = pieces[d][...]
    rhs[...] = lhs[...].T
    for i, at in enumerate(blocks):
        copies[i].wait()
        total = dot(buf[at, :], rhs[...]).T
        other[:, at] = total[: 2 * piece].astype(BF16)
        own[:, at] = total[2 * piece :]


def back(place, pieces, basis, steps=7):
    piece, k = pieces[0].shape
    n = basis.shape[0]
    m = RING * piece
    return pl.pallas_call(
        back_kernel,
        in_specs=[SMEM] + [VMEM] * RING + [ANY],
        out_specs=[VMEM] * 2,
        out_shape=[
            jax.ShapeDtypeStruct((m // 2, n), BF16),
            jax.ShapeDtypeStruct((m // 2, n), F32),
        ],
        scratch_shapes=[
            pltpu.VMEM((m, k), BF16),
            pltpu.VMEM((k, m), BF16),
            pltpu.VMEM((n, k), BF16),
            pltpu.SemaphoreType.DMA((steps,)),
        ],
        cost_estimate=cost(2 * m * k * n, 2 * k * n),
        compiler_params=params(52),
    )(place, *pieces, basis)


def ring_kernel(own, a, b, c, total, rounded):
    value = own[...] + a[...].astype(F32) + b[...].astype(F32) + c[...].astype(F32)
    total[...] = value
    rounded[...] = value.astype(BF16)


def ring_sum(parts):
    shape = parts[0].shape
    return pl.pallas_call(
        ring_kernel,
        in_specs=[VMEM] * RING,
        out_specs=[VMEM] * 2,
        out_shape=[jax.ShapeDtypeStruct(shape, F32), jax.ShapeDtypeStruct(shape, BF16)],
        cost_estimate=cost(3 * shape[0] * shape[1], 16 * shape[0] * shape[1]),
        compiler_params=params(16),
    )(*parts)


def scale_kernel(total, far, rows, cols, out):
    value = total[...] + far[...].astype(F32)
    out[...] = (value / (rows[...] * cols[...] + damping)).astype(BF16)


def scale(total, far, rows, cols):
    return pl.pallas_call(
        scale_kernel,
        in_specs=[VMEM] * 4,
        out_specs=VMEM,
        out_shape=jax.ShapeDtypeStruct(total.shape, BF16),
        cost_estimate=cost(8 * total.size, 8 * total.size),
        compiler_params=params(16),
    )(total, far, rows, cols)


def add_up(parts):
    total = parts[0].astype(F32)
    for i in range(1, parts.shape[0]):
        total += parts[i].astype(F32)
    return total


def tie(*values):
    return lax.optimization_barrier(values)


def per_device(query_ids, layer_index, gradient, out_basis, in_basis, out_eigen, in_eigen):
    loops, reds = lax.axis_size("loop"), lax.axis_size("red")
    chips = loops // 2
    queries = query_ids.shape[0]
    chunk = queries // CHUNKS
    piece = chunk // RING
    core = lax.axis_index("loop") % 2
    x = lax.axis_index("red") % RING
    place = jnp.stack([core, x]).astype(jnp.int32)
    half = gradient.shape[1] // 2
    swap = [(i, i ^ 1) for i in range(loops)]
    flip = [(i, (i + RING) % reds) for i in range(reds)]
    shift = [[(i, i - i % RING + (i + d) % RING) for i in range(reds)] for d in range(RING)]
    same_core = [[2 * i + c for i in range(chips)] for c in range(2)]

    def exchange(value):
        value = value.reshape(chips, -1, value.shape[1])
        return lax.all_to_all(value, "loop", 0, 0, axis_index_groups=same_core)

    got = lax.ppermute(gradient, "loop", swap)
    sel = select(query_ids, out_basis, chips)
    sel_got = lax.ppermute(sel, "loop", swap)
    part = partial_rows(place, sel, gradient)
    part = exchange(partial_rows(place, sel_got, got, part))
    eigen_rows = jnp.take(jnp.take(out_eigen, layer_index, axis=0)[0], query_ids)
    eigen_rows = eigen_rows.reshape(chips, 2, -1).transpose(1, 0, 2).reshape(queries)
    eigen_rows = lax.dynamic_slice_in_dim(eigen_rows, x * piece, piece, 0)[:, None]
    eigen_cols = jnp.take(in_eigen, layer_index, axis=0)
    rows_w, eigen_rows = tie(add_up(part).astype(BF16), eigen_rows)

    def ring(parts):
        return [parts[0]] + [lax.ppermute(parts[d], "red", shift[d]) for d in range(1, RING)]

    own = jnp.broadcast_to(rows_w[None], (chips,) + rows_w.shape).reshape(queries, half)
    own = exchange(own).reshape(queries, half)
    other = lax.ppermute(own, "loop", swap)
    rot = rotate(place, other, in_basis, rotate(place, own, in_basis))
    total, rounded = ring_sum(ring(rot))
    scaled = scale(total, lax.ppermute(rounded, "red", flip), eigen_rows, eigen_cols)
    send, keep = back(place, ring([scaled] * RING), in_basis)
    part = exchange((keep + lax.ppermute(send, "loop", swap).astype(F32)).astype(BF16))
    return add_up(part).astype(BF16)


def solution(mesh):
    return jax.shard_map(
        per_device,
        mesh=mesh,
        in_specs=(
            P(),
            P(),
            P("loop", "red"),
            P("loop", None),
            P("red", "loop"),
            P(),
            P(None, "loop"),
        ),
        out_specs=P("loop", "red"),
        check_vma=False,
    )
```

time: 207 us -> 212 us (1.024)
  blocking collectives: 16.7 us -> 51.7 us
  starting transfers between devices: 49.6 us -> 23.7 us
  waiting for transfers between devices: 76 us -> 69.8 us
    all_to_all x1 -> x2, blocking collectives: 16.7 us -> 51.7 us  [exchange(): return lax.all_to_all(value, 'loop', 0, 0, axis_index_groups=same_core)]
    all_to_all x4 -> x1, waiting for transfers between devices: 32.8 us -> 18.3 us  [exchange(): return lax.all_to_all(value, 'loop', 0, 0, axis_index_groups=same_core)]
    all_to_all x4 -> x1, starting transfers between devices: 19.3 us -> 6.15 us  [exchange(): return lax.all_to_all(value, 'loop', 0, 0, axis_index_groups=same_core)]
    ppermute x12 -> x6, starting transfers between devices: 17.6 us -> 8.74 us  [ring(): lax.ppermute(parts[d], 'red', shift[d])]
    ppermute x12 -> x6, waiting for transfers between devices: 32.7 us -> 38.6 us  [ring(): lax.ppermute(parts[d], 'red', shift[d])]
    ppermute x6 -> x3, waiting for transfers between devices: 8.94 us -> 12.9 us  [the longest x1 9.27 us: per_device(): lax.ppermute(rounded, 'red', flip)]
    ppermute x6 -> x3, starting transfers between devices: 11.3 us -> 7.38 us  [the longest x1 2.88 us: per_device(): lax.ppermute(rounded, 'red', flip)]
    unnamed x6 -> x10, local copies, waits for them, and re-layouts: 0.8 us -> 3.22 us
  transfers between devices with their start and end apart: 24 -> 12, of which waited for: 15 -> 8; matrix products, arithmetic and copies ran while one was open for 3% -> 3% of each run, Pallas kernels for 11% -> 11%
where the time goes in v4:
time: 212 us; the launch traced here: 211 us
  waiting for transfers between devices  69.8 us (33%)
  blocking collectives  51.7 us (24%)
  Pallas kernels  51.6 us (24%)
  starting transfers between devices  23.7 us (11%)
  local copies, waits for them, and re-layouts  6.85 us (3%)
  other arithmetic  5.98 us (3%)
    all_to_all x2, blocking collectives, exchange(): return lax.all_to_all(value, 'loop', 0, 0, axis_index_groups=same_core)  51.7 us
    ppermute x6, waiting for transfers between devices, ring(): lax.ppermute(parts[d], 'red', shift[d])  38.6 us
    all_to_all x1, waiting for transfers between devices, exchange(): return lax.all_to_all(value, 'loop', 0, 0, axis_index_groups=same_core)  18.3 us
    pallas_call x1, Pallas kernels, back(): pl.pallas_call(back_kernel, in_specs=[SMEM] + [VMEM] * RING + [ANY], out_...  13.4 us
    pallas_call x2, Pallas kernels, partial_rows(): pl.pallas_call(rows_kernel, in_specs=[SMEM, VMEM, ANY] + [VMEM] * len(bef...  11.7 us
    pallas_call x1, Pallas kernels, rotate(): pl.pallas_call(rotate_other_kernel, in_specs=[SMEM, VMEM, ANY, VMEM], out...  9.48 us
    ppermute x1, waiting for transfers between devices, per_device(): lax.ppermute(rounded, 'red', flip)  9.27 us
    ppermute x6, starting transfers between devices, ring(): lax.ppermute(parts[d], 'red', shift[d])  8.74 us
  transfers between devices with their start and end apart: 12, of which 8 were waited for; matrix products, arithmetic and copies ran while one was open for 3% of the time, Pallas kernels for 11%

profile of v4, /device:TPU:1, one launch (start us, length us, event | category | flops | bytes accessed | tf_op | source)
XLA Modules:
  0.0 210.5 jit_solution(17161204663238816454)
XLA Ops:
  0.0 1.4 collective-permute-start.1
  1.4 8.3 %shard_map.73.sel = bf16[512,512]{1,0:T(8,128)(2,1)} custom-call(s32[1,512]{1,0:T(1,128)} %bitcast.22, bf16[512,8192]{1,0:T(8,128)(2,1)} %basis.3), custom_call_target="tpu_custom_call" | custom-call | flops 4294967 | bytes 8388 | tf_op jit(solution)/shard_map/pallas_call | solution.py:70
  10.4 5.5 %shard_map.74.refs_0_ = f32[512,1792]{1,0:T(8,128)} custom-call(s32[2]{0:T(128)} %pad_add_fusion.place, bf16[512,512]{1,0:T(8,128)(2,1)} %shard_map.73.sel, bf16[512,3584]{1,0:T(8,128)(2,1)} %grad.1), custom_call_target="tpu_custom_call" | custom-call | flops 939524 | bytes 5505 | tf_op jit(solution)/shard_map/pallas_call | solution.py:112
  16.7 6.1 %shard_map.75 = bf16[512,1792]{1,0:T(8,128)(2,1)} custom-call(s32[2]{0:T(128)} %pad_add_fusion.place, bf16[512,512]{1,0:T(8,128)(2,1)} %copy-done.3, bf16[512,3584]{1,0:T(8,128)(2,1)} %collective-permute-done.1.grad, f32[512,1792]{1,0:T(8,128)} %shard_map.74.refs_0_), custom_call_target="tpu_custom_call" | custom-call | flops 939524 | bytes 5505 | tf_op jit(solution)/shard_map/pallas_call | solution.py:112
  22.9 6.1 %all-to-all-start = ((bf16[8,64,1792]{2,1,0:T(8,128)(2,1)}), bf16[8,64,1792]{2,1,0:T(8,128)(2,1)S(1)}, u32[]{:S(2)}, u32[]{:S(2)}) async-start(bf16[8,64,1792]{2,1,0:T(8,128)(2,1)} %bitcast.19), calls=%async_computation | async-start | bytes 3670016 | tf_op jit(solution)/shard_map/all_to_all | solution.py:292
  30.7 3.1 %gather_fusion = f32[512]{0:T(512)S(1)} fusion(f32[8192]{0:T(1024)S(1)} %bitcast.18, s32[1024]{0:T(1024)S(1)} %pad_clamp_fusion), kind=kCustom, calls=%fused_computation | custom fusion | bytes 6144 | tf_op jit(solution)/shard_map/jit(_take)/gather | solution.py:299
  34.1 18.3 %all-to-all-done = bf16[8,64,1792]{2,1,0:T(8,128)(2,1)S(1)} async-done(((bf16[8,64,1792]{2,1,0:T(8,128)(2,1)}), bf16[8,64,1792]{2,1,0:T(8,128)(2,1)S(1)}, u32[]{:S(2)}, u32[]{:S(2)}) %all-to-all-start) | async-done | bytes 1835040 | tf_op jit(solution)/shard_map/all_to_all | solution.py:292
  52.7 26.4 %all_to_all.15 = bf16[8,64,1792]{2,1,0:T(8,128)(2,1)S(1)} all-to-all(bf16[8,64,1792]{2,1,0:T(8,128)(2,1)S(1)} %broadcast_in_dim.49), channel_id=1, replica_groups={{0,16,32,48,64,80,96,112},{8,24,40,56,72,88,104,120},{1,17,33,49,65,81,..., dimensions={0} | all-to-all | bytes 3670016 | tf_op jit(solution)/shard_map/all_to_all | solution.py:292
  79.1 2.4 %collective-permute-start.2 = (bf16[512,1792]{1,0:T(8,128)(2,1)S(1)}, bf16[512,1792]{1,0:T(8,128)(2,1)S(1)}, u32[]{:S(2)}, u32[]{:S(2)}) collective-permute-start(bf16[512,1792]{1,0:T(8,128)(2,1)S(1)} %bitcast.16), channel_id=1, source_target_pairs={{0,8},{8,0},{16,24},{24,16},{32,40},{40,32},{48,56},{56,48},{64,72... | collective-permute-start | bytes 5505032 | tf_op jit(solution)/shard_map/ppermute | solution.py:310
  81.5 8.4 %shard_map.76.acc = f32[512,1792]{1,0:T(8,128)} custom-call(s32[2]{0:T(128)S(1)} %copy-done.1, bf16[512,1792]{1,0:T(8,128)(2,1)S(1)} %bitcast.17, bf16[3584,1792]{1,0:T(8,128)(2,1)} %refs_4_.1), custom_call_target="tpu_custom_call" | custom-call | flops 3288334 | bytes 6422 | tf_op jit(solution)/shard_map/pallas_call | solution.py:167
  91.2 9.5 %shard_map.77 = (f32[128,1792]{1,0:T(8,128)}, bf16[128,1792]{1,0:T(8,128)(2,1)S(1)}, bf16[128,1792]{1,0:T(8,128)(2,1)S(1)}, bf16[128,1792]{1,0:T(8,128)(2,1)S(1)}) custom-call(s32[2]{0:T(128)S(1)} %copy-done.1, bf16[512,1792]{1,0:T(8,128)(2,1)} %copy-done.2, bf16[3584,1792]{1,0:T(8,128)(2,1)} %refs_4_.1, f32[512,1792]{1,0:T(8,128)} %shard_map.76.acc), custom_call_target="tpu_custom_call" | custom-call | flops 3288334 | bytes 6422 | tf_op jit(solution)/shard_map/pallas_call | solution.py:176
  101.9 2.5 %collective-permute-start.4 = (bf16[128,1792]{1,0:T(8,128)(2,1)S(1)}, bf16[128,1792]{1,0:T(8,128)(2,1)S(1)}, u32[]{:S(2)}, u32[]{:S(2)}) collective-permute-start(bf16[128,1792]{1,0:T(8,128)(2,1)S(1)} %get-tuple-element.18), channel_id=1, source_target_pairs={{0,2},{1,3},{2,0},{3,1},{4,6},{5,7},{6,4},{7,5},{8,10},{9,11},{10,... | collective-permute-start | bytes 1376264 | tf_op jit(solution)/shard_map/ppermute | solution.py:306
  105.5 8.5 %collective-permute-done.3.a = bf16[128,1792]{1,0:T(8,128)(2,1)S(1)} collective-permute-done((bf16[128,1792]{1,0:T(8,128)(2,1)S(1)}, bf16[128,1792]{1,0:T(8,128)(2,1)S(1)}, u32[]{:S(2)}, u32[]{:S(2)}) %collective-permute-start.3) | collective-permute-done | bytes 458784 | tf_op jit(solution)/shard_map/ppermute | solution.py:306
  114.1 10.8 %collective-permute-done.4.b = bf16[128,1792]{1,0:T(8,128)(2,1)S(1)} collective-permute-done((bf16[128,1792]{1,0:T(8,128)(2,1)S(1)}, bf16[128,1792]{1,0:T(8,128)(2,1)S(1)}, u32[]{:S(2)}, u32[]{:S(2)}) %collective-permute-start.4) | collective-permute-done | bytes 458784 | tf_op jit(solution)/shard_map/ppermute | solution.py:306
  126.3 2.9 %collective-permute-start.6 = (bf16[128,1792]{1,0:T(8,128)(2,1)S(1)}, bf16[128,1792]{1,0:T(8,128)(2,1)S(1)}, u32[]{:S(2)}, u32[]{:S(2)}) collective-permute-start(bf16[128,1792]{1,0:T(8,128)(2,1)S(1)} %get-tuple-element.21), channel_id=1, source_target_pairs={{0,4},{1,5},{2,6},{3,7},{4,0},{5,1},{6,2},{7,3},{8,12},{9,13},{10,... | collective-permute-start | bytes 1376264 | tf_op jit(solution)/shard_map/ppermute | solution.py:313
  130.1 9.3 %collective-permute-done.6.far = bf16[128,1792]{1,0:T(8,128)(2,1)S(1)} collective-permute-done((bf16[128,1792]{1,0:T(8,128)(2,1)S(1)}, bf16[128,1792]{1,0:T(8,128)(2,1)S(1)}, u32[]{:S(2)}, u32[]{:S(2)}) %collective-permute-start.6) | collective-permute-done | bytes 458784 | tf_op jit(solution)/shard_map/ppermute | solution.py:313
  139.9 3.5 %collective-permute-start.8 = (bf16[128,1792]{1,0:T(8,128)(2,1)S(1)}, bf16[128,1792]{1,0:T(8,128)(2,1)S(1)}, u32[]{:S(2)}, u32[]{:S(2)}) collective-permute-start(bf16[128,1792]{1,0:T(8,128)(2,1)S(1)} %shard_map.79.refs_0_), channel_id=1, source_target_pairs={{0,2},{1,3},{2,0},{3,1},{4,6},{5,7},{6,4},{7,5},{8,10},{9,11},{10,... | collective-permute-start | bytes 1376264 | tf_op jit(solution)/shard_map/ppermute | solution.py:306
  143.4 7.8 %collective-permute-done.7.refs_1_ = bf16[128,1792]{1,0:T(8,128)(2,1)S(1)} collective-permute-done((bf16[128,1792]{1,0:T(8,128)(2,1)S(1)}, bf16[128,1792]{1,0:T(8,128)(2,1)S(1)}, u32[]{:S(2)}, u32[]{:S(2)}) %collective-permute-start.7) | collective-permute-done | bytes 458784 | tf_op jit(solution)/shard_map/ppermute | solution.py:306
  151.2 11.3 %collective-permute-done.8.refs_2_ = bf16[128,1792]{1,0:T(8,128)(2,1)S(1)} collective-permute-done((bf16[128,1792]{1,0:T(8,128)(2,1)S(1)}, bf16[128,1792]{1,0:T(8,128)(2,1)S(1)}, u32[]{:S(2)}, u32[]{:S(2)}) %collective-permute-start.8) | collective-permute-done | bytes 458784 | tf_op jit(solution)/shard_map/ppermute | solution.py:306
  162.7 13.4 %shard_map.80 = (bf16[256,3584]{1,0:T(8,128)(2,1)}, f32[256,3584]{1,0:T(8,128)}) custom-call(s32[2]{0:T(128)S(1)} %copy-done.1, bf16[128,1792]{1,0:T(8,128)(2,1)S(1)} %shard_map.79.refs_0_, bf16[128,1792]{1,0:T(8,128)(2,1)S(1)} %collective-permute-done.7.refs_1_, bf16[128,1792]{1,0:T(8,128)(2,1)S(1)} %collective-permute-done.8.refs_2_, ...), custom_call_target="tpu_custom_call" | custom-call | flops 6576668 | bytes 12845 | tf_op jit(solution)/shard_map/pallas_call | solution.py:211
  176.1 2.1 %collective-permute-start.10 = (bf16[256,3584]{1,0:T(8,128)(2,1)}, bf16[256,3584]{1,0:T(8,128)(2,1)S(1)}, u32[]{:S(2)}, u32[]{:S(2)}) collective-permute-start(bf16[256,3584]{1,0:T(8,128)(2,1)} %get-tuple-element.24), channel_id=1, source_target_pairs={{0,8},{8,0},{16,24},{24,16},{32,40},{40,32},{48,56},{56,48},{64,72... | collective-permute-start | bytes 5505032 | tf_op jit(solution)/shard_map/ppermute | solution.py:315
  178.2 3.6 %collective-permute-done.10 = bf16[256,3584]{1,0:T(8,128)(2,1)S(1)} collective-permute-done((bf16[256,3584]{1,0:T(8,128)(2,1)}, bf16[256,3584]{1,0:T(8,128)(2,1)S(1)}, u32[]{:S(2)}, u32[]{:S(2)}) %collective-permute-start.10) | collective-permute-done | bytes 1835040 | tf_op jit(solution)/shard_map/ppermute | solution.py:315
  181.8 2.4 %add_convert_fusion = bf16[256,3584]{1,0:T(8,128)(2,1)S(1)} fusion(f32[256,3584]{1,0:T(8,128)} %get-tuple-element.23, bf16[256,3584]{1,0:T(8,128)(2,1)S(1)} %collective-permute-done.10), kind=kLoop, calls=%fused_computation.1 | loop fusion | flops 2752512 | bytes 7340032 | tf_op jit(solution)/shard_map/convert_element_type | solution.py:315
  184.3 25.3 %all_to_all.16 = bf16[8,32,3584]{2,1,0:T(8,128)(2,1)S(1)} all-to-all(bf16[8,32,3584]{2,1,0:T(8,128)(2,1)S(1)} %bitcast.20), channel_id=1, replica_groups={{0,16,32,48,64,80,96,112},{8,24,40,56,72,88,104,120},{1,17,33,49,65,81,..., dimensions={0} | all-to-all | bytes 3670016 | tf_op jit(solution)/shard_map/all_to_all | solution.py:292
  (36 shorter events, 10.7 us)
Async XLA Ops:
  0.0 15.9 %collective-permute-start.1 = (bf16[512,3584]{1,0:T(8,128)(2,1)}, bf16[512,3584]{1,0:T(8,128)(2,1)}, u32[]{:S(2)}, u32[]{:S(2)}) collective-permute-start(bf16[512,3584]{1,0:T(8,128)(2,1)} %grad.1), channel_id=1, source_target_pairs={{0,8},{8,0},{16,24},{24,16},{32,40},{40,32},{48,56},{56,48},{64,72... | collective-permute-start | bytes 11010056 | tf_op jit(solution)/shard_map/ppermute | solution.py:294
  9.7 6.2 %collective-permute-start = (bf16[512,512]{1,0:T(8,128)(2,1)}, bf16[512,512]{1,0:T(8,128)(2,1)S(1)}, u32[]{:S(2)}, u32[]{:S(2)}) collective-permute-start(bf16[512,512]{1,0:T(8,128)(2,1)} %shard_map.73.sel), channel_id=1, source_target_pairs={{0,8},{8,0},{16,24},{24,16},{32,40},{40,32},{48,56},{56,48},{64,72... | collective-permute-start | bytes 1572872 | tf_op jit(solution)/shard_map/ppermute | solution.py:296
  15.9 0.8 copy-start.3
  22.8 6.8 %copy-start.4 = (s32[512]{0:T(512)S(1)}, s32[512]{0:T(512)}, u32[]{:S(2)}) copy-start(s32[512]{0:T(512)} %param.7) | copy-start | bytes 6148
  22.9 29.5 %all-to-all-start = ((bf16[8,64,1792]{2,1,0:T(8,128)(2,1)}), bf16[8,64,1792]{2,1,0:T(8,128)(2,1)S(1)}, u32[]{:S(2)}, u32[]{:S(2)}) async-start(bf16[8,64,1792]{2,1,0:T(8,128)(2,1)} %bitcast.19), calls=%async_computation | async-start | bytes 3670016 | tf_op jit(solution)/shard_map/all_to_all | solution.py:292
  52.7 28.8 %copy-start.1 = (s32[2]{0:T(128)S(1)}, s32[2]{0:T(128)}, u32[]{:S(2)}) copy-start(s32[2]{0:T(128)} %pad_add_fusion.place) | copy-start | bytes 28
  79.1 10.8 %collective-permute-start.2 = (bf16[512,1792]{1,0:T(8,128)(2,1)S(1)}, bf16[512,1792]{1,0:T(8,128)(2,1)S(1)}, u32[]{:S(2)}, u32[]{:S(2)}) collective-permute-start(bf16[512,1792]{1,0:T(8,128)(2,1)S(1)} %bitcast.16), channel_id=1, source_target_pairs={{0,8},{8,0},{16,24},{24,16},{32,40},{40,32},{48,56},{56,48},{64,72... | collective-permute-start | bytes 5505032 | tf_op jit(solution)/shard_map/ppermute | solution.py:310
  89.9 1.3 copy-start.2
  100.7 13.4 %collective-permute-start.3 = (bf16[128,1792]{1,0:T(8,128)(2,1)S(1)}, bf16[128,1792]{1,0:T(8,128)(2,1)S(1)}, u32[]{:S(2)}, u32[]{:S(2)}) collective-permute-start(bf16[128,1792]{1,0:T(8,128)(2,1)S(1)} %get-tuple-element.17), channel_id=1, source_target_pairs={{0,1},{1,2},{2,3},{3,0},{4,5},{5,6},{6,7},{7,4},{8,9},{9,10},{10,1... | collective-permute-start | bytes 1376264 | tf_op jit(solution)/shard_map/ppermute | solution.py:306
  101.9 23.0 %collective-permute-start.4 = (bf16[128,1792]{1,0:T(8,128)(2,1)S(1)}, bf16[128,1792]{1,0:T(8,128)(2,1)S(1)}, u32[]{:S(2)}, u32[]{:S(2)}) collective-permute-start(bf16[128,1792]{1,0:T(8,128)(2,1)S(1)} %get-tuple-element.18), channel_id=1, source_target_pairs={{0,2},{1,3},{2,0},{3,1},{4,6},{5,7},{6,4},{7,5},{8,10},{9,11},{10,... | collective-permute-start | bytes 1376264 | tf_op jit(solution)/shard_map/ppermute | solution.py:306
  104.4 20.5 %collective-permute-start.5 = (bf16[128,1792]{1,0:T(8,128)(2,1)S(1)}, bf16[128,1792]{1,0:T(8,128)(2,1)S(1)}, u32[]{:S(2)}, u32[]{:S(2)}) collective-permute-start(bf16[128,1792]{1,0:T(8,128)(2,1)S(1)} %get-tuple-element.19), channel_id=1, source_target_pairs={{0,3},{1,0},{2,1},{3,2},{4,7},{5,4},{6,5},{7,6},{8,11},{9,8},{10,9... | collective-permute-start | bytes 1376264 | tf_op jit(solution)/shard_map/ppermute | solution.py:306
  124.9 1.2 copy-start
  126.3 13.0 %collective-permute-start.6 = (bf16[128,1792]{1,0:T(8,128)(2,1)S(1)}, bf16[128,1792]{1,0:T(8,128)(2,1)S(1)}, u32[]{:S(2)}, u32[]{:S(2)}) collective-permute-start(bf16[128,1792]{1,0:T(8,128)(2,1)S(1)} %get-tuple-element.21), channel_id=1, source_target_pairs={{0,4},{1,5},{2,6},{3,7},{4,0},{5,1},{6,2},{7,3},{8,12},{9,13},{10,... | collective-permute-start | bytes 1376264 | tf_op jit(solution)/shard_map/ppermute | solution.py:313
  139.6 11.6 %collective-permute-start.7 = (bf16[128,1792]{1,0:T(8,128)(2,1)S(1)}, bf16[128,1792]{1,0:T(8,128)(2,1)S(1)}, u32[]{:S(2)}, u32[]{:S(2)}) collective-permute-start(bf16[128,1792]{1,0:T(8,128)(2,1)S(1)} %shard_map.79.refs_0_), channel_id=1, source_target_pairs={{0,1},{1,2},{2,3},{3,0},{4,5},{5,6},{6,7},{7,4},{8,9},{9,10},{10,1... | collective-permute-start | bytes 1376264 | tf_op jit(solution)/shard_map/ppermute | solution.py:306
  139.9 22.6 %collective-permute-start.8 = (bf16[128,1792]{1,0:T(8,128)(2,1)S(1)}, bf16[128,1792]{1,0:T(8,128)(2,1)S(1)}, u32[]{:S(2)}, u32[]{:S(2)}) collective-permute-start(bf16[128,1792]{1,0:T(8,128)(2,1)S(1)} %shard_map.79.refs_0_), channel_id=1, source_target_pairs={{0,2},{1,3},{2,0},{3,1},{4,6},{5,7},{6,4},{7,5},{8,10},{9,11},{10,... | collective-permute-start | bytes 1376264 | tf_op jit(solution)/shard_map/ppermute | solution.py:306
  143.4 19.3 %collective-permute-start.9 = (bf16[128,1792]{1,0:T(8,128)(2,1)S(1)}, bf16[128,1792]{1,0:T(8,128)(2,1)S(1)}, u32[]{:S(2)}, u32[]{:S(2)}) collective-permute-start(bf16[128,1792]{1,0:T(8,128)(2,1)S(1)} %shard_map.79.refs_0_), channel_id=1, source_target_pairs={{0,3},{1,0},{2,1},{3,2},{4,7},{5,4},{6,5},{7,6},{8,11},{9,8},{10,9... | collective-permute-start | bytes 1376264 | tf_op jit(solution)/shard_map/ppermute | solution.py:306
  176.1 5.7 %collective-permute-start.10 = (bf16[256,3584]{1,0:T(8,128)(2,1)}, bf16[256,3584]{1,0:T(8,128)(2,1)S(1)}, u32[]{:S(2)}, u32[]{:S(2)}) collective-permute-start(bf16[256,3584]{1,0:T(8,128)(2,1)} %get-tuple-element.24), channel_id=1, source_target_pairs={{0,8},{8,0},{16,24},{24,16},{32,40},{40,32},{48,56},{56,48},{64,72... | collective-permute-start | bytes 5505032 | tf_op jit(solution)/shard_map/ppermute | solution.py:315

commit v5 on v3

--- a/solution.py
+++ b/solution.py
@@ -19,7 +19,7 @@
 
 
 def cost(flops, nbytes):
-    return pl.CostEstimate(flops=flops // 1000, bytes_accessed=nbytes // 1000, transcendentals=0)
+    return pl.CostEstimate(flops=flops, bytes_accessed=nbytes, transcendentals=0)
 
 
 def dot(a, b, dims=NN):
@@ -133,10 +133,10 @@
 
 
 def rotate_kernel(place, own, other, basis, *refs, cuts):
-    outs, (lhs, buf, acc, sems) = refs[:RING], refs[RING:]
+    outs, (lhs, buf, acc, sems) = refs[:-4], refs[-4:]
     copies = fetch(basis, buf, sems, cuts)
-    core, x = place[0], place[1]
-    piece, half = outs[0].shape[0], own.shape[1]
+    core, x = place[0], place[1] if len(outs) > 1 else 0
+    piece, half = own.shape[0] // RING, own.shape[1]
     for d in range(RING):
         rows = pl.ds(pl.multiple_of(lax.rem(x + d, RING) * piece, piece), piece)
         to = pl.ds(d * piece, piece)
@@ -150,24 +150,27 @@
             value += acc[...]
         if i < len(cuts) - 1:
             acc[...] = value
+        elif len(outs) == 1:
+            outs[0][...] = value.astype(BF16)
         else:
             for d in range(RING):
                 outs[d][...] = value[d * piece : (d + 1) * piece].astype(outs[d].dtype)
 
 
-def rotate(place, own, other, basis):
+def rotate(place, own, other, basis, stacked=False):
     m, half = other.shape
     k, n = basis.shape
     piece = m // RING
+    outs = [jax.ShapeDtypeStruct((piece, n), F32 if d == 0 else BF16) for d in range(RING)]
+    if stacked:
+        outs = [jax.ShapeDtypeStruct((m, n), BF16)]
     block = half // 7
     cuts = [(h * half + at * block, size * block) for h in range(2) for at, size in ((0, 3), (3, 2), (5, 2))]
     return pl.pallas_call(
         functools.partial(rotate_kernel, cuts=cuts),
         in_specs=[SMEM, VMEM, VMEM, ANY],
-        out_specs=[VMEM] * RING,
-        out_shape=[
-            jax.ShapeDtypeStruct((piece, n), F32 if d == 0 else BF16) for d in range(RING)
-        ],
+        out_specs=[VMEM] * len(outs),
+        out_shape=outs,
         scratch_shapes=[
             pltpu.VMEM((2, m, half), BF16),
             pltpu.VMEM((k, n), BF16),
@@ -180,19 +183,26 @@
 
 
 def back_kernel(place, *refs, cuts):
-    pieces, (basis, other, own, lhs, rhs, buf, sems) = refs[:RING], refs[RING:]
+    pieces, (basis, other, own, lhs, buf, send, keep, sems, out_sems) = refs[:RING], refs[RING:]
     copies = fetch(basis, buf, sems, cuts)
     core, x = place[0], place[1]
     piece = pieces[0].shape[0]
     for d in range(RING):
         to = lax.rem(x + RING - d + 2 * (1 - core), RING)
         lhs[pl.ds(pl.multiple_of(to * piece, piece), piece), :] = pieces[d][...]
-    rhs[...] = lhs[...].T
+    stores = []
     for i, (start, size) in enumerate(cuts):
+        at = pl.ds(start, size)
         copies[i].wait()
-        total = dot(buf[start : start + size, :], rhs[...]).T
-        other[:, start : start + size] = total[: 2 * piece].astype(BF16)
-        own[:, start : start + size] = total[2 * piece :]
+        total = dot(lhs[...], buf[at, :], NT)
+        send[:, at] = total[: 2 * piece].astype(BF16)
+        keep[:, at] = total[2 * piece :]
+        stores.append(pltpu.make_async_copy(send.at[:, at], other.at[:, at], out_sems.at[0, i]))
+        stores[-1].start()
+        stores.append(pltpu.make_async_copy(keep.at[:, at], own.at[:, at], out_sems.at[1, i]))
+        stores[-1].start()
+    for store in stores:
+        store.wait()
 
 
 def back(place, pieces, basis):
@@ -203,20 +213,57 @@
     return pl.pallas_call(
         functools.partial(back_kernel, cuts=cuts),
         in_specs=[SMEM] + [VMEM] * RING + [ANY],
-        out_specs=[VMEM] * 2,
+        out_specs=[ANY] * 2,
         out_shape=[
             jax.ShapeDtypeStruct((m // 2, n), BF16),
             jax.ShapeDtypeStruct((m // 2, n), F32),
         ],
         scratch_shapes=[
             pltpu.VMEM((m, k), BF16),
-            pltpu.VMEM((k, m), BF16),
             pltpu.VMEM((n, k), BF16),
+            pltpu.VMEM((m // 2, n), BF16),
+            pltpu.VMEM((m // 2, n), F32),
             pltpu.SemaphoreType.DMA((len(cuts),)),
+            pltpu.SemaphoreType.DMA((2, len(cuts))),
         ],
         cost_estimate=cost(2 * m * k * n, 2 * k * n),
         compiler_params=params(50),
     )(place, *pieces, basis)
+
+
+def join_kernel(keep, got, out):
+    out[...] = (keep[...] + got[...].astype(F32)).astype(BF16)
+
+
+def join(keep, got):
+    return pl.pallas_call(
+        join_kernel,
+        in_specs=[VMEM] * 2,
+        out_specs=VMEM,
+        out_shape=jax.ShapeDtypeStruct(got.shape, BF16),
+        cost_estimate=cost(2 * got.size, 8 * got.size),
+        compiler_params=params(8),
+    )(keep, got)
+
+
+def stack_kernel(parts, total, rounded):
+    value = parts[0].astype(F32)
+    for d in range(1, RING):
+        value += parts[d].astype(F32)
+    total[...] = value
+    rounded[...] = value.astype(BF16)
+
+
+def stack_sum(parts):
+    shape = parts.shape[1:]
+    return pl.pallas_call(
+        stack_kernel,
+        in_specs=[VMEM],
+        out_specs=[VMEM] * 2,
+        out_shape=[jax.ShapeDtypeStruct(shape, F32), jax.ShapeDtypeStruct(shape, BF16)],
+        cost_estimate=cost(3 * parts.size, 4 * parts.size),
+        compiler_params=params(8),
+    )(parts)
 
 
 def ring_kernel(own, a, b, c, total, rounded):
@@ -275,6 +322,7 @@
     place = jnp.stack([core, x]).astype(jnp.int32)
     swap = [(i, i ^ 1) for i in range(loops)]
     flip = [(i, (i + RING) % reds) for i in range(reds)]
+    rings = [[h + i for i in range(RING)] for h in range(0, reds, RING)]
     shift = [[(i, i - i % RING + (i + d) % RING) for i in range(reds)] for d in range(RING)]
     same_core = [[2 * i + c for i in range(chips)] for c in range(2)]
 
@@ -309,27 +357,29 @@
     own_a = gather(rows_w[:share])
     rows_b, own_a = tie(rows_w[share:], own_a)
     own_b = gather(rows_b)
-    rot_a = rotate(place, own_a, swapped(own_a), in_basis)
-    ring_a = ring(rot_a)
+    ring_a = ring(rotate(place, own_a, swapped(own_a), in_basis))
     own_b, *ring_a = tie(own_b, *ring_a)
     other_b = swapped(own_b)
     total_a, rounded_a = ring_sum(ring_a)
+    far_a = lax.ppermute(rounded_a, "red", flip)
     other_b, total_a = tie(other_b, total_a)
-    rot_b = rotate(place, own_b, other_b, in_basis)
-    scaled_a = scale(total_a, lax.ppermute(rounded_a, "red", flip), factors[0], eigen_cols)
-    ring_b = ring(rot_b)
-    pieces_a = ring([scaled_a] * RING)
-    total_b, rounded_b = ring_sum(ring_b)
+    [rot_b] = rotate(place, own_b, other_b, in_basis, stacked=True)
+    rot_b, far_a = tie(rot_b.reshape(RING, piece, -1), far_a)
+    rot_b = lax.all_to_all(rot_b, "red", 0, 0, axis_index_groups=rings)
+    scaled_a = scale(total_a, far_a, factors[0], eigen_cols)
+    rot_b, *pieces_a = tie(rot_b, *ring([scaled_a] * RING))
+    total_b, rounded_b = stack_sum(rot_b)
+    far_b = lax.ppermute(rounded_b, "red", flip)
     pieces_a[0], total_b = tie(pieces_a[0], total_b)
     send_a, keep_a = back(place, pieces_a, in_basis)
-    scaled_b = scale(total_b, lax.ppermute(rounded_b, "red", flip), factors[1], eigen_cols)
+    send_a, far_b = tie(send_a, far_b)
+    part_a = join(keep_a, swapped(send_a))
+    scaled_b = scale(total_b, far_b, factors[1], eigen_cols)
     pieces_b = ring([scaled_b] * RING)
-    part_a = (keep_a + swapped(send_a).astype(F32)).astype(BF16)
-    pieces_b[0], part_a = tie(pieces_b[0], part_a)
     part_a = exchange(part_a)
     part_a, *pieces_b = tie(part_a, *pieces_b)
     send_b, keep_b = back(place, pieces_b, in_basis)
-    part_b = exchange((keep_b + swapped(send_b).astype(F32)).astype(BF16))
+    part_b = exchange(join(keep_b, swapped(send_b)))
     return jnp.concatenate([add_up(part_a).astype(BF16), add_up(part_b).astype(BF16)], 0)
 
 

time: 207 us -> 197 us (0.952)
  Pallas kernels: 50.6 us -> 47 us
  other arithmetic: 6.81 us -> 3.52 us
  starting transfers between devices: 49.6 us -> 47.5 us
    ppermute x2, waiting for transfers between devices: 6.84 us -> 0.01 us  [the longest x1 0.01 us: per_device(): far_a = lax.ppermute(rounded_a, 'red', flip)]
    pallas_call x2, Pallas kernels: 21.1 us -> 14.3 us  [back(): pl.pallas_call(functools.partial(back_kernel, cuts=cuts), in_specs=[SMEM]...]
    ppermute x12 -> x9, starting transfers between devices: 17.6 us -> 12.2 us  [ring(): lax.ppermute(parts[d], 'red', shift[d])]
    ppermute x12 -> x9, waiting for transfers between devices: 32.7 us -> 36.4 us  [ring(): lax.ppermute(parts[d], 'red', shift[d])]
    all_to_all x0 -> x1, starting transfers between devices: none -> 3.65 us  [per_device(): rot_b = lax.all_to_all(rot_b, 'red', 0, 0, axis_index_groups=rings)]
    convert_element_type x2 -> x0, other arithmetic: 3.35 us -> none  [the longest x1 2.26 us: per_device(): part_a = (keep_a + swapped(send_a).astype(F32)).astype(BF16)]
    pallas_call x0 -> x3, Pallas kernels: none -> 2.33 us  [the longest x2 2.21 us: join(): pl.pallas_call(join_kernel, in_specs=[VMEM] * 2, out_specs=VMEM, out_shap...]
    ppermute x4, waiting for transfers between devices: 2.11 us -> 4.2 us  [swapped(): return lax.ppermute(value, 'loop', swap)]
  transfers between devices with their start and end apart: 24 -> 22, of which waited for: 15 -> 15; matrix products, arithmetic and copies ran while one was open for 3% -> 4% of each run, Pallas kernels for 11% -> 16%
where the time goes in v5:
time: 197 us; the launch traced here: 196 us
  waiting for transfers between devices  75.2 us (38%)
  starting transfers between devices  47.5 us (24%)
  Pallas kernels  47 us (24%)
  blocking collectives  16.7 us (8%)
  local copies, waits for them, and re-layouts  5.57 us (3%)
  other arithmetic  3.52 us (2%)
    ppermute x9, waiting for transfers between devices, ring(): lax.ppermute(parts[d], 'red', shift[d])  36.4 us
    all_to_all x4, waiting for transfers between devices, exchange(): return lax.all_to_all(value, 'loop', 0, 0, axis_index_groups=same_core)  33.1 us
    all_to_all x4, starting transfers between devices, exchange(): return lax.all_to_all(value, 'loop', 0, 0, axis_index_groups=same_core)  19.3 us
    all_to_all x1, blocking collectives, exchange(): return lax.all_to_all(value, 'loop', 0, 0, axis_index_groups=same_core)  16.7 us
    pallas_call x2, Pallas kernels, rotate(): pl.pallas_call(functools.partial(rotate_kernel, cuts=cuts), in_specs=[SME...  15.2 us
    pallas_call x2, Pallas kernels, back(): pl.pallas_call(functools.partial(back_kernel, cuts=cuts), in_specs=[SMEM]...  14.3 us
    ppermute x9, starting transfers between devices, ring(): lax.ppermute(parts[d], 'red', shift[d])  12.2 us
    pallas_call x1, Pallas kernels, select(): pl.pallas_call(functools.partial(select_kernel, chips=chips), grid=(width...  8.29 us
  transfers between devices with their start and end apart: 22, of which 15 were waited for; matrix products, arithmetic and copies ran while one was open for 4% of the time, Pallas kernels for 16%

profile of v5, /device:TPU:1, one launch (start us, length us, event | category | flops | bytes accessed | tf_op | source)
XLA Modules:
  0.0 196.3 jit_solution(17903384283095410531)
XLA Ops:
  1.4 8.3 %shard_map.73.sel = bf16[512,512]{1,0:T(8,128)(2,1)} custom-call(s32[1,512]{1,0:T(1,128)} %bitcast.34, bf16[512,8192]{1,0:T(8,128)(2,1)} %basis.3), custom_call_target="tpu_custom_call" | custom-call | flops 4294967296 | bytes 8388608 | tf_op jit(solution)/shard_map/pallas_call | solution.py:70
  12.6 6.5 %shard_map.74 = bf16[512,1792]{1,0:T(8,128)(2,1)} custom-call(s32[2]{0:T(128)} %pad_add_fusion.place, bf16[512,512]{1,0:T(8,128)(2,1)} %shard_map.73.sel, bf16[512,512]{1,0:T(8,128)(2,1)} %copy-done.1, bf16[512,3584]{1,0:T(8,128)(2,1)} %grad.1, bf16[512,3584]{1,0:T(8,128)(2,1)} %collective-permute-done.1.grad2), custom_call_target="tpu_custom_call" | custom-call | flops 1879048192 | bytes 5505024 | tf_op jit(solution)/shard_map/pallas_call | solution.py:110
  19.1 6.1 %all-to-all-start = ((bf16[8,64,1792]{2,1,0:T(8,128)(2,1)}), bf16[8,64,1792]{2,1,0:T(8,128)(2,1)S(1)}, u32[]{:S(2)}, u32[]{:S(2)}) async-start(bf16[8,64,1792]{2,1,0:T(8,128)(2,1)} %bitcast.32), calls=%async_computation | async-start | bytes 3670016 | tf_op jit(solution)/shard_map/all_to_all | solution.py:331
  26.9 3.1 %gather_fusion = f32[512]{0:T(512)S(1)} fusion(f32[8192]{0:T(1024)S(1)} %bitcast.31, s32[1024]{0:T(1024)S(1)} %pad_clamp_fusion), kind=kCustom, calls=%fused_computation | custom fusion | bytes 6144 | tf_op jit(solution)/shard_map/jit(_take)/gather | solution.py:338
  30.5 18.2 %all-to-all-done = bf16[8,64,1792]{2,1,0:T(8,128)(2,1)S(1)} async-done(((bf16[8,64,1792]{2,1,0:T(8,128)(2,1)}), bf16[8,64,1792]{2,1,0:T(8,128)(2,1)S(1)}, u32[]{:S(2)}, u32[]{:S(2)}) %all-to-all-start) | async-done | bytes 1835040 | tf_op jit(solution)/shard_map/all_to_all | solution.py:331
  49.0 16.7 %all_to_all.30 = bf16[8,32,1792]{2,1,0:T(8,128)(2,1)S(1)} all-to-all(bf16[8,32,1792]{2,1,0:T(8,128)(2,1)S(1)} %broadcast_in_dim.59), channel_id=1, replica_groups={{0,16,32,48,64,80,96,112},{8,24,40,56,72,88,104,120},{1,17,33,49,65,81,..., dimensions={0} | all-to-all | bytes 1835008 | tf_op jit(solution)/shard_map/all_to_all | solution.py:331
  68.8 3.6 %all-to-all-start.2 = ((bf16[8,32,1792]{2,1,0:T(8,128)(2,1)}), bf16[8,32,1792]{2,1,0:T(8,128)(2,1)S(1)}, u32[]{:S(2)}, u32[]{:S(2)}) async-start(bf16[8,32,1792]{2,1,0:T(8,128)(2,1)} %broadcast_in_dim.60), calls=%async_computation.2 | async-start | bytes 1835008 | tf_op jit(solution)/shard_map/all_to_all | solution.py:331
  72.3 7.5 %shard_map.75 = (f32[64,1792]{1,0:T(8,128)S(1)}, bf16[64,1792]{1,0:T(8,128)(2,1)}, bf16[64,1792]{1,0:T(8,128)(2,1)}, bf16[64,1792]{1,0:T(8,128)(2,1)S(1)}) custom-call(s32[2]{0:T(128)S(1)} %copy-done, bf16[256,1792]{1,0:T(8,128)(2,1)S(1)} %bitcast.28, bf16[256,1792]{1,0:T(8,128)(2,1)S(1)} %collective-permute-done.2.other, bf16[3584,1792]{1,0:T(8,128)(2,1)} %refs_4_.3), custom_call_target="tpu_custom_call" | custom-call | flops 3288334336 | bytes 12845056 | tf_op jit(solution)/shard_map/pallas_call | solution.py:169
  81.1 2.5 %collective-permute-start.4 = (bf16[64,1792]{1,0:T(8,128)(2,1)}, bf16[64,1792]{1,0:T(8,128)(2,1)S(1)}, u32[]{:S(2)}, u32[]{:S(2)}) collective-permute-start(bf16[64,1792]{1,0:T(8,128)(2,1)} %get-tuple-element.50), channel_id=1, source_target_pairs={{0,2},{1,3},{2,0},{3,1},{4,6},{5,7},{6,4},{7,5},{8,10},{9,11},{10,... | collective-permute-start | bytes 688136 | tf_op jit(solution)/shard_map/ppermute | solution.py:352
  85.9 2.7 %collective-permute-done.3.a = bf16[64,1792]{1,0:T(8,128)(2,1)S(1)} collective-permute-done((bf16[64,1792]{1,0:T(8,128)(2,1)}, bf16[64,1792]{1,0:T(8,128)(2,1)S(1)}, u32[]{:S(2)}, u32[]{:S(2)}) %collective-permute-start.3) | collective-permute-done | bytes 229408 | tf_op jit(solution)/shard_map/ppermute | solution.py:352
  88.6 5.9 %collective-permute-done.4.b = bf16[64,1792]{1,0:T(8,128)(2,1)S(1)} collective-permute-done((bf16[64,1792]{1,0:T(8,128)(2,1)}, bf16[64,1792]{1,0:T(8,128)(2,1)S(1)}, u32[]{:S(2)}, u32[]{:S(2)}) %collective-permute-start.4) | collective-permute-done | bytes 229408 | tf_op jit(solution)/shard_map/ppermute | solution.py:352
  95.4 2.9 %collective-permute-start.7 = (bf16[64,1792]{1,0:T(8,128)(2,1)S(1)}, bf16[64,1792]{1,0:T(8,128)(2,1)S(1)}, u32[]{:S(2)}, u32[]{:S(2)}) collective-permute-start(bf16[64,1792]{1,0:T(8,128)(2,1)S(1)} %get-tuple-element.59), channel_id=1, source_target_pairs={{0,4},{1,5},{2,6},{3,7},{4,0},{5,1},{6,2},{7,3},{8,12},{9,13},{10,... | collective-permute-start | bytes 688136 | tf_op jit(solution)/shard_map/ppermute | solution.py:364
  98.3 7.7 %shard_map.77 = bf16[256,1792]{1,0:T(8,128)(2,1)} custom-call(s32[2]{0:T(128)S(1)} %copy-done, bf16[256,1792]{1,0:T(8,128)(2,1)S(1)} %bitcast.30, bf16[256,1792]{1,0:T(8,128)(2,1)S(1)} %collective-permute-done.6.other, bf16[3584,1792]{1,0:T(8,128)(2,1)} %refs_4_.3), custom_call_target="tpu_custom_call" | custom-call | flops 3288334336 | bytes 12845056 | tf_op jit(solution)/shard_map/pallas_call | solution.py:169
  106.0 3.7 %all-to-all-start.3 = ((bf16[4,64,1792]{2,1,0:T(8,128)(2,1)}), bf16[4,64,1792]{2,1,0:T(8,128)(2,1)S(1)}, u32[]{:S(2)}, u32[]{:S(2)}) async-start(bf16[4,64,1792]{2,1,0:T(8,128)(2,1)} %bitcast.13), calls=%async_computation.3 | async-start | bytes 1835008 | tf_op jit(solution)/shard_map/all_to_all | solution.py:368
  110.6 2.7 %collective-permute-start.10 = (bf16[64,1792]{1,0:T(8,128)(2,1)S(1)}, bf16[64,1792]{1,0:T(8,128)(2,1)S(1)}, u32[]{:S(2)}, u32[]{:S(2)}) collective-permute-start(bf16[64,1792]{1,0:T(8,128)(2,1)S(1)} %shard_map.78.refs_0_), channel_id=1, source_target_pairs={{0,3},{1,0},{2,1},{3,2},{4,7},{5,4},{6,5},{7,6},{8,11},{9,8},{10,9... | collective-permute-start | bytes 688136 | tf_op jit(solution)/shard_map/ppermute | solution.py:352
  115.1 11.2 %collective-permute-done.10.refs_3_ = bf16[64,1792]{1,0:T(8,128)(2,1)S(1)} collective-permute-done((bf16[64,1792]{1,0:T(8,128)(2,1)S(1)}, bf16[64,1792]{1,0:T(8,128)(2,1)S(1)}, u32[]{:S(2)}, u32[]{:S(2)}) %collective-permute-start.10) | collective-permute-done | bytes 229408 | tf_op jit(solution)/shard_map/ppermute | solution.py:352
  127.5 5.3 %collective-permute-done.9.refs_2_ = bf16[64,1792]{1,0:T(8,128)(2,1)S(1)} collective-permute-done((bf16[64,1792]{1,0:T(8,128)(2,1)S(1)}, bf16[64,1792]{1,0:T(8,128)(2,1)S(1)}, u32[]{:S(2)}, u32[]{:S(2)}) %collective-permute-start.9) | collective-permute-done | bytes 229408 | tf_op jit(solution)/shard_map/ppermute | solution.py:352
  134.6 7.1 %shard_map.80 = (bf16[128,3584]{1,0:T(8,128)(2,1)S(1)}, f32[128,3584]{1,0:T(8,128)S(1)}) custom-call(s32[2]{0:T(128)S(1)} %copy-done, bf16[64,1792]{1,0:T(8,128)(2,1)S(1)} %shard_map.78.refs_0_, bf16[64,1792]{1,0:T(8,128)(2,1)S(1)} %collective-permute-done.8.refs_1_, bf16[64,1792]{1,0:T(8,128)(2,1)S(1)} %collective-permute-done.9.refs_2_, ...), custom_call_target="tpu_custom_call" | custom-call | flops 3288334336 | bytes 12845056 | tf_op jit(solution)/shard_map/pallas_call | solution.py:213
  146.8 4.5 %all-to-all-start.4 = ((bf16[8,16,3584]{2,1,0:T(8,128)(2,1)}), bf16[8,16,3584]{2,1,0:T(8,128)(2,1)S(1)}, u32[]{:S(2)}, u32[]{:S(2)}) async-start(bf16[8,16,3584]{2,1,0:T(8,128)(2,1)} %bitcast.14), calls=%async_computation.4 | async-start | bytes 1835008 | tf_op jit(solution)/shard_map/all_to_all | solution.py:331
  154.4 5.5 %collective-permute-done.13.refs_1_ = bf16[64,1792]{1,0:T(8,128)(2,1)S(1)} collective-permute-done((bf16[64,1792]{1,0:T(8,128)(2,1)S(1)}, bf16[64,1792]{1,0:T(8,128)(2,1)S(1)}, u32[]{:S(2)}, u32[]{:S(2)}) %collective-permute-start.13) | collective-permute-done | bytes 229408 | tf_op jit(solution)/shard_map/ppermute | solution.py:352
  159.9 3.8 %collective-permute-done.14.refs_2_ = bf16[64,1792]{1,0:T(8,128)(2,1)S(1)} collective-permute-done((bf16[64,1792]{1,0:T(8,128)(2,1)S(1)}, bf16[64,1792]{1,0:T(8,128)(2,1)S(1)}, u32[]{:S(2)}, u32[]{:S(2)}) %collective-permute-start.14) | collective-permute-done | bytes 229408 | tf_op jit(solution)/shard_map/ppermute | solution.py:352
  164.8 7.1 %shard_map.83 = (bf16[128,3584]{1,0:T(8,128)(2,1)S(1)}, f32[128,3584]{1,0:T(8,128)S(1)}) custom-call(s32[2]{0:T(128)S(1)} %copy-done, bf16[64,1792]{1,0:T(8,128)(2,1)S(1)} %shard_map.82.refs_0_, bf16[64,1792]{1,0:T(8,128)(2,1)S(1)} %collective-permute-done.13.refs_1_, bf16[64,1792]{1,0:T(8,128)(2,1)S(1)} %collective-permute-done.14.refs_2_, ...), custom_call_target="tpu_custom_call" | custom-call | flops 3288334336 | bytes 12845056 | tf_op jit(solution)/shard_map/pallas_call | solution.py:213
  176.8 5.1 %all-to-all-start.5 = ((bf16[8,16,3584]{2,1,0:T(8,128)(2,1)}), bf16[8,16,3584]{2,1,0:T(8,128)(2,1)S(1)}, u32[]{:S(2)}, u32[]{:S(2)}) async-start(bf16[8,16,3584]{2,1,0:T(8,128)(2,1)} %bitcast.16), calls=%async_computation.5 | async-start | bytes 1835008 | tf_op jit(solution)/shard_map/all_to_all | solution.py:331
  182.0 13.4 %all-to-all-done.5 = bf16[8,16,3584]{2,1,0:T(8,128)(2,1)S(1)} async-done(((bf16[8,16,3584]{2,1,0:T(8,128)(2,1)}), bf16[8,16,3584]{2,1,0:T(8,128)(2,1)S(1)}, u32[]{:S(2)}, u32[]{:S(2)}) %all-to-all-start.5) | async-done | bytes 917536 | tf_op jit(solution)/shard_map/all_to_all | solution.py:331
  (62 shorter events, 34.4 us)
Async XLA Ops:
  0.0 11.8 %collective-permute-start.1 = (bf16[512,3584]{1,0:T(8,128)(2,1)}, bf16[512,3584]{1,0:T(8,128)(2,1)}, u32[]{:S(2)}, u32[]{:S(2)}) collective-permute-start(bf16[512,3584]{1,0:T(8,128)(2,1)} %grad.1), channel_id=1, source_target_pairs={{0,8},{8,0},{16,24},{24,16},{32,40},{40,32},{48,56},{56,48},{64,72... | collective-permute-start | bytes 11010056 | tf_op jit(solution)/shard_map/ppermute | solution.py:333
  9.7 2.1 %collective-permute-start = (bf16[512,512]{1,0:T(8,128)(2,1)}, bf16[512,512]{1,0:T(8,128)(2,1)S(1)}, u32[]{:S(2)}, u32[]{:S(2)}) collective-permute-start(bf16[512,512]{1,0:T(8,128)(2,1)} %shard_map.73.sel), channel_id=1, source_target_pairs={{0,8},{8,0},{16,24},{24,16},{32,40},{40,32},{48,56},{56,48},{64,72... | collective-permute-start | bytes 1572872 | tf_op jit(solution)/shard_map/ppermute | solution.py:335
  19.1 6.2 %copy-start.2 = (s32[512]{0:T(512)S(1)}, s32[512]{0:T(512)}, u32[]{:S(2)}) copy-start(s32[512]{0:T(512)} %param.7) | copy-start | bytes 6148
  19.1 29.6 %all-to-all-start = ((bf16[8,64,1792]{2,1,0:T(8,128)(2,1)}), bf16[8,64,1792]{2,1,0:T(8,128)(2,1)S(1)}, u32[]{:S(2)}, u32[]{:S(2)}) async-start(bf16[8,64,1792]{2,1,0:T(8,128)(2,1)} %bitcast.32), calls=%async_computation | async-start | bytes 3670016 | tf_op jit(solution)/shard_map/all_to_all | solution.py:331
  65.8 6.6 %copy-start = (s32[2]{0:T(128)S(1)}, s32[2]{0:T(128)}, u32[]{:S(2)}) copy-start(s32[2]{0:T(128)} %pad_add_fusion.place) | copy-start | bytes 28
  65.8 6.6 %collective-permute-start.2 = (bf16[256,1792]{1,0:T(8,128)(2,1)S(1)}, bf16[256,1792]{1,0:T(8,128)(2,1)S(1)}, u32[]{:S(2)}, u32[]{:S(2)}) collective-permute-start(bf16[256,1792]{1,0:T(8,128)(2,1)S(1)} %bitcast.27), channel_id=1, source_target_pairs={{0,8},{8,0},{16,24},{24,16},{32,40},{40,32},{48,56},{56,48},{64,72... | collective-permute-start | bytes 2752520 | tf_op jit(solution)/shard_map/ppermute | solution.py:355
  68.8 17.1 %all-to-all-start.2 = ((bf16[8,32,1792]{2,1,0:T(8,128)(2,1)}), bf16[8,32,1792]{2,1,0:T(8,128)(2,1)S(1)}, u32[]{:S(2)}, u32[]{:S(2)}) async-start(bf16[8,32,1792]{2,1,0:T(8,128)(2,1)} %broadcast_in_dim.60), calls=%async_computation.2 | async-start | bytes 1835008 | tf_op jit(solution)/shard_map/all_to_all | solution.py:331
  79.8 8.7 %collective-permute-start.3 = (bf16[64,1792]{1,0:T(8,128)(2,1)}, bf16[64,1792]{1,0:T(8,128)(2,1)S(1)}, u32[]{:S(2)}, u32[]{:S(2)}) collective-permute-start(bf16[64,1792]{1,0:T(8,128)(2,1)} %get-tuple-element.49), channel_id=1, source_target_pairs={{0,1},{1,2},{2,3},{3,0},{4,5},{5,6},{6,7},{7,4},{8,9},{9,10},{10,1... | collective-permute-start | bytes 688136 | tf_op jit(solution)/shard_map/ppermute | solution.py:352
  81.1 13.4 %collective-permute-start.4 = (bf16[64,1792]{1,0:T(8,128)(2,1)}, bf16[64,1792]{1,0:T(8,128)(2,1)S(1)}, u32[]{:S(2)}, u32[]{:S(2)}) collective-permute-start(bf16[64,1792]{1,0:T(8,128)(2,1)} %get-tuple-element.50), channel_id=1, source_target_pairs={{0,2},{1,3},{2,0},{3,1},{4,6},{5,7},{6,4},{7,5},{8,10},{9,11},{10,... | collective-permute-start | bytes 688136 | tf_op jit(solution)/shard_map/ppermute | solution.py:352
  83.6 10.9 %collective-permute-start.5 = (bf16[64,1792]{1,0:T(8,128)(2,1)S(1)}, bf16[64,1792]{1,0:T(8,128)(2,1)S(1)}, u32[]{:S(2)}, u32[]{:S(2)}) collective-permute-start(bf16[64,1792]{1,0:T(8,128)(2,1)S(1)} %get-tuple-element.51), channel_id=1, source_target_pairs={{0,3},{1,0},{2,1},{3,2},{4,7},{5,4},{6,5},{7,6},{8,11},{9,8},{10,9... | collective-permute-start | bytes 688136 | tf_op jit(solution)/shard_map/ppermute | solution.py:352
  94.5 3.8 %collective-permute-start.6 = (bf16[256,1792]{1,0:T(8,128)(2,1)S(1)}, bf16[256,1792]{1,0:T(8,128)(2,1)S(1)}, u32[]{:S(2)}, u32[]{:S(2)}) collective-permute-start(bf16[256,1792]{1,0:T(8,128)(2,1)S(1)} %bitcast.29), channel_id=1, source_target_pairs={{0,8},{8,0},{16,24},{24,16},{32,40},{40,32},{48,56},{56,48},{64,72... | collective-permute-start | bytes 2752520 | tf_op jit(solution)/shard_map/ppermute | solution.py:355
  95.4 10.6 %collective-permute-start.7 = (bf16[64,1792]{1,0:T(8,128)(2,1)S(1)}, bf16[64,1792]{1,0:T(8,128)(2,1)S(1)}, u32[]{:S(2)}, u32[]{:S(2)}) collective-permute-start(bf16[64,1792]{1,0:T(8,128)(2,1)S(1)} %get-tuple-element.59), channel_id=1, source_target_pairs={{0,4},{1,5},{2,6},{3,7},{4,0},{5,1},{6,2},{7,3},{8,12},{9,13},{10,... | collective-permute-start | bytes 688136 | tf_op jit(solution)/shard_map/ppermute | solution.py:364
  106.0 26.8 %all-to-all-start.3 = ((bf16[4,64,1792]{2,1,0:T(8,128)(2,1)}), bf16[4,64,1792]{2,1,0:T(8,128)(2,1)S(1)}, u32[]{:S(2)}, u32[]{:S(2)}) async-start(bf16[4,64,1792]{2,1,0:T(8,128)(2,1)} %bitcast.13), calls=%async_computation.3 | async-start | bytes 1835008 | tf_op jit(solution)/shard_map/all_to_all | solution.py:368
  110.6 15.7 %collective-permute-start.10 = (bf16[64,1792]{1,0:T(8,128)(2,1)S(1)}, bf16[64,1792]{1,0:T(8,128)(2,1)S(1)}, u32[]{:S(2)}, u32[]{:S(2)}) collective-permute-start(bf16[64,1792]{1,0:T(8,128)(2,1)S(1)} %shard_map.78.refs_0_), channel_id=1, source_target_pairs={{0,3},{1,0},{2,1},{3,2},{4,7},{5,4},{6,5},{7,6},{8,11},{9,8},{10,9... | collective-permute-start | bytes 688136 | tf_op jit(solution)/shard_map/ppermute | solution.py:352
  113.4 14.1 %collective-permute-start.8 = (bf16[64,1792]{1,0:T(8,128)(2,1)S(1)}, bf16[64,1792]{1,0:T(8,128)(2,1)S(1)}, u32[]{:S(2)}, u32[]{:S(2)}) collective-permute-start(bf16[64,1792]{1,0:T(8,128)(2,1)S(1)} %shard_map.78.refs_0_), channel_id=1, source_target_pairs={{0,1},{1,2},{2,3},{3,0},{4,5},{5,6},{6,7},{7,4},{8,9},{9,10},{10,1... | collective-permute-start | bytes 688136 | tf_op jit(solution)/shard_map/ppermute | solution.py:352
  113.4 19.3 %collective-permute-start.9 = (bf16[64,1792]{1,0:T(8,128)(2,1)S(1)}, bf16[64,1792]{1,0:T(8,128)(2,1)S(1)}, u32[]{:S(2)}, u32[]{:S(2)}) collective-permute-start(bf16[64,1792]{1,0:T(8,128)(2,1)S(1)} %shard_map.78.refs_0_), channel_id=1, source_target_pairs={{0,2},{1,3},{2,0},{3,1},{4,6},{5,7},{6,4},{7,5},{8,10},{9,11},{10,... | collective-permute-start | bytes 688136 | tf_op jit(solution)/shard_map/ppermute | solution.py:352
  132.9 8.9 %collective-permute-start.11 = (bf16[64,1792]{1,0:T(8,128)(2,1)S(1)}, bf16[64,1792]{1,0:T(8,128)(2,1)S(1)}, u32[]{:S(2)}, u32[]{:S(2)}) collective-permute-start(bf16[64,1792]{1,0:T(8,128)(2,1)S(1)} %get-tuple-element.73), channel_id=1, source_target_pairs={{0,4},{1,5},{2,6},{3,7},{4,0},{5,1},{6,2},{7,3},{8,12},{9,13},{10,... | collective-permute-start | bytes 688136 | tf_op jit(solution)/shard_map/ppermute | solution.py:372
  141.7 4.0 %collective-permute-start.12 = (bf16[128,3584]{1,0:T(8,128)(2,1)S(1)}, bf16[128,3584]{1,0:T(8,128)(2,1)S(1)}, u32[]{:S(2)}, u32[]{:S(2)}) collective-permute-start(bf16[128,3584]{1,0:T(8,128)(2,1)S(1)} %get-tuple-element.74), channel_id=1, source_target_pairs={{0,8},{8,0},{16,24},{24,16},{32,40},{40,32},{48,56},{56,48},{64,72... | collective-permute-start | bytes 2752520 | tf_op jit(solution)/shard_map/ppermute | solution.py:355
  146.8 18.0 %all-to-all-start.4 = ((bf16[8,16,3584]{2,1,0:T(8,128)(2,1)}), bf16[8,16,3584]{2,1,0:T(8,128)(2,1)S(1)}, u32[]{:S(2)}, u32[]{:S(2)}) async-start(bf16[8,16,3584]{2,1,0:T(8,128)(2,1)} %bitcast.14), calls=%async_computation.4 | async-start | bytes 1835008 | tf_op jit(solution)/shard_map/all_to_all | solution.py:331
  151.5 8.4 %collective-permute-start.13 = (bf16[64,1792]{1,0:T(8,128)(2,1)S(1)}, bf16[64,1792]{1,0:T(8,128)(2,1)S(1)}, u32[]{:S(2)}, u32[]{:S(2)}) collective-permute-start(bf16[64,1792]{1,0:T(8,128)(2,1)S(1)} %shard_map.82.refs_0_), channel_id=1, source_target_pairs={{0,1},{1,2},{2,3},{3,0},{4,5},{5,6},{6,7},{7,4},{8,9},{9,10},{10,1... | collective-permute-start | bytes 688136 | tf_op jit(solution)/shard_map/ppermute | solution.py:352
  151.9 11.8 %collective-permute-start.14 = (bf16[64,1792]{1,0:T(8,128)(2,1)S(1)}, bf16[64,1792]{1,0:T(8,128)(2,1)S(1)}, u32[]{:S(2)}, u32[]{:S(2)}) collective-permute-start(bf16[64,1792]{1,0:T(8,128)(2,1)S(1)} %shard_map.82.refs_0_), channel_id=1, source_target_pairs={{0,2},{1,3},{2,0},{3,1},{4,6},{5,7},{6,4},{7,5},{8,10},{9,11},{10,... | collective-permute-start | bytes 688136 | tf_op jit(solution)/shard_map/ppermute | solution.py:352
  153.7 10.9 %collective-permute-start.15 = (bf16[64,1792]{1,0:T(8,128)(2,1)S(1)}, bf16[64,1792]{1,0:T(8,128)(2,1)S(1)}, u32[]{:S(2)}, u32[]{:S(2)}) collective-permute-start(bf16[64,1792]{1,0:T(8,128)(2,1)S(1)} %shard_map.82.refs_0_), channel_id=1, source_target_pairs={{0,3},{1,0},{2,1},{3,2},{4,7},{5,4},{6,5},{7,6},{8,11},{9,8},{10,9... | collective-permute-start | bytes 688136 | tf_op jit(solution)/shard_map/ppermute | solution.py:352
  172.0 3.7 %collective-permute-start.16 = (bf16[128,3584]{1,0:T(8,128)(2,1)S(1)}, bf16[128,3584]{1,0:T(8,128)(2,1)S(1)}, u32[]{:S(2)}, u32[]{:S(2)}) collective-permute-start(bf16[128,3584]{1,0:T(8,128)(2,1)S(1)} %get-tuple-element.84), channel_id=1, source_target_pairs={{0,8},{8,0},{16,24},{24,16},{32,40},{40,32},{48,56},{56,48},{64,72... | collective-permute-start | bytes 2752520 | tf_op jit(solution)/shard_map/ppermute | solution.py:355
  176.8 18.7 %all-to-all-start.5 = ((bf16[8,16,3584]{2,1,0:T(8,128)(2,1)}), bf16[8,16,3584]{2,1,0:T(8,128)(2,1)S(1)}, u32[]{:S(2)}, u32[]{:S(2)}) async-start(bf16[8,16,3584]{2,1,0:T(8,128)(2,1)} %bitcast.16), calls=%async_computation.5 | async-start | bytes 1835008 | tf_op jit(solution)/shard_map/all_to_all | solution.py:331
  (1 other events, 0.8 us)

commit v6 on v5

--- a/solution.py
+++ b/solution.py
@@ -53,13 +53,11 @@
     @pl.when(step == pl.num_programs(0) - 1)
     def _():
         rows = acc[...].T.astype(BF16)
-        share = queries // chips // CHUNKS
-        run = share // 2
+        run = queries // chips // CHUNKS // 2
         for chip in range(chips):
             for core in range(2):
                 for n in range(CHUNKS):
-                    at = (core * chips + chip) * run
-                    to = at // share * (share * CHUNKS) + n * share + at % share
+                    to = ((n * 2 + core) * chips + chip) * run
                     at = ((chip * 2 + core) * CHUNKS + n) * run
                     out[to : to + run, :] = rows[at : at + run, :]
 
@@ -79,8 +77,9 @@
     )(ids[None, :], basis)
 
 
-def rows_kernel(place, sel, sel2, grad, grad2, out, buf, buf2, sems):
+def rows_kernel(place, sel, sel2, grad, grad2, out, buf, buf2, sems, *, chunk_index):
     steps = sems.shape[1]
+    rows = pl.ds(chunk_index * out.shape[0], out.shape[0])
     half = out.shape[1]
     block = half // steps
     copies = []
@@ -100,15 +99,15 @@
         to = pl.ds(i * block, block)
         copies[i][0].wait()
         copies[i][1].wait()
-        total = dot(sel[...], buf[:, to]) + dot(sel2[...], buf2[:, to])
+        total = dot(sel[rows, :], buf[:, to]) + dot(sel2[rows, :], buf2[:, to])
         out[:, to] = total.astype(BF16)
 
 
-def partial_rows(place, sel, sel2, grad, grad2, steps=2):
-    queries, units = sel.shape
+def partial_rows(place, sel, sel2, grad, grad2, chunk_index, steps=2):
+    queries, units = sel.shape[0] // CHUNKS, sel.shape[1]
     half = grad.shape[1] // 2
     return pl.pallas_call(
-        rows_kernel,
+        functools.partial(rows_kernel, chunk_index=chunk_index),
         in_specs=[SMEM, VMEM, VMEM, ANY, ANY],
         out_specs=VMEM,
         out_shape=jax.ShapeDtypeStruct((queries, half), BF16),
@@ -333,18 +332,18 @@
     got = lax.ppermute(gradient, "loop", swap)
     sel = select(query_ids, out_basis, chips)
     sel_got = lax.ppermute(sel, "loop", swap)
-    part = partial_rows(place, sel, sel_got, gradient, got)
-    part = exchange(part)
     eigen_rows = jnp.take(jnp.take(out_eigen, layer_index, axis=0)[0], query_ids)
     eigen_rows = eigen_rows.reshape(chips, 2, CHUNKS, -1).transpose(2, 1, 0, 3).reshape(CHUNKS, chunk)
     eigen_cols = jnp.take(in_eigen, layer_index, axis=0)
     factors = [
         lax.dynamic_slice_in_dim(eigen_rows[n], x * piece, piece, 0)[:, None] for n in range(CHUNKS)
     ]
-    rows_w, *factors = tie(add_up(part).astype(BF16), *factors)
-    share = rows_w.shape[0] // CHUNKS
-
-    def gather(rows):
+
+    def scatter(n):
+        return partial_rows(place, sel, sel_got, gradient, got, n)
+
+    def gather(parts):
+        rows = add_up(parts).astype(BF16)
         rows = jnp.broadcast_to(rows[None], (chips,) + rows.shape).reshape(chunk, -1)
         return exchange(rows).reshape(chunk, -1)
 
@@ -354,30 +353,27 @@
     def swapped(value):
         return lax.ppermute(value, "loop", swap)
 
-    own_a = gather(rows_w[:share])
-    rows_b, own_a = tie(rows_w[share:], own_a)
-    own_b = gather(rows_b)
+    part_a = scatter(0)
+    part_a, *factors = tie(exchange(part_a), *factors)
+    own_a = gather(part_a)
+    part_b, own_a = tie(scatter(1), own_a)
+    part_b = exchange(part_b)
     ring_a = ring(rotate(place, own_a, swapped(own_a), in_basis))
-    own_b, *ring_a = tie(own_b, *ring_a)
-    other_b = swapped(own_b)
+    part_b, *ring_a = tie(part_b, *ring_a)
+    own_b = gather(part_b)
     total_a, rounded_a = ring_sum(ring_a)
-    far_a = lax.ppermute(rounded_a, "red", flip)
-    other_b, total_a = tie(other_b, total_a)
-    [rot_b] = rotate(place, own_b, other_b, in_basis, stacked=True)
-    rot_b, far_a = tie(rot_b.reshape(RING, piece, -1), far_a)
-    rot_b = lax.all_to_all(rot_b, "red", 0, 0, axis_index_groups=rings)
-    scaled_a = scale(total_a, far_a, factors[0], eigen_cols)
-    rot_b, *pieces_a = tie(rot_b, *ring([scaled_a] * RING))
-    total_b, rounded_b = stack_sum(rot_b)
+    scaled_a = scale(total_a, lax.ppermute(rounded_a, "red", flip), factors[0], eigen_cols)
+    own_b, scaled_a = tie(own_b, scaled_a)
+    pieces_a = ring([scaled_a] * RING)
+    ring_b = ring(rotate(place, own_b, swapped(own_b), in_basis))
+    send_a, keep_a = back(place, pieces_a, in_basis)
+    send_a, *ring_b = tie(send_a, *ring_b)
+    total_b, rounded_b = ring_sum(ring_b)
     far_b = lax.ppermute(rounded_b, "red", flip)
-    pieces_a[0], total_b = tie(pieces_a[0], total_b)
-    send_a, keep_a = back(place, pieces_a, in_basis)
-    send_a, far_b = tie(send_a, far_b)
+    keep_a, far_b = tie(keep_a, far_b)
     part_a = join(keep_a, swapped(send_a))
     scaled_b = scale(total_b, far_b, factors[1], eigen_cols)
-    pieces_b = ring([scaled_b] * RING)
-    part_a = exchange(part_a)
-    part_a, *pieces_b = tie(part_a, *pieces_b)
+    part_a, *pieces_b = tie(exchange(part_a), *ring([scaled_b] * RING))
     send_b, keep_b = back(place, pieces_b, in_basis)
     part_b = exchange(join(keep_b, swapped(send_b)))
     return jnp.concatenate([add_up(part_a).astype(BF16), add_up(part_b).astype(BF16)], 0)

time: 197 us -> 195 us (0.990)
  blocking collectives: 16.7 us -> 0 us
  starting transfers between devices: 47.5 us -> 56 us
  Pallas kernels: 47 us -> 49 us
  waiting for transfers between devices: 75.2 us -> 77.2 us
    all_to_all x1 -> x0, blocking collectives: 16.7 us -> none  [exchange(): return lax.all_to_all(value, 'loop', 0, 0, axis_index_groups=same_core)]
    ppermute x9 -> x12, waiting for transfers between devices: 36.4 us -> 19.7 us  [ring(): lax.ppermute(parts[d], 'red', shift[d])]
    ppermute x1, waiting for transfers between devices: 0.01 us -> 13.5 us  [per_device(): lax.ppermute(rounded_a, 'red', flip)]
    all_to_all x4 -> x6, starting transfers between devices: 19.3 us -> 28.7 us  [exchange(): return lax.all_to_all(value, 'loop', 0, 0, axis_index_groups=same_core)]
    ppermute x1, waiting for transfers between devices: 0.01 us -> 8.4 us  [per_device(): far_b = lax.ppermute(rounded_b, 'red', flip)]
    ppermute x9 -> x12, starting transfers between devices: 12.2 us -> 16.4 us  [ring(): lax.ppermute(parts[d], 'red', shift[d])]
    all_to_all x1 -> x0, starting transfers between devices: 3.65 us -> none  [per_device(): rot_b = lax.all_to_all(rot_b, 'red', 0, 0, axis_index_groups=rings)]
    pallas_call x2, Pallas kernels: 6.61 us -> 10.2 us  [partial_rows(): pl.pallas_call(functools.partial(rows_kernel, chunk_index=chunk_index), i...]
  transfers between devices with their start and end apart: 22 -> 26, of which waited for: 15 -> 13; matrix products, arithmetic and copies ran while one was open for 4% -> 3% of each run, Pallas kernels for 16% -> 18%
where the time goes in v6:
time: 195 us
  waiting for transfers between devices  77.2 us (40%)
  starting transfers between devices  56 us (29%)
  Pallas kernels  49 us (25%)
  local copies, waits for them, and re-layouts  6.52 us (3%)
  other arithmetic  4.81 us (2%)
    all_to_all x6, waiting for transfers between devices, exchange(): return lax.all_to_all(value, 'loop', 0, 0, axis_index_groups=same_core)  33.5 us
    all_to_all x6, starting transfers between devices, exchange(): return lax.all_to_all(value, 'loop', 0, 0, axis_index_groups=same_core)  28.7 us
    ppermute x12, waiting for transfers between devices, ring(): lax.ppermute(parts[d], 'red', shift[d])  19.7 us
    ppermute x12, starting transfers between devices, ring(): lax.ppermute(parts[d], 'red', shift[d])  16.4 us
    pallas_call x2, Pallas kernels, back(): pl.pallas_call(functools.partial(back_kernel, cuts=cuts), in_specs=[SMEM]...  14.3 us
    pallas_call x2, Pallas kernels, rotate(): pl.pallas_call(functools.partial(rotate_kernel, cuts=cuts), in_specs=[SME...  13.5 us
    ppermute x1, waiting for transfers between devices, per_device(): lax.ppermute(rounded_a, 'red', flip)  13.5 us
    pallas_call x2, Pallas kernels, partial_rows(): pl.pallas_call(functools.partial(rows_kernel, chunk_index=chunk_index), i...  10.2 us
  transfers between devices with their start and end apart: 26, of which 13 were waited for; matrix products, arithmetic and copies ran while one was open for 3% of the time, Pallas kernels for 18%

profile of v6, /device:TPU:1, one launch (start us, length us, event | category | flops | bytes accessed | tf_op | source)
XLA Modules:
  0.0 194.5 jit_solution(2168941888015484174)
XLA Ops:
  1.4 8.3 %shard_map.73.sel = bf16[512,512]{1,0:T(8,128)(2,1)} custom-call(s32[1,512]{1,0:T(1,128)} %bitcast.37, bf16[512,8192]{1,0:T(8,128)(2,1)} %basis.3), custom_call_target="tpu_custom_call" | custom-call | flops 4294967296 | bytes 8388608 | tf_op jit(solution)/shard_map/pallas_call | solution.py:68
  12.8 5.1 %shard_map.75 = bf16[256,1792]{1,0:T(8,128)(2,1)} custom-call(s32[2]{0:T(128)} %pad_add_fusion.place, bf16[512,512]{1,0:T(8,128)(2,1)} %shard_map.73.sel, bf16[512,512]{1,0:T(8,128)(2,1)} %copy-done.1, bf16[512,3584]{1,0:T(8,128)(2,1)} %grad.3, bf16[512,3584]{1,0:T(8,128)(2,1)} %collective-permute-done.1.grad2), custom_call_target="tpu_custom_call" | custom-call | flops 939524096 | bytes 2752512 | tf_op jit(solution)/shard_map/pallas_call | solution.py:109
  17.9 6.1 %all-to-all-start = ((bf16[8,32,1792]{2,1,0:T(8,128)(2,1)}), bf16[8,32,1792]{2,1,0:T(8,128)(2,1)S(1)}, u32[]{:S(2)}, u32[]{:S(2)}) async-start(bf16[8,32,1792]{2,1,0:T(8,128)(2,1)} %bitcast.34), calls=%async_computation | async-start | bytes 1835008 | tf_op jit(solution)/shard_map/all_to_all | solution.py:330
  24.1 3.1 %gather_fusion = f32[512]{0:T(512)S(1)} fusion(f32[8192]{0:T(1024)S(1)} %bitcast.33, s32[1024]{0:T(1024)S(1)} %pad_clamp_fusion), kind=kCustom, calls=%fused_computation | custom fusion | bytes 6144 | tf_op jit(solution)/shard_map/jit(_take)/gather | solution.py:335
  27.6 9.8 %all-to-all-done = bf16[8,32,1792]{2,1,0:T(8,128)(2,1)S(1)} async-done(((bf16[8,32,1792]{2,1,0:T(8,128)(2,1)}), bf16[8,32,1792]{2,1,0:T(8,128)(2,1)S(1)}, u32[]{:S(2)}, u32[]{:S(2)}) %all-to-all-start) | async-done | bytes 917536 | tf_op jit(solution)/shard_map/all_to_all | solution.py:330
  38.6 3.8 %all-to-all-start.1 = ((bf16[8,32,1792]{2,1,0:T(8,128)(2,1)}), bf16[8,32,1792]{2,1,0:T(8,128)(2,1)S(1)}, u32[]{:S(2)}, u32[]{:S(2)}) async-start(bf16[8,32,1792]{2,1,0:T(8,128)(2,1)} %broadcast_in_dim.64), calls=%async_computation.1 | async-start | bytes 1835008 | tf_op jit(solution)/shard_map/all_to_all | solution.py:330
  42.4 5.1 %shard_map.74 = bf16[256,1792]{1,0:T(8,128)(2,1)} custom-call(s32[2]{0:T(128)} %pad_add_fusion.place, bf16[512,512]{1,0:T(8,128)(2,1)} %shard_map.73.sel, bf16[512,512]{1,0:T(8,128)(2,1)} %copy-done.1, bf16[512,3584]{1,0:T(8,128)(2,1)} %grad.3, bf16[512,3584]{1,0:T(8,128)(2,1)} %collective-permute-done.1.grad2), custom_call_target="tpu_custom_call" | custom-call | flops 939524096 | bytes 2752512 | tf_op jit(solution)/shard_map/pallas_call | solution.py:109
  47.5 8.3 %all-to-all-done.1 = bf16[8,32,1792]{2,1,0:T(8,128)(2,1)S(1)} async-done(((bf16[8,32,1792]{2,1,0:T(8,128)(2,1)}), bf16[8,32,1792]{2,1,0:T(8,128)(2,1)S(1)}, u32[]{:S(2)}, u32[]{:S(2)}) %all-to-all-start.1) | async-done | bytes 917536 | tf_op jit(solution)/shard_map/all_to_all | solution.py:330
  56.7 4.2 %all-to-all-start.2 = ((bf16[8,32,1792]{2,1,0:T(8,128)(2,1)}), bf16[8,32,1792]{2,1,0:T(8,128)(2,1)}, u32[]{:S(2)}, u32[]{:S(2)}) async-start(bf16[8,32,1792]{2,1,0:T(8,128)(2,1)} %bitcast.35), calls=%async_computation.2 | async-start | bytes 1835008 | tf_op jit(solution)/shard_map/all_to_all | solution.py:330
  61.0 6.8 %shard_map.76 = (f32[64,1792]{1,0:T(8,128)S(1)}, bf16[64,1792]{1,0:T(8,128)(2,1)S(1)}, bf16[64,1792]{1,0:T(8,128)(2,1)S(1)}, bf16[64,1792]{1,0:T(8,128)(2,1)S(1)}) custom-call(s32[2]{0:T(128)S(1)} %copy-done, bf16[256,1792]{1,0:T(8,128)(2,1)S(1)} %bitcast.32, bf16[256,1792]{1,0:T(8,128)(2,1)S(1)} %collective-permute-done.2.other, bf16[3584,1792]{1,0:T(8,128)(2,1)} %refs_4_.3), custom_call_target="tpu_custom_call" | custom-call | flops 3288334336 | bytes 12845056 | tf_op jit(solution)/shard_map/pallas_call | solution.py:168
  76.3 5.9 %collective-permute-done.4.b = bf16[64,1792]{1,0:T(8,128)(2,1)S(1)} collective-permute-done((bf16[64,1792]{1,0:T(8,128)(2,1)S(1)}, bf16[64,1792]{1,0:T(8,128)(2,1)S(1)}, u32[]{:S(2)}, u32[]{:S(2)}) %collective-permute-start.4) | collective-permute-done | bytes 229408 | tf_op jit(solution)/shard_map/ppermute | solution.py:351
  84.6 4.7 %all-to-all-start.3 = ((bf16[8,32,1792]{2,1,0:T(8,128)(2,1)}), bf16[8,32,1792]{2,1,0:T(8,128)(2,1)S(1)}, u32[]{:S(2)}, u32[]{:S(2)}) async-start(bf16[8,32,1792]{2,1,0:T(8,128)(2,1)} %broadcast_in_dim.66), calls=%async_computation.3 | async-start | bytes 1835008 | tf_op jit(solution)/shard_map/all_to_all | solution.py:330
  89.4 2.7 %collective-permute-start.6 = (bf16[64,1792]{1,0:T(8,128)(2,1)S(1)}, bf16[64,1792]{1,0:T(8,128)(2,1)S(1)}, u32[]{:S(2)}, u32[]{:S(2)}) collective-permute-start(bf16[64,1792]{1,0:T(8,128)(2,1)S(1)} %get-tuple-element.58), channel_id=1, source_target_pairs={{0,4},{1,5},{2,6},{3,7},{4,0},{5,1},{6,2},{7,3},{8,12},{9,13},{10,... | collective-permute-start | bytes 688136 | tf_op jit(solution)/shard_map/ppermute | solution.py:365
  93.0 13.5 %collective-permute-done.6.far = bf16[64,1792]{1,0:T(8,128)(2,1)S(1)} collective-permute-done((bf16[64,1792]{1,0:T(8,128)(2,1)S(1)}, bf16[64,1792]{1,0:T(8,128)(2,1)S(1)}, u32[]{:S(2)}, u32[]{:S(2)}) %collective-permute-start.6) | collective-permute-done | bytes 229408 | tf_op jit(solution)/shard_map/ppermute | solution.py:365
  109.7 2.9 %collective-permute-start.8 = (bf16[64,1792]{1,0:T(8,128)(2,1)S(1)}, bf16[64,1792]{1,0:T(8,128)(2,1)S(1)}, u32[]{:S(2)}, u32[]{:S(2)}) collective-permute-start(bf16[64,1792]{1,0:T(8,128)(2,1)S(1)} %shard_map.78.refs_0_), channel_id=1, source_target_pairs={{0,2},{1,3},{2,0},{3,1},{4,6},{5,7},{6,4},{7,5},{8,10},{9,11},{10,... | collective-permute-start | bytes 688136 | tf_op jit(solution)/shard_map/ppermute | solution.py:351
  113.0 6.8 %shard_map.80 = (f32[64,1792]{1,0:T(8,128)S(1)}, bf16[64,1792]{1,0:T(8,128)(2,1)S(1)}, bf16[64,1792]{1,0:T(8,128)(2,1)S(1)}, bf16[64,1792]{1,0:T(8,128)(2,1)S(1)}) custom-call(s32[2]{0:T(128)S(1)} %copy-done, bf16[256,1792]{1,0:T(8,128)(2,1)S(1)} %bitcast.30, bf16[256,1792]{1,0:T(8,128)(2,1)S(1)} %collective-permute-done.10.other, bf16[3584,1792]{1,0:T(8,128)(2,1)} %refs_4_.3), custom_call_target="tpu_custom_call" | custom-call | flops 3288334336 | bytes 12845056 | tf_op jit(solution)/shard_map/pallas_call | solution.py:168
  123.4 7.1 %shard_map.79 = (bf16[128,3584]{1,0:T(8,128)(2,1)S(1)}, f32[128,3584]{1,0:T(8,128)S(1)}) custom-call(s32[2]{0:T(128)S(1)} %copy-done, bf16[64,1792]{1,0:T(8,128)(2,1)S(1)} %shard_map.78.refs_0_, bf16[64,1792]{1,0:T(8,128)(2,1)S(1)} %collective-permute-done.7.refs_1_, bf16[64,1792]{1,0:T(8,128)(2,1)S(1)} %collective-permute-done.8.refs_2_, ...), custom_call_target="tpu_custom_call" | custom-call | flops 3288334336 | bytes 12845056 | tf_op jit(solution)/shard_map/pallas_call | solution.py:212
  135.1 8.4 %collective-permute-done.14.far = bf16[64,1792]{1,0:T(8,128)(2,1)S(1)} collective-permute-done((bf16[64,1792]{1,0:T(8,128)(2,1)S(1)}, bf16[64,1792]{1,0:T(8,128)(2,1)S(1)}, u32[]{:S(2)}, u32[]{:S(2)}) %collective-permute-start.14) | collective-permute-done | bytes 229408 | tf_op jit(solution)/shard_map/ppermute | solution.py:372
  144.6 4.6 %all-to-all-start.4 = ((bf16[8,16,3584]{2,1,0:T(8,128)(2,1)}), bf16[8,16,3584]{2,1,0:T(8,128)(2,1)S(1)}, u32[]{:S(2)}, u32[]{:S(2)}) async-start(bf16[8,16,3584]{2,1,0:T(8,128)(2,1)} %bitcast.15), calls=%async_computation.4 | async-start | bytes 1835008 | tf_op jit(solution)/shard_map/all_to_all | solution.py:330
  153.1 3.7 %collective-permute-done.16.refs_1_ = bf16[64,1792]{1,0:T(8,128)(2,1)S(1)} collective-permute-done((bf16[64,1792]{1,0:T(8,128)(2,1)S(1)}, bf16[64,1792]{1,0:T(8,128)(2,1)S(1)}, u32[]{:S(2)}, u32[]{:S(2)}) %collective-permute-start.16) | collective-permute-done | bytes 229408 | tf_op jit(solution)/shard_map/ppermute | solution.py:351
  156.8 5.7 %collective-permute-done.17.refs_2_ = bf16[64,1792]{1,0:T(8,128)(2,1)S(1)} collective-permute-done((bf16[64,1792]{1,0:T(8,128)(2,1)S(1)}, bf16[64,1792]{1,0:T(8,128)(2,1)S(1)}, u32[]{:S(2)}, u32[]{:S(2)}) %collective-permute-start.17) | collective-permute-done | bytes 229408 | tf_op jit(solution)/shard_map/ppermute | solution.py:351
  162.7 7.1 %shard_map.84 = (bf16[128,3584]{1,0:T(8,128)(2,1)S(1)}, f32[128,3584]{1,0:T(8,128)S(1)}) custom-call(s32[2]{0:T(128)S(1)} %copy-done, bf16[64,1792]{1,0:T(8,128)(2,1)S(1)} %shard_map.83.refs_0_, bf16[64,1792]{1,0:T(8,128)(2,1)S(1)} %collective-permute-done.16.refs_1_, bf16[64,1792]{1,0:T(8,128)(2,1)S(1)} %collective-permute-done.17.refs_2_, ...), custom_call_target="tpu_custom_call" | custom-call | flops 3288334336 | bytes 12845056 | tf_op jit(solution)/shard_map/pallas_call | solution.py:212
  175.0 5.1 %all-to-all-start.5 = ((bf16[8,16,3584]{2,1,0:T(8,128)(2,1)}), bf16[8,16,3584]{2,1,0:T(8,128)(2,1)S(1)}, u32[]{:S(2)}, u32[]{:S(2)}) async-start(bf16[8,16,3584]{2,1,0:T(8,128)(2,1)} %bitcast.17), calls=%async_computation.5 | async-start | bytes 1835008 | tf_op jit(solution)/shard_map/all_to_all | solution.py:330
  180.3 13.4 %all-to-all-done.5 = bf16[8,16,3584]{2,1,0:T(8,128)(2,1)S(1)} async-done(((bf16[8,16,3584]{2,1,0:T(8,128)(2,1)}), bf16[8,16,3584]{2,1,0:T(8,128)(2,1)S(1)}, u32[]{:S(2)}, u32[]{:S(2)}) %all-to-all-start.5) | async-done | bytes 917536 | tf_op jit(solution)/shard_map/all_to_all | solution.py:330
  (70 shorter events, 41.2 us)
Async XLA Ops:
  0.0 12.0 %collective-permute-start.1 = (bf16[512,3584]{1,0:T(8,128)(2,1)}, bf16[512,3584]{1,0:T(8,128)(2,1)}, u32[]{:S(2)}, u32[]{:S(2)}) collective-permute-start(bf16[512,3584]{1,0:T(8,128)(2,1)} %grad.3), channel_id=1, source_target_pairs={{0,8},{8,0},{16,24},{24,16},{32,40},{40,32},{48,56},{56,48},{64,72... | collective-permute-start | bytes 11010056 | tf_op jit(solution)/shard_map/ppermute | solution.py:332
  17.9 19.5 %all-to-all-start = ((bf16[8,32,1792]{2,1,0:T(8,128)(2,1)}), bf16[8,32,1792]{2,1,0:T(8,128)(2,1)S(1)}, u32[]{:S(2)}, u32[]{:S(2)}) async-start(bf16[8,32,1792]{2,1,0:T(8,128)(2,1)} %bitcast.34), calls=%async_computation | async-start | bytes 1835008 | tf_op jit(solution)/shard_map/all_to_all | solution.py:330
  38.6 17.2 %all-to-all-start.1 = ((bf16[8,32,1792]{2,1,0:T(8,128)(2,1)}), bf16[8,32,1792]{2,1,0:T(8,128)(2,1)S(1)}, u32[]{:S(2)}, u32[]{:S(2)}) async-start(bf16[8,32,1792]{2,1,0:T(8,128)(2,1)} %broadcast_in_dim.64), calls=%async_computation.1 | async-start | bytes 1835008 | tf_op jit(solution)/shard_map/all_to_all | solution.py:330
  55.8 5.2 %collective-permute-start.2 = (bf16[256,1792]{1,0:T(8,128)(2,1)S(1)}, bf16[256,1792]{1,0:T(8,128)(2,1)S(1)}, u32[]{:S(2)}, u32[]{:S(2)}) collective-permute-start(bf16[256,1792]{1,0:T(8,128)(2,1)S(1)} %bitcast.31), channel_id=1, source_target_pairs={{0,8},{8,0},{16,24},{24,16},{32,40},{40,32},{48,56},{56,48},{64,72... | collective-permute-start | bytes 2752520 | tf_op jit(solution)/shard_map/ppermute | solution.py:354
  56.7 17.9 %all-to-all-start.2 = ((bf16[8,32,1792]{2,1,0:T(8,128)(2,1)}), bf16[8,32,1792]{2,1,0:T(8,128)(2,1)}, u32[]{:S(2)}, u32[]{:S(2)}) async-start(bf16[8,32,1792]{2,1,0:T(8,128)(2,1)} %bitcast.35), calls=%async_computation.2 | async-start | bytes 1835008 | tf_op jit(solution)/shard_map/all_to_all | solution.py:330
  67.8 8.5 %collective-permute-start.3 = (bf16[64,1792]{1,0:T(8,128)(2,1)S(1)}, bf16[64,1792]{1,0:T(8,128)(2,1)S(1)}, u32[]{:S(2)}, u32[]{:S(2)}) collective-permute-start(bf16[64,1792]{1,0:T(8,128)(2,1)S(1)} %get-tuple-element.49), channel_id=1, source_target_pairs={{0,1},{1,2},{2,3},{3,0},{4,5},{5,6},{6,7},{7,4},{8,9},{9,10},{10,1... | collective-permute-start | bytes 688136 | tf_op jit(solution)/shard_map/ppermute | solution.py:351
  69.1 13.1 %collective-permute-start.4 = (bf16[64,1792]{1,0:T(8,128)(2,1)S(1)}, bf16[64,1792]{1,0:T(8,128)(2,1)S(1)}, u32[]{:S(2)}, u32[]{:S(2)}) collective-permute-start(bf16[64,1792]{1,0:T(8,128)(2,1)S(1)} %get-tuple-element.50), channel_id=1, source_target_pairs={{0,2},{1,3},{2,0},{3,1},{4,6},{5,7},{6,4},{7,5},{8,10},{9,11},{10,... | collective-permute-start | bytes 688136 | tf_op jit(solution)/shard_map/ppermute | solution.py:351
  71.5 10.7 %collective-permute-start.5 = (bf16[64,1792]{1,0:T(8,128)(2,1)S(1)}, bf16[64,1792]{1,0:T(8,128)(2,1)S(1)}, u32[]{:S(2)}, u32[]{:S(2)}) collective-permute-start(bf16[64,1792]{1,0:T(8,128)(2,1)S(1)} %get-tuple-element.51), channel_id=1, source_target_pairs={{0,3},{1,0},{2,1},{3,2},{4,7},{5,4},{6,5},{7,6},{8,11},{9,8},{10,9... | collective-permute-start | bytes 688136 | tf_op jit(solution)/shard_map/ppermute | solution.py:351
  84.6 22.1 %all-to-all-start.3 = ((bf16[8,32,1792]{2,1,0:T(8,128)(2,1)}), bf16[8,32,1792]{2,1,0:T(8,128)(2,1)S(1)}, u32[]{:S(2)}, u32[]{:S(2)}) async-start(bf16[8,32,1792]{2,1,0:T(8,128)(2,1)} %broadcast_in_dim.66), calls=%async_computation.3 | async-start | bytes 1835008 | tf_op jit(solution)/shard_map/all_to_all | solution.py:330
  89.4 17.1 %collective-permute-start.6 = (bf16[64,1792]{1,0:T(8,128)(2,1)S(1)}, bf16[64,1792]{1,0:T(8,128)(2,1)S(1)}, u32[]{:S(2)}, u32[]{:S(2)}) collective-permute-start(bf16[64,1792]{1,0:T(8,128)(2,1)S(1)} %get-tuple-element.58), channel_id=1, source_target_pairs={{0,4},{1,5},{2,6},{3,7},{4,0},{5,1},{6,2},{7,3},{8,12},{9,13},{10,... | collective-permute-start | bytes 688136 | tf_op jit(solution)/shard_map/ppermute | solution.py:365
  106.6 6.3 %collective-permute-start.10 = (bf16[256,1792]{1,0:T(8,128)(2,1)S(1)}, bf16[256,1792]{1,0:T(8,128)(2,1)S(1)}, u32[]{:S(2)}, u32[]{:S(2)}) collective-permute-start(bf16[256,1792]{1,0:T(8,128)(2,1)S(1)} %bitcast.29), channel_id=1, source_target_pairs={{0,8},{8,0},{16,24},{24,16},{32,40},{40,32},{48,56},{56,48},{64,72... | collective-permute-start | bytes 2752520 | tf_op jit(solution)/shard_map/ppermute | solution.py:354
  108.7 12.8 %collective-permute-start.7 = (bf16[64,1792]{1,0:T(8,128)(2,1)S(1)}, bf16[64,1792]{1,0:T(8,128)(2,1)S(1)}, u32[]{:S(2)}, u32[]{:S(2)}) collective-permute-start(bf16[64,1792]{1,0:T(8,128)(2,1)S(1)} %shard_map.78.refs_0_), channel_id=1, source_target_pairs={{0,1},{1,2},{2,3},{3,0},{4,5},{5,6},{6,7},{7,4},{8,9},{9,10},{10,1... | collective-permute-start | bytes 688136 | tf_op jit(solution)/shard_map/ppermute | solution.py:351
  109.7 13.7 %collective-permute-start.8 = (bf16[64,1792]{1,0:T(8,128)(2,1)S(1)}, bf16[64,1792]{1,0:T(8,128)(2,1)S(1)}, u32[]{:S(2)}, u32[]{:S(2)}) collective-permute-start(bf16[64,1792]{1,0:T(8,128)(2,1)S(1)} %shard_map.78.refs_0_), channel_id=1, source_target_pairs={{0,2},{1,3},{2,0},{3,1},{4,6},{5,7},{6,4},{7,5},{8,10},{9,11},{10,... | collective-permute-start | bytes 688136 | tf_op jit(solution)/shard_map/ppermute | solution.py:351
  112.6 10.8 %collective-permute-start.9 = (bf16[64,1792]{1,0:T(8,128)(2,1)S(1)}, bf16[64,1792]{1,0:T(8,128)(2,1)S(1)}, u32[]{:S(2)}, u32[]{:S(2)}) collective-permute-start(bf16[64,1792]{1,0:T(8,128)(2,1)S(1)} %shard_map.78.refs_0_), channel_id=1, source_target_pairs={{0,3},{1,0},{2,1},{3,2},{4,7},{5,4},{6,5},{7,6},{8,11},{9,8},{10,9... | collective-permute-start | bytes 688136 | tf_op jit(solution)/shard_map/ppermute | solution.py:351
  119.7 10.8 %collective-permute-start.11 = (bf16[64,1792]{1,0:T(8,128)(2,1)S(1)}, bf16[64,1792]{1,0:T(8,128)(2,1)S(1)}, u32[]{:S(2)}, u32[]{:S(2)}) collective-permute-start(bf16[64,1792]{1,0:T(8,128)(2,1)S(1)} %get-tuple-element.65), channel_id=1, source_target_pairs={{0,1},{1,2},{2,3},{3,0},{4,5},{5,6},{6,7},{7,4},{8,9},{9,10},{10,1... | collective-permute-start | bytes 688136 | tf_op jit(solution)/shard_map/ppermute | solution.py:351
  120.9 12.2 %collective-permute-start.12 = (bf16[64,1792]{1,0:T(8,128)(2,1)S(1)}, bf16[64,1792]{1,0:T(8,128)(2,1)S(1)}, u32[]{:S(2)}, u32[]{:S(2)}) collective-permute-start(bf16[64,1792]{1,0:T(8,128)(2,1)S(1)} %get-tuple-element.66), channel_id=1, source_target_pairs={{0,2},{1,3},{2,0},{3,1},{4,6},{5,7},{6,4},{7,5},{8,10},{9,11},{10,... | collective-permute-start | bytes 688136 | tf_op jit(solution)/shard_map/ppermute | solution.py:351
  121.5 11.6 %collective-permute-start.13 = (bf16[64,1792]{1,0:T(8,128)(2,1)S(1)}, bf16[64,1792]{1,0:T(8,128)(2,1)S(1)}, u32[]{:S(2)}, u32[]{:S(2)}) collective-permute-start(bf16[64,1792]{1,0:T(8,128)(2,1)S(1)} %get-tuple-element.67), channel_id=1, source_target_pairs={{0,3},{1,0},{2,1},{3,2},{4,7},{5,4},{6,5},{7,6},{8,11},{9,8},{10,9... | collective-permute-start | bytes 688136 | tf_op jit(solution)/shard_map/ppermute | solution.py:351
  133.1 10.4 %collective-permute-start.15 = (bf16[128,3584]{1,0:T(8,128)(2,1)S(1)}, bf16[128,3584]{1,0:T(8,128)(2,1)S(1)}, u32[]{:S(2)}, u32[]{:S(2)}) collective-permute-start(bf16[128,3584]{1,0:T(8,128)(2,1)S(1)} %get-tuple-element.74), channel_id=1, source_target_pairs={{0,8},{8,0},{16,24},{24,16},{32,40},{40,32},{48,56},{56,48},{64,72... | collective-permute-start | bytes 2752520 | tf_op jit(solution)/shard_map/ppermute | solution.py:354
  134.7 8.8 %collective-permute-start.14 = (bf16[64,1792]{1,0:T(8,128)(2,1)S(1)}, bf16[64,1792]{1,0:T(8,128)(2,1)S(1)}, u32[]{:S(2)}, u32[]{:S(2)}) collective-permute-start(bf16[64,1792]{1,0:T(8,128)(2,1)S(1)} %get-tuple-element.72), channel_id=1, source_target_pairs={{0,4},{1,5},{2,6},{3,7},{4,0},{5,1},{6,2},{7,3},{8,12},{9,13},{10,... | collective-permute-start | bytes 688136 | tf_op jit(solution)/shard_map/ppermute | solution.py:372
  144.6 18.1 %all-to-all-start.4 = ((bf16[8,16,3584]{2,1,0:T(8,128)(2,1)}), bf16[8,16,3584]{2,1,0:T(8,128)(2,1)S(1)}, u32[]{:S(2)}, u32[]{:S(2)}) async-start(bf16[8,16,3584]{2,1,0:T(8,128)(2,1)} %bitcast.15), calls=%async_computation.4 | async-start | bytes 1835008 | tf_op jit(solution)/shard_map/all_to_all | solution.py:330
  149.5 7.3 %collective-permute-start.16 = (bf16[64,1792]{1,0:T(8,128)(2,1)S(1)}, bf16[64,1792]{1,0:T(8,128)(2,1)S(1)}, u32[]{:S(2)}, u32[]{:S(2)}) collective-permute-start(bf16[64,1792]{1,0:T(8,128)(2,1)S(1)} %shard_map.83.refs_0_), channel_id=1, source_target_pairs={{0,1},{1,2},{2,3},{3,0},{4,5},{5,6},{6,7},{7,4},{8,9},{9,10},{10,1... | collective-permute-start | bytes 688136 | tf_op jit(solution)/shard_map/ppermute | solution.py:351
  150.4 12.1 %collective-permute-start.17 = (bf16[64,1792]{1,0:T(8,128)(2,1)S(1)}, bf16[64,1792]{1,0:T(8,128)(2,1)S(1)}, u32[]{:S(2)}, u32[]{:S(2)}) collective-permute-start(bf16[64,1792]{1,0:T(8,128)(2,1)S(1)} %shard_map.83.refs_0_), channel_id=1, source_target_pairs={{0,2},{1,3},{2,0},{3,1},{4,6},{5,7},{6,4},{7,5},{8,10},{9,11},{10,... | collective-permute-start | bytes 688136 | tf_op jit(solution)/shard_map/ppermute | solution.py:351
  153.1 9.7 %collective-permute-start.18 = (bf16[64,1792]{1,0:T(8,128)(2,1)S(1)}, bf16[64,1792]{1,0:T(8,128)(2,1)S(1)}, u32[]{:S(2)}, u32[]{:S(2)}) collective-permute-start(bf16[64,1792]{1,0:T(8,128)(2,1)S(1)} %shard_map.83.refs_0_), channel_id=1, source_target_pairs={{0,3},{1,0},{2,1},{3,2},{4,7},{5,4},{6,5},{7,6},{8,11},{9,8},{10,9... | collective-permute-start | bytes 688136 | tf_op jit(solution)/shard_map/ppermute | solution.py:351
  175.0 18.7 %all-to-all-start.5 = ((bf16[8,16,3584]{2,1,0:T(8,128)(2,1)}), bf16[8,16,3584]{2,1,0:T(8,128)(2,1)S(1)}, u32[]{:S(2)}, u32[]{:S(2)}) async-start(bf16[8,16,3584]{2,1,0:T(8,128)(2,1)} %bitcast.17), calls=%async_computation.5 | async-start | bytes 1835008 | tf_op jit(solution)/shard_map/all_to_all | solution.py:330
  (5 other events, 37.7 us)

commit v7 on v6

--- a/solution.py
+++ b/solution.py
@@ -53,18 +53,16 @@
     @pl.when(step == pl.num_programs(0) - 1)
     def _():
         rows = acc[...].T.astype(BF16)
-        run = queries // chips // CHUNKS // 2
+        run = queries // chips // 2
         for chip in range(chips):
             for core in range(2):
-                for n in range(CHUNKS):
-                    to = ((n * 2 + core) * chips + chip) * run
-                    at = ((chip * 2 + core) * CHUNKS + n) * run
-                    out[to : to + run, :] = rows[at : at + run, :]
+                at, to = (chip * 2 + core) * run, (core * chips + chip) * run
+                out[to : to + run, :] = rows[at : at + run, :]
 
 
 def select(ids, basis, chips, block=2048):
     rows, width = basis.shape
-    queries = ids.shape[0]
+    queries = ids.shape[1]
     return pl.pallas_call(
         functools.partial(select_kernel, chips=chips),
         grid=(width // block,),
@@ -74,12 +72,11 @@
         scratch_shapes=[pltpu.VMEM((rows, queries), F32)],
         cost_estimate=cost(2 * queries * rows * width, rows * width * 2),
         compiler_params=params(56),
-    )(ids[None, :], basis)
-
-
-def rows_kernel(place, sel, sel2, grad, grad2, out, buf, buf2, sems, *, chunk_index):
+    )(ids, basis)
+
+
+def rows_kernel(place, sel, sel2, grad, grad2, out, buf, buf2, sems):
     steps = sems.shape[1]
-    rows = pl.ds(chunk_index * out.shape[0], out.shape[0])
     half = out.shape[1]
     block = half // steps
     copies = []
@@ -99,15 +96,15 @@
         to = pl.ds(i * block, block)
         copies[i][0].wait()
         copies[i][1].wait()
-        total = dot(sel[rows, :], buf[:, to]) + dot(sel2[rows, :], buf2[:, to])
+        total = dot(sel[...], buf[:, to]) + dot(sel2[...], buf2[:, to])
         out[:, to] = total.astype(BF16)
 
 
-def partial_rows(place, sel, sel2, grad, grad2, chunk_index, steps=2):
-    queries, units = sel.shape[0] // CHUNKS, sel.shape[1]
+def partial_rows(place, sel, sel2, grad, grad2, steps=2):
+    queries, units = sel.shape
     half = grad.shape[1] // 2
     return pl.pallas_call(
-        functools.partial(rows_kernel, chunk_index=chunk_index),
+        rows_kernel,
         in_specs=[SMEM, VMEM, VMEM, ANY, ANY],
         out_specs=VMEM,
         out_shape=jax.ShapeDtypeStruct((queries, half), BF16),
@@ -245,23 +242,23 @@
     )(keep, got)
 
 
-def stack_kernel(parts, total, rounded):
+def spread_kernel(parts, out):
     value = parts[0].astype(F32)
-    for d in range(1, RING):
-        value += parts[d].astype(F32)
-    total[...] = value
-    rounded[...] = value.astype(BF16)
-
-
-def stack_sum(parts):
-    shape = parts.shape[1:]
-    return pl.pallas_call(
-        stack_kernel,
+    for i in range(1, parts.shape[0]):
+        value += parts[i].astype(F32)
+    value = value.astype(BF16)
+    for i in range(parts.shape[0]):
+        out[i] = value
+
+
+def spread(parts):
+    return pl.pallas_call(
+        spread_kernel,
         in_specs=[VMEM],
-        out_specs=[VMEM] * 2,
-        out_shape=[jax.ShapeDtypeStruct(shape, F32), jax.ShapeDtypeStruct(shape, BF16)],
-        cost_estimate=cost(3 * parts.size, 4 * parts.size),
-        compiler_params=params(8),
+        out_specs=VMEM,
+        out_shape=jax.ShapeDtypeStruct(parts.shape, BF16),
+        cost_estimate=cost(parts.size, 4 * parts.size),
+        compiler_params=params(12),
     )(parts)
 
 
@@ -321,7 +318,6 @@
     place = jnp.stack([core, x]).astype(jnp.int32)
     swap = [(i, i ^ 1) for i in range(loops)]
     flip = [(i, (i + RING) % reds) for i in range(reds)]
-    rings = [[h + i for i in range(RING)] for h in range(0, reds, RING)]
     shift = [[(i, i - i % RING + (i + d) % RING) for i in range(reds)] for d in range(RING)]
     same_core = [[2 * i + c for i in range(chips)] for c in range(2)]
 
@@ -330,8 +326,7 @@
         return lax.all_to_all(value, "loop", 0, 0, axis_index_groups=same_core)
 
     got = lax.ppermute(gradient, "loop", swap)
-    sel = select(query_ids, out_basis, chips)
-    sel_got = lax.ppermute(sel, "loop", swap)
+    ids = query_ids.reshape(loops, CHUNKS, -1).transpose(1, 0, 2).reshape(CHUNKS, 1, chunk)
     eigen_rows = jnp.take(jnp.take(out_eigen, layer_index, axis=0)[0], query_ids)
     eigen_rows = eigen_rows.reshape(chips, 2, CHUNKS, -1).transpose(2, 1, 0, 3).reshape(CHUNKS, chunk)
     eigen_cols = jnp.take(in_eigen, layer_index, axis=0)
@@ -339,24 +334,24 @@
         lax.dynamic_slice_in_dim(eigen_rows[n], x * piece, piece, 0)[:, None] for n in range(CHUNKS)
     ]
 
-    def scatter(n):
-        return partial_rows(place, sel, sel_got, gradient, got, n)
+    def scatter(ids):
+        sel = select(ids, out_basis, chips)
+        return partial_rows(place, sel, lax.ppermute(sel, "loop", swap), gradient, got)
 
     def gather(parts):
-        rows = add_up(parts).astype(BF16)
-        rows = jnp.broadcast_to(rows[None], (chips,) + rows.shape).reshape(chunk, -1)
-        return exchange(rows).reshape(chunk, -1)
+        return exchange(spread(parts).reshape(chunk, -1)).reshape(chunk, -1)
 
     def ring(parts):
-        return [parts[0]] + [lax.ppermute(parts[d], "red", shift[d]) for d in range(1, RING)]
+        got = {d: lax.ppermute(parts[d], "red", shift[d]) for d in (2, 1, 3)}
+        return [parts[0]] + [got[d] for d in range(1, RING)]
 
     def swapped(value):
         return lax.ppermute(value, "loop", swap)
 
-    part_a = scatter(0)
-    part_a, *factors = tie(exchange(part_a), *factors)
+    part_a = scatter(ids[0])
+    part_a, ids_b, *factors = tie(exchange(part_a), ids[1], *factors)
     own_a = gather(part_a)
-    part_b, own_a = tie(scatter(1), own_a)
+    part_b, own_a = tie(scatter(ids_b), own_a)
     part_b = exchange(part_b)
     ring_a = ring(rotate(place, own_a, swapped(own_a), in_basis))
     part_b, *ring_a = tie(part_b, *ring_a)

time: 195 us -> 196 us (level)
  waiting for transfers between devices: 77.2 us -> 68.9 us
  Pallas kernels: 49 us -> 56.2 us
  starting transfers between devices: 56 us -> 59.1 us
    all_to_all x6, waiting for transfers between devices: 33.5 us -> 23.8 us  [exchange(): return lax.all_to_all(value, 'loop', 0, 0, axis_index_groups=same_core)]
    pallas_call x1 -> x2, Pallas kernels: 8.28 us -> 13 us  [select(): pl.pallas_call(functools.partial(select_kernel, chips=chips), grid=(width...]
    ppermute x13 -> x14, starting transfers between devices: 16.4 us -> 18.5 us  [the longest x12 17.7 us: ring(): got = {d: lax.ppermute(parts[d], 'red', shift[d]) for d in (2, 1, 3)}]
    broadcast_in_dim x2 -> x0, local copies, waits for them, and re-layouts: 2.04 us -> none  [gather(): jnp.broadcast_to(rows[None], (chips,) + rows.shape).reshape(chunk, -1)]
    ppermute x13 -> x14, waiting for transfers between devices: 19.7 us -> 21.7 us  [the longest x12 20.3 us: ring(): got = {d: lax.ppermute(parts[d], 'red', shift[d]) for d in (2, 1, 3)}]
    pallas_call x2 -> x4, Pallas kernels: 10.2 us -> 11.9 us  [the longest x2 9.8 us: partial_rows(): pl.pallas_call(rows_kernel, in_specs=[SMEM, VMEM, VMEM, ANY, ANY], out_sp...]
  transfers between devices with their start and end apart: 26 -> 27, of which waited for: 13 -> 13; matrix products, arithmetic and copies ran while one was open for 3% -> 4% of each run, Pallas kernels for 18% -> 20%
where the time goes in v7:
time: 196 us
  waiting for transfers between devices  68.9 us (35%)
  starting transfers between devices  59.1 us (30%)
  Pallas kernels  56.2 us (29%)
  local copies, waits for them, and re-layouts  7.2 us (4%)
  other arithmetic  3.34 us (2%)
    all_to_all x6, starting transfers between devices, exchange(): return lax.all_to_all(value, 'loop', 0, 0, axis_index_groups=same_core)  30 us
    all_to_all x6, waiting for transfers between devices, exchange(): return lax.all_to_all(value, 'loop', 0, 0, axis_index_groups=same_core)  23.8 us
    ppermute x12, waiting for transfers between devices, ring(): got = {d: lax.ppermute(parts[d], 'red', shift[d]) for d in (2, 1, 3)}  20.3 us
    ppermute x12, starting transfers between devices, ring(): got = {d: lax.ppermute(parts[d], 'red', shift[d]) for d in (2, 1, 3)}  17.7 us
    pallas_call x2, Pallas kernels, back(): pl.pallas_call(functools.partial(back_kernel, cuts=cuts), in_specs=[SMEM]...  14.3 us
    pallas_call x2, Pallas kernels, rotate(): pl.pallas_call(functools.partial(rotate_kernel, cuts=cuts), in_specs=[SME...  14.3 us
    ppermute x1, waiting for transfers between devices, per_device(): lax.ppermute(rounded_a, 'red', flip)  13 us
    pallas_call x2, Pallas kernels, select(): pl.pallas_call(functools.partial(select_kernel, chips=chips), grid=(width...  13 us
  transfers between devices with their start and end apart: 27, of which 13 were waited for; matrix products, arithmetic and copies ran while one was open for 4% of the time, Pallas kernels for 20%

profile of v7, /device:TPU:1, one launch (start us, length us, event | category | flops | bytes accessed | tf_op | source)
XLA Modules:
  0.0 195.7 jit_solution(16339729716431140748)
XLA Ops:
  2.9 6.5 %shard_map.73.sel = bf16[256,512]{1,0:T(8,128)(2,1)} custom-call(s32[1,256]{1,0:T(1,128)} %squeeze.8.ids, bf16[512,8192]{1,0:T(8,128)(2,1)} %basis.5), custom_call_target="tpu_custom_call" | custom-call | flops 2147483648 | bytes 8388608 | tf_op jit(solution)/shard_map/pallas_call | solution.py:66
  12.4 4.9 %shard_map.74 = bf16[256,1792]{1,0:T(8,128)(2,1)} custom-call(s32[2]{0:T(128)} %pad_add_fusion.place, bf16[256,512]{1,0:T(8,128)(2,1)} %shard_map.73.sel, bf16[256,512]{1,0:T(8,128)(2,1)} %copy-done.1, bf16[512,3584]{1,0:T(8,128)(2,1)} %grad.3, bf16[512,3584]{1,0:T(8,128)(2,1)} %collective-permute-done.1.grad2), custom_call_target="tpu_custom_call" | custom-call | flops 939524096 | bytes 2752512 | tf_op jit(solution)/shard_map/pallas_call | solution.py:106
  17.3 6.1 %all-to-all-start = ((bf16[8,32,1792]{2,1,0:T(8,128)(2,1)}), bf16[8,32,1792]{2,1,0:T(8,128)(2,1)S(1)}, u32[]{:S(2)}, u32[]{:S(2)}) async-start(bf16[8,32,1792]{2,1,0:T(8,128)(2,1)} %bitcast.30), calls=%async_computation | async-start | bytes 1835008 | tf_op jit(solution)/shard_map/all_to_all | solution.py:326
  23.5 3.1 %gather_fusion = f32[512]{0:T(512)S(1)} fusion(f32[8192]{0:T(1024)S(1)} %bitcast.29, s32[1024]{0:T(1024)S(1)} %pad_clamp_fusion), kind=kCustom, calls=%fused_computation | custom fusion | bytes 6144 | tf_op jit(solution)/shard_map/jit(_take)/gather | solution.py:330
  27.7 9.2 %all-to-all-done.parts = bf16[8,32,1792]{2,1,0:T(8,128)(2,1)S(1)} async-done(((bf16[8,32,1792]{2,1,0:T(8,128)(2,1)}), bf16[8,32,1792]{2,1,0:T(8,128)(2,1)S(1)}, u32[]{:S(2)}, u32[]{:S(2)}) %all-to-all-start) | async-done | bytes 917536 | tf_op jit(solution)/shard_map/all_to_all | solution.py:326
  37.9 3.8 %all-to-all-start.1 = ((bf16[8,32,1792]{2,1,0:T(8,128)(2,1)}), bf16[8,32,1792]{2,1,0:T(8,128)(2,1)S(1)}, u32[]{:S(2)}, u32[]{:S(2)}) async-start(bf16[8,32,1792]{2,1,0:T(8,128)(2,1)} %shard_map.77), calls=%async_computation.1 | async-start | bytes 1835008 | tf_op jit(solution)/shard_map/all_to_all | solution.py:326
  41.8 6.5 %shard_map.75.sel = bf16[256,512]{1,0:T(8,128)(2,1)} custom-call(s32[1,256]{1,0:T(1,128)} %squeeze.9.ids, bf16[512,8192]{1,0:T(8,128)(2,1)} %basis.5), custom_call_target="tpu_custom_call" | custom-call | flops 2147483648 | bytes 8388608 | tf_op jit(solution)/shard_map/pallas_call | solution.py:66
  51.1 4.9 %shard_map.76 = bf16[256,1792]{1,0:T(8,128)(2,1)} custom-call(s32[2]{0:T(128)} %pad_add_fusion.place, bf16[256,512]{1,0:T(8,128)(2,1)} %shard_map.75.sel, bf16[256,512]{1,0:T(8,128)(2,1)} %copy-done.2, bf16[512,3584]{1,0:T(8,128)(2,1)} %grad.3, bf16[512,3584]{1,0:T(8,128)(2,1)} %collective-permute-done.1.grad2), custom_call_target="tpu_custom_call" | custom-call | flops 939524096 | bytes 2752512 | tf_op jit(solution)/shard_map/pallas_call | solution.py:106
  56.5 5.4 %all-to-all-start.2 = ((bf16[8,32,1792]{2,1,0:T(8,128)(2,1)}), bf16[8,32,1792]{2,1,0:T(8,128)(2,1)S(1)}, u32[]{:S(2)}, u32[]{:S(2)}) async-start(bf16[8,32,1792]{2,1,0:T(8,128)(2,1)} %bitcast.31), calls=%async_computation.2 | async-start | bytes 1835008 | tf_op jit(solution)/shard_map/all_to_all | solution.py:326
  61.9 7.5 %shard_map.78 = (f32[64,1792]{1,0:T(8,128)S(1)}, bf16[64,1792]{1,0:T(8,128)(2,1)}, bf16[64,1792]{1,0:T(8,128)(2,1)}, bf16[64,1792]{1,0:T(8,128)(2,1)S(1)}) custom-call(s32[2]{0:T(128)S(1)} %copy-done, bf16[256,1792]{1,0:T(8,128)(2,1)S(1)} %bitcast.28, bf16[256,1792]{1,0:T(8,128)(2,1)S(1)} %collective-permute-done.3.other, bf16[3584,1792]{1,0:T(8,128)(2,1)} %refs_4_.3), custom_call_target="tpu_custom_call" | custom-call | flops 3288334336 | bytes 12845056 | tf_op jit(solution)/shard_map/pallas_call | solution.py:165
  77.7 5.9 %collective-permute-done.5.b = bf16[64,1792]{1,0:T(8,128)(2,1)S(1)} collective-permute-done((bf16[64,1792]{1,0:T(8,128)(2,1)}, bf16[64,1792]{1,0:T(8,128)(2,1)S(1)}, u32[]{:S(2)}, u32[]{:S(2)}) %collective-permute-start.5) | collective-permute-done | bytes 229408 | tf_op jit(solution)/shard_map/ppermute | solution.py:345
  84.6 4.8 %all-to-all-start.3 = ((bf16[8,32,1792]{2,1,0:T(8,128)(2,1)}), bf16[8,32,1792]{2,1,0:T(8,128)(2,1)S(1)}, u32[]{:S(2)}, u32[]{:S(2)}) async-start(bf16[8,32,1792]{2,1,0:T(8,128)(2,1)} %shard_map.79), calls=%async_computation.3 | async-start | bytes 1835008 | tf_op jit(solution)/shard_map/all_to_all | solution.py:326
  89.5 2.7 %collective-permute-start.7 = (bf16[64,1792]{1,0:T(8,128)(2,1)S(1)}, bf16[64,1792]{1,0:T(8,128)(2,1)S(1)}, u32[]{:S(2)}, u32[]{:S(2)}) collective-permute-start(bf16[64,1792]{1,0:T(8,128)(2,1)S(1)} %get-tuple-element.60), channel_id=1, source_target_pairs={{0,4},{1,5},{2,6},{3,7},{4,0},{5,1},{6,2},{7,3},{8,12},{9,13},{10,... | collective-permute-start | bytes 688136 | tf_op jit(solution)/shard_map/ppermute | solution.py:360
  93.1 13.0 %collective-permute-done.7.far = bf16[64,1792]{1,0:T(8,128)(2,1)S(1)} collective-permute-done((bf16[64,1792]{1,0:T(8,128)(2,1)S(1)}, bf16[64,1792]{1,0:T(8,128)(2,1)S(1)}, u32[]{:S(2)}, u32[]{:S(2)}) %collective-permute-start.7) | collective-permute-done | bytes 229408 | tf_op jit(solution)/shard_map/ppermute | solution.py:360
  108.9 3.1 %collective-permute-start.10 = (bf16[64,1792]{1,0:T(8,128)(2,1)S(1)}, bf16[64,1792]{1,0:T(8,128)(2,1)S(1)}, u32[]{:S(2)}, u32[]{:S(2)}) collective-permute-start(bf16[64,1792]{1,0:T(8,128)(2,1)S(1)} %shard_map.81.refs_0_), channel_id=1, source_target_pairs={{0,3},{1,0},{2,1},{3,2},{4,7},{5,4},{6,5},{7,6},{8,11},{9,8},{10,9... | collective-permute-start | bytes 688136 | tf_op jit(solution)/shard_map/ppermute | solution.py:345
  113.2 6.8 %shard_map.83 = (f32[64,1792]{1,0:T(8,128)S(1)}, bf16[64,1792]{1,0:T(8,128)(2,1)S(1)}, bf16[64,1792]{1,0:T(8,128)(2,1)S(1)}, bf16[64,1792]{1,0:T(8,128)(2,1)S(1)}) custom-call(s32[2]{0:T(128)S(1)} %copy-done, bf16[256,1792]{1,0:T(8,128)(2,1)S(1)} %bitcast.26, bf16[256,1792]{1,0:T(8,128)(2,1)S(1)} %collective-permute-done.11.other, bf16[3584,1792]{1,0:T(8,128)(2,1)} %refs_4_.3), custom_call_target="tpu_custom_call" | custom-call | flops 3288334336 | bytes 12845056 | tf_op jit(solution)/shard_map/pallas_call | solution.py:165
  125.1 7.1 %shard_map.82 = (bf16[128,3584]{1,0:T(8,128)(2,1)S(1)}, f32[128,3584]{1,0:T(8,128)S(1)}) custom-call(s32[2]{0:T(128)S(1)} %copy-done, bf16[64,1792]{1,0:T(8,128)(2,1)S(1)} %shard_map.81.refs_0_, bf16[64,1792]{1,0:T(8,128)(2,1)S(1)} %collective-permute-done.8.refs_1_, bf16[64,1792]{1,0:T(8,128)(2,1)S(1)} %collective-permute-done.9.refs_2_, ...), custom_call_target="tpu_custom_call" | custom-call | flops 3288334336 | bytes 12845056 | tf_op jit(solution)/shard_map/pallas_call | solution.py:209
  136.6 8.4 %collective-permute-done.15.far = bf16[64,1792]{1,0:T(8,128)(2,1)S(1)} collective-permute-done((bf16[64,1792]{1,0:T(8,128)(2,1)S(1)}, bf16[64,1792]{1,0:T(8,128)(2,1)S(1)}, u32[]{:S(2)}, u32[]{:S(2)}) %collective-permute-start.15) | collective-permute-done | bytes 229408 | tf_op jit(solution)/shard_map/ppermute | solution.py:367
  146.0 4.6 %all-to-all-start.4 = ((bf16[8,16,3584]{2,1,0:T(8,128)(2,1)}), bf16[8,16,3584]{2,1,0:T(8,128)(2,1)S(1)}, u32[]{:S(2)}, u32[]{:S(2)}) async-start(bf16[8,16,3584]{2,1,0:T(8,128)(2,1)} %bitcast.13), calls=%async_computation.4 | async-start | bytes 1835008 | tf_op jit(solution)/shard_map/all_to_all | solution.py:326
  154.3 4.2 %collective-permute-done.17.refs_1_ = bf16[64,1792]{1,0:T(8,128)(2,1)S(1)} collective-permute-done((bf16[64,1792]{1,0:T(8,128)(2,1)S(1)}, bf16[64,1792]{1,0:T(8,128)(2,1)S(1)}, u32[]{:S(2)}, u32[]{:S(2)}) %collective-permute-start.17) | collective-permute-done | bytes 229408 | tf_op jit(solution)/shard_map/ppermute | solution.py:345
  158.5 4.3 %collective-permute-done.18.refs_2_ = bf16[64,1792]{1,0:T(8,128)(2,1)S(1)} collective-permute-done((bf16[64,1792]{1,0:T(8,128)(2,1)S(1)}, bf16[64,1792]{1,0:T(8,128)(2,1)S(1)}, u32[]{:S(2)}, u32[]{:S(2)}) %collective-permute-start.18) | collective-permute-done | bytes 229408 | tf_op jit(solution)/shard_map/ppermute | solution.py:345
  164.2 7.1 %shard_map.87 = (bf16[128,3584]{1,0:T(8,128)(2,1)S(1)}, f32[128,3584]{1,0:T(8,128)S(1)}) custom-call(s32[2]{0:T(128)S(1)} %copy-done, bf16[64,1792]{1,0:T(8,128)(2,1)S(1)} %shard_map.86.refs_0_, bf16[64,1792]{1,0:T(8,128)(2,1)S(1)} %collective-permute-done.17.refs_1_, bf16[64,1792]{1,0:T(8,128)(2,1)S(1)} %collective-permute-done.18.refs_2_, ...), custom_call_target="tpu_custom_call" | custom-call | flops 3288334336 | bytes 12845056 | tf_op jit(solution)/shard_map/pallas_call | solution.py:209
  176.1 5.1 %all-to-all-start.5 = ((bf16[8,16,3584]{2,1,0:T(8,128)(2,1)}), bf16[8,16,3584]{2,1,0:T(8,128)(2,1)S(1)}, u32[]{:S(2)}, u32[]{:S(2)}) async-start(bf16[8,16,3584]{2,1,0:T(8,128)(2,1)} %bitcast.15), calls=%async_computation.5 | async-start | bytes 1835008 | tf_op jit(solution)/shard_map/all_to_all | solution.py:326
  181.4 13.4 %all-to-all-done.5 = bf16[8,16,3584]{2,1,0:T(8,128)(2,1)S(1)} async-done(((bf16[8,16,3584]{2,1,0:T(8,128)(2,1)}), bf16[8,16,3584]{2,1,0:T(8,128)(2,1)S(1)}, u32[]{:S(2)}, u32[]{:S(2)}) %all-to-all-start.5) | async-done | bytes 917536 | tf_op jit(solution)/shard_map/all_to_all | solution.py:326
  (77 shorter events, 46.1 us)
Async XLA Ops:
  0.0 11.7 %collective-permute-start.1 = (bf16[512,3584]{1,0:T(8,128)(2,1)}, bf16[512,3584]{1,0:T(8,128)(2,1)}, u32[]{:S(2)}, u32[]{:S(2)}) collective-permute-start(bf16[512,3584]{1,0:T(8,128)(2,1)} %grad.3), channel_id=1, source_target_pairs={{0,8},{8,0},{16,24},{24,16},{32,40},{40,32},{48,56},{56,48},{64,72... | collective-permute-start | bytes 11010056 | tf_op jit(solution)/shard_map/ppermute | solution.py:328
  17.3 19.5 %all-to-all-start = ((bf16[8,32,1792]{2,1,0:T(8,128)(2,1)}), bf16[8,32,1792]{2,1,0:T(8,128)(2,1)S(1)}, u32[]{:S(2)}, u32[]{:S(2)}) async-start(bf16[8,32,1792]{2,1,0:T(8,128)(2,1)} %bitcast.30), calls=%async_computation | async-start | bytes 1835008 | tf_op jit(solution)/shard_map/all_to_all | solution.py:326
  37.9 18.1 %all-to-all-start.1 = ((bf16[8,32,1792]{2,1,0:T(8,128)(2,1)}), bf16[8,32,1792]{2,1,0:T(8,128)(2,1)S(1)}, u32[]{:S(2)}, u32[]{:S(2)}) async-start(bf16[8,32,1792]{2,1,0:T(8,128)(2,1)} %shard_map.77), calls=%async_computation.1 | async-start | bytes 1835008 | tf_op jit(solution)/shard_map/all_to_all | solution.py:326
  56.0 5.9 %collective-permute-start.3 = (bf16[256,1792]{1,0:T(8,128)(2,1)S(1)}, bf16[256,1792]{1,0:T(8,128)(2,1)S(1)}, u32[]{:S(2)}, u32[]{:S(2)}) collective-permute-start(bf16[256,1792]{1,0:T(8,128)(2,1)S(1)} %bitcast.27), channel_id=1, source_target_pairs={{0,8},{8,0},{16,24},{24,16},{32,40},{40,32},{48,56},{56,48},{64,72... | collective-permute-start | bytes 2752520 | tf_op jit(solution)/shard_map/ppermute | solution.py:349
  56.5 19.0 %all-to-all-start.2 = ((bf16[8,32,1792]{2,1,0:T(8,128)(2,1)}), bf16[8,32,1792]{2,1,0:T(8,128)(2,1)S(1)}, u32[]{:S(2)}, u32[]{:S(2)}) async-start(bf16[8,32,1792]{2,1,0:T(8,128)(2,1)} %bitcast.31), calls=%async_computation.2 | async-start | bytes 1835008 | tf_op jit(solution)/shard_map/all_to_all | solution.py:326
  69.4 8.2 %collective-permute-start.4 = (bf16[64,1792]{1,0:T(8,128)(2,1)}, bf16[64,1792]{1,0:T(8,128)(2,1)S(1)}, u32[]{:S(2)}, u32[]{:S(2)}) collective-permute-start(bf16[64,1792]{1,0:T(8,128)(2,1)} %get-tuple-element.51), channel_id=1, source_target_pairs={{0,1},{1,2},{2,3},{3,0},{4,5},{5,6},{6,7},{7,4},{8,9},{9,10},{10,1... | collective-permute-start | bytes 688136 | tf_op jit(solution)/shard_map/ppermute | solution.py:345
  70.7 12.9 %collective-permute-start.5 = (bf16[64,1792]{1,0:T(8,128)(2,1)}, bf16[64,1792]{1,0:T(8,128)(2,1)S(1)}, u32[]{:S(2)}, u32[]{:S(2)}) collective-permute-start(bf16[64,1792]{1,0:T(8,128)(2,1)} %get-tuple-element.52), channel_id=1, source_target_pairs={{0,2},{1,3},{2,0},{3,1},{4,6},{5,7},{6,4},{7,5},{8,10},{9,11},{10,... | collective-permute-start | bytes 688136 | tf_op jit(solution)/shard_map/ppermute | solution.py:345
  73.1 10.4 %collective-permute-start.6 = (bf16[64,1792]{1,0:T(8,128)(2,1)S(1)}, bf16[64,1792]{1,0:T(8,128)(2,1)S(1)}, u32[]{:S(2)}, u32[]{:S(2)}) collective-permute-start(bf16[64,1792]{1,0:T(8,128)(2,1)S(1)} %get-tuple-element.53), channel_id=1, source_target_pairs={{0,3},{1,0},{2,1},{3,2},{4,7},{5,4},{6,5},{7,6},{8,11},{9,8},{10,9... | collective-permute-start | bytes 688136 | tf_op jit(solution)/shard_map/ppermute | solution.py:345
  84.6 21.7 %all-to-all-start.3 = ((bf16[8,32,1792]{2,1,0:T(8,128)(2,1)}), bf16[8,32,1792]{2,1,0:T(8,128)(2,1)S(1)}, u32[]{:S(2)}, u32[]{:S(2)}) async-start(bf16[8,32,1792]{2,1,0:T(8,128)(2,1)} %shard_map.79), calls=%async_computation.3 | async-start | bytes 1835008 | tf_op jit(solution)/shard_map/all_to_all | solution.py:326
  89.5 16.6 %collective-permute-start.7 = (bf16[64,1792]{1,0:T(8,128)(2,1)S(1)}, bf16[64,1792]{1,0:T(8,128)(2,1)S(1)}, u32[]{:S(2)}, u32[]{:S(2)}) collective-permute-start(bf16[64,1792]{1,0:T(8,128)(2,1)S(1)} %get-tuple-element.60), channel_id=1, source_target_pairs={{0,4},{1,5},{2,6},{3,7},{4,0},{5,1},{6,2},{7,3},{8,12},{9,13},{10,... | collective-permute-start | bytes 688136 | tf_op jit(solution)/shard_map/ppermute | solution.py:360
  106.3 6.9 %collective-permute-start.11 = (bf16[256,1792]{1,0:T(8,128)(2,1)S(1)}, bf16[256,1792]{1,0:T(8,128)(2,1)S(1)}, u32[]{:S(2)}, u32[]{:S(2)}) collective-permute-start(bf16[256,1792]{1,0:T(8,128)(2,1)S(1)} %bitcast.25), channel_id=1, source_target_pairs={{0,8},{8,0},{16,24},{24,16},{32,40},{40,32},{48,56},{56,48},{64,72... | collective-permute-start | bytes 2752520 | tf_op jit(solution)/shard_map/ppermute | solution.py:349
  108.9 13.8 %collective-permute-start.10 = (bf16[64,1792]{1,0:T(8,128)(2,1)S(1)}, bf16[64,1792]{1,0:T(8,128)(2,1)S(1)}, u32[]{:S(2)}, u32[]{:S(2)}) collective-permute-start(bf16[64,1792]{1,0:T(8,128)(2,1)S(1)} %shard_map.81.refs_0_), channel_id=1, source_target_pairs={{0,3},{1,0},{2,1},{3,2},{4,7},{5,4},{6,5},{7,6},{8,11},{9,8},{10,9... | collective-permute-start | bytes 688136 | tf_op jit(solution)/shard_map/ppermute | solution.py:345
  112.0 13.1 %collective-permute-start.8 = (bf16[64,1792]{1,0:T(8,128)(2,1)S(1)}, bf16[64,1792]{1,0:T(8,128)(2,1)S(1)}, u32[]{:S(2)}, u32[]{:S(2)}) collective-permute-start(bf16[64,1792]{1,0:T(8,128)(2,1)S(1)} %shard_map.81.refs_0_), channel_id=1, source_target_pairs={{0,1},{1,2},{2,3},{3,0},{4,5},{5,6},{6,7},{7,4},{8,9},{9,10},{10,1... | collective-permute-start | bytes 688136 | tf_op jit(solution)/shard_map/ppermute | solution.py:345
  112.0 13.1 %collective-permute-start.9 = (bf16[64,1792]{1,0:T(8,128)(2,1)S(1)}, bf16[64,1792]{1,0:T(8,128)(2,1)S(1)}, u32[]{:S(2)}, u32[]{:S(2)}) collective-permute-start(bf16[64,1792]{1,0:T(8,128)(2,1)S(1)} %shard_map.81.refs_0_), channel_id=1, source_target_pairs={{0,2},{1,3},{2,0},{3,1},{4,6},{5,7},{6,4},{7,5},{8,10},{9,11},{10,... | collective-permute-start | bytes 688136 | tf_op jit(solution)/shard_map/ppermute | solution.py:345
  120.0 14.6 %collective-permute-start.12 = (bf16[64,1792]{1,0:T(8,128)(2,1)S(1)}, bf16[64,1792]{1,0:T(8,128)(2,1)S(1)}, u32[]{:S(2)}, u32[]{:S(2)}) collective-permute-start(bf16[64,1792]{1,0:T(8,128)(2,1)S(1)} %get-tuple-element.67), channel_id=1, source_target_pairs={{0,1},{1,2},{2,3},{3,0},{4,5},{5,6},{6,7},{7,4},{8,9},{9,10},{10,1... | collective-permute-start | bytes 688136 | tf_op jit(solution)/shard_map/ppermute | solution.py:345
  122.1 12.5 %collective-permute-start.13 = (bf16[64,1792]{1,0:T(8,128)(2,1)S(1)}, bf16[64,1792]{1,0:T(8,128)(2,1)S(1)}, u32[]{:S(2)}, u32[]{:S(2)}) collective-permute-start(bf16[64,1792]{1,0:T(8,128)(2,1)S(1)} %get-tuple-element.68), channel_id=1, source_target_pairs={{0,2},{1,3},{2,0},{3,1},{4,6},{5,7},{6,4},{7,5},{8,10},{9,11},{10,... | collective-permute-start | bytes 688136 | tf_op jit(solution)/shard_map/ppermute | solution.py:345
  122.7 11.9 %collective-permute-start.14 = (bf16[64,1792]{1,0:T(8,128)(2,1)S(1)}, bf16[64,1792]{1,0:T(8,128)(2,1)S(1)}, u32[]{:S(2)}, u32[]{:S(2)}) collective-permute-start(bf16[64,1792]{1,0:T(8,128)(2,1)S(1)} %get-tuple-element.69), channel_id=1, source_target_pairs={{0,3},{1,0},{2,1},{3,2},{4,7},{5,4},{6,5},{7,6},{8,11},{9,8},{10,9... | collective-permute-start | bytes 688136 | tf_op jit(solution)/shard_map/ppermute | solution.py:345
  134.6 10.3 %collective-permute-start.16 = (bf16[128,3584]{1,0:T(8,128)(2,1)S(1)}, bf16[128,3584]{1,0:T(8,128)(2,1)S(1)}, u32[]{:S(2)}, u32[]{:S(2)}) collective-permute-start(bf16[128,3584]{1,0:T(8,128)(2,1)S(1)} %get-tuple-element.76), channel_id=1, source_target_pairs={{0,8},{8,0},{16,24},{24,16},{32,40},{40,32},{48,56},{56,48},{64,72... | collective-permute-start | bytes 2752520 | tf_op jit(solution)/shard_map/ppermute | solution.py:349
  136.1 8.8 %collective-permute-start.15 = (bf16[64,1792]{1,0:T(8,128)(2,1)S(1)}, bf16[64,1792]{1,0:T(8,128)(2,1)S(1)}, u32[]{:S(2)}, u32[]{:S(2)}) collective-permute-start(bf16[64,1792]{1,0:T(8,128)(2,1)S(1)} %get-tuple-element.74), channel_id=1, source_target_pairs={{0,4},{1,5},{2,6},{3,7},{4,0},{5,1},{6,2},{7,3},{8,12},{9,13},{10,... | collective-permute-start | bytes 688136 | tf_op jit(solution)/shard_map/ppermute | solution.py:367
  146.0 18.1 %all-to-all-start.4 = ((bf16[8,16,3584]{2,1,0:T(8,128)(2,1)}), bf16[8,16,3584]{2,1,0:T(8,128)(2,1)S(1)}, u32[]{:S(2)}, u32[]{:S(2)}) async-start(bf16[8,16,3584]{2,1,0:T(8,128)(2,1)} %bitcast.13), calls=%async_computation.4 | async-start | bytes 1835008 | tf_op jit(solution)/shard_map/all_to_all | solution.py:326
  150.9 7.6 %collective-permute-start.17 = (bf16[64,1792]{1,0:T(8,128)(2,1)S(1)}, bf16[64,1792]{1,0:T(8,128)(2,1)S(1)}, u32[]{:S(2)}, u32[]{:S(2)}) collective-permute-start(bf16[64,1792]{1,0:T(8,128)(2,1)S(1)} %shard_map.86.refs_0_), channel_id=1, source_target_pairs={{0,1},{1,2},{2,3},{3,0},{4,5},{5,6},{6,7},{7,4},{8,9},{9,10},{10,1... | collective-permute-start | bytes 688136 | tf_op jit(solution)/shard_map/ppermute | solution.py:345
  151.2 11.6 %collective-permute-start.18 = (bf16[64,1792]{1,0:T(8,128)(2,1)S(1)}, bf16[64,1792]{1,0:T(8,128)(2,1)S(1)}, u32[]{:S(2)}, u32[]{:S(2)}) collective-permute-start(bf16[64,1792]{1,0:T(8,128)(2,1)S(1)} %shard_map.86.refs_0_), channel_id=1, source_target_pairs={{0,2},{1,3},{2,0},{3,1},{4,6},{5,7},{6,4},{7,5},{8,10},{9,11},{10,... | collective-permute-start | bytes 688136 | tf_op jit(solution)/shard_map/ppermute | solution.py:345
  153.3 10.9 %collective-permute-start.19 = (bf16[64,1792]{1,0:T(8,128)(2,1)S(1)}, bf16[64,1792]{1,0:T(8,128)(2,1)S(1)}, u32[]{:S(2)}, u32[]{:S(2)}) collective-permute-start(bf16[64,1792]{1,0:T(8,128)(2,1)S(1)} %shard_map.86.refs_0_), channel_id=1, source_target_pairs={{0,3},{1,0},{2,1},{3,2},{4,7},{5,4},{6,5},{7,6},{8,11},{9,8},{10,9... | collective-permute-start | bytes 688136 | tf_op jit(solution)/shard_map/ppermute | solution.py:345
  176.1 18.7 %all-to-all-start.5 = ((bf16[8,16,3584]{2,1,0:T(8,128)(2,1)}), bf16[8,16,3584]{2,1,0:T(8,128)(2,1)S(1)}, u32[]{:S(2)}, u32[]{:S(2)}) async-start(bf16[8,16,3584]{2,1,0:T(8,128)(2,1)} %bitcast.15), calls=%async_computation.5 | async-start | bytes 1835008 | tf_op jit(solution)/shard_map/all_to_all | solution.py:326
  (7 other events, 35.0 us)

commit v8 on v5

--- a/solution.py
+++ b/solution.py
@@ -231,19 +231,25 @@
     )(place, *pieces, basis)
 
 
-def join_kernel(keep, got, out):
-    out[...] = (keep[...] + got[...].astype(F32)).astype(BF16)
-
-
-def join(keep, got):
+def join_kernel(*refs):
+    out = refs[-1]
+    run = out.shape[1] // CHUNKS
+    for n in range(CHUNKS):
+        total = (refs[2 * n][...] + refs[2 * n + 1][...].astype(F32)).astype(BF16)
+        for chip in range(out.shape[0]):
+            out[chip, n * run : (n + 1) * run, :] = total[chip * run : (chip + 1) * run]
+
+
+def join(parts, chips):
+    rows, width = parts[0].shape
     return pl.pallas_call(
         join_kernel,
-        in_specs=[VMEM] * 2,
+        in_specs=[VMEM] * len(parts),
         out_specs=VMEM,
-        out_shape=jax.ShapeDtypeStruct(got.shape, BF16),
-        cost_estimate=cost(2 * got.size, 8 * got.size),
-        compiler_params=params(8),
-    )(keep, got)
+        out_shape=jax.ShapeDtypeStruct((chips, CHUNKS * rows // chips, width), BF16),
+        cost_estimate=cost(4 * rows * width, 16 * rows * width),
+        compiler_params=params(24),
+    )(*parts)
 
 
 def stack_kernel(parts, total, rounded):
@@ -327,7 +333,7 @@
     same_core = [[2 * i + c for i in range(chips)] for c in range(2)]
 
     def exchange(value):
-        value = value.reshape(chips, -1, value.shape[1])
+        value = value.reshape(chips, -1, value.shape[-1])
         return lax.all_to_all(value, "loop", 0, 0, axis_index_groups=same_core)
 
     got = lax.ppermute(gradient, "loop", swap)
@@ -357,30 +363,26 @@
     own_a = gather(rows_w[:share])
     rows_b, own_a = tie(rows_w[share:], own_a)
     own_b = gather(rows_b)
-    ring_a = ring(rotate(place, own_a, swapped(own_a), in_basis))
-    own_b, *ring_a = tie(own_b, *ring_a)
-    other_b = swapped(own_b)
+    rot_a = list(rotate(place, own_a, swapped(own_a), in_basis))
+    ring_a = ring(rot_a)
+    own_b, ring_a[2] = tie(own_b, ring_a[2])
+    ring_b = ring(rotate(place, own_b, swapped(own_b), in_basis))
     total_a, rounded_a = ring_sum(ring_a)
+    total_a, *ring_b = tie(total_a, *ring_b)
     far_a = lax.ppermute(rounded_a, "red", flip)
-    other_b, total_a = tie(other_b, total_a)
-    [rot_b] = rotate(place, own_b, other_b, in_basis, stacked=True)
-    rot_b, far_a = tie(rot_b.reshape(RING, piece, -1), far_a)
-    rot_b = lax.all_to_all(rot_b, "red", 0, 0, axis_index_groups=rings)
+    total_b, rounded_b = ring_sum(ring_b)
+    far_a, total_b = tie(far_a, total_b)
     scaled_a = scale(total_a, far_a, factors[0], eigen_cols)
-    rot_b, *pieces_a = tie(rot_b, *ring([scaled_a] * RING))
-    total_b, rounded_b = stack_sum(rot_b)
+    pieces_a = ring([scaled_a] * RING)
     far_b = lax.ppermute(rounded_b, "red", flip)
-    pieces_a[0], total_b = tie(pieces_a[0], total_b)
-    send_a, keep_a = back(place, pieces_a, in_basis)
-    send_a, far_b = tie(send_a, far_b)
-    part_a = join(keep_a, swapped(send_a))
+    far_b, *pieces_a = tie(far_b, *pieces_a)
     scaled_b = scale(total_b, far_b, factors[1], eigen_cols)
     pieces_b = ring([scaled_b] * RING)
-    part_a = exchange(part_a)
-    part_a, *pieces_b = tie(part_a, *pieces_b)
+    send_a, keep_a = back(place, pieces_a, in_basis)
+    pieces_b[0], send_a = tie(pieces_b[0], send_a)
     send_b, keep_b = back(place, pieces_b, in_basis)
-    part_b = exchange(join(keep_b, swapped(send_b)))
-    return jnp.concatenate([add_up(part_a).astype(BF16), add_up(part_b).astype(BF16)], 0)
+    part = join([keep_a, swapped(send_a), keep_b, swapped(send_b)], chips)
+    return add_up(exchange(part)).astype(BF16)
 
 
 def solution(mesh):

time: 197 us -> 186 us (0.944)
  blocking collectives: 16.7 us -> 44.5 us
  waiting for transfers between devices: 75.2 us -> 47.7 us
  starting transfers between devices: 47.5 us -> 36.9 us
  Pallas kernels: 47 us -> 44.9 us
    all_to_all x1 -> x2, blocking collectives: 16.7 us -> 44.5 us  [exchange(): return lax.all_to_all(value, 'loop', 0, 0, axis_index_groups=same_core)]
    ppermute x9 -> x12, waiting for transfers between devices: 36.4 us -> 23.3 us  [ring(): lax.ppermute(parts[d], 'red', shift[d])]
    all_to_all x4 -> x2, waiting for transfers between devices: 33.1 us -> 20.9 us  [exchange(): return lax.all_to_all(value, 'loop', 0, 0, axis_index_groups=same_core)]
    all_to_all x4 -> x2, starting transfers between devices: 19.3 us -> 9.69 us  [exchange(): return lax.all_to_all(value, 'loop', 0, 0, axis_index_groups=same_core)]
    all_to_all x1 -> x0, starting transfers between devices: 3.65 us -> none  [per_device(): rot_b = lax.all_to_all(rot_b, 'red', 0, 0, axis_index_groups=rings)]
    ppermute x9 -> x12, starting transfers between devices: 12.2 us -> 15.5 us  [ring(): lax.ppermute(parts[d], 'red', shift[d])]
    ppermute x4, waiting for transfers between devices: 4.2 us -> 2.1 us  [swapped(): return lax.ppermute(value, 'loop', swap)]
    pallas_call x3 -> x1, Pallas kernels: 2.33 us -> 0.33 us  [join(): pl.pallas_call(join_kernel, in_specs=[VMEM] * len(parts), out_specs=VMEM,...]
  transfers between devices with their start and end apart: 22 -> 22, of which waited for: 15 -> 11; matrix products, arithmetic and copies ran while one was open for 4% -> 4% of each run, Pallas kernels for 16% -> 20%
where the time goes in v8:
time: 186 us; the launch traced here: 185 us
  waiting for transfers between devices  47.7 us (26%)
  Pallas kernels  44.9 us (24%)
  blocking collectives  44.5 us (24%)
  starting transfers between devices  36.9 us (20%)
  local copies, waits for them, and re-layouts  6.25 us (3%)
  other arithmetic  3.54 us (2%)
    all_to_all x2, blocking collectives, exchange(): return lax.all_to_all(value, 'loop', 0, 0, axis_index_groups=same_core)  44.5 us
    ppermute x12, waiting for transfers between devices, ring(): lax.ppermute(parts[d], 'red', shift[d])  23.3 us
    all_to_all x2, waiting for transfers between devices, exchange(): return lax.all_to_all(value, 'loop', 0, 0, axis_index_groups=same_core)  20.9 us
    ppermute x12, starting transfers between devices, ring(): lax.ppermute(parts[d], 'red', shift[d])  15.5 us
    pallas_call x2, Pallas kernels, rotate(): pl.pallas_call(functools.partial(rotate_kernel, cuts=cuts), in_specs=[SME...  15 us
    pallas_call x2, Pallas kernels, back(): pl.pallas_call(functools.partial(back_kernel, cuts=cuts), in_specs=[SMEM]...  14.3 us
    all_to_all x2, starting transfers between devices, exchange(): return lax.all_to_all(value, 'loop', 0, 0, axis_index_groups=same_core)  9.69 us
    pallas_call x1, Pallas kernels, select(): pl.pallas_call(functools.partial(select_kernel, chips=chips), grid=(width...  8.28 us
  transfers between devices with their start and end apart: 22, of which 11 were waited for; matrix products, arithmetic and copies ran while one was open for 4% of the time, Pallas kernels for 20%

profile of v8, /device:TPU:1, one launch (start us, length us, event | category | flops | bytes accessed | tf_op | source)
XLA Modules:
  0.0 184.7 jit_solution(15823383983288576702)
XLA Ops:
  1.4 8.3 %shard_map.73.sel = bf16[512,512]{1,0:T(8,128)(2,1)} custom-call(s32[1,512]{1,0:T(1,128)} %bitcast.29, bf16[512,8192]{1,0:T(8,128)(2,1)} %basis.3), custom_call_target="tpu_custom_call" | custom-call | flops 4294967296 | bytes 8388608 | tf_op jit(solution)/shard_map/pallas_call | solution.py:70
  12.6 6.5 %shard_map.74 = bf16[512,1792]{1,0:T(8,128)(2,1)} custom-call(s32[2]{0:T(128)} %pad_add_fusion.place, bf16[512,512]{1,0:T(8,128)(2,1)} %shard_map.73.sel, bf16[512,512]{1,0:T(8,128)(2,1)} %copy-done.2, bf16[512,3584]{1,0:T(8,128)(2,1)} %grad.1, bf16[512,3584]{1,0:T(8,128)(2,1)} %collective-permute-done.1.grad2), custom_call_target="tpu_custom_call" | custom-call | flops 1879048192 | bytes 5505024 | tf_op jit(solution)/shard_map/pallas_call | solution.py:110
  19.1 6.1 %all-to-all-start = ((bf16[8,64,1792]{2,1,0:T(8,128)(2,1)}), bf16[8,64,1792]{2,1,0:T(8,128)(2,1)S(1)}, u32[]{:S(2)}, u32[]{:S(2)}) async-start(bf16[8,64,1792]{2,1,0:T(8,128)(2,1)} %bitcast.27), calls=%async_computation | async-start | bytes 3670016 | tf_op jit(solution)/shard_map/all_to_all | solution.py:337
  26.9 3.1 %gather_fusion = f32[512]{0:T(512)S(1)} fusion(f32[8192]{0:T(1024)S(1)} %bitcast.26, s32[1024]{0:T(1024)S(1)} %pad_clamp_fusion), kind=kCustom, calls=%fused_computation | custom fusion | bytes 6144 | tf_op jit(solution)/shard_map/jit(_take)/gather | solution.py:344
  30.5 18.2 %all-to-all-done = bf16[8,64,1792]{2,1,0:T(8,128)(2,1)S(1)} async-done(((bf16[8,64,1792]{2,1,0:T(8,128)(2,1)}), bf16[8,64,1792]{2,1,0:T(8,128)(2,1)S(1)}, u32[]{:S(2)}, u32[]{:S(2)}) %all-to-all-start) | async-done | bytes 1835040 | tf_op jit(solution)/shard_map/all_to_all | solution.py:337
  49.0 16.7 %all_to_all.20 = bf16[8,32,1792]{2,1,0:T(8,128)(2,1)S(1)} all-to-all(bf16[8,32,1792]{2,1,0:T(8,128)(2,1)S(1)} %broadcast_in_dim.59), channel_id=1, replica_groups={{0,16,32,48,64,80,96,112},{8,24,40,56,72,88,104,120},{1,17,33,49,65,81,..., dimensions={0} | all-to-all | bytes 1835008 | tf_op jit(solution)/shard_map/all_to_all | solution.py:337
  68.8 3.6 %all-to-all-start.2 = ((bf16[8,32,1792]{2,1,0:T(8,128)(2,1)}), bf16[8,32,1792]{2,1,0:T(8,128)(2,1)S(1)}, u32[]{:S(2)}, u32[]{:S(2)}) async-start(bf16[8,32,1792]{2,1,0:T(8,128)(2,1)} %broadcast_in_dim.60), calls=%async_computation.2 | async-start | bytes 1835008 | tf_op jit(solution)/shard_map/all_to_all | solution.py:337
  72.4 7.4 %shard_map.75 = (f32[64,1792]{1,0:T(8,128)S(1)}, bf16[64,1792]{1,0:T(8,128)(2,1)S(1)}, bf16[64,1792]{1,0:T(8,128)(2,1)}, bf16[64,1792]{1,0:T(8,128)(2,1)S(1)}) custom-call(s32[2]{0:T(128)S(1)} %copy-done, bf16[256,1792]{1,0:T(8,128)(2,1)S(1)} %bitcast.25, bf16[256,1792]{1,0:T(8,128)(2,1)S(1)} %collective-permute-done.2.other, bf16[3584,1792]{1,0:T(8,128)(2,1)} %refs_4_.3), custom_call_target="tpu_custom_call" | custom-call | flops 3288334336 | bytes 12845056 | tf_op jit(solution)/shard_map/pallas_call | solution.py:169
  80.5 2.7 %collective-permute-start.4 = (bf16[64,1792]{1,0:T(8,128)(2,1)}, bf16[64,1792]{1,0:T(8,128)(2,1)S(1)}, u32[]{:S(2)}, u32[]{:S(2)}) collective-permute-start(bf16[64,1792]{1,0:T(8,128)(2,1)} %get-tuple-element.47), channel_id=1, source_target_pairs={{0,2},{1,3},{2,0},{3,1},{4,6},{5,7},{6,4},{7,5},{8,10},{9,11},{10,... | collective-permute-start | bytes 688136 | tf_op jit(solution)/shard_map/ppermute | solution.py:358
  83.2 2.7 %all-to-all-done.2 = bf16[8,32,1792]{2,1,0:T(8,128)(2,1)S(1)} async-done(((bf16[8,32,1792]{2,1,0:T(8,128)(2,1)}), bf16[8,32,1792]{2,1,0:T(8,128)(2,1)S(1)}, u32[]{:S(2)}, u32[]{:S(2)}) %all-to-all-start.2) | async-done | bytes 917536 | tf_op jit(solution)/shard_map/all_to_all | solution.py:337
  85.9 3.5 %collective-permute-done.4.b = bf16[64,1792]{1,0:T(8,128)(2,1)S(1)} collective-permute-done((bf16[64,1792]{1,0:T(8,128)(2,1)}, bf16[64,1792]{1,0:T(8,128)(2,1)S(1)}, u32[]{:S(2)}, u32[]{:S(2)}) %collective-permute-start.4) | collective-permute-done | bytes 229408 | tf_op jit(solution)/shard_map/ppermute | solution.py:358
  92.9 7.6 %shard_map.77 = (f32[64,1792]{1,0:T(8,128)S(1)}, bf16[64,1792]{1,0:T(8,128)(2,1)}, bf16[64,1792]{1,0:T(8,128)(2,1)}, bf16[64,1792]{1,0:T(8,128)(2,1)}) custom-call(s32[2]{0:T(128)S(1)} %copy-done, bf16[256,1792]{1,0:T(8,128)(2,1)S(1)} %bitcast.23, bf16[256,1792]{1,0:T(8,128)(2,1)S(1)} %collective-permute-done.6.other, bf16[3584,1792]{1,0:T(8,128)(2,1)} %refs_4_.3), custom_call_target="tpu_custom_call" | custom-call | flops 3288334336 | bytes 12845056 | tf_op jit(solution)/shard_map/pallas_call | solution.py:169
  101.2 2.5 %collective-permute-start.8 = (bf16[64,1792]{1,0:T(8,128)(2,1)}, bf16[64,1792]{1,0:T(8,128)(2,1)S(1)}, u32[]{:S(2)}, u32[]{:S(2)}) collective-permute-start(bf16[64,1792]{1,0:T(8,128)(2,1)} %get-tuple-element.54), channel_id=1, source_target_pairs={{0,2},{1,3},{2,0},{3,1},{4,6},{5,7},{6,4},{7,5},{8,10},{9,11},{10,... | collective-permute-start | bytes 688136 | tf_op jit(solution)/shard_map/ppermute | solution.py:358
  104.9 2.7 %collective-permute-start.11 = (bf16[64,1792]{1,0:T(8,128)(2,1)S(1)}, bf16[64,1792]{1,0:T(8,128)(2,1)S(1)}, u32[]{:S(2)}, u32[]{:S(2)}) collective-permute-start(bf16[64,1792]{1,0:T(8,128)(2,1)S(1)} %get-tuple-element.62), channel_id=1, source_target_pairs={{0,4},{1,5},{2,6},{3,7},{4,0},{5,1},{6,2},{7,3},{8,12},{9,13},{10,... | collective-permute-start | bytes 688136 | tf_op jit(solution)/shard_map/ppermute | solution.py:372
  108.6 5.5 %collective-permute-done.8.b = bf16[64,1792]{1,0:T(8,128)(2,1)S(1)} collective-permute-done((bf16[64,1792]{1,0:T(8,128)(2,1)}, bf16[64,1792]{1,0:T(8,128)(2,1)S(1)}, u32[]{:S(2)}, u32[]{:S(2)}) %collective-permute-start.8) | collective-permute-done | bytes 229408 | tf_op jit(solution)/shard_map/ppermute | solution.py:358
  114.4 3.3 %collective-permute-start.14 = (bf16[64,1792]{1,0:T(8,128)(2,1)S(1)}, bf16[64,1792]{1,0:T(8,128)(2,1)S(1)}, u32[]{:S(2)}, u32[]{:S(2)}) collective-permute-start(bf16[64,1792]{1,0:T(8,128)(2,1)S(1)} %shard_map.79.refs_0_), channel_id=1, source_target_pairs={{0,3},{1,0},{2,1},{3,2},{4,7},{5,4},{6,5},{7,6},{8,11},{9,8},{10,9... | collective-permute-start | bytes 688136 | tf_op jit(solution)/shard_map/ppermute | solution.py:358
  118.5 2.6 %collective-permute-start.10 = (bf16[64,1792]{1,0:T(8,128)(2,1)S(1)}, bf16[64,1792]{1,0:T(8,128)(2,1)S(1)}, u32[]{:S(2)}, u32[]{:S(2)}) collective-permute-start(bf16[64,1792]{1,0:T(8,128)(2,1)S(1)} %get-tuple-element.60), channel_id=1, source_target_pairs={{0,4},{1,5},{2,6},{3,7},{4,0},{5,1},{6,2},{7,3},{8,12},{9,13},{10,... | collective-permute-start | bytes 688136 | tf_op jit(solution)/shard_map/ppermute | solution.py:377
  123.2 2.5 %collective-permute-done.13.refs_2_ = bf16[64,1792]{1,0:T(8,128)(2,1)S(1)} collective-permute-done((bf16[64,1792]{1,0:T(8,128)(2,1)S(1)}, bf16[64,1792]{1,0:T(8,128)(2,1)S(1)}, u32[]{:S(2)}, u32[]{:S(2)}) %collective-permute-start.13) | collective-permute-done | bytes 229408 | tf_op jit(solution)/shard_map/ppermute | solution.py:358
  125.6 6.0 %collective-permute-done.12.refs_1_ = bf16[64,1792]{1,0:T(8,128)(2,1)S(1)} collective-permute-done((bf16[64,1792]{1,0:T(8,128)(2,1)S(1)}, bf16[64,1792]{1,0:T(8,128)(2,1)S(1)}, u32[]{:S(2)}, u32[]{:S(2)}) %collective-permute-start.12) | collective-permute-done | bytes 229408 | tf_op jit(solution)/shard_map/ppermute | solution.py:358
  133.5 7.1 %shard_map.80 = (bf16[128,3584]{1,0:T(8,128)(2,1)S(1)}, f32[128,3584]{1,0:T(8,128)S(1)}) custom-call(s32[2]{0:T(128)S(1)} %copy-done, bf16[64,1792]{1,0:T(8,128)(2,1)S(1)} %shard_map.79.refs_0_, bf16[64,1792]{1,0:T(8,128)(2,1)S(1)} %collective-permute-done.12.refs_1_, bf16[64,1792]{1,0:T(8,128)(2,1)S(1)} %collective-permute-done.13.refs_2_, ...), custom_call_target="tpu_custom_call" | custom-call | flops 3288334336 | bytes 12845056 | tf_op jit(solution)/shard_map/pallas_call | solution.py:213
  142.3 3.6 %collective-permute-done.16.refs_1_ = bf16[64,1792]{1,0:T(8,128)(2,1)S(1)} collective-permute-done((bf16[64,1792]{1,0:T(8,128)(2,1)S(1)}, bf16[64,1792]{1,0:T(8,128)(2,1)S(1)}, u32[]{:S(2)}, u32[]{:S(2)}) %collective-permute-start.16) | collective-permute-done | bytes 229408 | tf_op jit(solution)/shard_map/ppermute | solution.py:358
  145.9 7.1 %shard_map.82 = (bf16[128,3584]{1,0:T(8,128)(2,1)S(1)}, f32[128,3584]{1,0:T(8,128)S(1)}) custom-call(s32[2]{0:T(128)S(1)} %copy-done, bf16[64,1792]{1,0:T(8,128)(2,1)S(1)} %shard_map.81.refs_0_, bf16[64,1792]{1,0:T(8,128)(2,1)S(1)} %collective-permute-done.16.refs_1_, bf16[64,1792]{1,0:T(8,128)(2,1)S(1)} %collective-permute-done.17.refs_2_, ...), custom_call_target="tpu_custom_call" | custom-call | flops 3288334336 | bytes 12845056 | tf_op jit(solution)/shard_map/pallas_call | solution.py:213
  153.7 2.1 %collective-permute-done.19.refs_3_ = bf16[128,3584]{1,0:T(8,128)(2,1)S(1)} collective-permute-done((bf16[128,3584]{1,0:T(8,128)(2,1)S(1)}, bf16[128,3584]{1,0:T(8,128)(2,1)S(1)}, u32[]{:S(2)}, u32[]{:S(2)}) %collective-permute-start.19) | collective-permute-done | bytes 917536 | tf_op jit(solution)/shard_map/ppermute | solution.py:361
  156.1 27.7 %all_to_all.21 = bf16[8,32,3584]{2,1,0:T(8,128)(2,1)S(1)} all-to-all(bf16[8,32,3584]{2,1,0:T(8,128)(2,1)S(1)} %shard_map.83), channel_id=1, replica_groups={{0,16,32,48,64,80,96,112},{8,24,40,56,72,88,104,120},{1,17,33,49,65,81,..., dimensions={0} | all-to-all | bytes 3670016 | tf_op jit(solution)/shard_map/all_to_all | solution.py:337
  (62 shorter events, 24.4 us)
Async XLA Ops:
  0.0 11.8 %collective-permute-start.1 = (bf16[512,3584]{1,0:T(8,128)(2,1)}, bf16[512,3584]{1,0:T(8,128)(2,1)}, u32[]{:S(2)}, u32[]{:S(2)}) collective-permute-start(bf16[512,3584]{1,0:T(8,128)(2,1)} %grad.1), channel_id=1, source_target_pairs={{0,8},{8,0},{16,24},{24,16},{32,40},{40,32},{48,56},{56,48},{64,72... | collective-permute-start | bytes 11010056 | tf_op jit(solution)/shard_map/ppermute | solution.py:339
  9.7 2.1 %collective-permute-start = (bf16[512,512]{1,0:T(8,128)(2,1)}, bf16[512,512]{1,0:T(8,128)(2,1)S(1)}, u32[]{:S(2)}, u32[]{:S(2)}) collective-permute-start(bf16[512,512]{1,0:T(8,128)(2,1)} %shard_map.73.sel), channel_id=1, source_target_pairs={{0,8},{8,0},{16,24},{24,16},{32,40},{40,32},{48,56},{56,48},{64,72... | collective-permute-start | bytes 1572872 | tf_op jit(solution)/shard_map/ppermute | solution.py:341
  19.1 6.2 %copy-start.3 = (s32[512]{0:T(512)S(1)}, s32[512]{0:T(512)}, u32[]{:S(2)}) copy-start(s32[512]{0:T(512)} %param.7) | copy-start | bytes 6148
  19.1 29.6 %all-to-all-start = ((bf16[8,64,1792]{2,1,0:T(8,128)(2,1)}), bf16[8,64,1792]{2,1,0:T(8,128)(2,1)S(1)}, u32[]{:S(2)}, u32[]{:S(2)}) async-start(bf16[8,64,1792]{2,1,0:T(8,128)(2,1)} %bitcast.27), calls=%async_computation | async-start | bytes 3670016 | tf_op jit(solution)/shard_map/all_to_all | solution.py:337
  65.8 6.6 %copy-start = (s32[2]{0:T(128)S(1)}, s32[2]{0:T(128)}, u32[]{:S(2)}) copy-start(s32[2]{0:T(128)} %pad_add_fusion.place) | copy-start | bytes 28
  65.8 6.6 %collective-permute-start.2 = (bf16[256,1792]{1,0:T(8,128)(2,1)S(1)}, bf16[256,1792]{1,0:T(8,128)(2,1)S(1)}, u32[]{:S(2)}, u32[]{:S(2)}) collective-permute-start(bf16[256,1792]{1,0:T(8,128)(2,1)S(1)} %bitcast.24), channel_id=1, source_target_pairs={{0,8},{8,0},{16,24},{24,16},{32,40},{40,32},{48,56},{56,48},{64,72... | collective-permute-start | bytes 2752520 | tf_op jit(solution)/shard_map/ppermute | solution.py:361
  68.8 17.1 %all-to-all-start.2 = ((bf16[8,32,1792]{2,1,0:T(8,128)(2,1)}), bf16[8,32,1792]{2,1,0:T(8,128)(2,1)S(1)}, u32[]{:S(2)}, u32[]{:S(2)}) async-start(bf16[8,32,1792]{2,1,0:T(8,128)(2,1)} %broadcast_in_dim.60), calls=%async_computation.2 | async-start | bytes 1835008 | tf_op jit(solution)/shard_map/all_to_all | solution.py:337
  80.5 9.0 %collective-permute-start.4 = (bf16[64,1792]{1,0:T(8,128)(2,1)}, bf16[64,1792]{1,0:T(8,128)(2,1)S(1)}, u32[]{:S(2)}, u32[]{:S(2)}) collective-permute-start(bf16[64,1792]{1,0:T(8,128)(2,1)} %get-tuple-element.47), channel_id=1, source_target_pairs={{0,2},{1,3},{2,0},{3,1},{4,6},{5,7},{6,4},{7,5},{8,10},{9,11},{10,... | collective-permute-start | bytes 688136 | tf_op jit(solution)/shard_map/ppermute | solution.py:358
  89.4 3.5 %collective-permute-start.6 = (bf16[256,1792]{1,0:T(8,128)(2,1)S(1)}, bf16[256,1792]{1,0:T(8,128)(2,1)S(1)}, u32[]{:S(2)}, u32[]{:S(2)}) collective-permute-start(bf16[256,1792]{1,0:T(8,128)(2,1)S(1)} %bitcast.22), channel_id=1, source_target_pairs={{0,8},{8,0},{16,24},{24,16},{32,40},{40,32},{48,56},{56,48},{64,72... | collective-permute-start | bytes 2752520 | tf_op jit(solution)/shard_map/ppermute | solution.py:361
  90.2 14.6 %collective-permute-start.3 = (bf16[64,1792]{1,0:T(8,128)(2,1)}, bf16[64,1792]{1,0:T(8,128)(2,1)S(1)}, u32[]{:S(2)}, u32[]{:S(2)}) collective-permute-start(bf16[64,1792]{1,0:T(8,128)(2,1)} %copy-done.1), channel_id=1, source_target_pairs={{0,1},{1,2},{2,3},{3,0},{4,5},{5,6},{6,7},{7,4},{8,9},{9,10},{10,1... | collective-permute-start | bytes 688136 | tf_op jit(solution)/shard_map/ppermute | solution.py:358
  91.4 13.4 %collective-permute-start.5 = (bf16[64,1792]{1,0:T(8,128)(2,1)S(1)}, bf16[64,1792]{1,0:T(8,128)(2,1)S(1)}, u32[]{:S(2)}, u32[]{:S(2)}) collective-permute-start(bf16[64,1792]{1,0:T(8,128)(2,1)S(1)} %get-tuple-element.49), channel_id=1, source_target_pairs={{0,3},{1,0},{2,1},{3,2},{4,7},{5,4},{6,5},{7,6},{8,11},{9,8},{10,9... | collective-permute-start | bytes 688136 | tf_op jit(solution)/shard_map/ppermute | solution.py:358
  100.5 8.1 %collective-permute-start.7 = (bf16[64,1792]{1,0:T(8,128)(2,1)}, bf16[64,1792]{1,0:T(8,128)(2,1)S(1)}, u32[]{:S(2)}, u32[]{:S(2)}) collective-permute-start(bf16[64,1792]{1,0:T(8,128)(2,1)} %get-tuple-element.53), channel_id=1, source_target_pairs={{0,1},{1,2},{2,3},{3,0},{4,5},{5,6},{6,7},{7,4},{8,9},{9,10},{10,1... | collective-permute-start | bytes 688136 | tf_op jit(solution)/shard_map/ppermute | solution.py:358
  101.2 12.9 %collective-permute-start.8 = (bf16[64,1792]{1,0:T(8,128)(2,1)}, bf16[64,1792]{1,0:T(8,128)(2,1)S(1)}, u32[]{:S(2)}, u32[]{:S(2)}) collective-permute-start(bf16[64,1792]{1,0:T(8,128)(2,1)} %get-tuple-element.54), channel_id=1, source_target_pairs={{0,2},{1,3},{2,0},{3,1},{4,6},{5,7},{6,4},{7,5},{8,10},{9,11},{10,... | collective-permute-start | bytes 688136 | tf_op jit(solution)/shard_map/ppermute | solution.py:358
  103.6 10.5 %collective-permute-start.9 = (bf16[64,1792]{1,0:T(8,128)(2,1)}, bf16[64,1792]{1,0:T(8,128)(2,1)S(1)}, u32[]{:S(2)}, u32[]{:S(2)}) collective-permute-start(bf16[64,1792]{1,0:T(8,128)(2,1)} %get-tuple-element.55), channel_id=1, source_target_pairs={{0,3},{1,0},{2,1},{3,2},{4,7},{5,4},{6,5},{7,6},{8,11},{9,8},{10,9... | collective-permute-start | bytes 688136 | tf_op jit(solution)/shard_map/ppermute | solution.py:358
  104.9 9.3 %collective-permute-start.11 = (bf16[64,1792]{1,0:T(8,128)(2,1)S(1)}, bf16[64,1792]{1,0:T(8,128)(2,1)S(1)}, u32[]{:S(2)}, u32[]{:S(2)}) collective-permute-start(bf16[64,1792]{1,0:T(8,128)(2,1)S(1)} %get-tuple-element.62), channel_id=1, source_target_pairs={{0,4},{1,5},{2,6},{3,7},{4,0},{5,1},{6,2},{7,3},{8,12},{9,13},{10,... | collective-permute-start | bytes 688136 | tf_op jit(solution)/shard_map/ppermute | solution.py:372
  114.4 8.8 %collective-permute-start.14 = (bf16[64,1792]{1,0:T(8,128)(2,1)S(1)}, bf16[64,1792]{1,0:T(8,128)(2,1)S(1)}, u32[]{:S(2)}, u32[]{:S(2)}) collective-permute-start(bf16[64,1792]{1,0:T(8,128)(2,1)S(1)} %shard_map.79.refs_0_), channel_id=1, source_target_pairs={{0,3},{1,0},{2,1},{3,2},{4,7},{5,4},{6,5},{7,6},{8,11},{9,8},{10,9... | collective-permute-start | bytes 688136 | tf_op jit(solution)/shard_map/ppermute | solution.py:358
  117.7 7.9 %collective-permute-start.13 = (bf16[64,1792]{1,0:T(8,128)(2,1)S(1)}, bf16[64,1792]{1,0:T(8,128)(2,1)S(1)}, u32[]{:S(2)}, u32[]{:S(2)}) collective-permute-start(bf16[64,1792]{1,0:T(8,128)(2,1)S(1)} %shard_map.79.refs_0_), channel_id=1, source_target_pairs={{0,2},{1,3},{2,0},{3,1},{4,6},{5,7},{6,4},{7,5},{8,10},{9,11},{10,... | collective-permute-start | bytes 688136 | tf_op jit(solution)/shard_map/ppermute | solution.py:358
  118.5 13.2 %collective-permute-start.12 = (bf16[64,1792]{1,0:T(8,128)(2,1)S(1)}, bf16[64,1792]{1,0:T(8,128)(2,1)S(1)}, u32[]{:S(2)}, u32[]{:S(2)}) collective-permute-start(bf16[64,1792]{1,0:T(8,128)(2,1)S(1)} %shard_map.79.refs_0_), channel_id=1, source_target_pairs={{0,1},{1,2},{2,3},{3,0},{4,5},{5,6},{6,7},{7,4},{8,9},{9,10},{10,1... | collective-permute-start | bytes 688136 | tf_op jit(solution)/shard_map/ppermute | solution.py:358
  118.5 13.2 %collective-permute-start.10 = (bf16[64,1792]{1,0:T(8,128)(2,1)S(1)}, bf16[64,1792]{1,0:T(8,128)(2,1)S(1)}, u32[]{:S(2)}, u32[]{:S(2)}) collective-permute-start(bf16[64,1792]{1,0:T(8,128)(2,1)S(1)} %get-tuple-element.60), channel_id=1, source_target_pairs={{0,4},{1,5},{2,6},{3,7},{4,0},{5,1},{6,2},{7,3},{8,12},{9,13},{10,... | collective-permute-start | bytes 688136 | tf_op jit(solution)/shard_map/ppermute | solution.py:377
  131.8 10.5 %collective-permute-start.18 = (bf16[64,1792]{1,0:T(8,128)(2,1)S(1)}, bf16[64,1792]{1,0:T(8,128)(2,1)S(1)}, u32[]{:S(2)}, u32[]{:S(2)}) collective-permute-start(bf16[64,1792]{1,0:T(8,128)(2,1)S(1)} %shard_map.81.refs_0_), channel_id=1, source_target_pairs={{0,3},{1,0},{2,1},{3,2},{4,7},{5,4},{6,5},{7,6},{8,11},{9,8},{10,9... | collective-permute-start | bytes 688136 | tf_op jit(solution)/shard_map/ppermute | solution.py:358
  131.9 10.4 %collective-permute-start.17 = (bf16[64,1792]{1,0:T(8,128)(2,1)S(1)}, bf16[64,1792]{1,0:T(8,128)(2,1)S(1)}, u32[]{:S(2)}, u32[]{:S(2)}) collective-permute-start(bf16[64,1792]{1,0:T(8,128)(2,1)S(1)} %shard_map.81.refs_0_), channel_id=1, source_target_pairs={{0,2},{1,3},{2,0},{3,1},{4,6},{5,7},{6,4},{7,5},{8,10},{9,11},{10,... | collective-permute-start | bytes 688136 | tf_op jit(solution)/shard_map/ppermute | solution.py:358
  132.8 13.2 %collective-permute-start.16 = (bf16[64,1792]{1,0:T(8,128)(2,1)S(1)}, bf16[64,1792]{1,0:T(8,128)(2,1)S(1)}, u32[]{:S(2)}, u32[]{:S(2)}) collective-permute-start(bf16[64,1792]{1,0:T(8,128)(2,1)S(1)} %shard_map.81.refs_0_), channel_id=1, source_target_pairs={{0,1},{1,2},{2,3},{3,0},{4,5},{5,6},{6,7},{7,4},{8,9},{9,10},{10,1... | collective-permute-start | bytes 688136 | tf_op jit(solution)/shard_map/ppermute | solution.py:358
  140.7 13.0 %collective-permute-start.15 = (bf16[128,3584]{1,0:T(8,128)(2,1)S(1)}, bf16[128,3584]{1,0:T(8,128)(2,1)S(1)}, u32[]{:S(2)}, u32[]{:S(2)}) collective-permute-start(bf16[128,3584]{1,0:T(8,128)(2,1)S(1)} %get-tuple-element.75), channel_id=1, source_target_pairs={{0,8},{8,0},{16,24},{24,16},{32,40},{40,32},{48,56},{56,48},{64,72... | collective-permute-start | bytes 2752520 | tf_op jit(solution)/shard_map/ppermute | solution.py:361
  153.1 2.7 %collective-permute-start.19 = (bf16[128,3584]{1,0:T(8,128)(2,1)S(1)}, bf16[128,3584]{1,0:T(8,128)(2,1)S(1)}, u32[]{:S(2)}, u32[]{:S(2)}) collective-permute-start(bf16[128,3584]{1,0:T(8,128)(2,1)S(1)} %get-tuple-element.78), channel_id=1, source_target_pairs={{0,8},{8,0},{16,24},{24,16},{32,40},{40,32},{48,56},{56,48},{64,72... | collective-permute-start | bytes 2752520 | tf_op jit(solution)/shard_map/ppermute | solution.py:361
  (2 other events, 1.5 us)

commit v9 on v8

--- a/solution.py
+++ b/solution.py
@@ -104,7 +104,7 @@
         out[:, to] = total.astype(BF16)
 
 
-def partial_rows(place, sel, sel2, grad, grad2, steps=2):
+def partial_rows(place, sel, sel2, grad, grad2, steps=7):
     queries, units = sel.shape
     half = grad.shape[1] // 2
     return pl.pallas_call(
@@ -323,6 +323,7 @@
     queries = query_ids.shape[0]
     chunk = queries // CHUNKS
     piece = chunk // RING
+    half = gradient.shape[1] // 2
     core = lax.axis_index("loop") % 2
     x = lax.axis_index("red") % RING
     place = jnp.stack([core, x]).astype(jnp.int32)
@@ -350,9 +351,8 @@
     rows_w, *factors = tie(add_up(part).astype(BF16), *factors)
     share = rows_w.shape[0] // CHUNKS
 
-    def gather(rows):
-        rows = jnp.broadcast_to(rows[None], (chips,) + rows.shape).reshape(chunk, -1)
-        return exchange(rows).reshape(chunk, -1)
+    def copied(rows):
+        return jnp.broadcast_to(rows[None], (chips,) + rows.shape).reshape(chunk, half)
 
     def ring(parts):
         return [parts[0]] + [lax.ppermute(parts[d], "red", shift[d]) for d in range(1, RING)]
@@ -360,12 +360,12 @@
     def swapped(value):
         return lax.ppermute(value, "loop", swap)
 
-    own_a = gather(rows_w[:share])
-    rows_b, own_a = tie(rows_w[share:], own_a)
-    own_b = gather(rows_b)
+    own_a = exchange(copied(rows_w[:share])).reshape(chunk, half)
+    rows_b, own_a = tie(copied(rows_w[share:]), own_a)
+    own_b = exchange(rows_b).reshape(chunk, half)
     rot_a = list(rotate(place, own_a, swapped(own_a), in_basis))
+    own_b, rot_a[0] = tie(own_b, rot_a[0])
     ring_a = ring(rot_a)
-    own_b, ring_a[2] = tie(own_b, ring_a[2])
     ring_b = ring(rotate(place, own_b, swapped(own_b), in_basis))
     total_a, rounded_a = ring_sum(ring_a)
     total_a, *ring_b = tie(total_a, *ring_b)
@@ -375,7 +375,6 @@
     scaled_a = scale(total_a, far_a, factors[0], eigen_cols)
     pieces_a = ring([scaled_a] * RING)
     far_b = lax.ppermute(rounded_b, "red", flip)
-    far_b, *pieces_a = tie(far_b, *pieces_a)
     scaled_b = scale(total_b, far_b, factors[1], eigen_cols)
     pieces_b = ring([scaled_b] * RING)
     send_a, keep_a = back(place, pieces_a, in_basis)

time: 186 us -> 182 us (0.978)
  waiting for transfers between devices: 47.7 us -> 43.9 us
  blocking collectives: 44.5 us -> 42.3 us
    ppermute x12, waiting for transfers between devices: 23.3 us -> 16.4 us  [ring(): lax.ppermute(parts[d], 'red', shift[d])]
    all_to_all x2, waiting for transfers between devices: 20.9 us -> 23.6 us  [exchange(): return lax.all_to_all(value, 'loop', 0, 0, axis_index_groups=same_core)]
    all_to_all x2, blocking collectives: 44.5 us -> 42.3 us  [exchange(): return lax.all_to_all(value, 'loop', 0, 0, axis_index_groups=same_core)]
  transfers between devices with their start and end apart: 22 -> 22, of which waited for: 11 -> 9; matrix products, arithmetic and copies ran while one was open for 4% -> 3% of each run, Pallas kernels for 20% -> 21%
where the time goes in v9:
time: 182 us; the launch traced here: 181 us
  Pallas kernels  45.9 us (25%)
  waiting for transfers between devices  43.9 us (24%)
  blocking collectives  42.3 us (23%)
  starting transfers between devices  37.2 us (20%)
  local copies, waits for them, and re-layouts  6.93 us (4%)
  other arithmetic  3.49 us (2%)
    all_to_all x2, blocking collectives, exchange(): return lax.all_to_all(value, 'loop', 0, 0, axis_index_groups=same_core)  42.3 us
    all_to_all x2, waiting for transfers between devices, exchange(): return lax.all_to_all(value, 'loop', 0, 0, axis_index_groups=same_core)  23.6 us
    ppermute x12, starting transfers between devices, ring(): lax.ppermute(parts[d], 'red', shift[d])  16.4 us
    ppermute x12, waiting for transfers between devices, ring(): lax.ppermute(parts[d], 'red', shift[d])  16.4 us
    pallas_call x2, Pallas kernels, back(): pl.pallas_call(functools.partial(back_kernel, cuts=cuts), in_specs=[SMEM]...  14.3 us
    pallas_call x2, Pallas kernels, rotate(): pl.pallas_call(functools.partial(rotate_kernel, cuts=cuts), in_specs=[SME...  14.3 us
    all_to_all x2, starting transfers between devices, exchange(): return lax.all_to_all(value, 'loop', 0, 0, axis_index_groups=same_core)  9.69 us
    pallas_call x1, Pallas kernels, select(): pl.pallas_call(functools.partial(select_kernel, chips=chips), grid=(width...  8.29 us
  transfers between devices with their start and end apart: 22, of which 9 were waited for; matrix products, arithmetic and copies ran while one was open for 3% of the time, Pallas kernels for 21%

profile of v9, /device:TPU:1, one launch (start us, length us, event | category | flops | bytes accessed | tf_op | source)
XLA Modules:
  0.0 180.6 jit_solution(11469361627629384245)
XLA Ops:
  1.4 8.3 %shard_map.73.sel = bf16[512,512]{1,0:T(8,128)(2,1)} custom-call(s32[1,512]{1,0:T(1,128)} %bitcast.31, bf16[512,8192]{1,0:T(8,128)(2,1)} %basis.3), custom_call_target="tpu_custom_call" | custom-call | flops 4294967296 | bytes 8388608 | tf_op jit(solution)/shard_map/pallas_call | solution.py:70
  10.3 1.5 collective-permute-done.sel2
  12.6 8.2 %shard_map.74 = bf16[512,1792]{1,0:T(8,128)(2,1)} custom-call(s32[2]{0:T(128)} %pad_add_fusion.place, bf16[512,512]{1,0:T(8,128)(2,1)} %shard_map.73.sel, bf16[512,512]{1,0:T(8,128)(2,1)} %copy-done.3, bf16[512,3584]{1,0:T(8,128)(2,1)} %grad.1, bf16[512,3584]{1,0:T(8,128)(2,1)} %collective-permute-done.1.grad2), custom_call_target="tpu_custom_call" | custom-call | flops 1879048192 | bytes 5505024 | tf_op jit(solution)/shard_map/pallas_call | solution.py:110
  20.9 6.1 %all-to-all-start = ((bf16[8,64,1792]{2,1,0:T(8,128)(2,1)}), bf16[8,64,1792]{2,1,0:T(8,128)(2,1)S(1)}, u32[]{:S(2)}, u32[]{:S(2)}) async-start(bf16[8,64,1792]{2,1,0:T(8,128)(2,1)} %bitcast.29), calls=%async_computation | async-start | bytes 3670016 | tf_op jit(solution)/shard_map/all_to_all | solution.py:338
  28.7 3.1 %gather_fusion = f32[512]{0:T(512)S(1)} fusion(f32[8192]{0:T(1024)S(1)} %bitcast.28, s32[1024]{0:T(1024)S(1)} %pad_clamp_fusion), kind=kCustom, calls=%fused_computation | custom fusion | bytes 6144 | tf_op jit(solution)/shard_map/jit(_take)/gather | solution.py:345
  32.2 18.2 %all-to-all-done = bf16[8,64,1792]{2,1,0:T(8,128)(2,1)S(1)} async-done(((bf16[8,64,1792]{2,1,0:T(8,128)(2,1)}), bf16[8,64,1792]{2,1,0:T(8,128)(2,1)S(1)}, u32[]{:S(2)}, u32[]{:S(2)}) %all-to-all-start) | async-done | bytes 1835040 | tf_op jit(solution)/shard_map/all_to_all | solution.py:338
  50.8 16.7 %all_to_all.20 = bf16[8,32,1792]{2,1,0:T(8,128)(2,1)S(1)} all-to-all(bf16[8,32,1792]{2,1,0:T(8,128)(2,1)S(1)} %broadcast_in_dim.60), channel_id=1, replica_groups={{0,16,32,48,64,80,96,112},{8,24,40,56,72,88,104,120},{1,17,33,49,65,81,..., dimensions={0} | all-to-all | bytes 1835008 | tf_op jit(solution)/shard_map/all_to_all | solution.py:338
  68.5 2.0 %collective-permute-start.2 = (bf16[256,1792]{1,0:T(8,128)(2,1)S(1)}, bf16[256,1792]{1,0:T(8,128)(2,1)S(1)}, u32[]{:S(2)}, u32[]{:S(2)}) collective-permute-start(bf16[256,1792]{1,0:T(8,128)(2,1)S(1)} %bitcast.26), channel_id=1, source_target_pairs={{0,8},{8,0},{16,24},{24,16},{32,40},{40,32},{48,56},{56,48},{64,72... | collective-permute-start | bytes 2752520 | tf_op jit(solution)/shard_map/ppermute | solution.py:361
  70.5 3.6 %all-to-all-start.2 = ((bf16[8,32,1792]{2,1,0:T(8,128)(2,1)}), bf16[8,32,1792]{2,1,0:T(8,128)(2,1)S(1)}, u32[]{:S(2)}, u32[]{:S(2)}) async-start(bf16[8,32,1792]{2,1,0:T(8,128)(2,1)} %broadcast_in_dim.59), calls=%async_computation.2 | async-start | bytes 1835008 | tf_op jit(solution)/shard_map/all_to_all | solution.py:338
  74.1 6.8 %shard_map.75 = (f32[64,1792]{1,0:T(8,128)S(1)}, bf16[64,1792]{1,0:T(8,128)(2,1)S(1)}, bf16[64,1792]{1,0:T(8,128)(2,1)S(1)}, bf16[64,1792]{1,0:T(8,128)(2,1)S(1)}) custom-call(s32[2]{0:T(128)S(1)} %copy-done, bf16[256,1792]{1,0:T(8,128)(2,1)S(1)} %bitcast.27, bf16[256,1792]{1,0:T(8,128)(2,1)S(1)} %collective-permute-done.2.other, bf16[3584,1792]{1,0:T(8,128)(2,1)} %refs_4_.3), custom_call_target="tpu_custom_call" | custom-call | flops 3288334336 | bytes 12845056 | tf_op jit(solution)/shard_map/pallas_call | solution.py:169
  82.2 5.4 %all-to-all-done.2 = bf16[8,32,1792]{2,1,0:T(8,128)(2,1)S(1)} async-done(((bf16[8,32,1792]{2,1,0:T(8,128)(2,1)}), bf16[8,32,1792]{2,1,0:T(8,128)(2,1)S(1)}, u32[]{:S(2)}, u32[]{:S(2)}) %all-to-all-start.2) | async-done | bytes 917536 | tf_op jit(solution)/shard_map/all_to_all | solution.py:338
  89.6 2.4 %collective-permute-start.4 = (bf16[64,1792]{1,0:T(8,128)(2,1)}, bf16[64,1792]{1,0:T(8,128)(2,1)S(1)}, u32[]{:S(2)}, u32[]{:S(2)}) collective-permute-start(bf16[64,1792]{1,0:T(8,128)(2,1)} %copy-done.1), channel_id=1, source_target_pairs={{0,2},{1,3},{2,0},{3,1},{4,6},{5,7},{6,4},{7,5},{8,10},{9,11},{10,... | collective-permute-start | bytes 688136 | tf_op jit(solution)/shard_map/ppermute | solution.py:358
  93.2 7.5 %shard_map.77 = (f32[64,1792]{1,0:T(8,128)S(1)}, bf16[64,1792]{1,0:T(8,128)(2,1)}, bf16[64,1792]{1,0:T(8,128)(2,1)}, bf16[64,1792]{1,0:T(8,128)(2,1)S(1)}) custom-call(s32[2]{0:T(128)S(1)} %copy-done, bf16[256,1792]{1,0:T(8,128)(2,1)S(1)} %bitcast.25, bf16[256,1792]{1,0:T(8,128)(2,1)S(1)} %collective-permute-done.6.other, bf16[3584,1792]{1,0:T(8,128)(2,1)} %refs_4_.3), custom_call_target="tpu_custom_call" | custom-call | flops 3288334336 | bytes 12845056 | tf_op jit(solution)/shard_map/pallas_call | solution.py:169
  101.9 1.6 collective-permute-start.9
  103.7 2.7 %collective-permute-start.10 = (bf16[64,1792]{1,0:T(8,128)(2,1)S(1)}, bf16[64,1792]{1,0:T(8,128)(2,1)S(1)}, u32[]{:S(2)}, u32[]{:S(2)}) collective-permute-start(bf16[64,1792]{1,0:T(8,128)(2,1)S(1)} %get-tuple-element.52), channel_id=1, source_target_pairs={{0,4},{1,5},{2,6},{3,7},{4,0},{5,1},{6,2},{7,3},{8,12},{9,13},{10,... | collective-permute-start | bytes 688136 | tf_op jit(solution)/shard_map/ppermute | solution.py:372
  107.2 6.1 %collective-permute-done.7.a = bf16[64,1792]{1,0:T(8,128)(2,1)S(1)} collective-permute-done((bf16[64,1792]{1,0:T(8,128)(2,1)}, bf16[64,1792]{1,0:T(8,128)(2,1)S(1)}, u32[]{:S(2)}, u32[]{:S(2)}) %collective-permute-start.7) | collective-permute-done | bytes 229408 | tf_op jit(solution)/shard_map/ppermute | solution.py:358
  113.8 2.7 %collective-permute-start.14 = (bf16[64,1792]{1,0:T(8,128)(2,1)S(1)}, bf16[64,1792]{1,0:T(8,128)(2,1)S(1)}, u32[]{:S(2)}, u32[]{:S(2)}) collective-permute-start(bf16[64,1792]{1,0:T(8,128)(2,1)S(1)} %get-tuple-element.62), channel_id=1, source_target_pairs={{0,4},{1,5},{2,6},{3,7},{4,0},{5,1},{6,2},{7,3},{8,12},{9,13},{10,... | collective-permute-start | bytes 688136 | tf_op jit(solution)/shard_map/ppermute | solution.py:377
  116.7 3.1 %collective-permute-start.13 = (bf16[64,1792]{1,0:T(8,128)(2,1)S(1)}, bf16[64,1792]{1,0:T(8,128)(2,1)S(1)}, u32[]{:S(2)}, u32[]{:S(2)}) collective-permute-start(bf16[64,1792]{1,0:T(8,128)(2,1)S(1)} %shard_map.79.refs_0_), channel_id=1, source_target_pairs={{0,3},{1,0},{2,1},{3,2},{4,7},{5,4},{6,5},{7,6},{8,11},{9,8},{10,9... | collective-permute-start | bytes 688136 | tf_op jit(solution)/shard_map/ppermute | solution.py:358
  120.7 4.1 %collective-permute-start.18 = (bf16[64,1792]{1,0:T(8,128)(2,1)S(1)}, bf16[64,1792]{1,0:T(8,128)(2,1)S(1)}, u32[]{:S(2)}, u32[]{:S(2)}) collective-permute-start(bf16[64,1792]{1,0:T(8,128)(2,1)S(1)} %shard_map.81.refs_0_), channel_id=1, source_target_pairs={{0,3},{1,0},{2,1},{3,2},{4,7},{5,4},{6,5},{7,6},{8,11},{9,8},{10,9... | collective-permute-start | bytes 688136 | tf_op jit(solution)/shard_map/ppermute | solution.py:358
  127.0 8.6 %collective-permute-done.11.refs_1_ = bf16[64,1792]{1,0:T(8,128)(2,1)S(1)} collective-permute-done((bf16[64,1792]{1,0:T(8,128)(2,1)S(1)}, bf16[64,1792]{1,0:T(8,128)(2,1)S(1)}, u32[]{:S(2)}, u32[]{:S(2)}) %collective-permute-start.11) | collective-permute-done | bytes 229408 | tf_op jit(solution)/shard_map/ppermute | solution.py:358
  135.6 7.1 %shard_map.80 = (bf16[128,3584]{1,0:T(8,128)(2,1)S(1)}, f32[128,3584]{1,0:T(8,128)S(1)}) custom-call(s32[2]{0:T(128)S(1)} %copy-done, bf16[64,1792]{1,0:T(8,128)(2,1)S(1)} %shard_map.79.refs_0_, bf16[64,1792]{1,0:T(8,128)(2,1)S(1)} %collective-permute-done.11.refs_1_, bf16[64,1792]{1,0:T(8,128)(2,1)S(1)} %collective-permute-done.12.refs_2_, ...), custom_call_target="tpu_custom_call" | custom-call | flops 3288334336 | bytes 12845056 | tf_op jit(solution)/shard_map/pallas_call | solution.py:213
  144.2 7.1 %shard_map.82 = (bf16[128,3584]{1,0:T(8,128)(2,1)S(1)}, f32[128,3584]{1,0:T(8,128)S(1)}) custom-call(s32[2]{0:T(128)S(1)} %copy-done, bf16[64,1792]{1,0:T(8,128)(2,1)S(1)} %shard_map.81.refs_0_, bf16[64,1792]{1,0:T(8,128)(2,1)S(1)} %collective-permute-done.16.refs_1_, bf16[64,1792]{1,0:T(8,128)(2,1)S(1)} %collective-permute-done.17.refs_2_, ...), custom_call_target="tpu_custom_call" | custom-call | flops 3288334336 | bytes 12845056 | tf_op jit(solution)/shard_map/pallas_call | solution.py:213
  151.5 2.4 %collective-permute-done.19.refs_3_ = bf16[128,3584]{1,0:T(8,128)(2,1)S(1)} collective-permute-done((bf16[128,3584]{1,0:T(8,128)(2,1)S(1)}, bf16[128,3584]{1,0:T(8,128)(2,1)S(1)}, u32[]{:S(2)}, u32[]{:S(2)}) %collective-permute-start.19) | collective-permute-done | bytes 917536 | tf_op jit(solution)/shard_map/ppermute | solution.py:361
  154.2 25.5 %all_to_all.21 = bf16[8,32,3584]{2,1,0:T(8,128)(2,1)S(1)} all-to-all(bf16[8,32,3584]{2,1,0:T(8,128)(2,1)S(1)} %shard_map.83), channel_id=1, replica_groups={{0,16,32,48,64,80,96,112},{8,24,40,56,72,88,104,120},{1,17,33,49,65,81,..., dimensions={0} | all-to-all | bytes 3670016 | tf_op jit(solution)/shard_map/all_to_all | solution.py:338
  (64 shorter events, 18.7 us)
Async XLA Ops:
  0.0 11.8 %collective-permute-start.1 = (bf16[512,3584]{1,0:T(8,128)(2,1)}, bf16[512,3584]{1,0:T(8,128)(2,1)}, u32[]{:S(2)}, u32[]{:S(2)}) collective-permute-start(bf16[512,3584]{1,0:T(8,128)(2,1)} %grad.1), channel_id=1, source_target_pairs={{0,8},{8,0},{16,24},{24,16},{32,40},{40,32},{48,56},{56,48},{64,72... | collective-permute-start | bytes 11010056 | tf_op jit(solution)/shard_map/ppermute | solution.py:340
  9.7 2.1 %collective-permute-start = (bf16[512,512]{1,0:T(8,128)(2,1)}, bf16[512,512]{1,0:T(8,128)(2,1)S(1)}, u32[]{:S(2)}, u32[]{:S(2)}) collective-permute-start(bf16[512,512]{1,0:T(8,128)(2,1)} %shard_map.73.sel), channel_id=1, source_target_pairs={{0,8},{8,0},{16,24},{24,16},{32,40},{40,32},{48,56},{56,48},{64,72... | collective-permute-start | bytes 1572872 | tf_op jit(solution)/shard_map/ppermute | solution.py:342
  20.9 6.2 %copy-start.4 = (s32[512]{0:T(512)S(1)}, s32[512]{0:T(512)}, u32[]{:S(2)}) copy-start(s32[512]{0:T(512)} %param.7) | copy-start | bytes 6148
  20.9 29.6 %all-to-all-start = ((bf16[8,64,1792]{2,1,0:T(8,128)(2,1)}), bf16[8,64,1792]{2,1,0:T(8,128)(2,1)S(1)}, u32[]{:S(2)}, u32[]{:S(2)}) async-start(bf16[8,64,1792]{2,1,0:T(8,128)(2,1)} %bitcast.29), calls=%async_computation | async-start | bytes 3670016 | tf_op jit(solution)/shard_map/all_to_all | solution.py:338
  67.5 6.6 %copy-start = (s32[2]{0:T(128)S(1)}, s32[2]{0:T(128)}, u32[]{:S(2)}) copy-start(s32[2]{0:T(128)} %pad_add_fusion.place) | copy-start | bytes 28
  68.5 5.6 %collective-permute-start.2 = (bf16[256,1792]{1,0:T(8,128)(2,1)S(1)}, bf16[256,1792]{1,0:T(8,128)(2,1)S(1)}, u32[]{:S(2)}, u32[]{:S(2)}) collective-permute-start(bf16[256,1792]{1,0:T(8,128)(2,1)S(1)} %bitcast.26), channel_id=1, source_target_pairs={{0,8},{8,0},{16,24},{24,16},{32,40},{40,32},{48,56},{56,48},{64,72... | collective-permute-start | bytes 2752520 | tf_op jit(solution)/shard_map/ppermute | solution.py:361
  70.5 17.1 %all-to-all-start.2 = ((bf16[8,32,1792]{2,1,0:T(8,128)(2,1)}), bf16[8,32,1792]{2,1,0:T(8,128)(2,1)S(1)}, u32[]{:S(2)}, u32[]{:S(2)}) async-start(bf16[8,32,1792]{2,1,0:T(8,128)(2,1)} %broadcast_in_dim.59), calls=%async_computation.2 | async-start | bytes 1835008 | tf_op jit(solution)/shard_map/all_to_all | solution.py:338
  87.6 5.5 %collective-permute-start.6 = (bf16[256,1792]{1,0:T(8,128)(2,1)S(1)}, bf16[256,1792]{1,0:T(8,128)(2,1)S(1)}, u32[]{:S(2)}, u32[]{:S(2)}) collective-permute-start(bf16[256,1792]{1,0:T(8,128)(2,1)S(1)} %bitcast.24), channel_id=1, source_target_pairs={{0,8},{8,0},{16,24},{24,16},{32,40},{40,32},{48,56},{56,48},{64,72... | collective-permute-start | bytes 2752520 | tf_op jit(solution)/shard_map/ppermute | solution.py:361
  88.3 13.6 %collective-permute-start.3 = (bf16[64,1792]{1,0:T(8,128)(2,1)}, bf16[64,1792]{1,0:T(8,128)(2,1)S(1)}, u32[]{:S(2)}, u32[]{:S(2)}) collective-permute-start(bf16[64,1792]{1,0:T(8,128)(2,1)} %copy-done.2), channel_id=1, source_target_pairs={{0,1},{1,2},{2,3},{3,0},{4,5},{5,6},{6,7},{7,4},{8,9},{9,10},{10,1... | collective-permute-start | bytes 688136 | tf_op jit(solution)/shard_map/ppermute | solution.py:358
  89.6 14.0 %collective-permute-start.4 = (bf16[64,1792]{1,0:T(8,128)(2,1)}, bf16[64,1792]{1,0:T(8,128)(2,1)S(1)}, u32[]{:S(2)}, u32[]{:S(2)}) collective-permute-start(bf16[64,1792]{1,0:T(8,128)(2,1)} %copy-done.1), channel_id=1, source_target_pairs={{0,2},{1,3},{2,0},{3,1},{4,6},{5,7},{6,4},{7,5},{8,10},{9,11},{10,... | collective-permute-start | bytes 688136 | tf_op jit(solution)/shard_map/ppermute | solution.py:358
  92.0 11.5 %collective-permute-start.5 = (bf16[64,1792]{1,0:T(8,128)(2,1)S(1)}, bf16[64,1792]{1,0:T(8,128)(2,1)S(1)}, u32[]{:S(2)}, u32[]{:S(2)}) collective-permute-start(bf16[64,1792]{1,0:T(8,128)(2,1)S(1)} %get-tuple-element.44), channel_id=1, source_target_pairs={{0,3},{1,0},{2,1},{3,2},{4,7},{5,4},{6,5},{7,6},{8,11},{9,8},{10,9... | collective-permute-start | bytes 688136 | tf_op jit(solution)/shard_map/ppermute | solution.py:358
  100.7 12.7 %collective-permute-start.7 = (bf16[64,1792]{1,0:T(8,128)(2,1)}, bf16[64,1792]{1,0:T(8,128)(2,1)S(1)}, u32[]{:S(2)}, u32[]{:S(2)}) collective-permute-start(bf16[64,1792]{1,0:T(8,128)(2,1)} %get-tuple-element.48), channel_id=1, source_target_pairs={{0,1},{1,2},{2,3},{3,0},{4,5},{5,6},{6,7},{7,4},{8,9},{9,10},{10,1... | collective-permute-start | bytes 688136 | tf_op jit(solution)/shard_map/ppermute | solution.py:358
  101.0 12.3 %collective-permute-start.8 = (bf16[64,1792]{1,0:T(8,128)(2,1)}, bf16[64,1792]{1,0:T(8,128)(2,1)S(1)}, u32[]{:S(2)}, u32[]{:S(2)}) collective-permute-start(bf16[64,1792]{1,0:T(8,128)(2,1)} %get-tuple-element.49), channel_id=1, source_target_pairs={{0,2},{1,3},{2,0},{3,1},{4,6},{5,7},{6,4},{7,5},{8,10},{9,11},{10,... | collective-permute-start | bytes 688136 | tf_op jit(solution)/shard_map/ppermute | solution.py:358
  101.9 11.8 %collective-permute-start.9 = (bf16[64,1792]{1,0:T(8,128)(2,1)S(1)}, bf16[64,1792]{1,0:T(8,128)(2,1)S(1)}, u32[]{:S(2)}, u32[]{:S(2)}) collective-permute-start(bf16[64,1792]{1,0:T(8,128)(2,1)S(1)} %get-tuple-element.50), channel_id=1, source_target_pairs={{0,3},{1,0},{2,1},{3,2},{4,7},{5,4},{6,5},{7,6},{8,11},{9,8},{10,9... | collective-permute-start | bytes 688136 | tf_op jit(solution)/shard_map/ppermute | solution.py:358
  103.7 12.9 %collective-permute-start.10 = (bf16[64,1792]{1,0:T(8,128)(2,1)S(1)}, bf16[64,1792]{1,0:T(8,128)(2,1)S(1)}, u32[]{:S(2)}, u32[]{:S(2)}) collective-permute-start(bf16[64,1792]{1,0:T(8,128)(2,1)S(1)} %get-tuple-element.52), channel_id=1, source_target_pairs={{0,4},{1,5},{2,6},{3,7},{4,0},{5,1},{6,2},{7,3},{8,12},{9,13},{10,... | collective-permute-start | bytes 688136 | tf_op jit(solution)/shard_map/ppermute | solution.py:372
  113.8 6.7 %collective-permute-start.14 = (bf16[64,1792]{1,0:T(8,128)(2,1)S(1)}, bf16[64,1792]{1,0:T(8,128)(2,1)S(1)}, u32[]{:S(2)}, u32[]{:S(2)}) collective-permute-start(bf16[64,1792]{1,0:T(8,128)(2,1)S(1)} %get-tuple-element.62), channel_id=1, source_target_pairs={{0,4},{1,5},{2,6},{3,7},{4,0},{5,1},{6,2},{7,3},{8,12},{9,13},{10,... | collective-permute-start | bytes 688136 | tf_op jit(solution)/shard_map/ppermute | solution.py:377
  116.7 9.7 %collective-permute-start.13 = (bf16[64,1792]{1,0:T(8,128)(2,1)S(1)}, bf16[64,1792]{1,0:T(8,128)(2,1)S(1)}, u32[]{:S(2)}, u32[]{:S(2)}) collective-permute-start(bf16[64,1792]{1,0:T(8,128)(2,1)S(1)} %shard_map.79.refs_0_), channel_id=1, source_target_pairs={{0,3},{1,0},{2,1},{3,2},{4,7},{5,4},{6,5},{7,6},{8,11},{9,8},{10,9... | collective-permute-start | bytes 688136 | tf_op jit(solution)/shard_map/ppermute | solution.py:358
  119.8 7.2 %collective-permute-start.12 = (bf16[64,1792]{1,0:T(8,128)(2,1)S(1)}, bf16[64,1792]{1,0:T(8,128)(2,1)S(1)}, u32[]{:S(2)}, u32[]{:S(2)}) collective-permute-start(bf16[64,1792]{1,0:T(8,128)(2,1)S(1)} %shard_map.79.refs_0_), channel_id=1, source_target_pairs={{0,2},{1,3},{2,0},{3,1},{4,6},{5,7},{6,4},{7,5},{8,10},{9,11},{10,... | collective-permute-start | bytes 688136 | tf_op jit(solution)/shard_map/ppermute | solution.py:358
  120.1 15.4 %collective-permute-start.11 = (bf16[64,1792]{1,0:T(8,128)(2,1)S(1)}, bf16[64,1792]{1,0:T(8,128)(2,1)S(1)}, u32[]{:S(2)}, u32[]{:S(2)}) collective-permute-start(bf16[64,1792]{1,0:T(8,128)(2,1)S(1)} %shard_map.79.refs_0_), channel_id=1, source_target_pairs={{0,1},{1,2},{2,3},{3,0},{4,5},{5,6},{6,7},{7,4},{8,9},{9,10},{10,1... | collective-permute-start | bytes 688136 | tf_op jit(solution)/shard_map/ppermute | solution.py:358
  120.7 23.5 %collective-permute-start.18 = (bf16[64,1792]{1,0:T(8,128)(2,1)S(1)}, bf16[64,1792]{1,0:T(8,128)(2,1)S(1)}, u32[]{:S(2)}, u32[]{:S(2)}) collective-permute-start(bf16[64,1792]{1,0:T(8,128)(2,1)S(1)} %shard_map.81.refs_0_), channel_id=1, source_target_pairs={{0,3},{1,0},{2,1},{3,2},{4,7},{5,4},{6,5},{7,6},{8,11},{9,8},{10,9... | collective-permute-start | bytes 688136 | tf_op jit(solution)/shard_map/ppermute | solution.py:358
  124.8 19.4 %collective-permute-start.17 = (bf16[64,1792]{1,0:T(8,128)(2,1)S(1)}, bf16[64,1792]{1,0:T(8,128)(2,1)S(1)}, u32[]{:S(2)}, u32[]{:S(2)}) collective-permute-start(bf16[64,1792]{1,0:T(8,128)(2,1)S(1)} %shard_map.81.refs_0_), channel_id=1, source_target_pairs={{0,2},{1,3},{2,0},{3,1},{4,6},{5,7},{6,4},{7,5},{8,10},{9,11},{10,... | collective-permute-start | bytes 688136 | tf_op jit(solution)/shard_map/ppermute | solution.py:358
  126.3 17.8 %collective-permute-start.16 = (bf16[64,1792]{1,0:T(8,128)(2,1)S(1)}, bf16[64,1792]{1,0:T(8,128)(2,1)S(1)}, u32[]{:S(2)}, u32[]{:S(2)}) collective-permute-start(bf16[64,1792]{1,0:T(8,128)(2,1)S(1)} %shard_map.81.refs_0_), channel_id=1, source_target_pairs={{0,1},{1,2},{2,3},{3,0},{4,5},{5,6},{6,7},{7,4},{8,9},{9,10},{10,1... | collective-permute-start | bytes 688136 | tf_op jit(solution)/shard_map/ppermute | solution.py:358
  142.7 8.7 %collective-permute-start.15 = (bf16[128,3584]{1,0:T(8,128)(2,1)S(1)}, bf16[128,3584]{1,0:T(8,128)(2,1)S(1)}, u32[]{:S(2)}, u32[]{:S(2)}) collective-permute-start(bf16[128,3584]{1,0:T(8,128)(2,1)S(1)} %get-tuple-element.65), channel_id=1, source_target_pairs={{0,8},{8,0},{16,24},{24,16},{32,40},{40,32},{48,56},{56,48},{64,72... | collective-permute-start | bytes 2752520 | tf_op jit(solution)/shard_map/ppermute | solution.py:361
  151.3 2.6 %collective-permute-start.19 = (bf16[128,3584]{1,0:T(8,128)(2,1)S(1)}, bf16[128,3584]{1,0:T(8,128)(2,1)S(1)}, u32[]{:S(2)}, u32[]{:S(2)}) collective-permute-start(bf16[128,3584]{1,0:T(8,128)(2,1)S(1)} %get-tuple-element.68), channel_id=1, source_target_pairs={{0,8},{8,0},{16,24},{24,16},{32,40},{40,32},{48,56},{56,48},{64,72... | collective-permute-start | bytes 2752520 | tf_op jit(solution)/shard_map/ppermute | solution.py:361
  (3 other events, 2.2 us)

commit v10 on v9

--- a/solution.py
+++ b/solution.py
@@ -64,7 +64,7 @@
                     out[to : to + run, :] = rows[at : at + run, :]
 
 
-def select(ids, basis, chips, block=2048):
+def select(ids, basis, chips, block=4096):
     rows, width = basis.shape
     queries = ids.shape[0]
     return pl.pallas_call(
@@ -104,7 +104,7 @@
         out[:, to] = total.astype(BF16)
 
 
-def partial_rows(place, sel, sel2, grad, grad2, steps=7):
+def partial_rows(place, sel, sel2, grad, grad2, steps=2):
     queries, units = sel.shape
     half = grad.shape[1] // 2
     return pl.pallas_call(
@@ -135,7 +135,7 @@
 def rotate_kernel(place, own, other, basis, *refs, cuts):
     outs, (lhs, buf, acc, sems) = refs[:-4], refs[-4:]
     copies = fetch(basis, buf, sems, cuts)
-    core, x = place[0], place[1] if len(outs) > 1 else 0
+    core, x = place[0], place[1]
     piece, half = own.shape[0] // RING, own.shape[1]
     for d in range(RING):
         rows = pl.ds(pl.multiple_of(lax.rem(x + d, RING) * piece, piece), piece)
@@ -150,20 +150,16 @@
             value += acc[...]
         if i < len(cuts) - 1:
             acc[...] = value
-        elif len(outs) == 1:
-            outs[0][...] = value.astype(BF16)
         else:
             for d in range(RING):
                 outs[d][...] = value[d * piece : (d + 1) * piece].astype(outs[d].dtype)
 
 
-def rotate(place, own, other, basis, stacked=False):
+def rotate(place, own, other, basis):
     m, half = other.shape
     k, n = basis.shape
     piece = m // RING
     outs = [jax.ShapeDtypeStruct((piece, n), F32 if d == 0 else BF16) for d in range(RING)]
-    if stacked:
-        outs = [jax.ShapeDtypeStruct((m, n), BF16)]
     block = half // 7
     cuts = [(h * half + at * block, size * block) for h in range(2) for at, size in ((0, 3), (3, 2), (5, 2))]
     return pl.pallas_call(
@@ -252,26 +248,6 @@
     )(*parts)
 
 
-def stack_kernel(parts, total, rounded):
-    value = parts[0].astype(F32)
-    for d in range(1, RING):
-        value += parts[d].astype(F32)
-    total[...] = value
-    rounded[...] = value.astype(BF16)
-
-
-def stack_sum(parts):
-    shape = parts.shape[1:]
-    return pl.pallas_call(
-        stack_kernel,
-        in_specs=[VMEM],
-        out_specs=[VMEM] * 2,
-        out_shape=[jax.ShapeDtypeStruct(shape, F32), jax.ShapeDtypeStruct(shape, BF16)],
-        cost_estimate=cost(3 * parts.size, 4 * parts.size),
-        compiler_params=params(8),
-    )(parts)
-
-
 def ring_kernel(own, a, b, c, total, rounded):
     value = own[...] + a[...].astype(F32) + b[...].astype(F32) + c[...].astype(F32)
     total[...] = value
@@ -329,7 +305,6 @@
     place = jnp.stack([core, x]).astype(jnp.int32)
     swap = [(i, i ^ 1) for i in range(loops)]
     flip = [(i, (i + RING) % reds) for i in range(reds)]
-    rings = [[h + i for i in range(RING)] for h in range(0, reds, RING)]
     shift = [[(i, i - i % RING + (i + d) % RING) for i in range(reds)] for d in range(RING)]
     same_core = [[2 * i + c for i in range(chips)] for c in range(2)]
 

time: 182 us -> 180 us (0.989)
  Pallas kernels: 45.9 us -> 43.9 us
where the time goes in v10:
time: 180 us; the launch traced here: 179 us
  Pallas kernels  43.9 us (24%)
  waiting for transfers between devices  43.9 us (24%)
  blocking collectives  42.3 us (24%)
  starting transfers between devices  37.2 us (21%)
  local copies, waits for them, and re-layouts  6.93 us (4%)
  other arithmetic  3.49 us (2%)
    all_to_all x2, blocking collectives, exchange(): return lax.all_to_all(value, 'loop', 0, 0, axis_index_groups=same_core)  42.3 us
    all_to_all x2, waiting for transfers between devices, exchange(): return lax.all_to_all(value, 'loop', 0, 0, axis_index_groups=same_core)  23.6 us
    ppermute x12, starting transfers between devices, ring(): lax.ppermute(parts[d], 'red', shift[d])  16.4 us
    ppermute x12, waiting for transfers between devices, ring(): lax.ppermute(parts[d], 'red', shift[d])  16.4 us
    pallas_call x2, Pallas kernels, back(): pl.pallas_call(functools.partial(back_kernel, cuts=cuts), in_specs=[SMEM]...  14.3 us
    pallas_call x2, Pallas kernels, rotate(): pl.pallas_call(functools.partial(rotate_kernel, cuts=cuts), in_specs=[SME...  14.3 us
    all_to_all x2, starting transfers between devices, exchange(): return lax.all_to_all(value, 'loop', 0, 0, axis_index_groups=same_core)  9.69 us
    pallas_call x1, Pallas kernels, select(): pl.pallas_call(functools.partial(select_kernel, chips=chips), grid=(width...  8.03 us
  transfers between devices with their start and end apart: 22, of which 9 were waited for; matrix products, arithmetic and copies ran while one was open for 3% of the time, Pallas kernels for 21%

profile of v10, /device:TPU:1, one launch (start us, length us, event | category | flops | bytes accessed | tf_op | source)
XLA Modules:
  0.0 178.6 jit_solution(15431456554116161573)
XLA Ops:
  1.4 8.0 %shard_map.73.sel = bf16[512,512]{1,0:T(8,128)(2,1)} custom-call(s32[1,512]{1,0:T(1,128)} %bitcast.31, bf16[512,8192]{1,0:T(8,128)(2,1)} %basis.3), custom_call_target="tpu_custom_call" | custom-call | flops 4294967296 | bytes 8388608 | tf_op jit(solution)/shard_map/pallas_call | solution.py:70
  10.1 1.5 collective-permute-done.sel2
  12.4 6.5 %shard_map.74 = bf16[512,1792]{1,0:T(8,128)(2,1)} custom-call(s32[2]{0:T(128)} %pad_add_fusion.place, bf16[512,512]{1,0:T(8,128)(2,1)} %shard_map.73.sel, bf16[512,512]{1,0:T(8,128)(2,1)} %copy-done.3, bf16[512,3584]{1,0:T(8,128)(2,1)} %grad.1, bf16[512,3584]{1,0:T(8,128)(2,1)} %collective-permute-done.1.grad2), custom_call_target="tpu_custom_call" | custom-call | flops 1879048192 | bytes 5505024 | tf_op jit(solution)/shard_map/pallas_call | solution.py:110
  18.9 6.1 %all-to-all-start = ((bf16[8,64,1792]{2,1,0:T(8,128)(2,1)}), bf16[8,64,1792]{2,1,0:T(8,128)(2,1)S(1)}, u32[]{:S(2)}, u32[]{:S(2)}) async-start(bf16[8,64,1792]{2,1,0:T(8,128)(2,1)} %bitcast.29), calls=%async_computation | async-start | bytes 3670016 | tf_op jit(solution)/shard_map/all_to_all | solution.py:313
  26.7 3.1 %gather_fusion = f32[512]{0:T(512)S(1)} fusion(f32[8192]{0:T(1024)S(1)} %bitcast.28, s32[1024]{0:T(1024)S(1)} %pad_clamp_fusion), kind=kCustom, calls=%fused_computation | custom fusion | bytes 6144 | tf_op jit(solution)/shard_map/jit(_take)/gather | solution.py:320
  30.2 18.2 %all-to-all-done = bf16[8,64,1792]{2,1,0:T(8,128)(2,1)S(1)} async-done(((bf16[8,64,1792]{2,1,0:T(8,128)(2,1)}), bf16[8,64,1792]{2,1,0:T(8,128)(2,1)S(1)}, u32[]{:S(2)}, u32[]{:S(2)}) %all-to-all-start) | async-done | bytes 1835040 | tf_op jit(solution)/shard_map/all_to_all | solution.py:313
  48.8 16.7 %all_to_all.20 = bf16[8,32,1792]{2,1,0:T(8,128)(2,1)S(1)} all-to-all(bf16[8,32,1792]{2,1,0:T(8,128)(2,1)S(1)} %broadcast_in_dim.60), channel_id=1, replica_groups={{0,16,32,48,64,80,96,112},{8,24,40,56,72,88,104,120},{1,17,33,49,65,81,..., dimensions={0} | all-to-all | bytes 1835008 | tf_op jit(solution)/shard_map/all_to_all | solution.py:313
  66.5 2.0 %collective-permute-start.2 = (bf16[256,1792]{1,0:T(8,128)(2,1)S(1)}, bf16[256,1792]{1,0:T(8,128)(2,1)S(1)}, u32[]{:S(2)}, u32[]{:S(2)}) collective-permute-start(bf16[256,1792]{1,0:T(8,128)(2,1)S(1)} %bitcast.26), channel_id=1, source_target_pairs={{0,8},{8,0},{16,24},{24,16},{32,40},{40,32},{48,56},{56,48},{64,72... | collective-permute-start | bytes 2752520 | tf_op jit(solution)/shard_map/ppermute | solution.py:336
  68.5 3.6 %all-to-all-start.2 = ((bf16[8,32,1792]{2,1,0:T(8,128)(2,1)}), bf16[8,32,1792]{2,1,0:T(8,128)(2,1)S(1)}, u32[]{:S(2)}, u32[]{:S(2)}) async-start(bf16[8,32,1792]{2,1,0:T(8,128)(2,1)} %broadcast_in_dim.59), calls=%async_computation.2 | async-start | bytes 1835008 | tf_op jit(solution)/shard_map/all_to_all | solution.py:313
  72.1 6.8 %shard_map.75 = (f32[64,1792]{1,0:T(8,128)S(1)}, bf16[64,1792]{1,0:T(8,128)(2,1)S(1)}, bf16[64,1792]{1,0:T(8,128)(2,1)S(1)}, bf16[64,1792]{1,0:T(8,128)(2,1)S(1)}) custom-call(s32[2]{0:T(128)S(1)} %copy-done, bf16[256,1792]{1,0:T(8,128)(2,1)S(1)} %bitcast.27, bf16[256,1792]{1,0:T(8,128)(2,1)S(1)} %collective-permute-done.2.other, bf16[3584,1792]{1,0:T(8,128)(2,1)} %refs_4_.3), custom_call_target="tpu_custom_call" | custom-call | flops 3288334336 | bytes 12845056 | tf_op jit(solution)/shard_map/pallas_call | solution.py:165
  80.2 5.4 %all-to-all-done.2 = bf16[8,32,1792]{2,1,0:T(8,128)(2,1)S(1)} async-done(((bf16[8,32,1792]{2,1,0:T(8,128)(2,1)}), bf16[8,32,1792]{2,1,0:T(8,128)(2,1)S(1)}, u32[]{:S(2)}, u32[]{:S(2)}) %all-to-all-start.2) | async-done | bytes 917536 | tf_op jit(solution)/shard_map/all_to_all | solution.py:313
  87.5 2.4 %collective-permute-start.4 = (bf16[64,1792]{1,0:T(8,128)(2,1)}, bf16[64,1792]{1,0:T(8,128)(2,1)S(1)}, u32[]{:S(2)}, u32[]{:S(2)}) collective-permute-start(bf16[64,1792]{1,0:T(8,128)(2,1)} %copy-done.1), channel_id=1, source_target_pairs={{0,2},{1,3},{2,0},{3,1},{4,6},{5,7},{6,4},{7,5},{8,10},{9,11},{10,... | collective-permute-start | bytes 688136 | tf_op jit(solution)/shard_map/ppermute | solution.py:333
  91.2 7.5 %shard_map.77 = (f32[64,1792]{1,0:T(8,128)S(1)}, bf16[64,1792]{1,0:T(8,128)(2,1)}, bf16[64,1792]{1,0:T(8,128)(2,1)}, bf16[64,1792]{1,0:T(8,128)(2,1)S(1)}) custom-call(s32[2]{0:T(128)S(1)} %copy-done, bf16[256,1792]{1,0:T(8,128)(2,1)S(1)} %bitcast.25, bf16[256,1792]{1,0:T(8,128)(2,1)S(1)} %collective-permute-done.6.other, bf16[3584,1792]{1,0:T(8,128)(2,1)} %refs_4_.3), custom_call_target="tpu_custom_call" | custom-call | flops 3288334336 | bytes 12845056 | tf_op jit(solution)/shard_map/pallas_call | solution.py:165
  99.9 1.6 collective-permute-start.9
  101.7 2.7 %collective-permute-start.10 = (bf16[64,1792]{1,0:T(8,128)(2,1)S(1)}, bf16[64,1792]{1,0:T(8,128)(2,1)S(1)}, u32[]{:S(2)}, u32[]{:S(2)}) collective-permute-start(bf16[64,1792]{1,0:T(8,128)(2,1)S(1)} %get-tuple-element.52), channel_id=1, source_target_pairs={{0,4},{1,5},{2,6},{3,7},{4,0},{5,1},{6,2},{7,3},{8,12},{9,13},{10,... | collective-permute-start | bytes 688136 | tf_op jit(solution)/shard_map/ppermute | solution.py:347
  105.2 6.1 %collective-permute-done.7.a = bf16[64,1792]{1,0:T(8,128)(2,1)S(1)} collective-permute-done((bf16[64,1792]{1,0:T(8,128)(2,1)}, bf16[64,1792]{1,0:T(8,128)(2,1)S(1)}, u32[]{:S(2)}, u32[]{:S(2)}) %collective-permute-start.7) | collective-permute-done | bytes 229408 | tf_op jit(solution)/shard_map/ppermute | solution.py:333
  111.8 2.7 %collective-permute-start.14 = (bf16[64,1792]{1,0:T(8,128)(2,1)S(1)}, bf16[64,1792]{1,0:T(8,128)(2,1)S(1)}, u32[]{:S(2)}, u32[]{:S(2)}) collective-permute-start(bf16[64,1792]{1,0:T(8,128)(2,1)S(1)} %get-tuple-element.62), channel_id=1, source_target_pairs={{0,4},{1,5},{2,6},{3,7},{4,0},{5,1},{6,2},{7,3},{8,12},{9,13},{10,... | collective-permute-start | bytes 688136 | tf_op jit(solution)/shard_map/ppermute | solution.py:352
  114.7 3.1 %collective-permute-start.13 = (bf16[64,1792]{1,0:T(8,128)(2,1)S(1)}, bf16[64,1792]{1,0:T(8,128)(2,1)S(1)}, u32[]{:S(2)}, u32[]{:S(2)}) collective-permute-start(bf16[64,1792]{1,0:T(8,128)(2,1)S(1)} %shard_map.79.refs_0_), channel_id=1, source_target_pairs={{0,3},{1,0},{2,1},{3,2},{4,7},{5,4},{6,5},{7,6},{8,11},{9,8},{10,9... | collective-permute-start | bytes 688136 | tf_op jit(solution)/shard_map/ppermute | solution.py:333
  118.7 4.1 %collective-permute-start.18 = (bf16[64,1792]{1,0:T(8,128)(2,1)S(1)}, bf16[64,1792]{1,0:T(8,128)(2,1)S(1)}, u32[]{:S(2)}, u32[]{:S(2)}) collective-permute-start(bf16[64,1792]{1,0:T(8,128)(2,1)S(1)} %shard_map.81.refs_0_), channel_id=1, source_target_pairs={{0,3},{1,0},{2,1},{3,2},{4,7},{5,4},{6,5},{7,6},{8,11},{9,8},{10,9... | collective-permute-start | bytes 688136 | tf_op jit(solution)/shard_map/ppermute | solution.py:333
  124.9 8.6 %collective-permute-done.11.refs_1_ = bf16[64,1792]{1,0:T(8,128)(2,1)S(1)} collective-permute-done((bf16[64,1792]{1,0:T(8,128)(2,1)S(1)}, bf16[64,1792]{1,0:T(8,128)(2,1)S(1)}, u32[]{:S(2)}, u32[]{:S(2)}) %collective-permute-start.11) | collective-permute-done | bytes 229408 | tf_op jit(solution)/shard_map/ppermute | solution.py:333
  133.5 7.1 %shard_map.80 = (bf16[128,3584]{1,0:T(8,128)(2,1)S(1)}, f32[128,3584]{1,0:T(8,128)S(1)}) custom-call(s32[2]{0:T(128)S(1)} %copy-done, bf16[64,1792]{1,0:T(8,128)(2,1)S(1)} %shard_map.79.refs_0_, bf16[64,1792]{1,0:T(8,128)(2,1)S(1)} %collective-permute-done.11.refs_1_, bf16[64,1792]{1,0:T(8,128)(2,1)S(1)} %collective-permute-done.12.refs_2_, ...), custom_call_target="tpu_custom_call" | custom-call | flops 3288334336 | bytes 12845056 | tf_op jit(solution)/shard_map/pallas_call | solution.py:209
  142.2 7.1 %shard_map.82 = (bf16[128,3584]{1,0:T(8,128)(2,1)S(1)}, f32[128,3584]{1,0:T(8,128)S(1)}) custom-call(s32[2]{0:T(128)S(1)} %copy-done, bf16[64,1792]{1,0:T(8,128)(2,1)S(1)} %shard_map.81.refs_0_, bf16[64,1792]{1,0:T(8,128)(2,1)S(1)} %collective-permute-done.16.refs_1_, bf16[64,1792]{1,0:T(8,128)(2,1)S(1)} %collective-permute-done.17.refs_2_, ...), custom_call_target="tpu_custom_call" | custom-call | flops 3288334336 | bytes 12845056 | tf_op jit(solution)/shard_map/pallas_call | solution.py:209
  149.4 2.4 %collective-permute-done.19.refs_3_ = bf16[128,3584]{1,0:T(8,128)(2,1)S(1)} collective-permute-done((bf16[128,3584]{1,0:T(8,128)(2,1)S(1)}, bf16[128,3584]{1,0:T(8,128)(2,1)S(1)}, u32[]{:S(2)}, u32[]{:S(2)}) %collective-permute-start.19) | collective-permute-done | bytes 917536 | tf_op jit(solution)/shard_map/ppermute | solution.py:336
  152.2 25.5 %all_to_all.21 = bf16[8,32,3584]{2,1,0:T(8,128)(2,1)S(1)} all-to-all(bf16[8,32,3584]{2,1,0:T(8,128)(2,1)S(1)} %shard_map.83), channel_id=1, replica_groups={{0,16,32,48,64,80,96,112},{8,24,40,56,72,88,104,120},{1,17,33,49,65,81,..., dimensions={0} | all-to-all | bytes 3670016 | tf_op jit(solution)/shard_map/all_to_all | solution.py:313
  (64 shorter events, 18.6 us)
Async XLA Ops:
  0.0 11.6 %collective-permute-start.1 = (bf16[512,3584]{1,0:T(8,128)(2,1)}, bf16[512,3584]{1,0:T(8,128)(2,1)}, u32[]{:S(2)}, u32[]{:S(2)}) collective-permute-start(bf16[512,3584]{1,0:T(8,128)(2,1)} %grad.1), channel_id=1, source_target_pairs={{0,8},{8,0},{16,24},{24,16},{32,40},{40,32},{48,56},{56,48},{64,72... | collective-permute-start | bytes 11010056 | tf_op jit(solution)/shard_map/ppermute | solution.py:315
  9.5 2.1 %collective-permute-start = (bf16[512,512]{1,0:T(8,128)(2,1)}, bf16[512,512]{1,0:T(8,128)(2,1)S(1)}, u32[]{:S(2)}, u32[]{:S(2)}) collective-permute-start(bf16[512,512]{1,0:T(8,128)(2,1)} %shard_map.73.sel), channel_id=1, source_target_pairs={{0,8},{8,0},{16,24},{24,16},{32,40},{40,32},{48,56},{56,48},{64,72... | collective-permute-start | bytes 1572872 | tf_op jit(solution)/shard_map/ppermute | solution.py:317
  18.9 6.2 %copy-start.4 = (s32[512]{0:T(512)S(1)}, s32[512]{0:T(512)}, u32[]{:S(2)}) copy-start(s32[512]{0:T(512)} %param.7) | copy-start | bytes 6148
  18.9 29.6 %all-to-all-start = ((bf16[8,64,1792]{2,1,0:T(8,128)(2,1)}), bf16[8,64,1792]{2,1,0:T(8,128)(2,1)S(1)}, u32[]{:S(2)}, u32[]{:S(2)}) async-start(bf16[8,64,1792]{2,1,0:T(8,128)(2,1)} %bitcast.29), calls=%async_computation | async-start | bytes 3670016 | tf_op jit(solution)/shard_map/all_to_all | solution.py:313
  65.5 6.6 %copy-start = (s32[2]{0:T(128)S(1)}, s32[2]{0:T(128)}, u32[]{:S(2)}) copy-start(s32[2]{0:T(128)} %pad_add_fusion.place) | copy-start | bytes 28
  66.5 5.6 %collective-permute-start.2 = (bf16[256,1792]{1,0:T(8,128)(2,1)S(1)}, bf16[256,1792]{1,0:T(8,128)(2,1)S(1)}, u32[]{:S(2)}, u32[]{:S(2)}) collective-permute-start(bf16[256,1792]{1,0:T(8,128)(2,1)S(1)} %bitcast.26), channel_id=1, source_target_pairs={{0,8},{8,0},{16,24},{24,16},{32,40},{40,32},{48,56},{56,48},{64,72... | collective-permute-start | bytes 2752520 | tf_op jit(solution)/shard_map/ppermute | solution.py:336
  68.5 17.1 %all-to-all-start.2 = ((bf16[8,32,1792]{2,1,0:T(8,128)(2,1)}), bf16[8,32,1792]{2,1,0:T(8,128)(2,1)S(1)}, u32[]{:S(2)}, u32[]{:S(2)}) async-start(bf16[8,32,1792]{2,1,0:T(8,128)(2,1)} %broadcast_in_dim.59), calls=%async_computation.2 | async-start | bytes 1835008 | tf_op jit(solution)/shard_map/all_to_all | solution.py:313
  85.6 5.5 %collective-permute-start.6 = (bf16[256,1792]{1,0:T(8,128)(2,1)S(1)}, bf16[256,1792]{1,0:T(8,128)(2,1)S(1)}, u32[]{:S(2)}, u32[]{:S(2)}) collective-permute-start(bf16[256,1792]{1,0:T(8,128)(2,1)S(1)} %bitcast.24), channel_id=1, source_target_pairs={{0,8},{8,0},{16,24},{24,16},{32,40},{40,32},{48,56},{56,48},{64,72... | collective-permute-start | bytes 2752520 | tf_op jit(solution)/shard_map/ppermute | solution.py:336
  86.3 13.6 %collective-permute-start.3 = (bf16[64,1792]{1,0:T(8,128)(2,1)}, bf16[64,1792]{1,0:T(8,128)(2,1)S(1)}, u32[]{:S(2)}, u32[]{:S(2)}) collective-permute-start(bf16[64,1792]{1,0:T(8,128)(2,1)} %copy-done.2), channel_id=1, source_target_pairs={{0,1},{1,2},{2,3},{3,0},{4,5},{5,6},{6,7},{7,4},{8,9},{9,10},{10,1... | collective-permute-start | bytes 688136 | tf_op jit(solution)/shard_map/ppermute | solution.py:333
  87.5 14.0 %collective-permute-start.4 = (bf16[64,1792]{1,0:T(8,128)(2,1)}, bf16[64,1792]{1,0:T(8,128)(2,1)S(1)}, u32[]{:S(2)}, u32[]{:S(2)}) collective-permute-start(bf16[64,1792]{1,0:T(8,128)(2,1)} %copy-done.1), channel_id=1, source_target_pairs={{0,2},{1,3},{2,0},{3,1},{4,6},{5,7},{6,4},{7,5},{8,10},{9,11},{10,... | collective-permute-start | bytes 688136 | tf_op jit(solution)/shard_map/ppermute | solution.py:333
  90.0 11.5 %collective-permute-start.5 = (bf16[64,1792]{1,0:T(8,128)(2,1)S(1)}, bf16[64,1792]{1,0:T(8,128)(2,1)S(1)}, u32[]{:S(2)}, u32[]{:S(2)}) collective-permute-start(bf16[64,1792]{1,0:T(8,128)(2,1)S(1)} %get-tuple-element.44), channel_id=1, source_target_pairs={{0,3},{1,0},{2,1},{3,2},{4,7},{5,4},{6,5},{7,6},{8,11},{9,8},{10,9... | collective-permute-start | bytes 688136 | tf_op jit(solution)/shard_map/ppermute | solution.py:333
  98.7 12.7 %collective-permute-start.7 = (bf16[64,1792]{1,0:T(8,128)(2,1)}, bf16[64,1792]{1,0:T(8,128)(2,1)S(1)}, u32[]{:S(2)}, u32[]{:S(2)}) collective-permute-start(bf16[64,1792]{1,0:T(8,128)(2,1)} %get-tuple-element.48), channel_id=1, source_target_pairs={{0,1},{1,2},{2,3},{3,0},{4,5},{5,6},{6,7},{7,4},{8,9},{9,10},{10,1... | collective-permute-start | bytes 688136 | tf_op jit(solution)/shard_map/ppermute | solution.py:333
  99.0 12.3 %collective-permute-start.8 = (bf16[64,1792]{1,0:T(8,128)(2,1)}, bf16[64,1792]{1,0:T(8,128)(2,1)S(1)}, u32[]{:S(2)}, u32[]{:S(2)}) collective-permute-start(bf16[64,1792]{1,0:T(8,128)(2,1)} %get-tuple-element.49), channel_id=1, source_target_pairs={{0,2},{1,3},{2,0},{3,1},{4,6},{5,7},{6,4},{7,5},{8,10},{9,11},{10,... | collective-permute-start | bytes 688136 | tf_op jit(solution)/shard_map/ppermute | solution.py:333
  99.9 11.8 %collective-permute-start.9 = (bf16[64,1792]{1,0:T(8,128)(2,1)S(1)}, bf16[64,1792]{1,0:T(8,128)(2,1)S(1)}, u32[]{:S(2)}, u32[]{:S(2)}) collective-permute-start(bf16[64,1792]{1,0:T(8,128)(2,1)S(1)} %get-tuple-element.50), channel_id=1, source_target_pairs={{0,3},{1,0},{2,1},{3,2},{4,7},{5,4},{6,5},{7,6},{8,11},{9,8},{10,9... | collective-permute-start | bytes 688136 | tf_op jit(solution)/shard_map/ppermute | solution.py:333
  101.7 12.9 %collective-permute-start.10 = (bf16[64,1792]{1,0:T(8,128)(2,1)S(1)}, bf16[64,1792]{1,0:T(8,128)(2,1)S(1)}, u32[]{:S(2)}, u32[]{:S(2)}) collective-permute-start(bf16[64,1792]{1,0:T(8,128)(2,1)S(1)} %get-tuple-element.52), channel_id=1, source_target_pairs={{0,4},{1,5},{2,6},{3,7},{4,0},{5,1},{6,2},{7,3},{8,12},{9,13},{10,... | collective-permute-start | bytes 688136 | tf_op jit(solution)/shard_map/ppermute | solution.py:347
  111.8 6.7 %collective-permute-start.14 = (bf16[64,1792]{1,0:T(8,128)(2,1)S(1)}, bf16[64,1792]{1,0:T(8,128)(2,1)S(1)}, u32[]{:S(2)}, u32[]{:S(2)}) collective-permute-start(bf16[64,1792]{1,0:T(8,128)(2,1)S(1)} %get-tuple-element.62), channel_id=1, source_target_pairs={{0,4},{1,5},{2,6},{3,7},{4,0},{5,1},{6,2},{7,3},{8,12},{9,13},{10,... | collective-permute-start | bytes 688136 | tf_op jit(solution)/shard_map/ppermute | solution.py:352
  114.7 9.7 %collective-permute-start.13 = (bf16[64,1792]{1,0:T(8,128)(2,1)S(1)}, bf16[64,1792]{1,0:T(8,128)(2,1)S(1)}, u32[]{:S(2)}, u32[]{:S(2)}) collective-permute-start(bf16[64,1792]{1,0:T(8,128)(2,1)S(1)} %shard_map.79.refs_0_), channel_id=1, source_target_pairs={{0,3},{1,0},{2,1},{3,2},{4,7},{5,4},{6,5},{7,6},{8,11},{9,8},{10,9... | collective-permute-start | bytes 688136 | tf_op jit(solution)/shard_map/ppermute | solution.py:333
  117.8 7.2 %collective-permute-start.12 = (bf16[64,1792]{1,0:T(8,128)(2,1)S(1)}, bf16[64,1792]{1,0:T(8,128)(2,1)S(1)}, u32[]{:S(2)}, u32[]{:S(2)}) collective-permute-start(bf16[64,1792]{1,0:T(8,128)(2,1)S(1)} %shard_map.79.refs_0_), channel_id=1, source_target_pairs={{0,2},{1,3},{2,0},{3,1},{4,6},{5,7},{6,4},{7,5},{8,10},{9,11},{10,... | collective-permute-start | bytes 688136 | tf_op jit(solution)/shard_map/ppermute | solution.py:333
  118.1 15.4 %collective-permute-start.11 = (bf16[64,1792]{1,0:T(8,128)(2,1)S(1)}, bf16[64,1792]{1,0:T(8,128)(2,1)S(1)}, u32[]{:S(2)}, u32[]{:S(2)}) collective-permute-start(bf16[64,1792]{1,0:T(8,128)(2,1)S(1)} %shard_map.79.refs_0_), channel_id=1, source_target_pairs={{0,1},{1,2},{2,3},{3,0},{4,5},{5,6},{6,7},{7,4},{8,9},{9,10},{10,1... | collective-permute-start | bytes 688136 | tf_op jit(solution)/shard_map/ppermute | solution.py:333
  118.7 23.5 %collective-permute-start.18 = (bf16[64,1792]{1,0:T(8,128)(2,1)S(1)}, bf16[64,1792]{1,0:T(8,128)(2,1)S(1)}, u32[]{:S(2)}, u32[]{:S(2)}) collective-permute-start(bf16[64,1792]{1,0:T(8,128)(2,1)S(1)} %shard_map.81.refs_0_), channel_id=1, source_target_pairs={{0,3},{1,0},{2,1},{3,2},{4,7},{5,4},{6,5},{7,6},{8,11},{9,8},{10,9... | collective-permute-start | bytes 688136 | tf_op jit(solution)/shard_map/ppermute | solution.py:333
  122.8 19.4 %collective-permute-start.17 = (bf16[64,1792]{1,0:T(8,128)(2,1)S(1)}, bf16[64,1792]{1,0:T(8,128)(2,1)S(1)}, u32[]{:S(2)}, u32[]{:S(2)}) collective-permute-start(bf16[64,1792]{1,0:T(8,128)(2,1)S(1)} %shard_map.81.refs_0_), channel_id=1, source_target_pairs={{0,2},{1,3},{2,0},{3,1},{4,6},{5,7},{6,4},{7,5},{8,10},{9,11},{10,... | collective-permute-start | bytes 688136 | tf_op jit(solution)/shard_map/ppermute | solution.py:333
  124.3 17.8 %collective-permute-start.16 = (bf16[64,1792]{1,0:T(8,128)(2,1)S(1)}, bf16[64,1792]{1,0:T(8,128)(2,1)S(1)}, u32[]{:S(2)}, u32[]{:S(2)}) collective-permute-start(bf16[64,1792]{1,0:T(8,128)(2,1)S(1)} %shard_map.81.refs_0_), channel_id=1, source_target_pairs={{0,1},{1,2},{2,3},{3,0},{4,5},{5,6},{6,7},{7,4},{8,9},{9,10},{10,1... | collective-permute-start | bytes 688136 | tf_op jit(solution)/shard_map/ppermute | solution.py:333
  140.7 8.8 %collective-permute-start.15 = (bf16[128,3584]{1,0:T(8,128)(2,1)S(1)}, bf16[128,3584]{1,0:T(8,128)(2,1)S(1)}, u32[]{:S(2)}, u32[]{:S(2)}) collective-permute-start(bf16[128,3584]{1,0:T(8,128)(2,1)S(1)} %get-tuple-element.65), channel_id=1, source_target_pairs={{0,8},{8,0},{16,24},{24,16},{32,40},{40,32},{48,56},{56,48},{64,72... | collective-permute-start | bytes 2752520 | tf_op jit(solution)/shard_map/ppermute | solution.py:336
  149.3 2.6 %collective-permute-start.19 = (bf16[128,3584]{1,0:T(8,128)(2,1)S(1)}, bf16[128,3584]{1,0:T(8,128)(2,1)S(1)}, u32[]{:S(2)}, u32[]{:S(2)}) collective-permute-start(bf16[128,3584]{1,0:T(8,128)(2,1)S(1)} %get-tuple-element.68), channel_id=1, source_target_pairs={{0,8},{8,0},{16,24},{24,16},{32,40},{40,32},{48,56},{56,48},{64,72... | collective-permute-start | bytes 2752520 | tf_op jit(solution)/shard_map/ppermute | solution.py:336
  (3 other events, 2.2 us)

commit v11 on v10

--- a/solution.py
+++ b/solution.py
@@ -118,7 +118,7 @@
             pltpu.SemaphoreType.DMA((2, steps)),
         ],
         cost_estimate=cost(4 * queries * units * half, 6 * queries * half),
-        compiler_params=params(56),
+        compiler_params=params(50),
     )(place, sel, sel2, grad, grad2)
 
 

time: 180 us -> 181 us (level)
  starting transfers between devices: 37.2 us -> 39.6 us
    ppermute x4, starting transfers between devices: 4.29 us -> 6.79 us  [swapped(): return lax.ppermute(value, 'loop', swap)]
  transfers between devices with their start and end apart: 22 -> 22, of which waited for: 9 -> 8; matrix products, arithmetic and copies ran while one was open for 3% -> 3% of each run, Pallas kernels for 21% -> 21%
where the time goes in v11:
time: 181 us; the launch traced here: 179 us
  waiting for transfers between devices  43.3 us (24%)
  Pallas kernels  43.1 us (24%)
  blocking collectives  42.3 us (23%)
  starting transfers between devices  39.6 us (22%)
  local copies, waits for them, and re-layouts  7.19 us (4%)
  other arithmetic  2.95 us (2%)
    all_to_all x2, blocking collectives, exchange(): return lax.all_to_all(value, 'loop', 0, 0, axis_index_groups=same_core)  42.3 us
    all_to_all x2, waiting for transfers between devices, exchange(): return lax.all_to_all(value, 'loop', 0, 0, axis_index_groups=same_core)  23.6 us
    ppermute x12, starting transfers between devices, ring(): lax.ppermute(parts[d], 'red', shift[d])  16.3 us
    ppermute x12, waiting for transfers between devices, ring(): lax.ppermute(parts[d], 'red', shift[d])  15.2 us
    pallas_call x2, Pallas kernels, back(): pl.pallas_call(functools.partial(back_kernel, cuts=cuts), in_specs=[SMEM]...  14.3 us
    pallas_call x2, Pallas kernels, rotate(): pl.pallas_call(functools.partial(rotate_kernel, cuts=cuts), in_specs=[SME...  14.2 us
    all_to_all x2, starting transfers between devices, exchange(): return lax.all_to_all(value, 'loop', 0, 0, axis_index_groups=same_core)  9.69 us
    pallas_call x1, Pallas kernels, select(): pl.pallas_call(functools.partial(select_kernel, chips=chips), grid=(width...  8.04 us
  transfers between devices with their start and end apart: 22, of which 8 were waited for; matrix products, arithmetic and copies ran while one was open for 3% of the time, Pallas kernels for 21%

profile of v11, /device:TPU:1, one launch (start us, length us, event | category | flops | bytes accessed | tf_op | source)
XLA Modules:
  0.0 179.3 jit_solution(11365921929917500507)
XLA Ops:
  1.4 8.0 %shard_map.73.sel = bf16[512,512]{1,0:T(8,128)(2,1)} custom-call(s32[1,512]{1,0:T(1,128)} %bitcast.30, bf16[512,8192]{1,0:T(8,128)(2,1)} %basis.3), custom_call_target="tpu_custom_call" | custom-call | flops 4294967296 | bytes 8388608 | tf_op jit(solution)/shard_map/pallas_call | solution.py:70
  9.5 2.0 %collective-permute-done.sel2 = bf16[512,512]{1,0:T(8,128)(2,1)S(1)} collective-permute-done((bf16[512,512]{1,0:T(8,128)(2,1)}, bf16[512,512]{1,0:T(8,128)(2,1)S(1)}, u32[]{:S(2)}, u32[]{:S(2)}) %collective-permute-start) | collective-permute-done | bytes 524320 | tf_op jit(solution)/shard_map/ppermute | solution.py:317
  12.6 5.8 %shard_map.74 = bf16[512,1792]{1,0:T(8,128)(2,1)} custom-call(s32[2]{0:T(128)S(1)} %pad_add_fusion.place, bf16[512,512]{1,0:T(8,128)(2,1)S(1)} %copy-done, bf16[512,512]{1,0:T(8,128)(2,1)S(1)} %collective-permute-done.sel2, bf16[512,3584]{1,0:T(8,128)(2,1)} %grad.1, bf16[512,3584]{1,0:T(8,128)(2,1)} %collective-permute-done.1.grad2), custom_call_target="tpu_custom_call" | custom-call | flops 1879048192 | bytes 5505024 | tf_op jit(solution)/shard_map/pallas_call | solution.py:110
  18.5 6.1 %all-to-all-start = ((bf16[8,64,1792]{2,1,0:T(8,128)(2,1)}), bf16[8,64,1792]{2,1,0:T(8,128)(2,1)S(1)}, u32[]{:S(2)}, u32[]{:S(2)}) async-start(bf16[8,64,1792]{2,1,0:T(8,128)(2,1)} %bitcast.3), calls=%async_computation | async-start | bytes 3670016 | tf_op jit(solution)/shard_map/all_to_all | solution.py:313
  26.3 3.1 %gather_fusion = f32[512]{0:T(512)S(1)} fusion(f32[8192]{0:T(1024)S(1)} %bitcast.28, s32[1024]{0:T(1024)S(1)} %pad_clamp_fusion), kind=kCustom, calls=%fused_computation | custom fusion | bytes 6144 | tf_op jit(solution)/shard_map/jit(_take)/gather | solution.py:320
  29.8 18.2 %all-to-all-done = bf16[8,64,1792]{2,1,0:T(8,128)(2,1)S(1)} async-done(((bf16[8,64,1792]{2,1,0:T(8,128)(2,1)}), bf16[8,64,1792]{2,1,0:T(8,128)(2,1)S(1)}, u32[]{:S(2)}, u32[]{:S(2)}) %all-to-all-start) | async-done | bytes 1835040 | tf_op jit(solution)/shard_map/all_to_all | solution.py:313
  48.4 16.7 %all_to_all.20 = bf16[8,32,1792]{2,1,0:T(8,128)(2,1)S(1)} all-to-all(bf16[8,32,1792]{2,1,0:T(8,128)(2,1)S(1)} %broadcast_in_dim.60), channel_id=1, replica_groups={{0,16,32,48,64,80,96,112},{8,24,40,56,72,88,104,120},{1,17,33,49,65,81,..., dimensions={0} | all-to-all | bytes 1835008 | tf_op jit(solution)/shard_map/all_to_all | solution.py:313
  68.1 3.6 %all-to-all-start.2 = ((bf16[8,32,1792]{2,1,0:T(8,128)(2,1)}), bf16[8,32,1792]{2,1,0:T(8,128)(2,1)S(1)}, u32[]{:S(2)}, u32[]{:S(2)}) async-start(bf16[8,32,1792]{2,1,0:T(8,128)(2,1)} %broadcast_in_dim.59), calls=%async_computation.2 | async-start | bytes 1835008 | tf_op jit(solution)/shard_map/all_to_all | solution.py:313
  71.7 6.8 %shard_map.75 = (f32[64,1792]{1,0:T(8,128)S(1)}, bf16[64,1792]{1,0:T(8,128)(2,1)S(1)}, bf16[64,1792]{1,0:T(8,128)(2,1)S(1)}, bf16[64,1792]{1,0:T(8,128)(2,1)S(1)}) custom-call(s32[2]{0:T(128)S(1)} %pad_add_fusion.place, bf16[256,1792]{1,0:T(8,128)(2,1)S(1)} %bitcast.27, bf16[256,1792]{1,0:T(8,128)(2,1)S(1)} %collective-permute-done.2.other, ...), custom_call_target="tpu_custom_call" | custom-call | flops 3288334336 | bytes 12845056 | tf_op jit(solution)/shard_map/pallas_call | solution.py:165
  79.8 5.4 %all-to-all-done.2 = bf16[8,32,1792]{2,1,0:T(8,128)(2,1)S(1)} async-done(((bf16[8,32,1792]{2,1,0:T(8,128)(2,1)}), bf16[8,32,1792]{2,1,0:T(8,128)(2,1)S(1)}, u32[]{:S(2)}, u32[]{:S(2)}) %all-to-all-start.2) | async-done | bytes 917536 | tf_op jit(solution)/shard_map/all_to_all | solution.py:313
  87.1 2.4 %collective-permute-start.4 = (bf16[64,1792]{1,0:T(8,128)(2,1)}, bf16[64,1792]{1,0:T(8,128)(2,1)S(1)}, u32[]{:S(2)}, u32[]{:S(2)}) collective-permute-start(bf16[64,1792]{1,0:T(8,128)(2,1)} %copy-done.1), channel_id=1, source_target_pairs={{0,2},{1,3},{2,0},{3,1},{4,6},{5,7},{6,4},{7,5},{8,10},{9,11},{10,... | collective-permute-start | bytes 688136 | tf_op jit(solution)/shard_map/ppermute | solution.py:333
  90.8 7.4 %shard_map.77 = (f32[64,1792]{1,0:T(8,128)S(1)}, bf16[64,1792]{1,0:T(8,128)(2,1)}, bf16[64,1792]{1,0:T(8,128)(2,1)S(1)}, bf16[64,1792]{1,0:T(8,128)(2,1)S(1)}) custom-call(s32[2]{0:T(128)S(1)} %pad_add_fusion.place, bf16[256,1792]{1,0:T(8,128)(2,1)S(1)} %bitcast.25, bf16[256,1792]{1,0:T(8,128)(2,1)S(1)} %collective-permute-done.6.other, ...), custom_call_target="tpu_custom_call" | custom-call | flops 3288334336 | bytes 12845056 | tf_op jit(solution)/shard_map/pallas_call | solution.py:165
  101.2 2.7 %collective-permute-start.10 = (bf16[64,1792]{1,0:T(8,128)(2,1)S(1)}, bf16[64,1792]{1,0:T(8,128)(2,1)S(1)}, u32[]{:S(2)}, u32[]{:S(2)}) collective-permute-start(bf16[64,1792]{1,0:T(8,128)(2,1)S(1)} %get-tuple-element.52), channel_id=1, source_target_pairs={{0,4},{1,5},{2,6},{3,7},{4,0},{5,1},{6,2},{7,3},{8,12},{9,13},{10,... | collective-permute-start | bytes 688136 | tf_op jit(solution)/shard_map/ppermute | solution.py:347
  104.7 6.1 %collective-permute-done.7.a = bf16[64,1792]{1,0:T(8,128)(2,1)S(1)} collective-permute-done((bf16[64,1792]{1,0:T(8,128)(2,1)}, bf16[64,1792]{1,0:T(8,128)(2,1)S(1)}, u32[]{:S(2)}, u32[]{:S(2)}) %collective-permute-start.7) | collective-permute-done | bytes 229408 | tf_op jit(solution)/shard_map/ppermute | solution.py:333
  111.2 2.7 %collective-permute-start.14 = (bf16[64,1792]{1,0:T(8,128)(2,1)S(1)}, bf16[64,1792]{1,0:T(8,128)(2,1)S(1)}, u32[]{:S(2)}, u32[]{:S(2)}) collective-permute-start(bf16[64,1792]{1,0:T(8,128)(2,1)S(1)} %get-tuple-element.62), channel_id=1, source_target_pairs={{0,4},{1,5},{2,6},{3,7},{4,0},{5,1},{6,2},{7,3},{8,12},{9,13},{10,... | collective-permute-start | bytes 688136 | tf_op jit(solution)/shard_map/ppermute | solution.py:352
  114.1 3.5 %collective-permute-start.13 = (bf16[64,1792]{1,0:T(8,128)(2,1)S(1)}, bf16[64,1792]{1,0:T(8,128)(2,1)S(1)}, u32[]{:S(2)}, u32[]{:S(2)}) collective-permute-start(bf16[64,1792]{1,0:T(8,128)(2,1)S(1)} %shard_map.79.refs_0_), channel_id=1, source_target_pairs={{0,3},{1,0},{2,1},{3,2},{4,7},{5,4},{6,5},{7,6},{8,11},{9,8},{10,9... | collective-permute-start | bytes 688136 | tf_op jit(solution)/shard_map/ppermute | solution.py:333
  118.5 4.4 %collective-permute-start.18 = (bf16[64,1792]{1,0:T(8,128)(2,1)S(1)}, bf16[64,1792]{1,0:T(8,128)(2,1)S(1)}, u32[]{:S(2)}, u32[]{:S(2)}) collective-permute-start(bf16[64,1792]{1,0:T(8,128)(2,1)S(1)} %shard_map.81.refs_0_), channel_id=1, source_target_pairs={{0,3},{1,0},{2,1},{3,2},{4,7},{5,4},{6,5},{7,6},{8,11},{9,8},{10,9... | collective-permute-start | bytes 688136 | tf_op jit(solution)/shard_map/ppermute | solution.py:333
  123.0 2.1 %collective-permute-done.13.refs_3_ = bf16[64,1792]{1,0:T(8,128)(2,1)S(1)} collective-permute-done((bf16[64,1792]{1,0:T(8,128)(2,1)S(1)}, bf16[64,1792]{1,0:T(8,128)(2,1)S(1)}, u32[]{:S(2)}, u32[]{:S(2)}) %collective-permute-start.13) | collective-permute-done | bytes 229408 | tf_op jit(solution)/shard_map/ppermute | solution.py:333
  125.1 6.7 %collective-permute-done.11.refs_1_ = bf16[64,1792]{1,0:T(8,128)(2,1)S(1)} collective-permute-done((bf16[64,1792]{1,0:T(8,128)(2,1)S(1)}, bf16[64,1792]{1,0:T(8,128)(2,1)S(1)}, u32[]{:S(2)}, u32[]{:S(2)}) %collective-permute-start.11) | collective-permute-done | bytes 229408 | tf_op jit(solution)/shard_map/ppermute | solution.py:333
  131.8 7.1 %shard_map.80 = (bf16[128,3584]{1,0:T(8,128)(2,1)S(1)}, f32[128,3584]{1,0:T(8,128)S(1)}) custom-call(s32[2]{0:T(128)S(1)} %pad_add_fusion.place, bf16[64,1792]{1,0:T(8,128)(2,1)S(1)} %shard_map.79.refs_0_, bf16[64,1792]{1,0:T(8,128)(2,1)S(1)} %collective-permute-done.11.refs_1_, bf16[64,1792]{1,0:T(8,128)(2,1)S(1)} %collective-permute-done.12.refs_2_, ...), custom_call_target="tpu_custom_call" | custom-call | flops 3288334336 | bytes 12845056 | tf_op jit(solution)/shard_map/pallas_call | solution.py:209
  138.9 4.0 %collective-permute-start.15 = (bf16[128,3584]{1,0:T(8,128)(2,1)S(1)}, bf16[128,3584]{1,0:T(8,128)(2,1)S(1)}, u32[]{:S(2)}, u32[]{:S(2)}) collective-permute-start(bf16[128,3584]{1,0:T(8,128)(2,1)S(1)} %get-tuple-element.65), channel_id=1, source_target_pairs={{0,8},{8,0},{16,24},{24,16},{32,40},{40,32},{48,56},{56,48},{64,72... | collective-permute-start | bytes 2752520 | tf_op jit(solution)/shard_map/ppermute | solution.py:336
  142.9 7.1 %shard_map.82 = (bf16[128,3584]{1,0:T(8,128)(2,1)S(1)}, f32[128,3584]{1,0:T(8,128)S(1)}) custom-call(s32[2]{0:T(128)S(1)} %pad_add_fusion.place, bf16[64,1792]{1,0:T(8,128)(2,1)S(1)} %shard_map.81.refs_0_, bf16[64,1792]{1,0:T(8,128)(2,1)S(1)} %collective-permute-done.16.refs_1_, bf16[64,1792]{1,0:T(8,128)(2,1)S(1)} %collective-permute-done.17.refs_2_, ...), custom_call_target="tpu_custom_call" | custom-call | flops 3288334336 | bytes 12845056 | tf_op jit(solution)/shard_map/pallas_call | solution.py:209
  150.2 2.4 %collective-permute-done.19.refs_3_ = bf16[128,3584]{1,0:T(8,128)(2,1)S(1)} collective-permute-done((bf16[128,3584]{1,0:T(8,128)(2,1)S(1)}, bf16[128,3584]{1,0:T(8,128)(2,1)S(1)}, u32[]{:S(2)}, u32[]{:S(2)}) %collective-permute-start.19) | collective-permute-done | bytes 917536 | tf_op jit(solution)/shard_map/ppermute | solution.py:336
  152.9 25.5 %all_to_all.21 = bf16[8,32,3584]{2,1,0:T(8,128)(2,1)S(1)} all-to-all(bf16[8,32,3584]{2,1,0:T(8,128)(2,1)S(1)} %shard_map.83), channel_id=1, replica_groups={{0,16,32,48,64,80,96,112},{8,24,40,56,72,88,104,120},{1,17,33,49,65,81,..., dimensions={0} | all-to-all | bytes 3670016 | tf_op jit(solution)/shard_map/all_to_all | solution.py:313
  (62 shorter events, 18.3 us)
Async XLA Ops:
  0.0 11.6 %collective-permute-start.1 = (bf16[512,3584]{1,0:T(8,128)(2,1)}, bf16[512,3584]{1,0:T(8,128)(2,1)}, u32[]{:S(2)}, u32[]{:S(2)}) collective-permute-start(bf16[512,3584]{1,0:T(8,128)(2,1)} %grad.1), channel_id=1, source_target_pairs={{0,8},{8,0},{16,24},{24,16},{32,40},{40,32},{48,56},{56,48},{64,72... | collective-permute-start | bytes 11010056 | tf_op jit(solution)/shard_map/ppermute | solution.py:315
  9.5 2.1 %collective-permute-start = (bf16[512,512]{1,0:T(8,128)(2,1)}, bf16[512,512]{1,0:T(8,128)(2,1)S(1)}, u32[]{:S(2)}, u32[]{:S(2)}) collective-permute-start(bf16[512,512]{1,0:T(8,128)(2,1)} %shard_map.73.sel), channel_id=1, source_target_pairs={{0,8},{8,0},{16,24},{24,16},{32,40},{40,32},{48,56},{56,48},{64,72... | collective-permute-start | bytes 1572872 | tf_op jit(solution)/shard_map/ppermute | solution.py:317
  11.6 1.0 copy-start
  18.5 6.2 %copy-start.3 = (s32[512]{0:T(512)S(1)}, s32[512]{0:T(512)}, u32[]{:S(2)}) copy-start(s32[512]{0:T(512)} %param.7) | copy-start | bytes 6148
  18.5 29.6 %all-to-all-start = ((bf16[8,64,1792]{2,1,0:T(8,128)(2,1)}), bf16[8,64,1792]{2,1,0:T(8,128)(2,1)S(1)}, u32[]{:S(2)}, u32[]{:S(2)}) async-start(bf16[8,64,1792]{2,1,0:T(8,128)(2,1)} %bitcast.3), calls=%async_computation | async-start | bytes 3670016 | tf_op jit(solution)/shard_map/all_to_all | solution.py:313
  66.1 5.6 %collective-permute-start.2 = (bf16[256,1792]{1,0:T(8,128)(2,1)S(1)}, bf16[256,1792]{1,0:T(8,128)(2,1)S(1)}, u32[]{:S(2)}, u32[]{:S(2)}) collective-permute-start(bf16[256,1792]{1,0:T(8,128)(2,1)S(1)} %bitcast.26), channel_id=1, source_target_pairs={{0,8},{8,0},{16,24},{24,16},{32,40},{40,32},{48,56},{56,48},{64,72... | collective-permute-start | bytes 2752520 | tf_op jit(solution)/shard_map/ppermute | solution.py:336
  68.1 17.1 %all-to-all-start.2 = ((bf16[8,32,1792]{2,1,0:T(8,128)(2,1)}), bf16[8,32,1792]{2,1,0:T(8,128)(2,1)S(1)}, u32[]{:S(2)}, u32[]{:S(2)}) async-start(bf16[8,32,1792]{2,1,0:T(8,128)(2,1)} %broadcast_in_dim.59), calls=%async_computation.2 | async-start | bytes 1835008 | tf_op jit(solution)/shard_map/all_to_all | solution.py:313
  85.2 5.5 %collective-permute-start.6 = (bf16[256,1792]{1,0:T(8,128)(2,1)S(1)}, bf16[256,1792]{1,0:T(8,128)(2,1)S(1)}, u32[]{:S(2)}, u32[]{:S(2)}) collective-permute-start(bf16[256,1792]{1,0:T(8,128)(2,1)S(1)} %bitcast.24), channel_id=1, source_target_pairs={{0,8},{8,0},{16,24},{24,16},{32,40},{40,32},{48,56},{56,48},{64,72... | collective-permute-start | bytes 2752520 | tf_op jit(solution)/shard_map/ppermute | solution.py:336
  85.9 13.5 %collective-permute-start.3 = (bf16[64,1792]{1,0:T(8,128)(2,1)}, bf16[64,1792]{1,0:T(8,128)(2,1)S(1)}, u32[]{:S(2)}, u32[]{:S(2)}) collective-permute-start(bf16[64,1792]{1,0:T(8,128)(2,1)} %copy-done.2), channel_id=1, source_target_pairs={{0,1},{1,2},{2,3},{3,0},{4,5},{5,6},{6,7},{7,4},{8,9},{9,10},{10,1... | collective-permute-start | bytes 688136 | tf_op jit(solution)/shard_map/ppermute | solution.py:333
  87.1 13.9 %collective-permute-start.4 = (bf16[64,1792]{1,0:T(8,128)(2,1)}, bf16[64,1792]{1,0:T(8,128)(2,1)S(1)}, u32[]{:S(2)}, u32[]{:S(2)}) collective-permute-start(bf16[64,1792]{1,0:T(8,128)(2,1)} %copy-done.1), channel_id=1, source_target_pairs={{0,2},{1,3},{2,0},{3,1},{4,6},{5,7},{6,4},{7,5},{8,10},{9,11},{10,... | collective-permute-start | bytes 688136 | tf_op jit(solution)/shard_map/ppermute | solution.py:333
  89.6 11.5 %collective-permute-start.5 = (bf16[64,1792]{1,0:T(8,128)(2,1)S(1)}, bf16[64,1792]{1,0:T(8,128)(2,1)S(1)}, u32[]{:S(2)}, u32[]{:S(2)}) collective-permute-start(bf16[64,1792]{1,0:T(8,128)(2,1)S(1)} %get-tuple-element.44), channel_id=1, source_target_pairs={{0,3},{1,0},{2,1},{3,2},{4,7},{5,4},{6,5},{7,6},{8,11},{9,8},{10,9... | collective-permute-start | bytes 688136 | tf_op jit(solution)/shard_map/ppermute | solution.py:333
  98.2 12.7 %collective-permute-start.7 = (bf16[64,1792]{1,0:T(8,128)(2,1)}, bf16[64,1792]{1,0:T(8,128)(2,1)S(1)}, u32[]{:S(2)}, u32[]{:S(2)}) collective-permute-start(bf16[64,1792]{1,0:T(8,128)(2,1)} %get-tuple-element.48), channel_id=1, source_target_pairs={{0,1},{1,2},{2,3},{3,0},{4,5},{5,6},{6,7},{7,4},{8,9},{9,10},{10,1... | collective-permute-start | bytes 688136 | tf_op jit(solution)/shard_map/ppermute | solution.py:333
  98.6 12.3 %collective-permute-start.8 = (bf16[64,1792]{1,0:T(8,128)(2,1)S(1)}, bf16[64,1792]{1,0:T(8,128)(2,1)S(1)}, u32[]{:S(2)}, u32[]{:S(2)}) collective-permute-start(bf16[64,1792]{1,0:T(8,128)(2,1)S(1)} %get-tuple-element.49), channel_id=1, source_target_pairs={{0,2},{1,3},{2,0},{3,1},{4,6},{5,7},{6,4},{7,5},{8,10},{9,11},{10,... | collective-permute-start | bytes 688136 | tf_op jit(solution)/shard_map/ppermute | solution.py:333
  99.4 11.7 %collective-permute-start.9 = (bf16[64,1792]{1,0:T(8,128)(2,1)S(1)}, bf16[64,1792]{1,0:T(8,128)(2,1)S(1)}, u32[]{:S(2)}, u32[]{:S(2)}) collective-permute-start(bf16[64,1792]{1,0:T(8,128)(2,1)S(1)} %get-tuple-element.50), channel_id=1, source_target_pairs={{0,3},{1,0},{2,1},{3,2},{4,7},{5,4},{6,5},{7,6},{8,11},{9,8},{10,9... | collective-permute-start | bytes 688136 | tf_op jit(solution)/shard_map/ppermute | solution.py:333
  101.2 12.8 %collective-permute-start.10 = (bf16[64,1792]{1,0:T(8,128)(2,1)S(1)}, bf16[64,1792]{1,0:T(8,128)(2,1)S(1)}, u32[]{:S(2)}, u32[]{:S(2)}) collective-permute-start(bf16[64,1792]{1,0:T(8,128)(2,1)S(1)} %get-tuple-element.52), channel_id=1, source_target_pairs={{0,4},{1,5},{2,6},{3,7},{4,0},{5,1},{6,2},{7,3},{8,12},{9,13},{10,... | collective-permute-start | bytes 688136 | tf_op jit(solution)/shard_map/ppermute | solution.py:347
  111.2 7.1 %collective-permute-start.14 = (bf16[64,1792]{1,0:T(8,128)(2,1)S(1)}, bf16[64,1792]{1,0:T(8,128)(2,1)S(1)}, u32[]{:S(2)}, u32[]{:S(2)}) collective-permute-start(bf16[64,1792]{1,0:T(8,128)(2,1)S(1)} %get-tuple-element.62), channel_id=1, source_target_pairs={{0,4},{1,5},{2,6},{3,7},{4,0},{5,1},{6,2},{7,3},{8,12},{9,13},{10,... | collective-permute-start | bytes 688136 | tf_op jit(solution)/shard_map/ppermute | solution.py:352
  114.1 11.0 %collective-permute-start.13 = (bf16[64,1792]{1,0:T(8,128)(2,1)S(1)}, bf16[64,1792]{1,0:T(8,128)(2,1)S(1)}, u32[]{:S(2)}, u32[]{:S(2)}) collective-permute-start(bf16[64,1792]{1,0:T(8,128)(2,1)S(1)} %shard_map.79.refs_0_), channel_id=1, source_target_pairs={{0,3},{1,0},{2,1},{3,2},{4,7},{5,4},{6,5},{7,6},{8,11},{9,8},{10,9... | collective-permute-start | bytes 688136 | tf_op jit(solution)/shard_map/ppermute | solution.py:333
  117.6 7.6 %collective-permute-start.12 = (bf16[64,1792]{1,0:T(8,128)(2,1)S(1)}, bf16[64,1792]{1,0:T(8,128)(2,1)S(1)}, u32[]{:S(2)}, u32[]{:S(2)}) collective-permute-start(bf16[64,1792]{1,0:T(8,128)(2,1)S(1)} %shard_map.79.refs_0_), channel_id=1, source_target_pairs={{0,2},{1,3},{2,0},{3,1},{4,6},{5,7},{6,4},{7,5},{8,10},{9,11},{10,... | collective-permute-start | bytes 688136 | tf_op jit(solution)/shard_map/ppermute | solution.py:333
  117.6 14.2 %collective-permute-start.11 = (bf16[64,1792]{1,0:T(8,128)(2,1)S(1)}, bf16[64,1792]{1,0:T(8,128)(2,1)S(1)}, u32[]{:S(2)}, u32[]{:S(2)}) collective-permute-start(bf16[64,1792]{1,0:T(8,128)(2,1)S(1)} %shard_map.79.refs_0_), channel_id=1, source_target_pairs={{0,1},{1,2},{2,3},{3,0},{4,5},{5,6},{6,7},{7,4},{8,9},{9,10},{10,1... | collective-permute-start | bytes 688136 | tf_op jit(solution)/shard_map/ppermute | solution.py:333
  118.5 24.4 %collective-permute-start.18 = (bf16[64,1792]{1,0:T(8,128)(2,1)S(1)}, bf16[64,1792]{1,0:T(8,128)(2,1)S(1)}, u32[]{:S(2)}, u32[]{:S(2)}) collective-permute-start(bf16[64,1792]{1,0:T(8,128)(2,1)S(1)} %shard_map.81.refs_0_), channel_id=1, source_target_pairs={{0,3},{1,0},{2,1},{3,2},{4,7},{5,4},{6,5},{7,6},{8,11},{9,8},{10,9... | collective-permute-start | bytes 688136 | tf_op jit(solution)/shard_map/ppermute | solution.py:333
  122.9 20.0 %collective-permute-start.17 = (bf16[64,1792]{1,0:T(8,128)(2,1)S(1)}, bf16[64,1792]{1,0:T(8,128)(2,1)S(1)}, u32[]{:S(2)}, u32[]{:S(2)}) collective-permute-start(bf16[64,1792]{1,0:T(8,128)(2,1)S(1)} %shard_map.81.refs_0_), channel_id=1, source_target_pairs={{0,2},{1,3},{2,0},{3,1},{4,6},{5,7},{6,4},{7,5},{8,10},{9,11},{10,... | collective-permute-start | bytes 688136 | tf_op jit(solution)/shard_map/ppermute | solution.py:333
  125.1 17.8 %collective-permute-start.16 = (bf16[64,1792]{1,0:T(8,128)(2,1)S(1)}, bf16[64,1792]{1,0:T(8,128)(2,1)S(1)}, u32[]{:S(2)}, u32[]{:S(2)}) collective-permute-start(bf16[64,1792]{1,0:T(8,128)(2,1)S(1)} %shard_map.81.refs_0_), channel_id=1, source_target_pairs={{0,1},{1,2},{2,3},{3,0},{4,5},{5,6},{6,7},{7,4},{8,9},{9,10},{10,1... | collective-permute-start | bytes 688136 | tf_op jit(solution)/shard_map/ppermute | solution.py:333
  138.9 11.2 %collective-permute-start.15 = (bf16[128,3584]{1,0:T(8,128)(2,1)S(1)}, bf16[128,3584]{1,0:T(8,128)(2,1)S(1)}, u32[]{:S(2)}, u32[]{:S(2)}) collective-permute-start(bf16[128,3584]{1,0:T(8,128)(2,1)S(1)} %get-tuple-element.65), channel_id=1, source_target_pairs={{0,8},{8,0},{16,24},{24,16},{32,40},{40,32},{48,56},{56,48},{64,72... | collective-permute-start | bytes 2752520 | tf_op jit(solution)/shard_map/ppermute | solution.py:336
  150.0 2.6 %collective-permute-start.19 = (bf16[128,3584]{1,0:T(8,128)(2,1)S(1)}, bf16[128,3584]{1,0:T(8,128)(2,1)S(1)}, u32[]{:S(2)}, u32[]{:S(2)}) collective-permute-start(bf16[128,3584]{1,0:T(8,128)(2,1)S(1)} %get-tuple-element.68), channel_id=1, source_target_pairs={{0,8},{8,0},{16,24},{24,16},{32,40},{40,32},{48,56},{56,48},{64,72... | collective-permute-start | bytes 2752520 | tf_op jit(solution)/shard_map/ppermute | solution.py:336
  (2 other events, 1.4 us)
